TPU v7x, 32 devices: a whole 2x2x4 slice. The times are simulated.
32 devices in a mesh: wide: 8 (over z, x), narrow: 4 (over y, core).
Axes of the slice: x: 2, y: 2, z: 4, core: 2. Of those that a mesh axis runs over, the one named last changes fastest.
Arguments:
- images: bfloat16 [128, 50, 1024], P(('wide', 'narrow')), may hold values from -6 to 6
- cotangent: bfloat16 [128, 50, 1024], P(('wide', 'narrow')), may hold values from -6 to 6
- kept_tokens: int32 [128, 50], P('wide'), may hold values from 0 to 1, as said below
- owner_slots: int32 [2, 768], replicated, may hold values from 0 to 767, as said below
- master_blocks: float32 [2, 768, 128, 128], P(None, ('wide', 'narrow')), may hold values from -0.75 to 0.75
- small_params: float32 [2, 12288], P(None, ('wide', 'narrow')), may hold values from -1.2 to 1.4
- left_basis: float32 [2, 768, 128, 128], P(None, ('wide', 'narrow')), may hold values from -0.5 to 0.5
- right_basis: float32 [2, 768, 128, 128], P(None, ('wide', 'narrow')), may hold values from -0.5 to 0.5
- first_moment: float32 [2, 768, 128, 128], P(None, ('wide', 'narrow')), may hold values from -0.0011954564 to 0.0011954564
- second_moment: float32 [2, 768, 128, 128], P(None, ('wide', 'narrow')), may hold values from 1.9848832e-08 to 1.5879066e-07
- small_first: float32 [2, 12288], P(None, ('wide', 'narrow')), may hold values from -0.0047818255 to 0.0047818255
- small_second: float32 [2, 12288], P(None, ('wide', 'narrow')), may hold values from 3.175813e-07 to 2.5406505e-06
Outputs:
- block_output: bfloat16 [128, 50, 1024], P(('wide', 'narrow'))
- input_grad: float32 [128, 50, 1024], P(('wide', 'narrow'))
- grad_norm: float32 [1], replicated
- new_first: float32 [2, 768, 128, 128], P(None, ('wide', 'narrow'))
- new_second: float32 [2, 768, 128, 128], P(None, ('wide', 'narrow'))
- new_master: float32 [2, 768, 128, 128], P(None, ('wide', 'narrow'))
- new_weights_bf16: bfloat16 [2, 768, 128, 128], P(None, ('wide', 'narrow'))
- new_small_first: float32 [2, 12288], P(None, ('wide', 'narrow'))
- new_small_second: float32 [2, 12288], P(None, ('wide', 'narrow'))
- new_small: float32 [2, 12288], P(None, ('wide', 'narrow'))
- new_small_bf16: bfloat16 [2, 12288], P(None, ('wide', 'narrow'))
Inputs may be any that keep to these rules, and one draw needn't show every extreme that they name: `kept_tokens`: each image keeps at least 25 of its tokens; some image keeps all of them and some exactly 25. `owner_slots`: each row is a permutation of the slots 0 to 767. Call the share of a tile j, where a QKV tile in column c has j = (c % 8) // 2, an output tile in row r has j = r // 2, an up tile in column c has j = c // 8 and a down tile in row r has j = r // 8. Every tile of share j lies in a slot s with (s // 24) % 4 = j.
All inputs are finite; a program needn't handle non-finite values.
Results may differ from a plain program's by a relative error of at most 0.02.
Values may be sent and summed in bfloat16 or wider, within the bound.
No kernel may reach another device: no remote copies, remote signals or barrier semaphores. Data moves between devices by JAX's collectives and lax.ppermute only.
A program may use at most 192 MiB of HBM per device.

v0:
```python
import jax
import jax.numpy as jnp
from jax import lax
from jax.sharding import PartitionSpec as P

D = 1024
HEAD_DIM = 64
FF = 4096
S = 50
LAYERS = 2
BLK = 128


precise = lax.Precision.HIGHEST


def layer_norm(hidden, gain_vec, offset):
    centre = hidden - jnp.mean(hidden, axis=-1, keepdims=True)
    spread = jnp.mean(centre * centre, axis=-1, keepdims=True)
    return centre * lax.rsqrt(spread + 1e-06) * gain_vec + offset


def exact_gelu(upward):
    return jax.nn.gelu(upward, approximate=False)


def split_small(small_all):
    pieces = [small_all[piece_index * D : (piece_index + 1) * D] for piece_index in range(8)]
    return pieces + [small_all[8 * D :]]


def from_blocks(blocks, row_count, col_count):
    tiled = blocks.reshape(row_count // BLK, col_count // BLK, BLK, BLK)
    return tiled.transpose(0, 2, 1, 3).reshape(row_count, col_count)


def to_blocks(matrix):
    row_count, col_count = matrix.shape
    tiled = matrix.reshape(row_count // BLK, BLK, col_count // BLK, BLK)
    return tiled.transpose(0, 2, 1, 3).reshape(-1, BLK, BLK)


def tile_ids(shard, narrow_count):
    tile_rows = D // BLK
    shard_cols = D // (narrow_count * BLK)
    shard_hidden = FF // (narrow_count * BLK)
    count_qkv = tile_rows * 3 * tile_rows
    start_up = count_qkv + tile_rows * tile_rows
    start_down = start_up + tile_rows * (FF // BLK)
    row_part = jnp.arange(tile_rows)[:, None, None]
    third = jnp.arange(3)[None, :, None]
    column_part = jnp.arange(shard_cols)[None, None, :]
    qkv_ids = (
        row_part * 3 * tile_rows + third * tile_rows + shard * shard_cols + column_part
    ).reshape(-1)
    out_ids = (
        count_qkv
        + (shard * shard_cols + jnp.arange(shard_cols)[:, None]) * tile_rows
        + jnp.arange(tile_rows)[None, :]
    ).reshape(-1)
    up_ids = (
        start_up
        + jnp.arange(tile_rows)[:, None] * (FF // BLK)
        + shard * shard_hidden
        + jnp.arange(shard_hidden)[None, :]
    ).reshape(-1)
    down_ids = (
        start_down
        + (shard * shard_hidden + jnp.arange(shard_hidden)[:, None]) * tile_rows
        + jnp.arange(tile_rows)[None, :]
    ).reshape(-1)
    return jnp.concatenate([qkv_ids, out_ids, up_ids, down_ids])


def gathered_index(owners_layer, shard, per_device, narrow_count):
    slots = jnp.take(owners_layer, tile_ids(shard, narrow_count))
    return slots // per_device // narrow_count * per_device + slots % per_device


def assemble(gathered, index, narrow_count):
    ordered = jnp.take(gathered, index, axis=0)
    width_local = D // narrow_count
    hidden_local = FF // narrow_count
    count_qkv = D // BLK * (3 * width_local // BLK)
    count_out = width_local // BLK * (D // BLK)
    count_up = D // BLK * (hidden_local // BLK)
    start_up = count_qkv + count_out
    start_down = start_up + count_up
    return (
        from_blocks(ordered[:count_qkv], D, 3 * width_local),
        from_blocks(ordered[count_qkv:start_up], width_local, D),
        from_blocks(ordered[start_up:start_down], D, hidden_local),
        from_blocks(ordered[start_down:], hidden_local, D),
    )


def heads_of(flat, img_count):
    return flat.reshape(img_count, S, -1, HEAD_DIM)


def masked_scores(query_heads, key_heads, kept_keys):
    raw_scores = jnp.einsum(
        "nqhd,nkhd->nhqk", query_heads, key_heads, preferred_element_type=jnp.float32
    ) * HEAD_DIM ** (-0.5)
    return jnp.where(kept_keys, raw_scores, -1e30)


def local_small(small_all, shard, narrow_count):
    (
        gain_one,
        offset_one,
        bias_query,
        bias_value,
        bias_out,
        gain_two,
        offset_two,
        bias_down,
        bias_up,
    ) = split_small(small_all)
    width_local = D // narrow_count
    hidden_local = FF // narrow_count
    query_part = lax.dynamic_slice_in_dim(bias_query, shard * width_local, width_local)
    value_part = lax.dynamic_slice_in_dim(bias_value, shard * width_local, width_local)
    up_part = lax.dynamic_slice_in_dim(bias_up, shard * hidden_local, hidden_local)
    return (
        gain_one,
        offset_one,
        query_part,
        value_part,
        bias_out,
        gain_two,
        offset_two,
        bias_down,
        up_part,
    )


def forward_layer(hidden, matrices, small_all, kept_keys, img_group, shard, narrow_count):
    w_qkv, w_out, w_up, w_down = matrices
    (
        gain_one,
        offset_one,
        query_part,
        value_part,
        bias_out,
        gain_two,
        offset_two,
        bias_down,
        up_part,
    ) = local_small(small_all, shard, narrow_count)
    width_local = D // narrow_count
    normed, norm_back_one = jax.vjp(layer_norm, hidden, gain_one, offset_one)
    normed_all = lax.all_gather(normed.astype(jnp.bfloat16), "narrow", axis=0, tiled=True)
    projected = jnp.dot(normed_all, w_qkv, preferred_element_type=jnp.float32)
    query_heads = heads_of(
        (projected[:, :width_local] + query_part).astype(jnp.bfloat16), img_group
    )
    key_heads = heads_of(
        projected[:, width_local : 2 * width_local].astype(jnp.bfloat16), img_group
    )
    value_heads = heads_of(
        (projected[:, 2 * width_local :] + value_part).astype(jnp.bfloat16), img_group
    )
    scores = masked_scores(query_heads, key_heads, kept_keys)
    row_max = jnp.max(scores, axis=-1, keepdims=True)
    exp_scores = jnp.exp(scores - row_max)
    row_total = jnp.sum(exp_scores, axis=-1, keepdims=True)
    attention = exp_scores / row_total
    log_total = row_max + jnp.log(row_total)
    attended = (
        jnp.einsum(
            "nhqk,nkhd->nqhd",
            attention.astype(jnp.bfloat16),
            value_heads,
            preferred_element_type=jnp.float32,
        )
        .reshape(-1, width_local)
        .astype(jnp.bfloat16)
    )
    middle = hidden + (
        lax.psum_scatter(
            jnp.dot(attended, w_out, preferred_element_type=jnp.float32).astype(jnp.bfloat16),
            "narrow",
            scatter_dimension=0,
            tiled=True,
        ).astype(jnp.float32)
        + bias_out
    )
    normed_two, norm_back_two = jax.vjp(layer_norm, middle, gain_two, offset_two)
    normed_two_all = lax.all_gather(normed_two.astype(jnp.bfloat16), "narrow", axis=0, tiled=True)
    upward = jnp.dot(normed_two_all, w_up, preferred_element_type=jnp.float32) + up_part
    activated, gelu_back = jax.vjp(exact_gelu, upward)
    activated_bf = activated.astype(jnp.bfloat16)
    result = middle + (
        lax.psum_scatter(
            jnp.dot(activated_bf, w_down, preferred_element_type=jnp.float32).astype(jnp.bfloat16),
            "narrow",
            scatter_dimension=0,
            tiled=True,
        ).astype(jnp.float32)
        + bias_down
    )
    saved = (
        normed_all,
        query_heads,
        key_heads,
        value_heads,
        log_total,
        attended,
        norm_back_one,
        norm_back_two,
        normed_two_all,
        gelu_back,
        activated_bf,
    )
    return (result, saved)


def backward_layer(upstream, matrices, saved, kept_keys, img_group, shard, narrow_count):
    w_qkv, w_out, w_up, w_down = matrices
    (
        normed_all,
        query_heads,
        key_heads,
        value_heads,
        log_total,
        attended,
        norm_back_one,
        norm_back_two,
        normed_two_all,
        gelu_back,
        activated_bf,
    ) = saved
    width_local = D // narrow_count
    hidden_local = FF // narrow_count
    grad_down_own = upstream.astype(jnp.bfloat16)
    bias_down_grad = jnp.sum(grad_down_own.astype(jnp.float32), axis=0)
    grad_down = lax.all_gather(grad_down_own, "narrow", axis=0, tiled=True)
    row_count = grad_down.shape[0]
    w_down_grad = jnp.einsum(
        "nf,nd->fd", activated_bf, grad_down, preferred_element_type=jnp.float32
    )
    grad_act = jnp.einsum("nd,fd->nf", grad_down, w_down, preferred_element_type=jnp.float32)
    (grad_up_full,) = gelu_back(grad_act)
    grad_up = grad_up_full.astype(jnp.bfloat16)
    bias_up_grad = jnp.sum(grad_up.astype(jnp.float32), axis=0)
    w_up_grad = jnp.einsum("nd,nf->df", normed_two_all, grad_up, preferred_element_type=jnp.float32)
    grad_normed_two = lax.psum_scatter(
        jnp.einsum("nf,df->nd", grad_up, w_up, preferred_element_type=jnp.float32).astype(
            jnp.bfloat16
        ),
        "narrow",
        scatter_dimension=0,
        tiled=True,
    ).astype(jnp.float32)
    grad_middle_norm, gain_two_grad, offset_two_grad = norm_back_two(grad_normed_two)
    grad_middle = upstream + grad_middle_norm
    grad_branch_own = grad_middle.astype(jnp.bfloat16)
    bias_out_grad = jnp.sum(grad_branch_own.astype(jnp.float32), axis=0)
    grad_branch = lax.all_gather(grad_branch_own, "narrow", axis=0, tiled=True)
    w_out_grad = jnp.einsum("nc,nd->cd", attended, grad_branch, preferred_element_type=jnp.float32)
    grad_attended = jnp.einsum(
        "nd,cd->nc", grad_branch, w_out, preferred_element_type=jnp.float32
    ).astype(jnp.bfloat16)
    grad_heads = heads_of(grad_attended, img_group)
    scores = masked_scores(query_heads, key_heads, kept_keys)
    attention = jnp.exp(scores - log_total)
    grad_attention = jnp.einsum(
        "nqhd,nkhd->nhqk", grad_heads, value_heads, preferred_element_type=jnp.float32
    )
    grad_values = jnp.einsum(
        "nhqk,nqhd->nkhd",
        attention.astype(jnp.bfloat16),
        grad_heads,
        preferred_element_type=jnp.float32,
    )
    grad_scores = (
        attention * (grad_attention - jnp.sum(attention * grad_attention, axis=-1, keepdims=True))
    ).astype(jnp.bfloat16)
    grad_queries = jnp.einsum(
        "nhqk,nkhd->nqhd", grad_scores, key_heads, preferred_element_type=jnp.float32
    ) * HEAD_DIM ** (-0.5)
    grad_keys = jnp.einsum(
        "nhqk,nqhd->nkhd", grad_scores, query_heads, preferred_element_type=jnp.float32
    ) * HEAD_DIM ** (-0.5)
    grad_projected = jnp.concatenate(
        [
            grad_queries.reshape(row_count, width_local),
            grad_keys.reshape(row_count, width_local),
            grad_values.reshape(row_count, width_local),
        ],
        axis=1,
    ).astype(jnp.bfloat16)
    bias_query_grad = jnp.sum(grad_projected[:, :width_local].astype(jnp.float32), axis=0)
    bias_value_grad = jnp.sum(grad_projected[:, 2 * width_local :].astype(jnp.float32), axis=0)
    w_qkv_grad = jnp.einsum(
        "nd,ne->de", normed_all, grad_projected, preferred_element_type=jnp.float32
    )
    grad_normed = lax.psum_scatter(
        jnp.einsum("ne,de->nd", grad_projected, w_qkv, preferred_element_type=jnp.float32).astype(
            jnp.bfloat16
        ),
        "narrow",
        scatter_dimension=0,
        tiled=True,
    ).astype(jnp.float32)
    grad_hidden_norm, gain_one_grad, offset_one_grad = norm_back_one(grad_normed)
    downstream = grad_middle + grad_hidden_norm
    small_terms = jnp.zeros((8 * D + FF,), jnp.float32)
    small_terms = lax.dynamic_update_slice_in_dim(small_terms, gain_one_grad, 0, 0)
    small_terms = lax.dynamic_update_slice_in_dim(small_terms, offset_one_grad, D, 0)
    small_terms = lax.dynamic_update_slice_in_dim(
        small_terms, bias_query_grad, 2 * D + shard * width_local, 0
    )
    small_terms = lax.dynamic_update_slice_in_dim(
        small_terms, bias_value_grad, 3 * D + shard * width_local, 0
    )
    small_terms = lax.dynamic_update_slice_in_dim(small_terms, bias_out_grad, 4 * D, 0)
    small_terms = lax.dynamic_update_slice_in_dim(small_terms, gain_two_grad, 5 * D, 0)
    small_terms = lax.dynamic_update_slice_in_dim(small_terms, offset_two_grad, 6 * D, 0)
    small_terms = lax.dynamic_update_slice_in_dim(small_terms, bias_down_grad, 7 * D, 0)
    small_terms = lax.dynamic_update_slice_in_dim(
        small_terms, bias_up_grad, 8 * D + shard * hidden_local, 0
    )
    block_terms = jnp.concatenate(
        [
            to_blocks(w_qkv_grad),
            to_blocks(w_out_grad),
            to_blocks(w_up_grad),
            to_blocks(w_down_grad),
        ],
        axis=0,
    )
    return (downstream, block_terms, small_terms)


def rotate_in(left_basis, grads, right_basis):
    inner = jnp.einsum("lbki,lbkj->lbij", left_basis, grads, precision=precise)
    return jnp.einsum("lbij,lbjm->lbim", inner, right_basis, precision=precise)


def rotate_out(left_basis, update, right_basis):
    inner = jnp.einsum("lbik,lbkj->lbij", left_basis, update, precision=precise)
    return jnp.einsum("lbij,lbmj->lbim", inner, right_basis, precision=precise)


def shards(
    images,
    cotangent,
    kept_tokens,
    owner_slots,
    master_blocks,
    small_params,
    left_basis,
    right_basis,
    first_moment,
    second_moment,
    small_first,
    small_second,
):
    shard = lax.axis_index("narrow")
    narrow_count = lax.axis_size("narrow")
    per_device = master_blocks.shape[1]
    img_group = kept_tokens.shape[0]
    own_rows = images.shape[0] * S
    kept_keys = (kept_tokens > 0)[:, None, None, :]
    hidden = images.astype(jnp.float32).reshape(own_rows, D)
    layer_mats = []
    layer_index = []
    saved_list = []
    for which_layer in range(LAYERS):
        index = gathered_index(owner_slots[which_layer], shard, per_device, narrow_count)
        gathered = lax.all_gather(
            master_blocks[which_layer].astype(jnp.bfloat16), "wide", axis=0, tiled=True
        )
        small_all = lax.all_gather(
            small_params[which_layer].astype(jnp.bfloat16), ("wide", "narrow"), axis=0, tiled=True
        ).astype(jnp.float32)
        matrices = assemble(gathered, index, narrow_count)
        hidden, saved = forward_layer(
            hidden, matrices, small_all, kept_keys, img_group, shard, narrow_count
        )
        layer_mats.append(matrices)
        layer_index.append(index)
        saved_list.append(saved)
    block_output = hidden.astype(jnp.bfloat16).reshape(images.shape)
    upstream = cotangent.astype(jnp.float32).reshape(own_rows, D)
    block_locals = [None] * LAYERS
    small_locals = [None] * LAYERS
    for which_layer in reversed(range(LAYERS)):
        index = layer_index[which_layer]
        regathered = lax.all_gather(
            master_blocks[which_layer].astype(jnp.bfloat16), "wide", axis=0, tiled=True
        )
        matrices = assemble(regathered, index, narrow_count)
        upstream, block_terms, small_terms = backward_layer(
            upstream, matrices, saved_list[which_layer], kept_keys, img_group, shard, narrow_count
        )
        local_count = index.shape[0]
        inverse = (
            jnp.zeros((local_count,), jnp.int32)
            .at[index]
            .set(jnp.arange(local_count, dtype=jnp.int32))
        )
        block_locals[which_layer] = jnp.take(block_terms, inverse, axis=0)
        small_locals[which_layer] = small_terms
    input_grad = upstream.reshape(images.shape)
    grad_blocks = lax.psum_scatter(
        jnp.stack(block_locals).astype(jnp.bfloat16), "wide", scatter_dimension=1, tiled=True
    ).astype(jnp.float32)
    grad_small = lax.psum_scatter(
        jnp.stack(small_locals), ("wide", "narrow"), scatter_dimension=1, tiled=True
    )
    local_sum = jnp.sum(grad_blocks * grad_blocks) + jnp.sum(grad_small * grad_small)
    total_sum = lax.psum(local_sum, ("wide", "narrow"))
    grad_norm = jnp.sqrt(total_sum)
    clip_factor = 1.0 / jnp.maximum(grad_norm, 1.0)
    rotated = rotate_in(left_basis, clip_factor * grad_blocks, right_basis)
    new_first = 0.5 * first_moment + 0.5 * rotated
    new_second = 0.5 * second_moment + 0.5 * rotated * rotated
    direction = new_first / (jnp.sqrt(new_second) + 1e-08)
    new_master = master_blocks - 0.02 * rotate_out(left_basis, direction, right_basis)
    clipped_small = clip_factor * grad_small
    new_small_first = 0.5 * small_first + 0.5 * clipped_small
    new_small_second = 0.5 * small_second + 0.5 * clipped_small * clipped_small
    new_small = small_params - 0.3 * new_small_first / (jnp.sqrt(new_small_second) + 1e-08)
    return (
        block_output,
        input_grad,
        grad_norm.reshape(1),
        new_first,
        new_second,
        new_master,
        new_master.astype(jnp.bfloat16),
        new_small_first,
        new_small_second,
        new_small,
        new_small.astype(jnp.bfloat16),
    )


def solution(mesh):
    in_specs = (
        P(("wide", "narrow"), None, None),
        P(("wide", "narrow"), None, None),
        P("wide", None),
        P(),
        P(None, ("wide", "narrow"), None, None),
        P(None, ("wide", "narrow")),
        P(None, ("wide", "narrow"), None, None),
        P(None, ("wide", "narrow"), None, None),
        P(None, ("wide", "narrow"), None, None),
        P(None, ("wide", "narrow"), None, None),
        P(None, ("wide", "narrow")),
        P(None, ("wide", "narrow")),
    )
    out_specs = (
        P(("wide", "narrow"), None, None),
        P(("wide", "narrow"), None, None),
        P(),
        P(None, ("wide", "narrow"), None, None),
        P(None, ("wide", "narrow"), None, None),
        P(None, ("wide", "narrow"), None, None),
        P(None, ("wide", "narrow"), None, None),
        P(None, ("wide", "narrow")),
        P(None, ("wide", "narrow")),
        P(None, ("wide", "narrow")),
        P(None, ("wide", "narrow")),
    )
    return jax.shard_map(shards, mesh=mesh, in_specs=in_specs, out_specs=out_specs, check_vma=False)
```

profile of v0, /device:TPU:0, one launch (start us, length us, event | category | flops | bytes accessed | tf_op | source)
XLA Modules:
  0.0 1259.5 jit_solution(12566314765654116043)
XLA Ops:
  7.2 3.5 fusion.176
  22.3 44.8 %all-gather = bf16[1,12288]{1,0:T(2,128)(2,1)S(1)} all-gather(bf16[1,384]{1,0:T(2,128)(2,1)S(1)} %get-tuple-element.133), channel_id=2, replica_groups=mesh['wide'=8,'narrow'=4] {'wide','narrow'}, dimensions={1}, use_global_device_ids=true | all-gather | bytes 25344 | tf_op jit(solution)/shard_map/all_gather | solution.py:376
  75.6 36.9 %all-gather.33.cloned.1.call-done = bf16[1,192,128,128]{3,2,0,1:T(8,128)(2,1)} async-done(((bf16[1,24,128,128]{3,2,0,1:T(8,128)(2,1)}), bf16[1,192,128,128]{3,2,0,1:T(8,128)(2,1)}) %all-gather.33.cloned.1.call-update) | async-done | bytes 6291472 | tf_op jit(solution)/shard_map/all_gather | solution.py:373
  112.5 10.9 gather_fusion.3
  123.4 88.8 %all-gather.31.cloned.1.call-done = bf16[1,192,128,128]{3,2,0,1:T(8,128)(2,1)} async-done(((bf16[1,24,128,128]{3,2,0,1:T(8,128)(2,1)}), bf16[1,192,128,128]{3,2,0,1:T(8,128)(2,1)}) %all-gather.31.cloned.1.call-update) | async-done | bytes 6291472 | tf_op jit(solution)/shard_map/all_gather | solution.py:373
  212.2 10.9 gather_fusion.1
  223.1 8.5 broadcast_select_fusion
  236.7 2.8 copy.166
  239.5 3.4 fusion.75
  247.9 3.0 reshape.529
  257.5 2.9 convolution_convert_fusion.3
  260.5 26.9 %reduce-scatter.16.cloned.1.call-done = bf16[200,1024]{1,0:T(8,128)(2,1)} async-done(((bf16[800,1024]{1,0:T(8,128)(2,1)}), bf16[200,1024]{1,0:T(8,128)(2,1)}) %reduce-scatter.16.cloned.1.call-update) | async-done | bytes 409616 | tf_op jit(solution)/shard_map/reduce_scatter | solution.py:181
  295.5 2.8 copy.174
  301.0 11.1 all-gather.17.cloned.1.call-done
  312.1 12.9 %multiply_convert_fusion.1 = (bf16[800,1024]{1,0:T(8,128)(2,1)S(1)}, f32[800,1024]{1,0:T(8,128)}, f32[800,1024]{1,0:T(8,128)}) fusion(f32[1024]{0:T(1024)S(1)} %bitcast.418, bf16[800,1024]{1,0:T(8,128)(2,1)} %all-gather.17.cloned.1.call-done, bf16[128,8,8,128]{3,2,1,0:T(8,128)(2,1)} %bitcast.346), kind=kOutput, calls=%fused_computation.51 | convolution fusion | flops 1731788800 | bytes 11931648 | tf_op jit(solution)/shard_map/dot_general | solution.py:191
  326.2 3.0 fusion.54
  329.3 40.8 %all-gather.2 = bf16[1,12288]{1,0:T(2,128)(2,1)S(1)} all-gather(bf16[1,384]{1,0:T(2,128)(2,1)S(1)} %copy-done.96), channel_id=4, replica_groups=mesh['wide'=8,'narrow'=4] {'wide','narrow'}, dimensions={1}, use_global_device_ids=true | all-gather | bytes 25344 | tf_op jit(solution)/shard_map/all_gather | solution.py:376
  376.4 2.8 slice.224
  380.4 3.0 copy.175
  383.4 7.6 all-gather.19.cloned.1.call-done
  391.0 3.4 fusion.72
  408.5 3.0 convolution_convert_fusion.2
  411.6 28.5 %reduce-scatter.20.cloned.1.call-done = bf16[200,1024]{1,0:T(8,128)(2,1)} async-done(((bf16[800,1024]{1,0:T(8,128)(2,1)}), bf16[200,1024]{1,0:T(8,128)(2,1)}) %reduce-scatter.20.cloned.1.call-update) | async-done | bytes 409616 | tf_op jit(solution)/shard_map/reduce_scatter | solution.py:181
  451.7 3.0 fusion.174
  460.1 4.6 all-gather.21.cloned.1.call-done
  464.7 13.3 %multiply_convert_fusion = (bf16[800,1024]{1,0:T(8,128)(2,1)}, f32[800,1024]{1,0:T(8,128)}, f32[800,1024]{1,0:T(8,128)}) fusion(f32[1024]{0:T(1024)S(1)} %bitcast.421, bf16[800,1024]{1,0:T(8,128)(2,1)} %all-gather.21.cloned.1.call-done, bf16[128,8,8,128]{3,2,1,0:T(8,128)(2,1)} %bitcast.352), kind=kOutput, calls=%fused_computation.38 | convolution fusion | flops 1731788800 | bytes 11931648 | tf_op jit(solution)/shard_map/dot_general | solution.py:191
  478.0 8.7 all-gather.23.cloned.1.call-done
  486.7 7.7 convert_reduce_fusion
  495.6 3.1 fusion.57
  498.8 5.2 fusion.60
  504.1 23.1 %reduce-scatter.24.cloned.1.call-done = bf16[200,1024]{1,0:T(8,128)(2,1)} async-done(((bf16[800,1024]{1,0:T(8,128)(2,1)}), bf16[200,1024]{1,0:T(8,128)(2,1)}) %reduce-scatter.24.cloned.1.call-update) | async-done | bytes 409616 | tf_op jit(solution)/shard_map/reduce_scatter | solution.py:248
  529.5 28.6 %reduce-scatter.22.cloned.1.call-done = bf16[200,1024]{1,0:T(8,128)(2,1)} async-done(((bf16[800,1024]{1,0:T(8,128)(2,1)}), bf16[200,1024]{1,0:T(8,128)(2,1)}) %reduce-scatter.22.cloned.1.call-update) | async-done | bytes 409616 | tf_op jit(solution)/shard_map/reduce_scatter | solution.py:195
  562.4 20.1 %all-gather.25.cloned.1.call-done = bf16[800,1024]{1,0:T(8,128)(2,1)} async-done(((bf16[200,1024]{1,0:T(8,128)(2,1)}), bf16[800,1024]{1,0:T(8,128)(2,1)}) %all-gather.25.cloned.1.call-update) | async-done | bytes 1638416 | tf_op jit(solution)/shard_map/all_gather | solution.py:260
  582.4 2.9 convolution_convert_fusion.9
  612.2 4.0 convolution_convert_fusion.1
  616.3 28.5 %reduce-scatter.26.cloned.1.call-done = bf16[200,1024]{1,0:T(8,128)(2,1)} async-done(((bf16[800,1024]{1,0:T(8,128)(2,1)}), bf16[200,1024]{1,0:T(8,128)(2,1)}) %reduce-scatter.26.cloned.1.call-update) | async-done | bytes 409616 | tf_op jit(solution)/shard_map/reduce_scatter | solution.py:299
  649.3 3.8 convert_reduce_fusion.9
  653.2 20.1 %all-gather.27.cloned.1.call-done = bf16[800,1024]{1,0:T(8,128)(2,1)} async-done(((bf16[200,1024]{1,0:T(8,128)(2,1)}), bf16[800,1024]{1,0:T(8,128)(2,1)}) %all-gather.27.cloned.1.call-update) | async-done | bytes 1638416 | tf_op jit(solution)/shard_map/all_gather | solution.py:238
  673.3 7.7 convert_reduce_fusion.1
  682.1 3.1 fusion.51
  698.7 4.3 convolution_bitcast_fusion
  720.1 3.6 convolution_bitcast_fusion.4
  725.3 3.2 copy.210
  730.9 5.4 pad_maximum_fusion.1
  736.3 11.1 gather_fusion.5
  748.7 6.8 fusion.1
  759.6 2.9 convolution_convert_fusion.8
  789.2 4.0 convolution_convert_fusion
  795.8 4.3 convolution_bitcast_fusion.2
  812.5 3.2 copy.204
  818.2 5.4 pad_maximum_fusion
  823.6 11.0 gather_fusion.4
  836.4 6.8 fusion
  848.2 4.0 copy.239
  852.2 6.2 pad_maximum_fusion.2
  859.9 9.5 copy.413
  874.2 3.0 add_add_fusion.4
  879.5 88.0 %reduce-scatter.34.cloned.1.call-done = f32[384,2]{1,0:T(8,128)} async-done(((f32[12288,2]{1,0:T(8,128)}), f32[384,2]{1,0:T(8,128)}) %reduce-scatter.34.cloned.1.call-update) | async-done | bytes 3088
  969.2 208.2 %reduce-scatter.32.cloned.1.call-done = bf16[24,32768]{1,0:T(8,128)(2,1)} async-done(((bf16[192,32768]{1,0:T(8,128)(2,1)}), bf16[24,32768]{1,0:T(8,128)(2,1)}) %reduce-scatter.32.cloned.1.call-update) | async-done | bytes 1572880
  1185.5 39.2 %psum.7 = f32[]{:T(128)} all-reduce(f32[]{:T(128)S(6)} %add.616), channel_id=1, replica_groups=mesh['wide'=8,'narrow'=4] {'wide','narrow'}, use_global_device_ids=true, to_apply=%region_54.58 | all-reduce | flops 1 | bytes 8 | tf_op jit(solution)/shard_map/psum | solution.py:415
  1225.5 7.4 fusion.22
  1233.0 4.5 fusion.23
  1237.5 4.9 fusion.24
  1242.5 8.2 fusion.182
  (481 shorter events, 235.7 us)
Async XLA Ops:
  7.2 1225.8 %copy-start = (f32[2,24,128,128]{3,2,1,0:T(8,128)S(1)}, f32[2,24,128,128]{3,2,1,0:T(8,128)}, u32[]{:S(2)}) copy-start(f32[2,24,128,128]{3,2,1,0:T(8,128)} %param.25) | copy-start | bytes 9437188
  7.2 105.3 %all-gather.33.cloned.1.call-start = ((), (), s32[]{:S(2)}) async-start(), calls=%async_computation.27 | async-start | bytes 7077888 | tf_op jit(solution)/shard_map/all_gather | solution.py:373
  10.7 201.4 %all-gather.31.cloned.1.call-start = ((), (), s32[]{:S(2)}) async-start(), calls=%async_computation.26 | async-start | bytes 7077888 | tf_op jit(solution)/shard_map/all_gather | solution.py:373
  11.5 228.0 %all-gather.15.cloned.1.call-start = ((), (), s32[]{:S(2)}) async-start(), calls=%async_computation.10 | async-start | bytes 2048000 | tf_op jit(solution)/shard_map/all_gather | solution.py:153
  18.6 53.4 %copy-start.97 = (s32[2,768]{1,0:T(2,128)S(1)}, s32[2,768]{1,0:T(2,128)}, u32[]{:S(2)}) copy-start(s32[2,768]{1,0:T(2,128)} %param.21) | copy-start | bytes 18436
  18.6 56.5 %copy-start.95 = (s32[16,50]{1,0:T(8,128)S(1)}, s32[16,50]{1,0:T(8,128)}, u32[]{:S(2)}) copy-start(s32[16,50]{1,0:T(8,128)} %param.20) | copy-start | bytes 9604
  18.8 52.9 %copy-start.89 = (f32[200]{0:T(256)}, f32[200]{0:T(256)S(1)}, u32[]{:S(2)}) copy-start(f32[200]{0:T(256)S(1)} %add.531) | copy-start | bytes 2404
  18.8 52.5 %copy-start.79 = (f32[200]{0:T(256)}, f32[200]{0:T(256)S(1)}, u32[]{:S(2)}) copy-start(f32[200]{0:T(256)S(1)} %rsqrt.40) | copy-start | bytes 2404
  71.1 216.3 %reduce-scatter.16.cloned.1.call-start = ((), (), s32[]{:S(2)}) async-start(), calls=%async_computation.11 | async-start | bytes 2048000 | tf_op jit(solution)/shard_map/reduce_scatter | solution.py:181
  75.0 48.4 %copy-start.106 = (s32[192]{0:T(256)}, s32[192]{0:T(256)S(1)}, u32[]{:S(2)}) copy-start(s32[192]{0:T(256)S(1)} %get-tuple-element.94) | copy-start | bytes 2308
  75.0 48.4 %copy-start.107 = (s32[192]{0:T(256)}, s32[192]{0:T(256)S(1)}, u32[]{:S(2)}) copy-start(s32[192]{0:T(256)S(1)} %get-tuple-element.135) | copy-start | bytes 2308
  257.4 31.6 %copy-start.19 = (bf16[800,256]{1,0:T(8,128)(2,1)}, bf16[800,256]{1,0:T(8,128)(2,1)S(1)}, u32[]{:S(2)}) copy-start(bf16[800,256]{1,0:T(8,128)(2,1)S(1)} %convert_element_type.229) | copy-start | bytes 1228804
  260.4 51.6 %all-gather.17.cloned.1.call-start = ((), (), s32[]{:S(2)}) async-start(), calls=%async_computation.12 | async-start | bytes 2048000 | tf_op jit(solution)/shard_map/all_gather | solution.py:190
  291.9 79.5 %reduce-scatter.18.cloned.1.call-start = ((), (), s32[]{:S(2)}) async-start(), calls=%async_computation.13 | async-start | bytes 2048000 | tf_op jit(solution)/shard_map/reduce_scatter | solution.py:195
  292.7 19.3 %copy-start.103 = (f32[1,1024]{1,0:T(1,128)}, f32[1,1024]{1,0:T(1,128)S(1)}, u32[]{:S(2)}) copy-start(f32[1,1024]{1,0:T(1,128)S(1)} %constant_dynamic-slice_fusion.3) | copy-start | bytes 12292
  312.1 14.1 %copy-start.40 = (bf16[8,8,128,128]{3,1,2,0:T(8,128)(2,1)S(1)}, bf16[8,8,128,128]{3,1,2,0:T(8,128)(2,1)}, u32[]{:S(2)}) copy-start(bf16[8,8,128,128]{3,1,2,0:T(8,128)(2,1)} %copy.174) | copy-start | bytes 6291460
  326.2 45.2 %copy-start.65 = (f32[1,1024]{1,0:T(1,128)S(1)}, f32[1,1024]{1,0:T(1,128)}, u32[]{:S(2)}) copy-start(f32[1,1024]{1,0:T(1,128)} %get-tuple-element.131) | copy-start | bytes 12292
  329.2 61.8 %all-gather.19.cloned.1.call-start = ((), (), s32[]{:S(2)}) async-start(), calls=%async_computation.14 | async-start | bytes 2048000 | tf_op jit(solution)/shard_map/all_gather | solution.py:153
  374.7 65.3 %reduce-scatter.20.cloned.1.call-start = ((), (), s32[]{:S(2)}) async-start(), calls=%async_computation.15 | async-start | bytes 2048000 | tf_op jit(solution)/shard_map/reduce_scatter | solution.py:181
  408.5 33.2 %copy-start.21 = (bf16[800,256]{1,0:T(8,128)(2,1)}, bf16[800,256]{1,0:T(8,128)(2,1)S(1)}, u32[]{:S(2)}) copy-start(bf16[800,256]{1,0:T(8,128)(2,1)S(1)} %convert_element_type.245) | copy-start | bytes 1228804
  411.5 53.2 %all-gather.21.cloned.1.call-start = ((), (), s32[]{:S(2)}) async-start(), calls=%async_computation.16 | async-start | bytes 2048000 | tf_op jit(solution)/shard_map/all_gather | solution.py:190
  444.6 42.2 %all-gather.23.cloned.1.call-start = ((), (), s32[]{:S(2)}) async-start(), calls=%async_computation.18 | async-start | bytes 2048000 | tf_op jit(solution)/shard_map/all_gather | solution.py:238
  450.8 76.4 %reduce-scatter.24.cloned.1.call-start = ((), (), s32[]{:S(2)}) async-start(), calls=%async_computation.19 | async-start | bytes 2048000 | tf_op jit(solution)/shard_map/reduce_scatter | solution.py:248
  486.7 8.9 copy-start.41
  498.7 59.4 %reduce-scatter.22.cloned.1.call-start = ((), (), s32[]{:S(2)}) async-start(), calls=%async_computation.17 | async-start | bytes 2048000 | tf_op jit(solution)/shard_map/reduce_scatter | solution.py:195
  498.8 28.5 %copy-start.58 = (f32[1,1024]{1,0:T(1,128)S(1)}, f32[1,1024]{1,0:T(1,128)}, u32[]{:S(2)}) copy-start(f32[1,1024]{1,0:T(1,128)} %get-tuple-element.117) | copy-start | bytes 12292
  498.8 28.5 %copy-start.63 = (f32[200]{0:T(256)S(1)}, f32[200]{0:T(256)}, u32[]{:S(2)}) copy-start(f32[200]{0:T(256)} %copy-done.62) | copy-start | bytes 2404
  498.8 28.5 %copy-start.77 = (f32[200]{0:T(256)S(1)}, f32[200]{0:T(256)}, u32[]{:S(2)}) copy-start(f32[200]{0:T(256)} %copy-done.76) | copy-start | bytes 2404
  498.8 30.7 %copy-start.88 = (f32[200]{0:T(256)S(1)}, f32[200]{0:T(256)}, u32[]{:S(2)}) copy-start(f32[200]{0:T(256)} %copy-done.87) | copy-start | bytes 2404
  498.8 59.3 %copy-start.66 = (f32[1,1024]{1,0:T(1,128)S(1)}, f32[1,1024]{1,0:T(1,128)}, u32[]{:S(2)}) copy-start(f32[1,1024]{1,0:T(1,128)} %get-tuple-element.116) | copy-start | bytes 12292
  504.1 58.3 %copy-start.51 = (f32[16,4,50]{2,1,0:T(4,128)S(1)}, f32[16,4,50]{2,1,0:T(4,128)}, u32[]{:S(2)}) copy-start(f32[16,4,50]{2,1,0:T(4,128)} %copy-done.50) | copy-start | bytes 38404
  504.1 58.3 %copy-start.53 = (f32[16,4,50]{2,1,0:T(4,128)S(1)}, f32[16,4,50]{2,1,0:T(4,128)}, u32[]{:S(2)}) copy-start(f32[16,4,50]{2,1,0:T(4,128)} %copy-done.52) | copy-start | bytes 38404
  504.1 78.3 %all-gather.25.cloned.1.call-start = ((), (), s32[]{:S(2)}) async-start(), calls=%async_computation.20 | async-start | bytes 2048000 | tf_op jit(solution)/shard_map/all_gather | solution.py:260
  562.3 82.5 %reduce-scatter.26.cloned.1.call-start = ((), (), s32[]{:S(2)}) async-start(), calls=%async_computation.21 | async-start | bytes 2048000 | tf_op jit(solution)/shard_map/reduce_scatter | solution.py:299
  599.0 12.0 copy-start.22
  612.2 32.6 %copy-start.57 = (f32[1,1024]{1,0:T(1,128)S(1)}, f32[1,1024]{1,0:T(1,128)}, u32[]{:S(2)}) copy-start(f32[1,1024]{1,0:T(1,128)} %copy-done.56) | copy-start | bytes 12292
  612.2 32.6 %copy-start.60 = (f32[200]{0:T(256)S(1)}, f32[200]{0:T(256)}, u32[]{:S(2)}) copy-start(f32[200]{0:T(256)} %copy-done.59) | copy-start | bytes 2404
  612.2 34.8 %copy-start.86 = (f32[200]{0:T(256)S(1)}, f32[200]{0:T(256)}, u32[]{:S(2)}) copy-start(f32[200]{0:T(256)} %copy-done.85) | copy-start | bytes 2404
  612.2 34.8 %copy-start.82 = (f32[200]{0:T(256)S(1)}, f32[200]{0:T(256)}, u32[]{:S(2)}) copy-start(f32[200]{0:T(256)} %copy-done.81) | copy-start | bytes 2404
  616.2 33.1 %copy-start.93 = (f32[200]{0:T(256)S(1)}, f32[200]{0:T(256)}, u32[]{:S(2)}) copy-start(f32[200]{0:T(256)} %copy-done.92) | copy-start | bytes 2404
  616.2 57.1 %all-gather.27.cloned.1.call-start = ((), (), s32[]{:S(2)}) async-start(), calls=%async_computation.22 | async-start | bytes 2048000 | tf_op jit(solution)/shard_map/all_gather | solution.py:238
  646.9 26.3 %copy-start.104 = (f32[1,1024]{1,0:T(1,128)S(1)}, f32[1,1024]{1,0:T(1,128)}, u32[]{:S(2)}) copy-start(f32[1,1024]{1,0:T(1,128)} %copy-done.103) | copy-start | bytes 12292
  653.1 60.7 %reduce-scatter.28.cloned.1.call-start = ((), (), s32[]{:S(2)}) async-start(), calls=%async_computation.23 | async-start | bytes 2048000 | tf_op jit(solution)/shard_map/reduce_scatter | solution.py:248
  673.3 8.9 copy-start.39
  682.1 13.2 %copy-start.20 = (bf16[800,256]{1,0:T(8,128)(2,1)S(1)}, bf16[800,256]{1,0:T(8,128)(2,1)}, u32[]{:S(2)}) copy-start(bf16[800,256]{1,0:T(8,128)(2,1)} %copy-done.19) | copy-start | bytes 1228804
  685.2 74.4 %all-gather.29.cloned.1.call-start = ((), (), s32[]{:S(2)}) async-start(), calls=%async_computation.24 | async-start | bytes 2048000 | tf_op jit(solution)/shard_map/all_gather | solution.py:260
  720.0 123.2 %reduce-scatter.30.cloned.1.call-start = ((), (), s32[]{:S(2)}) async-start(), calls=%async_computation.25 | async-start | bytes 2048000 | tf_op jit(solution)/shard_map/reduce_scatter | solution.py:299
  736.3 11.1 copy-start.23
  748.6 9.2 copy-start.69
  748.6 9.8 copy-start.68
  748.6 10.4 copy-start.67
  755.4 9.6 copy-start.42
  793.2 174.3 %reduce-scatter.34.cloned.1.call-start = ((), (), s32[]{:S(2)}) async-start(), calls=%async_computation.29 | async-start | bytes 6488064
  836.4 8.5 copy-start.90
  836.4 8.5 copy-start.80
  836.4 10.8 copy-start.98
  836.4 10.8 copy-start.73
  836.4 10.8 copy-start.71
  836.4 10.8 copy-start.70
  836.4 10.9 copy-start.78
  836.4 10.9 copy-start.105
  852.2 325.1 %reduce-scatter.32.cloned.1.call-start = ((), (), s32[]{:S(2)}) async-start(), calls=%async_computation.28 | async-start | bytes 14155776
  1242.4 8.3 copy-start.83
  1242.5 8.3 copy-start.108
  (74 other events, 201.8 us)
Sparse Core Ops, SparseCore 0:
  10.9 101.6 all-gather.32
  115.3 96.8 all-gather.30
  214.3 18.1 all-gather.14
  260.5 26.7 reduce-scatter.15
  292.0 19.9 all-gather.16
  329.3 28.5 reduce-scatter.17
  374.8 16.0 all-gather.18
  411.6 28.3 reduce-scatter.19
  444.7 19.9 all-gather.20
  466.7 19.9 all-gather.22
  498.8 28.3 reduce-scatter.23
  529.7 28.3 reduce-scatter.21
  562.4 19.9 all-gather.24
  616.3 28.3 reduce-scatter.25
  653.2 19.9 all-gather.26
  685.3 28.4 reduce-scatter.27
  720.2 19.9 all-gather.28
  793.3 28.4 reduce-scatter.29
  852.3 115.1 reduce-scatter.33
  970.9 206.3 reduce-scatter.31
where the time goes:
time: 1270 us; the launch traced here: 1260 us
  waiting for transfers between devices  633 us (50%)
  local copies, waits for them, and re-layouts  229 us (18%)
  matrix products  150 us (12%)
  blocking collectives  125 us (10%)
  other arithmetic  102 us (8%)
  between operations  19.2 us (2%)
    unnamed x22, waiting for transfers between devices  297 us
    all_gather x2, waiting for transfers between devices, shards(): lax.all_gather(master_blocks[which_layer].astype(jnp.bfloat16), 'wide', a...  126 us
    all_gather x2, blocking collectives, shards(): lax.all_gather(small_params[which_layer].astype(jnp.bfloat16), ('wide', '...  85.6 us
    reduce_scatter x2, waiting for transfers between devices, forward_layer(): lax.psum_scatter(jnp.dot(attended, w_out, preferred_element_type=jnp.floa...  55.4 us
    unnamed x255, local copies, waits for them, and re-layouts  52.1 us
    psum x1, blocking collectives, shards(): total_sum = lax.psum(local_sum, ('wide', 'narrow'))  39.2 us
    all_gather x2, waiting for transfers between devices, backward_layer(): grad_down = lax.all_gather(grad_down_own, 'narrow', axis=0, tiled=True)  28.8 us
    reduce_scatter x2, waiting for transfers between devices, forward_layer(): lax.psum_scatter(jnp.dot(activated_bf, w_down, preferred_element_type=jnp...  28.6 us
  transfers between devices with their start and end apart: 20, of which 16 were waited for; matrix products, arithmetic and copies ran while one was open for 20% of the time, Pallas kernels for 0%

commit v1 on v0

v1 whole, which is shorter than its diff:
```python
import functools

import jax
import jax.numpy as jnp
from jax import lax
from jax.experimental import pallas as pl
from jax.experimental.pallas import tpu as pltpu
from jax.sharding import PartitionSpec as P

D = 1024
HEAD_DIM = 64
FF = 4096
S = 50
LAYERS = 2
BLK = 128
NARROW = 4

BF = jnp.bfloat16
F32 = jnp.float32

WID = D // 2
HID = FF // 2
SHARE_TILES = 192
ATT_ROWS = 2 * D
MLP_ROWS = 4 * D

CORE = [(j, j ^ 1) for j in range(NARROW)]
ACROSS = [(j, j ^ 2) for j in range(NARROW)]
ANY = pl.BlockSpec(memory_space=pl.ANY)
SMEM = pl.BlockSpec(memory_space=pltpu.SMEM)
VMEM = pl.BlockSpec(memory_space=pltpu.VMEM)


def params(mib):
    return pltpu.CompilerParams(vmem_limit_bytes=mib << 20)


def cost(flops, nbytes):
    return pl.CostEstimate(flops=flops, bytes_accessed=nbytes, transcendentals=0)


def dot(a, b):
    return jnp.dot(a, b, preferred_element_type=F32)


def dot_nt(a, b):
    return lax.dot_general(a, b, (((1,), (1,)), ((), ())), preferred_element_type=F32)


def dot_tn(a, b):
    return lax.dot_general(a, b, (((0,), (0,)), ((), ())), preferred_element_type=F32)


def stats(x):
    centre = x - jnp.mean(x, axis=-1, keepdims=True)
    spread = jnp.mean(centre * centre, axis=-1, keepdims=True)
    return centre, lax.rsqrt(spread + 1e-06)


def norm_back(grad, xhat, rstd, gain):
    gn = grad * gain
    return rstd * (
        gn
        - jnp.mean(gn, axis=-1, keepdims=True)
        - xhat * jnp.mean(gn * xhat, axis=-1, keepdims=True)
    )


def key_bias(kept_row, rows):
    def image_of(dim):
        pos = lax.broadcasted_iota(jnp.int32, (rows, rows), dim)
        image = jnp.zeros((rows, rows), jnp.int32)
        for edge in range(S, rows, S):
            image = image + (pos >= edge).astype(jnp.int32)
        return image

    allowed = (image_of(0) == image_of(1)) & (kept_row > 0.0)
    return jnp.where(allowed, 0.0, -1e30)


def lane_half(x, half):
    lane = lax.broadcasted_iota(jnp.int32, x.shape, 1)
    keep = (lane < HEAD_DIM) if half == 0 else (lane >= HEAD_DIM)
    return jnp.where(keep, x, jnp.zeros_like(x))


def attention_forward(first, *refs):
    if first:
        x_ref, vecs, kept, weights, n1_ref, qkv_ref, lse_ref, att_ref, part_ref = refs
        hidden = x_ref[...].astype(F32)
    else:
        (mid_ref, own_ref, got_ref, prev, vecs, kept, weights) = refs[:7]
        hidden_ref, n1_ref, qkv_ref, lse_ref, att_ref, part_ref = refs[7:]
        hidden = mid_ref[...] + (
            own_ref[...].astype(F32) + got_ref[...].astype(F32) + prev[6:7, :]
        )
        hidden_ref[...] = hidden
    rows = hidden.shape[0]
    centre, rstd = stats(hidden)
    n1 = (centre * rstd * vecs[0:1, :] + vecs[1:2, :]).astype(BF)
    n1_ref[...] = n1
    qkv_ref[:, 0:WID] = (dot(n1, weights[0:D, 0:WID]) + vecs[2:3, 0:WID]).astype(BF)
    qkv_ref[:, WID : 2 * WID] = dot(n1, weights[0:D, WID:D]).astype(BF)
    qkv_ref[:, 2 * WID :] = (dot(n1, weights[D : 2 * D, 0:WID]) + vecs[2:3, WID:D]).astype(BF)
    bias = key_bias(kept[0:1, :], rows)
    lane = lax.broadcasted_iota(jnp.int32, (rows, BLK), 1)
    lse_all = jnp.zeros((rows, BLK), F32)
    for pair in range(WID // BLK):
        cols = slice(pair * BLK, (pair + 1) * BLK)
        q = qkv_ref[:, cols] * jnp.asarray(0.125, BF)
        k = qkv_ref[:, WID + pair * BLK : WID + (pair + 1) * BLK]
        v = qkv_ref[:, 2 * WID + pair * BLK : 2 * WID + (pair + 1) * BLK]
        outs = []
        for half in range(2):
            scores = dot_nt(lane_half(q, half), k) + bias
            top = jnp.max(scores, axis=-1, keepdims=True)
            raised = jnp.exp(scores - top)
            total = jnp.sum(raised, axis=-1, keepdims=True)
            outs.append(dot((raised * (1.0 / total)).astype(BF), v))
            lse_all = jnp.where(lane == 2 * pair + half, top + jnp.log(total), lse_all)
        att_ref[:, cols] = jnp.where(lane < HEAD_DIM, outs[0], outs[1]).astype(BF)
    lse_ref[...] = lse_all
    att = att_ref[...]
    part_ref[:, 0:WID] = dot(att, weights[D : D + WID, WID:D]).astype(BF)
    part_ref[:, WID:D] = dot(att, weights[D + WID : 2 * D, WID:D]).astype(BF)


def call_attention_forward(first, operands, vecs, kept, weights):
    rows = operands[0].shape[0]
    outs = [
        jax.ShapeDtypeStruct((rows, D), BF),
        jax.ShapeDtypeStruct((rows, 3 * WID), BF),
        jax.ShapeDtypeStruct((rows, BLK), F32),
        jax.ShapeDtypeStruct((rows, WID), BF),
        jax.ShapeDtypeStruct((rows, D), BF),
    ]
    if not first:
        outs = [jax.ShapeDtypeStruct((rows, D), F32)] + outs
    args = list(operands) + [vecs, kept, weights]
    return pl.pallas_call(
        functools.partial(attention_forward, first),
        out_shape=outs,
        grid=(1,),
        in_specs=[full(*a.shape) for a in args[:-1]] + [full(ATT_ROWS, D)],
        out_specs=[full(*o.shape) for o in outs],
        compiler_params=params(32),
        cost_estimate=cost(2 * rows * D * 4 * WID * 2, 6 << 20),
        name="attention_forward",
    )(*args)


STEPS = 4
STEP_HID = HID // STEPS


def mlp_forward(hid_ref, own_ref, got_ref, vecs, up_ref, down_ref, *rest):
    mid_ref, n2_ref, act_ref, slope_ref, part_ref, total = rest
    step = pl.program_id(0)

    @pl.when(step == 0)
    def _():
        middle = hid_ref[...].astype(F32) + (
            own_ref[...].astype(F32) + got_ref[...].astype(F32) + vecs[3:4, :]
        )
        mid_ref[...] = middle
        centre, rstd = stats(middle)
        n2_ref[...] = (centre * rstd * vecs[4:5, :] + vecs[5:6, :]).astype(BF)

    row = 7 + step // 2
    bias = jnp.where(
        step % 2 == 0, vecs[pl.ds(row, 1), 0:STEP_HID], vecs[pl.ds(row, 1), STEP_HID:D]
    )
    upward = dot(n2_ref[...], up_ref[...]) + bias
    cdf = 0.5 + 0.5 * lax.erf(upward * 0.7071067811865476)
    act = (upward * cdf).astype(BF)
    act_ref[...] = act
    slope_ref[...] = (
        cdf + upward * (jnp.exp(-0.5 * upward * upward) * 0.3989422804014327)
    ).astype(BF)
    term = dot(act, down_ref[...])

    @pl.when(step == 0)
    def _():
        total[...] = term

    @pl.when((step > 0) & (step < STEPS - 1))
    def _():
        total[...] += term

    @pl.when(step == STEPS - 1)
    def _():
        part_ref[...] = (total[...] + term).astype(BF)


def full(rows, cols):
    return pl.BlockSpec((rows, cols), lambda s: (0, 0))


def mlp_weight_specs():
    return [
        pl.BlockSpec((D, STEP_HID), lambda s: (2 + s // 2, s % 2)),
        pl.BlockSpec((STEP_HID, D), lambda s: (2 * STEPS + s, 0)),
    ]


def call_mlp_forward(hidden, own, got, vecs, weights):
    rows = hidden.shape[0]
    return pl.pallas_call(
        mlp_forward,
        grid=(STEPS,),
        out_shape=[
            jax.ShapeDtypeStruct((rows, D), F32),
            jax.ShapeDtypeStruct((rows, D), BF),
            jax.ShapeDtypeStruct((rows, HID), BF),
            jax.ShapeDtypeStruct((rows, HID), BF),
            jax.ShapeDtypeStruct((rows, D), BF),
        ],
        in_specs=[full(rows, D), full(rows, D), full(rows, D), full(16, D)] + mlp_weight_specs(),
        out_specs=[
            full(rows, D),
            full(rows, D),
            pl.BlockSpec((rows, STEP_HID), lambda s: (0, s)),
            pl.BlockSpec((rows, STEP_HID), lambda s: (0, s)),
            full(rows, D),
        ],
        scratch_shapes=[pltpu.VMEM((rows, D), F32)],
        compiler_params=params(32),
        cost_estimate=cost(2 * rows * D * 2 * HID * 2, 12 << 20),
        name="mlp_forward",
    )(hidden, own, got, vecs, weights, weights)


def mlp_backward(first, *refs):
    if first:
        grad_ref, mid_ref, slope_ref, vecs, down_ref, up_ref = refs[:6]
        gd_ref, gu_ref, part_ref, sums_ref, total = refs[6:]
    else:
        (gm_ref, own_ref, got_ref, hid_ref, above) = refs[:5]
        mid_ref, slope_ref, vecs, down_ref, up_ref = refs[5:10]
        grad_out_ref, gd_ref, gu_ref, part_ref, sums_ref, total = refs[10:]
    step = pl.program_id(0)

    @pl.when(step == 0)
    def _():
        if first:
            gd_ref[...] = grad_ref[...]
        else:
            centre, rstd = stats(hid_ref[...])
            grad = own_ref[...].astype(F32) + got_ref[...].astype(F32)
            grad_hidden = gm_ref[...] + norm_back(grad, centre * rstd, rstd, above[0:1, :])
            grad_out_ref[...] = grad_hidden
            gd_ref[...] = grad_hidden.astype(BF)
        sums_ref[...] = jnp.zeros_like(sums_ref)
        sums_ref[2:3, :] = jnp.sum(gd_ref[...].astype(F32), axis=0, keepdims=True)

    grad_up = (slope_ref[...].astype(F32) * dot_nt(gd_ref[...], down_ref[...])).astype(BF)
    gu_ref[...] = grad_up
    sums = jnp.sum(grad_up.astype(F32), axis=0, keepdims=True)
    for at in range(STEPS):

        @pl.when(step == at)
        def _():
            sums_ref[3 + at // 2 : 4 + at // 2, (at % 2) * STEP_HID : (at % 2 + 1) * STEP_HID] = (
                sums
            )

    term = dot_nt(grad_up, up_ref[...])

    @pl.when(step == 0)
    def _():
        total[...] = term

    @pl.when((step > 0) & (step < STEPS - 1))
    def _():
        total[...] += term

    @pl.when(step == STEPS - 1)
    def _():
        grad = total[...] + term
        part_ref[...] = grad.astype(BF)
        centre, rstd = stats(mid_ref[...])
        sums_ref[0:1, :] = jnp.sum(grad * (centre * rstd), axis=0, keepdims=True)
        sums_ref[1:2, :] = jnp.sum(grad, axis=0, keepdims=True)


def call_mlp_backward(first, operands, middle, slope, vecs, weights):
    rows = middle.shape[0]
    specs = [full(rows, D)] if first else [full(rows, D)] * 4 + [full(16, D)]
    outs = [
        jax.ShapeDtypeStruct((rows, D), BF),
        jax.ShapeDtypeStruct((rows, HID), BF),
        jax.ShapeDtypeStruct((rows, D), BF),
        jax.ShapeDtypeStruct((8, D), F32),
    ]
    out_specs = [
        full(rows, D),
        pl.BlockSpec((rows, STEP_HID), lambda s: (0, s)),
        full(rows, D),
        full(8, D),
    ]
    if not first:
        outs = [jax.ShapeDtypeStruct((rows, D), F32)] + outs
        out_specs = [full(rows, D)] + out_specs
    return pl.pallas_call(
        functools.partial(mlp_backward, first),
        grid=(STEPS,),
        out_shape=outs,
        in_specs=specs
        + [full(rows, D), pl.BlockSpec((rows, STEP_HID), lambda s: (0, s)), full(16, D)]
        + mlp_weight_specs()[::-1],
        out_specs=out_specs,
        scratch_shapes=[pltpu.VMEM((rows, D), F32)],
        compiler_params=params(36),
        cost_estimate=cost(2 * rows * D * 2 * HID * 2, 12 << 20),
        name="mlp_backward",
    )(*operands, middle, slope, vecs, weights, weights)


def attention_backward(
    grad_ref,
    own_ref,
    got_ref,
    mid_ref,
    hid_ref,
    qkv_ref,
    lse_ref,
    vecs,
    kept,
    weights,
    gm_ref,
    gb_ref,
    gp_ref,
    part_ref,
    sums_ref,
):
    rows = grad_ref.shape[0]
    centre, rstd = stats(mid_ref[...])
    grad_two = own_ref[...].astype(F32) + got_ref[...].astype(F32)
    grad_middle = grad_ref[...].astype(F32) + norm_back(
        grad_two, centre * rstd, rstd, vecs[4:5, :]
    )
    gm_ref[...] = grad_middle
    gb = grad_middle.astype(BF)
    gb_ref[...] = gb
    sums_ref[...] = jnp.zeros_like(sums_ref)
    sums_ref[3:4, :] = jnp.sum(gb.astype(F32), axis=0, keepdims=True)
    grad_att = (
        dot_nt(gb[:, 0:WID], weights[D : D + WID, WID:D])
        + dot_nt(gb[:, WID:D], weights[D + WID : 2 * D, WID:D])
    ).astype(BF)
    bias = key_bias(kept[0:1, :], rows)
    lane = lax.broadcasted_iota(jnp.int32, (rows, BLK), 1)
    for pair in range(WID // BLK):
        cols = slice(pair * BLK, (pair + 1) * BLK)
        key_cols = slice(WID + pair * BLK, WID + (pair + 1) * BLK)
        value_cols = slice(2 * WID + pair * BLK, 2 * WID + (pair + 1) * BLK)
        q = qkv_ref[:, cols] * jnp.asarray(0.125, BF)
        k = qkv_ref[:, key_cols]
        v = qkv_ref[:, value_cols]
        g = grad_att[:, cols]
        got = []
        for half in range(2):
            head = 2 * pair + half
            scores = dot_nt(lane_half(q, half), k) + bias
            att = jnp.exp(scores - lse_ref[:, head : head + 1])
            grad_a = dot_nt(lane_half(g, half), v)
            inner = jnp.sum(att * grad_a, axis=-1, keepdims=True)
            grad_s = (att * (grad_a - inner)).astype(BF)
            got.append((dot(grad_s, k) * 0.125, dot_tn(grad_s, q), dot_tn(att.astype(BF), g)))
        for at, where in enumerate((cols, key_cols, value_cols)):
            gp_ref[:, where] = jnp.where(lane < HEAD_DIM, got[0][at], got[1][at]).astype(BF)
    sums_ref[2:3, 0:WID] = jnp.sum(gp_ref[:, 0:WID].astype(F32), axis=0, keepdims=True)
    sums_ref[2:3, WID:D] = jnp.sum(gp_ref[:, 2 * WID :].astype(F32), axis=0, keepdims=True)
    grad = (
        dot_nt(gp_ref[:, 0:WID], weights[0:D, 0:WID])
        + dot_nt(gp_ref[:, WID : 2 * WID], weights[0:D, WID:D])
        + dot_nt(gp_ref[:, 2 * WID :], weights[D : 2 * D, 0:WID])
    )
    part_ref[...] = grad.astype(BF)
    centre, rstd = stats(hid_ref[...].astype(F32))
    sums_ref[0:1, :] = jnp.sum(grad * (centre * rstd), axis=0, keepdims=True)
    sums_ref[1:2, :] = jnp.sum(grad, axis=0, keepdims=True)


def call_attention_backward(*args):
    rows = args[0].shape[0]
    outs = [
        jax.ShapeDtypeStruct((rows, D), F32),
        jax.ShapeDtypeStruct((rows, D), BF),
        jax.ShapeDtypeStruct((rows, 3 * WID), BF),
        jax.ShapeDtypeStruct((rows, D), BF),
        jax.ShapeDtypeStruct((8, D), F32),
    ]
    return pl.pallas_call(
        attention_backward,
        grid=(1,),
        out_shape=outs,
        in_specs=[full(*a.shape) for a in args[:-1]] + [full(ATT_ROWS, D)],
        out_specs=[full(*o.shape) for o in outs],
        compiler_params=params(40),
        cost_estimate=cost(2 * rows * D * 4 * WID * 3, 8 << 20),
        name="attention_backward",
    )(*args)


def mlp_grads(slot_own, slot_par, *refs):
    acts, gds, n2s, gus = refs[0:2], refs[2:4], refs[4:6], refs[6:8]
    own_ref, par_ref, down_buf, up_buf, sems = refs[8:]
    step = pl.program_id(0)
    at = lax.rem(step, 2)
    tiles = STEP_HID // 2 // BLK

    def copies(of_step, act_on):
        part = lax.rem(of_step, 2)
        first = lax.rem(of_step, STEPS) * tiles

        def one(index, carry):
            tile = lax.div(index, 8)
            block = lax.rem(index, 8)
            down_id = 128 + (first + tile) * 8 + block
            up_id = 64 + block * 8 + first + tile
            for slots, out in ((slot_own, own_ref), (slot_par, par_ref)):
                mine = (of_step < STEPS) if out is own_ref else (of_step >= STEPS)

                @pl.when(mine)
                def _():
                    down_row = pl.multiple_of(slots[down_id] * BLK, BLK)
                    up_row = pl.multiple_of(slots[up_id] * BLK, BLK)
                    tile_row = pl.multiple_of(tile * BLK, BLK)
                    block_row = pl.multiple_of(block * BLK, BLK)
                    act_on(
                        pltpu.make_async_copy(
                            down_buf.at[part, pl.ds(tile_row, BLK), pl.ds(block_row, BLK)],
                            out.at[pl.ds(down_row, BLK), :],
                            sems.at[part],
                        )
                    )
                    act_on(
                        pltpu.make_async_copy(
                            up_buf.at[part, pl.ds(block_row, BLK), pl.ds(tile_row, BLK)],
                            out.at[pl.ds(up_row, BLK), :],
                            sems.at[part],
                        )
                    )

            return carry

        lax.fori_loop(0, tiles * 8, one, 0)

    @pl.when(step >= 2)
    def _():
        copies(step - 2, lambda c: c.wait())

    down_buf[at] = sum(dot_tn(a[...], g[...]) for a, g in zip(acts, gds)).astype(BF)
    up_buf[at] = sum(dot_tn(n[...], g[...]) for n, g in zip(n2s, gus)).astype(BF)
    copies(step, lambda c: c.start())

    @pl.when(step == 2 * STEPS - 1)
    def _():
        copies(step - 1, lambda c: c.wait())
        copies(step, lambda c: c.wait())


def call_mlp_grads(slots, acts, gds, n2s, gus):
    rows = gds[0].shape[0]
    wide = STEP_HID // 2
    by_hidden = pl.BlockSpec((rows, wide), lambda s, a, b: (0, s))
    whole = pl.BlockSpec((rows, D), lambda s, a, b: (0, 0))
    buffer = jax.ShapeDtypeStruct((SHARE_TILES * BLK, BLK), BF)
    return pl.pallas_call(
        mlp_grads,
        grid_spec=pltpu.PrefetchScalarGridSpec(
            num_scalar_prefetch=2,
            grid=(2 * STEPS,),
            in_specs=[by_hidden] * 2 + [whole] * 4 + [by_hidden] * 2,
            out_specs=[ANY, ANY],
            scratch_shapes=[
                pltpu.VMEM((2, wide, D), BF),
                pltpu.VMEM((2, D, wide), BF),
                pltpu.SemaphoreType.DMA((2,)),
            ],
        ),
        out_shape=[buffer, buffer],
        compiler_params=params(32),
        cost_estimate=cost(2 * 2 * rows * D * 2 * HID * 2, 16 << 20),
        name="mlp_grads",
    )(*slots, *acts, *gds, *n2s, *gus)


def attention_grads(slot_own, slot_par, *refs):
    atts, gbs, n1s, gqs, gks, gvs = (refs[2 * i : 2 * i + 2] for i in range(6))
    own_ref, par_ref, out_buf, qkv_buf, sems = refs[14:]
    step = pl.program_id(0)
    at = lax.rem(step, 2)
    per_share = D // NARROW // BLK

    def copies(of_step, act_on):
        part = lax.rem(of_step, 2)
        column = lax.rem(of_step, per_share)

        def one(block, carry):
            block_row = pl.multiple_of(block * BLK, BLK)
            for slots, out in ((slot_own, own_ref), (slot_par, par_ref)):
                mine = (of_step < per_share) if out is own_ref else (of_step >= per_share)

                @pl.when(mine)
                def _():
                    row = pl.multiple_of(slots[48 + column * 8 + block] * BLK, BLK)
                    act_on(
                        pltpu.make_async_copy(
                            out_buf.at[part, :, pl.ds(block_row, BLK)],
                            out.at[pl.ds(row, BLK), :],
                            sems.at[part],
                        )
                    )
                    for third in range(3):
                        tile = block * 6 + third * 2 + column
                        row = pl.multiple_of(slots[tile] * BLK, BLK)
                        act_on(
                            pltpu.make_async_copy(
                                qkv_buf.at[part, third, pl.ds(block_row, BLK), :],
                                out.at[pl.ds(row, BLK), :],
                                sems.at[part],
                            )
                        )

            return carry

        lax.fori_loop(0, 8, one, 0)

    @pl.when(step >= 2)
    def _():
        copies(step - 2, lambda c: c.wait())

    out_buf[at] = sum(dot_tn(a[...], g[...]) for a, g in zip(atts, gbs)).astype(BF)
    for third, grads in enumerate((gqs, gks, gvs)):
        qkv_buf[at, third] = sum(dot_tn(n[...], g[...]) for n, g in zip(n1s, grads)).astype(BF)
    copies(step, lambda c: c.start())

    @pl.when(step == 2 * per_share - 1)
    def _():
        copies(step - 1, lambda c: c.wait())
        copies(step, lambda c: c.wait())


def call_attention_grads(slots, atts, gbs, n1s, gps, own, par):
    rows = gbs[0].shape[0]
    steps = WID // BLK
    whole = pl.BlockSpec((rows, D), lambda s, a, b: (0, 0))

    def by_column(third):
        return pl.BlockSpec((rows, BLK), lambda s, a, b: (0, third * steps + s))

    return pl.pallas_call(
        attention_grads,
        grid_spec=pltpu.PrefetchScalarGridSpec(
            num_scalar_prefetch=2,
            grid=(steps,),
            in_specs=[by_column(0)] * 2
            + [whole] * 4
            + [by_column(0)] * 2
            + [by_column(1)] * 2
            + [by_column(2)] * 2
            + [ANY, ANY],
            out_specs=[ANY, ANY],
            scratch_shapes=[
                pltpu.VMEM((2, BLK, D), BF),
                pltpu.VMEM((2, 3, D, BLK), BF),
                pltpu.SemaphoreType.DMA((2,)),
            ],
        ),
        out_shape=[jax.ShapeDtypeStruct(own.shape, BF)] * 2,
        input_output_aliases={14: 0, 15: 1},
        compiler_params=params(24),
        cost_estimate=cost(2 * 2 * rows * D * 4 * WID, 8 << 20),
        name="attention_grads",
    )(*slots, *atts, *gbs, *n1s, *gps, *gps, *gps, own, par)


def place_of(tile, share):
    quarter = WID // 2
    block, rest = tile // 6, tile % 6
    third, column = rest // 2, rest % 2
    qkv_row = jnp.where(third == 2, D, 0) + block * BLK
    qkv_col = jnp.where(third == 1, WID, 0) + share * quarter + column * BLK
    out = tile - 48
    out_block, out_col = out // 8, out % 8
    out_row = D + jnp.where(out_col >= 4, WID, 0) + share * quarter + out_block * BLK
    out_col = WID + (out_col % 4) * BLK
    up = tile - 64
    up_row, up_col = 2 * D + share * D + (up // 8) * BLK, (up % 8) * BLK
    down = tile - 128
    down_row, down_col = 4 * D + share * D + (down // 8) * BLK, (down % 8) * BLK
    kind = (tile >= 48).astype(jnp.int32) + (tile >= 64) + (tile >= 128)
    row = jnp.select([kind == 0, kind == 1, kind == 2], [qkv_row, out_row, up_row], down_row)
    col = jnp.select([kind == 0, kind == 1, kind == 2], [qkv_col, out_col, up_col], down_col)
    return row, col


def assemble_kernel(plan, rows, cols, *refs):
    sources = refs[: len(plan)]
    out_ref, held, in_sems, out_sem = refs[-4:]
    loads, base = [], 0
    for at, (src, (share, first, count)) in enumerate(zip(sources, plan)):
        size = count * BLK
        load = pltpu.make_async_copy(
            src.at[pl.ds(0, size), :], held.at[pl.ds(base * BLK, size), :], in_sems.at[at]
        )
        load.start()
        loads.append((load, base))
        base += count

    def run(at, act_on):
        share, first, count = plan[at]

        def one(i, carry):
            row = pl.multiple_of(rows[share, first + i], BLK)
            col = pl.multiple_of(cols[share, first + i], BLK)
            from_row = pl.multiple_of((loads[at][1] + i) * BLK, BLK)
            act_on(
                pltpu.make_async_copy(
                    held.at[pl.ds(from_row, BLK), :],
                    out_ref.at[pl.ds(row, BLK), pl.ds(col, BLK)],
                    out_sem,
                )
            )
            return carry

        lax.fori_loop(0, count, one, 0)

    for at in range(len(plan)):
        loads[at][0].wait()
        run(at, lambda c: c.start())
    for at in range(len(plan)):
        run(at, lambda c: c.wait())


def assemble(table, pieces, weights):
    plan = [piece[:3] for piece in pieces]
    arrays = [piece[3] for piece in pieces]
    total = sum(piece[2] for piece in pieces)
    shape = jax.ShapeDtypeStruct((6 * D, D), BF)
    alias = {} if weights is None else {2 + len(arrays): 0}
    args = list(table) + arrays + ([] if weights is None else [weights])
    return pl.pallas_call(
        functools.partial(assemble_kernel, plan),
        out_shape=shape,
        in_specs=[SMEM, SMEM] + [ANY] * (len(args) - 2),
        out_specs=ANY,
        scratch_shapes=[
            pltpu.VMEM((total * BLK, BLK), BF),
            pltpu.SemaphoreType.DMA((len(arrays),)),
            pltpu.SemaphoreType.DMA,
        ],
        input_output_aliases=alias,
        compiler_params=params(16),
        cost_estimate=cost(0, total * BLK * BLK * 8),
        name="assemble",
    )(*args)


def ring(size):
    order = list(range(0, size, 2)) + list(range(size - 1, 0, -2))
    ahead = [(order[i], order[(i + 1) % size]) for i in range(size)]
    position = [order.index(i) for i in range(size)]
    return order, position, ahead, [(b, a) for a, b in ahead]


def ring_gather(unit, size, per_device):
    _, _, ahead, behind = ring(size)
    far = size // 2
    front = per_device // 2
    pieces = []
    up = down = unit
    for step in range(1, far):
        up, down = lax.ppermute(up, "wide", ahead), lax.ppermute(down, "wide", behind)
        pieces.append((size - step, 0, per_device, up))
        pieces.append((step, 0, per_device, down))
    up = lax.ppermute(up[: front * BLK], "wide", ahead)
    down = lax.ppermute(down[front * BLK :], "wide", behind)
    pieces.append((far, 0, front, up))
    pieces.append((far, front, per_device - front, down))
    return pieces


def ring_scatter(unit_of, size, cut):
    _, _, ahead, behind = ring(size)
    far = size // 2

    def send(value, perm):
        return lax.ppermute(value.astype(BF), "wide", perm)

    last = unit_of(far)
    up = send(last[:cut], ahead).astype(F32)
    down = send(last[cut:], behind).astype(F32)
    for step in range(far - 1, 0, -1):
        term_up, term_down = unit_of(step), unit_of(size - step)
        if step == far - 1:
            up = jnp.concatenate([term_up[:cut] + up, term_up[cut:]])
            down = jnp.concatenate([term_down[:cut], term_down[cut:] + down])
        else:
            up, down = term_up + up, term_down + down
        up, down = send(up, ahead).astype(F32), send(down, behind).astype(F32)
    return unit_of(0) + up + down


def tile_ids(share):
    tile_rows = D // BLK
    shard_cols = D // (NARROW * BLK)
    shard_hidden = FF // (NARROW * BLK)
    count_qkv = tile_rows * 3 * tile_rows
    start_up = count_qkv + tile_rows * tile_rows
    start_down = start_up + tile_rows * (FF // BLK)
    row_part = jnp.arange(tile_rows)[:, None, None]
    third = jnp.arange(3)[None, :, None]
    column_part = jnp.arange(shard_cols)[None, None, :]
    qkv_ids = (
        row_part * 3 * tile_rows + third * tile_rows + share * shard_cols + column_part
    ).reshape(-1)
    out_ids = (
        count_qkv
        + (share * shard_cols + jnp.arange(shard_cols)[:, None]) * tile_rows
        + jnp.arange(tile_rows)[None, :]
    ).reshape(-1)
    up_ids = (
        start_up
        + jnp.arange(tile_rows)[:, None] * (FF // BLK)
        + share * shard_hidden
        + jnp.arange(shard_hidden)[None, :]
    ).reshape(-1)
    down_ids = (
        start_down
        + (share * shard_hidden + jnp.arange(shard_hidden)[:, None]) * tile_rows
        + jnp.arange(tile_rows)[None, :]
    ).reshape(-1)
    return jnp.concatenate([qkv_ids, out_ids, up_ids, down_ids])


def share_vectors(small_all, me):
    pieces = [small_all[i * D : (i + 1) * D] for i in range(8)]
    bias_up = small_all[8 * D :]

    def both(vector, width):
        own = lax.dynamic_slice_in_dim(vector, me * width, width)
        par = lax.dynamic_slice_in_dim(vector, (me ^ 1) * width, width)
        return jnp.concatenate([own, par])

    quarter = D // NARROW
    heads = jnp.concatenate([both(pieces[2], quarter), both(pieces[3], quarter)])
    rows = [pieces[0], pieces[1], heads, pieces[4], pieces[5], pieces[6], pieces[7]]
    up = both(bias_up, FF // NARROW)
    rows = rows + [up[0:D], up[D:]]
    return jnp.pad(jnp.stack(rows), ((0, 7), (0, 0)))


def small_vector(mlp_sums, att_sums, me):
    half = me // 2
    mine = [(half == t).astype(F32) for t in range(2)]
    mlp = mlp_sums[0] + mlp_sums[1]
    att = att_sums[0] + att_sums[1]
    bias_down = mine[0] * mlp_sums[0][2] + mine[1] * mlp_sums[1][2]
    bias_out = mine[0] * att_sums[0][3] + mine[1] * att_sums[1][3]
    odd = (me % 2) == 1

    def spread(own, par):
        placed = jnp.where(odd, jnp.concatenate([par, own]), jnp.concatenate([own, par]))
        return [jnp.where(half == 0, placed, 0.0), jnp.where(half == 1, placed, 0.0)]

    quarter = D // NARROW
    heads = att[2]
    return jnp.concatenate(
        [att[0], att[1]]
        + spread(heads[0:quarter], heads[quarter : 2 * quarter])
        + spread(heads[2 * quarter : 3 * quarter], heads[3 * quarter :])
        + [bias_out, mlp[0], mlp[1], bias_down]
        + spread(mlp[3], mlp[4])
    )


def total_over_mesh(value):
    value = jnp.broadcast_to(value.reshape(1, 1), (8, BLK))
    for axis in ("narrow", "wide"):
        size = lax.axis_size(axis)
        bit = 1
        while bit < size:
            value = value + lax.ppermute(value, axis, [(i, i ^ bit) for i in range(size)])
            bit *= 2
    return value[0, 0]


def rotate_in_kernel(grad_ref, left_ref, right_ref, out_ref):
    for block in range(out_ref.shape[0]):
        grad = grad_ref[block * BLK : (block + 1) * BLK, :].astype(BF)
        inner = dot_tn(left_ref[0, block].astype(BF), grad)
        out_ref[block] = dot(inner.astype(BF), right_ref[0, block].astype(BF))


def rotate_in(layer, grads, left_basis, right_basis):
    count = left_basis.shape[1]
    group = 6
    spec = pl.BlockSpec((group, BLK, BLK), lambda i: (i, 0, 0))
    flat = pl.BlockSpec((group * BLK, BLK), lambda i: (i, 0))
    basis = pl.BlockSpec((1, group, BLK, BLK), lambda i: (layer, i, 0, 0))
    return pl.pallas_call(
        rotate_in_kernel,
        grid=(count // group,),
        out_shape=jax.ShapeDtypeStruct((count, BLK, BLK), F32),
        in_specs=[flat, basis, basis],
        out_specs=spec,
        compiler_params=params(16),
        cost_estimate=cost(count * 4 * BLK**3, count * BLK * BLK * 14),
        name="rotate_in",
    )(grads, left_basis, right_basis)


def update_kernel(clip_ref, rot0, rot1, left, right, first, second, master, *outs):
    new_first, new_second, new_master, new_weights = outs
    step = pl.program_id(0)
    half = pl.num_programs(0) // 2
    clip = clip_ref[0]
    for block in range(rot0.shape[0]):
        rotated = clip * jnp.where(step < half, rot0[block], rot1[block])
        one = 0.5 * first[0, block] + 0.5 * rotated
        two = 0.5 * second[0, block] + 0.5 * rotated * rotated
        new_first[0, block] = one
        new_second[0, block] = two
        direction = one / (jnp.sqrt(two) + 1e-08)
        inner = dot(left[0, block].astype(BF), direction.astype(BF))
        turned = dot_nt(inner.astype(BF), right[0, block].astype(BF))
        weights = master[0, block] - 0.02 * turned
        new_master[0, block] = weights
        new_weights[0, block] = weights.astype(BF)


def update(clip, rots, left, right, first, second, master):
    count = rots[0].shape[0]
    group = 3
    steps = count // group
    spec = pl.BlockSpec((1, group, BLK, BLK), lambda i: (i // steps, i % steps, 0, 0))
    low = pl.BlockSpec((group, BLK, BLK), lambda i: (jnp.minimum(i, steps - 1), 0, 0))
    high = pl.BlockSpec((group, BLK, BLK), lambda i: (jnp.maximum(i - steps, 0), 0, 0))
    shape = jax.ShapeDtypeStruct(master.shape, F32)
    return pl.pallas_call(
        update_kernel,
        grid=(2 * steps,),
        out_shape=[shape, shape, shape, jax.ShapeDtypeStruct(master.shape, BF)],
        in_specs=[SMEM, low, high] + [spec] * 5,
        out_specs=[spec] * 4,
        compiler_params=params(24),
        cost_estimate=cost(count * 8 * BLK**3, count * BLK * BLK * 2 * 38),
        name="update",
    )(clip, *rots, left, right, first, second, master)


def shards(
    images,
    cotangent,
    kept_tokens,
    owner_slots,
    master_blocks,
    small_params,
    left_basis,
    right_basis,
    first_moment,
    second_moment,
    small_first,
    small_second,
):
    me = lax.axis_index("narrow")
    half, core = me // 2, me % 2
    wide = lax.axis_size("wide")
    per_device = master_blocks.shape[1]
    own_small = small_params.shape[1]
    own_images = images.shape[0]
    rows = own_images * S

    small_bf = small_params.astype(BF)
    small_pair = jnp.stack([small_bf, lax.ppermute(small_bf, "narrow", ACROSS)])
    small_rows = -(-small_pair.size // (16 * BLK)) * 16
    small_pad = jnp.pad(small_pair.reshape(-1), (0, small_rows * BLK - small_pair.size))
    small_pad = small_pad.reshape(small_rows, BLK)

    def chunks(own):
        other = lax.ppermute(own, "narrow", ACROSS)
        return [jnp.where(half == t, own, other) for t in range(2)]

    hidden_in = chunks(images.reshape(rows, D))
    cot = chunks(cotangent.reshape(rows, D))
    kept = [
        lax.dynamic_slice_in_dim(kept_tokens, (2 * t + core) * own_images, own_images, 0)
        .reshape(1, rows)
        .astype(F32)
        for t in range(2)
    ]

    order, position, _, _ = ring(wide)
    place = jnp.take(jnp.asarray(position, jnp.int32), lax.axis_index("wide"))
    around = jnp.take(jnp.asarray(order, jnp.int32), (place + jnp.arange(wide)) % wide)

    slots, tables = [], []
    for layer in range(LAYERS):
        owners = owner_slots[layer]
        layer_slots, layer_rows, layer_cols = [], [], []
        for at, share in enumerate((me, me ^ 1)):
            slot = jnp.take(owners, tile_ids(share))
            at_wide, at_pos = slot // per_device // NARROW, slot % per_device
            distance = (jnp.take(jnp.asarray(position, jnp.int32), at_wide) - place) % wide
            relative = distance * per_device + at_pos
            layer_slots.append(relative)
            here = relative[None, :] == jnp.arange(SHARE_TILES)[:, None]
            tile = jnp.sum(jnp.where(here, jnp.arange(SHARE_TILES)[None, :], 0), axis=1)
            row, col = place_of(tile, at)
            layer_rows.append(row)
            layer_cols.append(col)
        slots.append(layer_slots)
        tables.append((jnp.stack(layer_rows), jnp.stack(layer_cols)))

    def core_swap(value):
        return lax.ppermute(value, "narrow", CORE)

    weights, units = [], []
    for layer in range(LAYERS):
        unit = master_blocks[layer].astype(BF).reshape(per_device * BLK, BLK)
        if layer == 0:
            unit = jnp.concatenate([unit, small_pad], axis=0)
        pieces = [(0, 0, per_device, unit)] + ring_gather(unit, wide, per_device)
        pieces = [piece + (core_swap(piece[3]),) for piece in pieces]
        matrix = None
        for group in (pieces[: wide - 3], pieces[wide - 3 : wide - 1], pieces[wide - 1 :]):
            group = [
                (share, distance * per_device + first, count, pair[share])
                for distance, first, count, *pair in group
                for share in range(2)
            ]
            matrix = assemble(tables[layer], group, matrix)
        weights.append(matrix)
        units.append(pieces)

    tails = [[None] * wide, [None] * wide]
    for distance, first, count, *pair in units[0]:
        if first + count == per_device:
            for share in range(2):
                tails[share][distance] = pair[share][count * BLK :]
    tails = [
        jnp.stack(t).reshape(wide, small_rows * BLK)[:, : small_pair.size]
        .reshape(wide, 2, LAYERS, own_small)
        for t in tails
    ]
    by_distance = jnp.stack([tails[0][:, 0], tails[1][:, 0], tails[0][:, 1], tails[1][:, 1]], axis=1)
    to_order = (jnp.asarray(position, jnp.int32) - place) % wide
    in_order = jnp.take(by_distance, to_order, axis=0)
    in_order = jnp.take(in_order, jnp.arange(NARROW) ^ me, axis=1).astype(F32)
    small_all = in_order.transpose(2, 0, 1, 3).reshape(LAYERS, -1)
    vecs = [share_vectors(small_all[layer], me) for layer in range(LAYERS)]

    def exchange(part):
        return lax.ppermute(part, "narrow", ACROSS)

    saved = []
    state = None
    for layer in range(LAYERS):
        att_w = mlp_w = weights[layer]
        kept_layer = []
        for t in range(2):
            if layer == 0:
                out = call_attention_forward(True, (hidden_in[t],), vecs[0], kept[t], att_w)
                hidden = hidden_in[t]
            else:
                hidden, *out = call_attention_forward(
                    False, state[t] + (vecs[layer - 1],), vecs[layer], kept[t], att_w
                )
            n1, qkv, lse, att, part = out
            kept_layer.append([hidden, n1, qkv, lse, att, part, exchange(part)])
        state = []
        for t in range(2):
            hidden, n1, qkv, lse, att, part, got = kept_layer[t]
            middle, n2, act, slope, down_part = call_mlp_forward(
                hidden, part, got, vecs[layer], mlp_w
            )
            kept_layer[t] = (hidden, n1, qkv, lse, att, middle, n2, act, slope)
            if layer < LAYERS - 1:
                state.append((middle, down_part, exchange(down_part)))
            else:
                state.append((middle, down_part))
        saved.append((att_w, mlp_w, kept_layer))

    def mine(pair):
        return jnp.where(half == 0, pair[0], pair[1])

    def theirs(pair):
        return jnp.where(half == 0, pair[1], pair[0])

    down_parts = [state[t][1] for t in range(2)]
    middles = [state[t][0] for t in range(2)]
    final = mine(middles) + (
        mine(down_parts).astype(F32)
        + exchange(theirs(down_parts)).astype(F32)
        + vecs[LAYERS - 1][6]
    )
    block_output = final.astype(BF).reshape(images.shape)

    upstream = None
    reduced = [None] * LAYERS
    small_terms = [None] * LAYERS
    for layer in reversed(range(LAYERS)):
        att_w, mlp_w, kept_layer = saved[layer]
        top = layer == LAYERS - 1
        work = []
        for t in range(2):
            hidden, n1, qkv, lse, att, middle, n2, act, slope = kept_layer[t]
            if top:
                grad = cot[t]
                gd, gu, part, sums = call_mlp_backward(
                    True, (grad,), middle, slope, vecs[layer], mlp_w
                )
            else:
                grad, gd, gu, part, sums = call_mlp_backward(
                    False, upstream[t] + (vecs[layer + 1],), middle, slope, vecs[layer], mlp_w
                )
            work.append([grad, gd, gu, part, sums, exchange(part)])
        own, par = call_mlp_grads(
            slots[layer],
            [k[7] for k in kept_layer],
            [w[1] for w in work],
            [k[6] for k in kept_layer],
            [w[2] for w in work],
        )
        back = []
        for t in range(2):
            hidden, n1, qkv, lse, att, middle, n2, act, slope = kept_layer[t]
            grad, gd, gu, part, sums, got = work[t]
            gm, gb, gp, att_part, att_sums = call_attention_backward(
                grad, part, got, middle, hidden, qkv, lse, vecs[layer], kept[t], att_w
            )
            back.append((gm, gb, gp, att_part, att_sums))
        if layer > 0:
            upstream = [
                (back[t][0], back[t][3], exchange(back[t][3]), kept_layer[t][0]) for t in range(2)
            ]
        own, par = call_attention_grads(
            slots[layer],
            [k[4] for k in kept_layer],
            [b[1] for b in back],
            [k[1] for k in kept_layer],
            [b[2] for b in back],
            own,
            par,
        )
        terms = small_vector([w[4] for w in work], [b[4] for b in back], me)
        terms = jnp.take(terms.reshape(wide, NARROW, own_small), around, axis=0)
        terms = jnp.take(terms, jnp.arange(NARROW) ^ me, axis=1)
        near = terms[:, 0:2] + exchange(terms[:, 2:4])
        small_sum = near[:, 0] + core_swap(near[:, 1])
        tail_rows = -(-own_small // (16 * BLK)) * 16
        small_tail = jnp.pad(small_sum, ((0, 0), (0, tail_rows * BLK - own_small)))
        small_tail = small_tail.reshape(wide, tail_rows, BLK)
        unit_len = per_device * BLK

        def unit_of(distance, own=own, par=par, small_tail=small_tail, unit_len=unit_len):
            at = slice(distance * unit_len, (distance + 1) * unit_len)
            term = own[at].astype(F32) + core_swap(par[at]).astype(F32)
            return jnp.concatenate([term, small_tail[distance]])

        reduced[layer] = ring_scatter(unit_of, wide, (per_device // 2) * BLK)
        if layer == 0:
            parts = [b[3] for b in back]
            hidden = mine([k[0] for k in kept_layer]).astype(F32)
            centre, rstd = stats(hidden)
            grad = mine(parts).astype(F32) + exchange(theirs(parts)).astype(F32)
            lower = norm_back(grad, centre * rstd, rstd, vecs[0][0:1])
            input_grad = (mine([b[0] for b in back]) + lower).reshape(images.shape)

    tail = per_device * BLK
    grad_small = jnp.stack([r[tail:].reshape(-1)[:own_small] for r in reduced])
    local_sum = jnp.sum(grad_small * grad_small)
    for grads in reduced:
        local_sum = local_sum + jnp.sum(grads[:tail] * grads[:tail])
    grad_norm = jnp.sqrt(total_over_mesh(local_sum))
    clip_factor = 1.0 / jnp.maximum(grad_norm, 1.0)
    rots = [
        rotate_in(layer, reduced[layer], left_basis, right_basis) for layer in range(LAYERS)
    ]
    new_first, new_second, new_master, new_weights = update(
        clip_factor.reshape(1),
        rots,
        left_basis,
        right_basis,
        first_moment,
        second_moment,
        master_blocks,
    )
    clipped_small = clip_factor * grad_small
    new_small_first = 0.5 * small_first + 0.5 * clipped_small
    new_small_second = 0.5 * small_second + 0.5 * clipped_small * clipped_small
    new_small = small_params - 0.3 * new_small_first / (jnp.sqrt(new_small_second) + 1e-08)
    return (
        block_output,
        input_grad,
        grad_norm.reshape(1),
        new_first,
        new_second,
        new_master,
        new_weights,
        new_small_first,
        new_small_second,
        new_small,
        new_small.astype(BF),
    )


def solution(mesh):
    both = ("wide", "narrow")
    rows = P(both, None, None)
    blocks = P(None, both, None, None)
    small = P(None, both)
    in_specs = (
        rows,
        rows,
        P("wide", None),
        P(),
        blocks,
        small,
        blocks,
        blocks,
        blocks,
        blocks,
        small,
        small,
    )
    out_specs = (rows, rows, P(), blocks, blocks, blocks, blocks, small, small, small, small)
    return jax.shard_map(shards, mesh=mesh, in_specs=in_specs, out_specs=out_specs, check_vma=False)
```

time: 1270 us -> 688 us (0.54)
  waiting for transfers between devices: 633 us -> 193 us
  Pallas kernels: 0 us -> 177 us
  matrix products: 150 us -> 0 us
  blocking collectives: 125 us -> 0 us
  starting transfers between devices: 0.83 us -> 69.3 us
  other arithmetic: 102 us -> 45.8 us
  local copies, waits for them, and re-layouts: 229 us -> 187 us
    unnamed x22 -> x0, waiting for transfers between devices: 297 us -> none
    all_gather x10 -> x0, waiting for transfers between devices: 198 us -> none  [the longest x2 126 us: shards(): lax.all_gather(master_blocks[which_layer].astype(jnp.bfloat16), 'wide', a...]
    ppermute x0 -> x92, waiting for transfers between devices: none -> 193 us  [the longest x16 98.5 us: send(): return lax.ppermute(value.astype(BF), 'wide', perm)]
    pallas_call x0 -> x29, Pallas kernels: none -> 177 us  [the longest x4 29.7 us: call_attention_backward(): pl.pallas_call(attention_backward, grid=(1,), out_shape=outs, in_specs=[f...]
    dot_general x40 -> x0, matrix products: 150 us -> none  [the longest x2 26.3 us: forward_layer(): jnp.dot(normed_two_all, w_up, preferred_element_type=jnp.float32) + up_part]
    reduce_scatter x8 -> x0, waiting for transfers between devices: 138 us -> none  [the longest x2 55.4 us: forward_layer(): lax.psum_scatter(jnp.dot(attended, w_out, preferred_element_type=jnp.floa...]
    unnamed x255 -> x512, local copies, waits for them, and re-layouts: 52.1 us -> 149 us
    all_gather x2 -> x0, blocking collectives: 85.6 us -> none  [shards(): lax.all_gather(small_params[which_layer].astype(jnp.bfloat16), ('wide', '...]
  transfers between devices with their start and end apart: 20 -> 92, of which waited for: 16 -> 28; matrix products, arithmetic and copies ran while one was open for 20% -> 12% of each run, Pallas kernels for 0% -> 23%
where the time goes in v1:
time: 688 us; the launch traced here: 680 us
  waiting for transfers between devices  193 us (28%)
  local copies, waits for them, and re-layouts  187 us (27%)
  Pallas kernels  177 us (26%)
  starting transfers between devices  69.3 us (10%)
  other arithmetic  45.8 us (7%)
  between operations  8.44 us (1%)
    unnamed x512, local copies, waits for them, and re-layouts  149 us
    ppermute x16, waiting for transfers between devices, send(): return lax.ppermute(value.astype(BF), 'wide', perm)  98.5 us
    ppermute x6, waiting for transfers between devices, ring_gather(): lax.ppermute(up, 'wide', ahead)  36.3 us
    pallas_call x4, Pallas kernels, call_attention_backward(): pl.pallas_call(attention_backward, grid=(1,), out_shape=outs, in_specs=[f...  29.7 us
    pallas_call x2, Pallas kernels, call_mlp_grads(): pl.pallas_call(mlp_grads, grid_spec=pltpu.PrefetchScalarGridSpec(num_scal...  27.2 us
    pallas_call x4, Pallas kernels, call_mlp_backward(): pl.pallas_call(functools.partial(mlp_backward, first), grid=(STEPS,), out...  26.7 us
    pallas_call x6, Pallas kernels, assemble(): pl.pallas_call(functools.partial(assemble_kernel, plan), out_shape=shape,...  26.5 us
    ppermute x6, waiting for transfers between devices, ring_gather(): lax.ppermute(down, 'wide', behind)  25.5 us
  transfers between devices with their start and end apart: 92, of which 28 were waited for; matrix products, arithmetic and copies ran while one was open for 12% of the time, Pallas kernels for 23%

profile of v1, /device:TPU:0, one launch (start us, length us, event | category | flops | bytes accessed | tf_op | source)
XLA Modules:
  0.0 679.9 jit_solution(13820010530918242037)
XLA Ops:
  3.8 3.1 collective-permute-start.21
  26.6 8.5 %collective-permute-done.43 = bf16[200,1024]{1,0:T(8,128)(2,1)S(1)} collective-permute-done((bf16[200,1024]{1,0:T(8,128)(2,1)}, bf16[200,1024]{1,0:T(8,128)(2,1)S(1)}, u32[]{:S(2)}, u32[]{:S(2)}) %collective-permute-start.43) | collective-permute-done | bytes 409632 | tf_op jit(solution)/shard_map/ppermute | solution.py:884
  41.9 13.9 %collective-permute-done.2.refs_4_ = bf16[3088,128]{1,0:T(8,128)(2,1)} collective-permute-done((bf16[3088,128]{1,0:T(8,128)(2,1)S(1)}, bf16[3088,128]{1,0:T(8,128)(2,1)}, u32[]{:S(2)}, u32[]{:S(2)}) %collective-permute-start.2) | collective-permute-done | bytes 790560 | tf_op jit(solution)/shard_map/ppermute | solution.py:676
  58.2 14.0 %collective-permute-done.22.refs_6_ = bf16[3072,128]{1,0:T(8,128)(2,1)} collective-permute-done((bf16[3072,128]{1,0:T(8,128)(2,1)}, bf16[3072,128]{1,0:T(8,128)(2,1)}, u32[]{:S(2)}, u32[]{:S(2)}) %collective-permute-start.22) | collective-permute-done | bytes 786464 | tf_op jit(solution)/shard_map/ppermute | solution.py:676
  81.2 11.6 %collective-permute-done.3.refs_8_ = bf16[3088,128]{1,0:T(8,128)(2,1)S(1)} collective-permute-done((bf16[3088,128]{1,0:T(8,128)(2,1)}, bf16[3088,128]{1,0:T(8,128)(2,1)S(1)}, u32[]{:S(2)}, u32[]{:S(2)}) %collective-permute-start.3) | collective-permute-done | bytes 790560 | tf_op jit(solution)/shard_map/ppermute | solution.py:676
  93.6 5.0 collective-permute-done.7.refs_6_
  100.2 12.5 %collective-permute-done.23.refs_0_ = bf16[3072,128]{1,0:T(8,128)(2,1)S(1)} collective-permute-done((bf16[3072,128]{1,0:T(8,128)(2,1)}, bf16[3072,128]{1,0:T(8,128)(2,1)S(1)}, u32[]{:S(2)}, u32[]{:S(2)}) %collective-permute-start.23) | collective-permute-done | bytes 786464 | tf_op jit(solution)/shard_map/ppermute | solution.py:676
  116.6 6.7 assemble.9.refs_4_
  123.4 4.5 copy-done
  129.9 3.3 collective-permute-done.8.refs_0_
  139.3 7.2 %collective-permute-done.17.refs_0_ = bf16[1536,128]{1,0:T(8,128)(2,1)S(1)} collective-permute-done((bf16[1536,128]{1,0:T(8,128)(2,1)S(1)}, bf16[1536,128]{1,0:T(8,128)(2,1)S(1)}, u32[]{:S(2)}, u32[]{:S(2)}) %collective-permute-start.17) | collective-permute-done | bytes 393248 | tf_op jit(solution)/shard_map/ppermute | solution.py:679
  147.2 6.7 assemble.6.refs_4_
  154.0 4.5 copy-done.6
  160.7 4.6 copy-done.1
  166.4 3.6 assemble.10.refs_4_
  172.3 2.7 assemble.11.refs_6_.up_ref.down_ref.refs_4_.refs_5_.weights
  175.0 4.5 copy-done.2
  181.0 4.0 assemble.7.refs_4_
  185.0 4.5 copy-done.7
  191.7 4.6 copy-done.8
  196.2 2.7 assemble.8.refs_3_.up_ref.down_ref.refs_8_.refs_9_.weights
  199.0 4.5 copy-done.9
  203.5 4.6 copy-done.10
  212.9 4.6 copy-done.11
  222.8 4.5 mlp_forward.6
  230.5 3.9 collective-permute-done.19.got_ref
  234.5 5.5 mlp_forward.4
  243.2 4.6 copy-done.3
  248.8 3.5 attention_forward.7
  255.5 4.6 copy-done.4
  260.1 3.6 attention_forward.5
  267.1 4.6 copy-done.5
  272.6 4.5 mlp_forward.7
  283.0 4.5 mlp_forward.5
  293.0 5.3 mlp_backward.4
  300.4 5.4 mlp_backward.6
  306.0 13.8 %mlp_grads.3 = (bf16[24576,128]{1,0:T(8,128)(2,1)S(1)}, bf16[24576,128]{1,0:T(8,128)(2,1)S(1)}) custom-call(s32[192]{0:T(256)S(1)} %copy-done.143, s32[192]{0:T(256)S(1)} %copy-done.146, bf16[200,2048]{1,0:T(8,128)(2,1)S(1)} %copy-done.155, bf16[200,2048]{1,0:T(8,128)(2,1)S(1)} %copy-done.153, bf16[200,1024]{1,0:T(8,128)(2,1)S(1)} %get-tuple-element.189.refs_2_, ...), custom_call_target="tpu_custom_call" | custom-call | flops 6710886400 | bytes 16777216 | tf_op jit(solution)/shard_map/mlp_grads/pallas_call | solution.py:470
  326.4 7.4 %attention_backward.4 = (f32[200,1024]{1,0:T(8,128)S(1)}, bf16[200,1024]{1,0:T(8,128)(2,1)S(1)}, bf16[200,1536]{1,0:T(8,128)(2,1)S(1)}, bf16[200,1024]{1,0:T(8,128)(2,1)S(1)}, f32[8,1024]{1,0:T(8,128)S(1)}) custom-call(bf16[200,1024]{1,0:T(8,128)(2,1)S(1)} %copy-done.51, bf16[200,1024]{1,0:T(8,128)(2,1)S(1)} %get-tuple-element.130.own_ref, ...), custom_call_target="tpu_custom_call" | custom-call | flops 2516582400 | bytes 8388608 | tf_op jit(solution)/shard_map/attention_backward/pallas_call | solution.py:394
  336.2 7.4 %attention_backward.6 = (f32[200,1024]{1,0:T(8,128)S(1)}, bf16[200,1024]{1,0:T(8,128)(2,1)S(1)}, bf16[200,1536]{1,0:T(8,128)(2,1)S(1)}, bf16[200,1024]{1,0:T(8,128)(2,1)S(1)}, f32[8,1024]{1,0:T(8,128)S(1)}) custom-call(bf16[200,1024]{1,0:T(8,128)(2,1)S(1)} %copy-done.50, bf16[200,1024]{1,0:T(8,128)(2,1)S(1)} %get-tuple-element.142.own_ref, ...), custom_call_target="tpu_custom_call" | custom-call | flops 2516582400 | bytes 8388608 | tf_op jit(solution)/shard_map/attention_backward/pallas_call | solution.py:394
  361.6 2.8 copy-done.19
  364.4 2.8 copy-done.26
  372.3 11.4 %attention_grads.3 = (bf16[24576,128]{1,0:T(8,128)(2,1)S(1)}, bf16[24576,128]{1,0:T(8,128)(2,1)S(1)}) custom-call(s32[192]{0:T(256)S(1)} %copy-done.144, s32[192]{0:T(256)S(1)} %copy-done.147, bf16[200,512]{1,0:T(8,128)(2,1)S(1)} %copy-done.125, bf16[200,512]{1,0:T(8,128)(2,1)S(1)} %copy-done.123, ...), custom_call_target="tpu_custom_call", output_to_operand_aliasing={{0}: (14, {}), {1}: (15, {})} | custom-call | flops 1677721600 | bytes 8388608 | tf_op jit(solution)/shard_map/attention_grads/pallas_call | solution.py:554
  389.1 5.6 fusion.139
  404.8 8.1 %mlp_backward.5 = (f32[200,1024]{1,0:T(8,128)S(1)}, bf16[200,1024]{1,0:T(8,128)(2,1)S(1)}, bf16[200,2048]{1,0:T(8,128)(2,1)S(1)}, bf16[200,1024]{1,0:T(8,128)(2,1)S(1)}, f32[8,1024]{1,0:T(8,128)S(1)}) custom-call(f32[200,1024]{1,0:T(8,128)S(1)} %copy-done.69, bf16[200,1024]{1,0:T(8,128)(2,1)S(1)} %copy-done.115, ...), custom_call_target="tpu_custom_call" | custom-call | flops 3355443200 | bytes 12582912 | tf_op jit(solution)/shard_map/mlp_backward/pallas_call | solution.py:304
  413.1 7.9 %mlp_backward.7 = (f32[200,1024]{1,0:T(8,128)S(1)}, bf16[200,1024]{1,0:T(8,128)(2,1)S(1)}, bf16[200,2048]{1,0:T(8,128)(2,1)S(1)}, bf16[200,1024]{1,0:T(8,128)(2,1)S(1)}, f32[8,1024]{1,0:T(8,128)S(1)}) custom-call(f32[200,1024]{1,0:T(8,128)S(1)} %copy-done.67, bf16[200,1024]{1,0:T(8,128)(2,1)S(1)} %copy-done.113, ...), custom_call_target="tpu_custom_call" | custom-call | flops 3355443200 | bytes 12582912 | tf_op jit(solution)/shard_map/mlp_backward/pallas_call | solution.py:304
  423.3 13.4 %mlp_grads.2 = (bf16[24576,128]{1,0:T(8,128)(2,1)S(1)}, bf16[24576,128]{1,0:T(8,128)(2,1)S(1)}) custom-call(s32[192]{0:T(256)S(1)} %copy-done.137, s32[192]{0:T(256)S(1)} %copy-done.140, bf16[200,2048]{1,0:T(8,128)(2,1)S(1)} %copy-done.151, bf16[200,2048]{1,0:T(8,128)(2,1)S(1)} %copy-done.149, bf16[200,1024]{1,0:T(8,128)(2,1)S(1)} %get-tuple-element.165.refs_2_, ...), custom_call_target="tpu_custom_call" | custom-call | flops 6710886400 | bytes 16777216 | tf_op jit(solution)/shard_map/mlp_grads/pallas_call | solution.py:470
  442.6 5.8 convert_add_fusion.3
  450.5 7.3 %attention_backward.5 = (f32[200,1024]{1,0:T(8,128)S(1)}, bf16[200,1024]{1,0:T(8,128)(2,1)S(1)}, bf16[200,1536]{1,0:T(8,128)(2,1)S(1)}, bf16[200,1024]{1,0:T(8,128)(2,1)S(1)}, f32[8,1024]{1,0:T(8,128)S(1)}) custom-call(f32[200,1024]{1,0:T(8,128)S(1)} %get-tuple-element.136.grad_ref, bf16[200,1024]{1,0:T(8,128)(2,1)S(1)} %get-tuple-element.137.own_ref, ...), custom_call_target="tpu_custom_call" | custom-call | flops 2516582400 | bytes 8388608 | tf_op jit(solution)/shard_map/attention_backward/pallas_call | solution.py:394
  458.9 7.6 %attention_backward.7 = (f32[200,1024]{1,0:T(8,128)S(1)}, bf16[200,1024]{1,0:T(8,128)(2,1)S(1)}, bf16[200,1536]{1,0:T(8,128)(2,1)S(1)}, bf16[200,1024]{1,0:T(8,128)(2,1)S(1)}, f32[8,1024]{1,0:T(8,128)S(1)}) custom-call(f32[200,1024]{1,0:T(8,128)S(1)} %get-tuple-element.148.grad_ref, bf16[200,1024]{1,0:T(8,128)(2,1)S(1)} %get-tuple-element.149.own_ref, ...), custom_call_target="tpu_custom_call" | custom-call | flops 2516582400 | bytes 8388608 | tf_op jit(solution)/shard_map/attention_backward/pallas_call | solution.py:394
  475.7 2.8 copy-done.16
  478.4 2.8 copy-done.22
  483.2 11.4 %attention_grads.2 = (bf16[24576,128]{1,0:T(8,128)(2,1)S(1)}, bf16[24576,128]{1,0:T(8,128)(2,1)S(1)}) custom-call(s32[192]{0:T(256)S(1)} %copy-done.138, s32[192]{0:T(256)S(1)} %copy-done.141, bf16[200,512]{1,0:T(8,128)(2,1)S(1)} %copy-done.121, bf16[200,512]{1,0:T(8,128)(2,1)S(1)} %get-tuple-element.156.refs_1_, ...), custom_call_target="tpu_custom_call", output_to_operand_aliasing={{0}: (14, {}), {1}: (15, {})} | custom-call | flops 1677721600 | bytes 8388608 | tf_op jit(solution)/shard_map/attention_grads/pallas_call | solution.py:554
  497.3 2.7 copy-done.23
  499.9 3.3 fusion.138
  504.0 2.7 collective-permute-done.71
  513.8 6.2 collective-permute-done.83
  529.4 12.4 %collective-permute-done.77 = bf16[3088,128]{1,0:T(8,128)(2,1)S(1)} collective-permute-done((bf16[3088,128]{1,0:T(8,128)(2,1)S(1)}, bf16[3088,128]{1,0:T(8,128)(2,1)S(1)}, u32[]{:S(2)}, u32[]{:S(2)}) %collective-permute-start.77) | collective-permute-done | bytes 790560 | tf_op jit(solution)/shard_map/ppermute | solution.py:691
  543.1 7.1 %collective-permute-done.58 = bf16[1536,128]{1,0:T(8,128)(2,1)S(1)} collective-permute-done((bf16[1536,128]{1,0:T(8,128)(2,1)S(1)}, bf16[1536,128]{1,0:T(8,128)(2,1)S(1)}, u32[]{:S(2)}, u32[]{:S(2)}) %collective-permute-start.58) | collective-permute-done | bytes 393248 | tf_op jit(solution)/shard_map/ppermute | solution.py:691
  554.5 12.7 %collective-permute-done.78 = bf16[3088,128]{1,0:T(8,128)(2,1)S(1)} collective-permute-done((bf16[3088,128]{1,0:T(8,128)(2,1)S(1)}, bf16[3088,128]{1,0:T(8,128)(2,1)S(1)}, u32[]{:S(2)}, u32[]{:S(2)}) %collective-permute-start.78) | collective-permute-done | bytes 790560 | tf_op jit(solution)/shard_map/ppermute | solution.py:691
  568.4 15.7 %collective-permute-done.59 = bf16[3088,128]{1,0:T(8,128)(2,1)S(1)} collective-permute-done((bf16[3088,128]{1,0:T(8,128)(2,1)S(1)}, bf16[3088,128]{1,0:T(8,128)(2,1)S(1)}, u32[]{:S(2)}, u32[]{:S(2)}) %collective-permute-start.59) | collective-permute-done | bytes 790560 | tf_op jit(solution)/shard_map/ppermute | solution.py:691
  589.1 28.0 %collective-permute-done.60 = bf16[3088,128]{1,0:T(8,128)(2,1)S(1)} collective-permute-done((bf16[3088,128]{1,0:T(8,128)(2,1)S(1)}, bf16[3088,128]{1,0:T(8,128)(2,1)S(1)}, u32[]{:S(2)}, u32[]{:S(2)}) %collective-permute-start.60) | collective-permute-done | bytes 790560 | tf_op jit(solution)/shard_map/ppermute | solution.py:691
  621.8 14.3 %collective-permute-done.61 = bf16[3088,128]{1,0:T(8,128)(2,1)S(1)} collective-permute-done((bf16[3088,128]{1,0:T(8,128)(2,1)S(1)}, bf16[3088,128]{1,0:T(8,128)(2,1)S(1)}, u32[]{:S(2)}, u32[]{:S(2)}) %collective-permute-start.61) | collective-permute-done | bytes 790560 | tf_op jit(solution)/shard_map/ppermute | solution.py:691
  643.7 3.4 collective-permute-done.88
  668.9 9.7 %update.1 = (f32[2,24,128,128]{3,2,1,0:T(8,128)}, f32[2,24,128,128]{3,2,1,0:T(8,128)}, f32[2,24,128,128]{3,2,1,0:T(8,128)}, bf16[2,24,128,128]{3,2,1,0:T(8,128)(2,1)}) custom-call(f32[1]{0:T(128)} %bitcast.79.clip_ref, f32[24,128,128]{2,1,0:T(8,128)S(1)} %rotate_in.2.rot0, f32[24,128,128]{2,1,0:T(8,128)S(1)} %rotate_in.3.rot1, ...), custom_call_target="tpu_custom_call" | custom-call | flops 402653184 | bytes 29884416 | tf_op jit(solution)/shard_map/update/pallas_call | solution.py:843
  (904 shorter events, 234.4 us)
Async XLA Ops:
  3.8 33.0 %collective-permute-start.21 = (bf16[3072,128]{1,0:T(8,128)(2,1)S(1)}, bf16[3072,128]{1,0:T(8,128)(2,1)}, u32[]{:S(2)}, u32[]{:S(2)}) collective-permute-start(bf16[3072,128]{1,0:T(8,128)(2,1)S(1)} %bitcast.209), channel_id=1, source_target_pairs={{0,8},{8,16},{16,24},{24,28},{28,20},{20,12},{12,4},{4,0},{1,9},{9... | collective-permute-start | bytes 2359304 | tf_op jit(solution)/shard_map/ppermute | solution.py:676
  6.8 30.8 %collective-permute-start.26 = (bf16[3072,128]{1,0:T(8,128)(2,1)S(1)}, bf16[3072,128]{1,0:T(8,128)(2,1)}, u32[]{:S(2)}, u32[]{:S(2)}) collective-permute-start(bf16[3072,128]{1,0:T(8,128)(2,1)S(1)} %bitcast.210), channel_id=1, source_target_pairs={{8,0},{16,8},{24,16},{28,24},{20,28},{12,20},{4,12},{0,4},{9,1},{1... | collective-permute-start | bytes 2359304 | tf_op jit(solution)/shard_map/ppermute | solution.py:676
  6.9 33.6 %collective-permute-start.33 = (bf16[3072,128]{1,0:T(8,128)(2,1)S(1)}, bf16[3072,128]{1,0:T(8,128)(2,1)S(1)}, u32[]{:S(2)}, u32[]{:S(2)}) collective-permute-start(bf16[3072,128]{1,0:T(8,128)(2,1)S(1)} %bitcast.211), channel_id=1, source_target_pairs={{0,1},{1,0},{2,3},{3,2},{4,5},{5,4},{6,7},{7,6},{8,9},{9,8},{10,11... | collective-permute-start | bytes 2359304 | tf_op jit(solution)/shard_map/ppermute | solution.py:919
  7.9 18.7 %collective-permute-start = (bf16[200,1024]{1,0:T(8,128)(2,1)}, bf16[200,1024]{1,0:T(8,128)(2,1)}, u32[]{:S(2)}, u32[]{:S(2)}) collective-permute-start(bf16[200,1024]{1,0:T(8,128)(2,1)} %reshape.719), channel_id=1, source_target_pairs={{0,2},{1,3},{2,0},{3,1},{4,6},{5,7},{6,4},{7,5},{8,10},{9,11},{10,... | collective-permute-start | bytes 1228808 | tf_op jit(solution)/shard_map/ppermute | solution.py:884
  35.1 20.6 %collective-permute-start.2 = (bf16[3088,128]{1,0:T(8,128)(2,1)S(1)}, bf16[3088,128]{1,0:T(8,128)(2,1)}, u32[]{:S(2)}, u32[]{:S(2)}) collective-permute-start(bf16[3088,128]{1,0:T(8,128)(2,1)S(1)} %pad_maximum_fusion.2.refs_0_), channel_id=1, source_target_pairs={{8,0},{16,8},{24,16},{28,24},{20,28},{12,20},{4,12},{0,4},{9,1},{1... | collective-permute-start | bytes 2371592 | tf_op jit(solution)/shard_map/ppermute | solution.py:676
  36.8 20.6 %collective-permute-start.6 = (bf16[3088,128]{1,0:T(8,128)(2,1)S(1)}, bf16[3088,128]{1,0:T(8,128)(2,1)S(1)}, u32[]{:S(2)}, u32[]{:S(2)}) collective-permute-start(bf16[3088,128]{1,0:T(8,128)(2,1)S(1)} %pad_maximum_fusion.2.refs_0_), channel_id=1, source_target_pairs={{0,8},{8,16},{16,24},{24,28},{28,20},{20,12},{12,4},{4,0},{1,9},{9... | collective-permute-start | bytes 2371592 | tf_op jit(solution)/shard_map/ppermute | solution.py:676
  37.6 34.5 %collective-permute-start.22 = (bf16[3072,128]{1,0:T(8,128)(2,1)}, bf16[3072,128]{1,0:T(8,128)(2,1)}, u32[]{:S(2)}, u32[]{:S(2)}) collective-permute-start(bf16[3072,128]{1,0:T(8,128)(2,1)} %collective-permute-done.21.refs_2_), channel_id=1, source_target_pairs={{0,8},{8,16},{16,24},{24,28},{28,20},{20,12},{12,4},{4,0},{1,9},{9... | collective-permute-start | bytes 2359304 | tf_op jit(solution)/shard_map/ppermute | solution.py:676
  41.3 37.2 %collective-permute-start.34 = (bf16[3072,128]{1,0:T(8,128)(2,1)}, bf16[3072,128]{1,0:T(8,128)(2,1)}, u32[]{:S(2)}, u32[]{:S(2)}) collective-permute-start(bf16[3072,128]{1,0:T(8,128)(2,1)} %collective-permute-done.21.refs_2_), channel_id=1, source_target_pairs={{0,1},{1,0},{2,3},{3,2},{4,5},{5,4},{6,7},{7,6},{8,9},{9,8},{10,11... | collective-permute-start | bytes 2359304 | tf_op jit(solution)/shard_map/ppermute | solution.py:919
  41.3 36.7 %collective-permute-start.27 = (bf16[3072,128]{1,0:T(8,128)(2,1)}, bf16[3072,128]{1,0:T(8,128)(2,1)}, u32[]{:S(2)}, u32[]{:S(2)}) collective-permute-start(bf16[3072,128]{1,0:T(8,128)(2,1)} %collective-permute-done.26.refs_4_), channel_id=1, source_target_pairs={{8,0},{16,8},{24,16},{28,24},{20,28},{12,20},{4,12},{0,4},{9,1},{1... | collective-permute-start | bytes 2359304 | tf_op jit(solution)/shard_map/ppermute | solution.py:676
  55.7 22.8 %collective-permute-start.35 = (bf16[3072,128]{1,0:T(8,128)(2,1)}, bf16[3072,128]{1,0:T(8,128)(2,1)}, u32[]{:S(2)}, u32[]{:S(2)}) collective-permute-start(bf16[3072,128]{1,0:T(8,128)(2,1)} %collective-permute-done.26.refs_4_), channel_id=1, source_target_pairs={{0,1},{1,0},{2,3},{3,2},{4,5},{5,4},{6,7},{7,6},{8,9},{9,8},{10,11... | collective-permute-start | bytes 2359304 | tf_op jit(solution)/shard_map/ppermute | solution.py:919
  57.4 22.9 %collective-permute-start.10 = (bf16[3088,128]{1,0:T(8,128)(2,1)}, bf16[3088,128]{1,0:T(8,128)(2,1)}, u32[]{:S(2)}, u32[]{:S(2)}) collective-permute-start(bf16[3088,128]{1,0:T(8,128)(2,1)} %collective-permute-done.2.refs_4_), channel_id=1, source_target_pairs={{0,1},{1,0},{2,3},{3,2},{4,5},{5,4},{6,7},{7,6},{8,9},{9,8},{10,11... | collective-permute-start | bytes 2371592 | tf_op jit(solution)/shard_map/ppermute | solution.py:919
  72.2 20.7 %collective-permute-start.3 = (bf16[3088,128]{1,0:T(8,128)(2,1)}, bf16[3088,128]{1,0:T(8,128)(2,1)S(1)}, u32[]{:S(2)}, u32[]{:S(2)}) collective-permute-start(bf16[3088,128]{1,0:T(8,128)(2,1)} %collective-permute-done.2.refs_4_), channel_id=1, source_target_pairs={{8,0},{16,8},{24,16},{28,24},{20,28},{12,20},{4,12},{0,4},{9,1},{1... | collective-permute-start | bytes 2371592 | tf_op jit(solution)/shard_map/ppermute | solution.py:676
  78.0 20.6 %collective-permute-start.7 = (bf16[3088,128]{1,0:T(8,128)(2,1)S(1)}, bf16[3088,128]{1,0:T(8,128)(2,1)S(1)}, u32[]{:S(2)}, u32[]{:S(2)}) collective-permute-start(bf16[3088,128]{1,0:T(8,128)(2,1)S(1)} %copy-done.77), channel_id=1, source_target_pairs={{0,8},{8,16},{16,24},{24,28},{28,20},{20,12},{12,4},{4,0},{1,9},{9... | collective-permute-start | bytes 2371592 | tf_op jit(solution)/shard_map/ppermute | solution.py:676
  78.5 20.1 %collective-permute-start.16 = (bf16[3088,128]{1,0:T(8,128)(2,1)S(1)}, bf16[3088,128]{1,0:T(8,128)(2,1)S(1)}, u32[]{:S(2)}, u32[]{:S(2)}) collective-permute-start(bf16[3088,128]{1,0:T(8,128)(2,1)S(1)} %copy-done.77), channel_id=1, source_target_pairs={{0,1},{1,0},{2,3},{3,2},{4,5},{5,4},{6,7},{7,6},{8,9},{9,8},{10,11... | collective-permute-start | bytes 2371592 | tf_op jit(solution)/shard_map/ppermute | solution.py:919
  78.6 34.1 %collective-permute-start.23 = (bf16[3072,128]{1,0:T(8,128)(2,1)}, bf16[3072,128]{1,0:T(8,128)(2,1)S(1)}, u32[]{:S(2)}, u32[]{:S(2)}) collective-permute-start(bf16[3072,128]{1,0:T(8,128)(2,1)} %collective-permute-done.22.refs_6_), channel_id=1, source_target_pairs={{0,8},{8,16},{16,24},{24,28},{28,20},{20,12},{12,4},{4,0},{1,9},{9... | collective-permute-start | bytes 2359304 | tf_op jit(solution)/shard_map/ppermute | solution.py:676
  80.2 33.6 %collective-permute-start.28 = (bf16[3072,128]{1,0:T(8,128)(2,1)}, bf16[3072,128]{1,0:T(8,128)(2,1)}, u32[]{:S(2)}, u32[]{:S(2)}) collective-permute-start(bf16[3072,128]{1,0:T(8,128)(2,1)} %collective-permute-done.27.refs_8_), channel_id=1, source_target_pairs={{8,0},{16,8},{24,16},{28,24},{20,28},{12,20},{4,12},{0,4},{9,1},{1... | collective-permute-start | bytes 2359304 | tf_op jit(solution)/shard_map/ppermute | solution.py:676
  92.9 21.0 %collective-permute-start.36 = (bf16[3072,128]{1,0:T(8,128)(2,1)}, bf16[3072,128]{1,0:T(8,128)(2,1)S(1)}, u32[]{:S(2)}, u32[]{:S(2)}) collective-permute-start(bf16[3072,128]{1,0:T(8,128)(2,1)} %collective-permute-done.22.refs_6_), channel_id=1, source_target_pairs={{0,1},{1,0},{2,3},{3,2},{4,5},{5,4},{6,7},{7,6},{8,9},{9,8},{10,11... | collective-permute-start | bytes 2359304 | tf_op jit(solution)/shard_map/ppermute | solution.py:919
  98.6 17.0 %collective-permute-start.37 = (bf16[3072,128]{1,0:T(8,128)(2,1)}, bf16[3072,128]{1,0:T(8,128)(2,1)S(1)}, u32[]{:S(2)}, u32[]{:S(2)}) collective-permute-start(bf16[3072,128]{1,0:T(8,128)(2,1)} %collective-permute-done.27.refs_8_), channel_id=1, source_target_pairs={{0,1},{1,0},{2,3},{3,2},{4,5},{5,4},{6,7},{7,6},{8,9},{9,8},{10,11... | collective-permute-start | bytes 2359304 | tf_op jit(solution)/shard_map/ppermute | solution.py:919
  98.6 29.3 %collective-permute-start.4 = (bf16[3088,128]{1,0:T(8,128)(2,1)S(1)}, bf16[3088,128]{1,0:T(8,128)(2,1)}, u32[]{:S(2)}, u32[]{:S(2)}) collective-permute-start(bf16[3088,128]{1,0:T(8,128)(2,1)S(1)} %collective-permute-done.3.refs_8_), channel_id=1, source_target_pairs={{8,0},{16,8},{24,16},{28,24},{20,28},{12,20},{4,12},{0,4},{9,1},{1... | collective-permute-start | bytes 2371592 | tf_op jit(solution)/shard_map/ppermute | solution.py:676
  112.6 20.6 %collective-permute-start.8 = (bf16[3088,128]{1,0:T(8,128)(2,1)S(1)}, bf16[3088,128]{1,0:T(8,128)(2,1)}, u32[]{:S(2)}, u32[]{:S(2)}) collective-permute-start(bf16[3088,128]{1,0:T(8,128)(2,1)S(1)} %collective-permute-done.7.refs_6_), channel_id=1, source_target_pairs={{0,8},{8,16},{16,24},{24,28},{28,20},{20,12},{12,4},{4,0},{1,9},{9... | collective-permute-start | bytes 2371592 | tf_op jit(solution)/shard_map/ppermute | solution.py:676
  113.8 21.2 %collective-permute-start.11 = (bf16[3088,128]{1,0:T(8,128)(2,1)S(1)}, bf16[3088,128]{1,0:T(8,128)(2,1)S(1)}, u32[]{:S(2)}, u32[]{:S(2)}) collective-permute-start(bf16[3088,128]{1,0:T(8,128)(2,1)S(1)} %collective-permute-done.3.refs_8_), channel_id=1, source_target_pairs={{0,1},{1,0},{2,3},{3,2},{4,5},{5,4},{6,7},{7,6},{8,9},{9,8},{10,11... | collective-permute-start | bytes 2371592 | tf_op jit(solution)/shard_map/ppermute | solution.py:919
  113.9 21.5 %collective-permute-start.15 = (bf16[3088,128]{1,0:T(8,128)(2,1)S(1)}, bf16[3088,128]{1,0:T(8,128)(2,1)S(1)}, u32[]{:S(2)}, u32[]{:S(2)}) collective-permute-start(bf16[3088,128]{1,0:T(8,128)(2,1)S(1)} %collective-permute-done.7.refs_6_), channel_id=1, source_target_pairs={{0,1},{1,0},{2,3},{3,2},{4,5},{5,4},{6,7},{7,6},{8,9},{9,8},{10,11... | collective-permute-start | bytes 2371592 | tf_op jit(solution)/shard_map/ppermute | solution.py:919
  115.6 22.0 %collective-permute-start.24 = (bf16[1536,128]{1,0:T(8,128)(2,1)S(1)}, bf16[1536,128]{1,0:T(8,128)(2,1)S(1)}, u32[]{:S(2)}, u32[]{:S(2)}) collective-permute-start(bf16[1536,128]{1,0:T(8,128)(2,1)S(1)} %slice.794), channel_id=1, source_target_pairs={{0,8},{8,16},{16,24},{24,28},{28,20},{20,12},{12,4},{4,0},{1,9},{9... | collective-permute-start | bytes 1179656 | tf_op jit(solution)/shard_map/ppermute | solution.py:679
  133.2 25.7 %collective-permute-start.31 = (bf16[3072,128]{1,0:T(8,128)(2,1)S(1)}, bf16[3072,128]{1,0:T(8,128)(2,1)S(1)}, u32[]{:S(2)}, u32[]{:S(2)}) collective-permute-start(bf16[3072,128]{1,0:T(8,128)(2,1)S(1)} %collective-permute-done.23.refs_0_), channel_id=1, source_target_pairs={{0,1},{1,0},{2,3},{3,2},{4,5},{5,4},{6,7},{7,6},{8,9},{9,8},{10,11... | collective-permute-start | bytes 2359304 | tf_op jit(solution)/shard_map/ppermute | solution.py:919
  135.4 24.7 %collective-permute-start.32 = (bf16[3072,128]{1,0:T(8,128)(2,1)}, bf16[3072,128]{1,0:T(8,128)(2,1)}, u32[]{:S(2)}, u32[]{:S(2)}) collective-permute-start(bf16[3072,128]{1,0:T(8,128)(2,1)} %collective-permute-done.28.refs_2_), channel_id=1, source_target_pairs={{0,1},{1,0},{2,3},{3,2},{4,5},{5,4},{6,7},{7,6},{8,9},{9,8},{10,11... | collective-permute-start | bytes 2359304 | tf_op jit(solution)/shard_map/ppermute | solution.py:919
  137.5 21.0 %collective-permute-start.5 = (bf16[1552,128]{1,0:T(8,128)(2,1)S(1)}, bf16[1552,128]{1,0:T(8,128)(2,1)S(1)}, u32[]{:S(2)}, u32[]{:S(2)}) collective-permute-start(bf16[1552,128]{1,0:T(8,128)(2,1)S(1)} %slice.753), channel_id=1, source_target_pairs={{8,0},{16,8},{24,16},{28,24},{20,28},{12,20},{4,12},{0,4},{9,1},{1... | collective-permute-start | bytes 1191944 | tf_op jit(solution)/shard_map/ppermute | solution.py:680
  139.3 40.3 %collective-permute-start.12 = (bf16[3088,128]{1,0:T(8,128)(2,1)}, bf16[3088,128]{1,0:T(8,128)(2,1)}, u32[]{:S(2)}, u32[]{:S(2)}) collective-permute-start(bf16[3088,128]{1,0:T(8,128)(2,1)} %collective-permute-done.4.refs_2_), channel_id=1, source_target_pairs={{0,1},{1,0},{2,3},{3,2},{4,5},{5,4},{6,7},{7,6},{8,9},{9,8},{10,11... | collective-permute-start | bytes 2371592 | tf_op jit(solution)/shard_map/ppermute | solution.py:919
  146.5 33.8 %collective-permute-start.14 = (bf16[3088,128]{1,0:T(8,128)(2,1)}, bf16[3088,128]{1,0:T(8,128)(2,1)}, u32[]{:S(2)}, u32[]{:S(2)}) collective-permute-start(bf16[3088,128]{1,0:T(8,128)(2,1)} %collective-permute-done.8.refs_0_), channel_id=1, source_target_pairs={{0,1},{1,0},{2,3},{3,2},{4,5},{5,4},{6,7},{7,6},{8,9},{9,8},{10,11... | collective-permute-start | bytes 2371592 | tf_op jit(solution)/shard_map/ppermute | solution.py:919
  160.1 31.5 %collective-permute-start.18 = (bf16[1536,128]{1,0:T(8,128)(2,1)}, bf16[1536,128]{1,0:T(8,128)(2,1)}, u32[]{:S(2)}, u32[]{:S(2)}) collective-permute-start(bf16[1536,128]{1,0:T(8,128)(2,1)} %copy-done.118), channel_id=1, source_target_pairs={{0,1},{1,0},{2,3},{3,2},{4,5},{5,4},{6,7},{7,6},{8,9},{9,8},{10,11... | collective-permute-start | bytes 1179656 | tf_op jit(solution)/shard_map/ppermute | solution.py:919
  170.8 18.8 %collective-permute-start.13 = (bf16[1552,128]{1,0:T(8,128)(2,1)S(1)}, bf16[1552,128]{1,0:T(8,128)(2,1)S(1)}, u32[]{:S(2)}, u32[]{:S(2)}) collective-permute-start(bf16[1552,128]{1,0:T(8,128)(2,1)S(1)} %collective-permute-done.5.refs_2_), channel_id=1, source_target_pairs={{0,1},{1,0},{2,3},{3,2},{4,5},{5,4},{6,7},{7,6},{8,9},{9,8},{10,11... | collective-permute-start | bytes 1191944 | tf_op jit(solution)/shard_map/ppermute | solution.py:919
  290.7 57.3 %collective-permute-start.42 = (bf16[200,1024]{1,0:T(8,128)(2,1)S(1)}, bf16[200,1024]{1,0:T(8,128)(2,1)S(1)}, u32[]{:S(2)}, u32[]{:S(2)}) collective-permute-start(bf16[200,1024]{1,0:T(8,128)(2,1)S(1)} %broadcast_select_fusion.5), channel_id=1, source_target_pairs={{0,2},{1,3},{2,0},{3,1},{4,6},{5,7},{6,4},{7,5},{8,10},{9,11},{10,... | collective-permute-start | bytes 1228808 | tf_op jit(solution)/shard_map/ppermute | solution.py:957
  298.3 28.0 %collective-permute-start.44 = (bf16[200,1024]{1,0:T(8,128)(2,1)S(1)}, bf16[200,1024]{1,0:T(8,128)(2,1)S(1)}, u32[]{:S(2)}, u32[]{:S(2)}) collective-permute-start(bf16[200,1024]{1,0:T(8,128)(2,1)S(1)} %get-tuple-element.130.own_ref), channel_id=1, source_target_pairs={{0,2},{1,3},{2,0},{3,1},{4,6},{5,7},{6,4},{7,5},{8,10},{9,11},{10,... | collective-permute-start | bytes 1228808 | tf_op jit(solution)/shard_map/ppermute | solution.py:957
  305.8 30.4 %collective-permute-start.47 = (bf16[200,1024]{1,0:T(8,128)(2,1)S(1)}, bf16[200,1024]{1,0:T(8,128)(2,1)S(1)}, u32[]{:S(2)}, u32[]{:S(2)}) collective-permute-start(bf16[200,1024]{1,0:T(8,128)(2,1)S(1)} %get-tuple-element.142.own_ref), channel_id=1, source_target_pairs={{0,2},{1,3},{2,0},{3,1},{4,6},{5,7},{6,4},{7,5},{8,10},{9,11},{10,... | collective-permute-start | bytes 1228808 | tf_op jit(solution)/shard_map/ppermute | solution.py:957
  353.2 47.9 %collective-permute-start.45 = (bf16[200,1024]{1,0:T(8,128)(2,1)}, bf16[200,1024]{1,0:T(8,128)(2,1)}, u32[]{:S(2)}, u32[]{:S(2)}) collective-permute-start(bf16[200,1024]{1,0:T(8,128)(2,1)} %copy-done.114), channel_id=1, source_target_pairs={{0,2},{1,3},{2,0},{3,1},{4,6},{5,7},{6,4},{7,5},{8,10},{9,11},{10,... | collective-permute-start | bytes 1228808 | tf_op jit(solution)/shard_map/ppermute | solution.py:957
  355.1 57.8 %collective-permute-start.48 = (bf16[200,1024]{1,0:T(8,128)(2,1)}, bf16[200,1024]{1,0:T(8,128)(2,1)}, u32[]{:S(2)}, u32[]{:S(2)}) collective-permute-start(bf16[200,1024]{1,0:T(8,128)(2,1)} %copy-done.112), channel_id=1, source_target_pairs={{0,2},{1,3},{2,0},{3,1},{4,6},{5,7},{6,4},{7,5},{8,10},{9,11},{10,... | collective-permute-start | bytes 1228808 | tf_op jit(solution)/shard_map/ppermute | solution.py:957
  399.1 22.6 %collective-permute-start.74 = (bf16[3072,128]{1,0:T(8,128)(2,1)}, bf16[3072,128]{1,0:T(8,128)(2,1)}, u32[]{:S(2)}, u32[]{:S(2)}) collective-permute-start(bf16[3072,128]{1,0:T(8,128)(2,1)} %get-tuple-element.326), channel_id=1, source_target_pairs={{0,1},{1,0},{2,3},{3,2},{4,5},{5,4},{6,7},{7,6},{8,9},{9,8},{10,11... | collective-permute-start | bytes 2359304 | tf_op jit(solution)/shard_map/ppermute | solution.py:919
  399.2 22.9 %collective-permute-start.82 = (bf16[3072,128]{1,0:T(8,128)(2,1)}, bf16[3072,128]{1,0:T(8,128)(2,1)}, u32[]{:S(2)}, u32[]{:S(2)}) collective-permute-start(bf16[3072,128]{1,0:T(8,128)(2,1)} %get-tuple-element.327), channel_id=1, source_target_pairs={{0,1},{1,0},{2,3},{3,2},{4,5},{5,4},{6,7},{7,6},{8,9},{9,8},{10,11... | collective-permute-start | bytes 2359304 | tf_op jit(solution)/shard_map/ppermute | solution.py:919
  399.7 22.5 %collective-permute-start.81 = (bf16[3072,128]{1,0:T(8,128)(2,1)}, bf16[3072,128]{1,0:T(8,128)(2,1)}, u32[]{:S(2)}, u32[]{:S(2)}) collective-permute-start(bf16[3072,128]{1,0:T(8,128)(2,1)} %get-tuple-element.328), channel_id=1, source_target_pairs={{0,1},{1,0},{2,3},{3,2},{4,5},{5,4},{6,7},{7,6},{8,9},{9,8},{10,11... | collective-permute-start | bytes 2359304 | tf_op jit(solution)/shard_map/ppermute | solution.py:919
  401.1 35.6 %collective-permute-start.80 = (bf16[3072,128]{1,0:T(8,128)(2,1)}, bf16[3072,128]{1,0:T(8,128)(2,1)S(1)}, u32[]{:S(2)}, u32[]{:S(2)}) collective-permute-start(bf16[3072,128]{1,0:T(8,128)(2,1)} %get-tuple-element.329), channel_id=1, source_target_pairs={{0,1},{1,0},{2,3},{3,2},{4,5},{5,4},{6,7},{7,6},{8,9},{9,8},{10,11... | collective-permute-start | bytes 2359304 | tf_op jit(solution)/shard_map/ppermute | solution.py:919
  412.9 26.6 %collective-permute-start.75 = (bf16[3072,128]{1,0:T(8,128)(2,1)}, bf16[3072,128]{1,0:T(8,128)(2,1)S(1)}, u32[]{:S(2)}, u32[]{:S(2)}) collective-permute-start(bf16[3072,128]{1,0:T(8,128)(2,1)} %get-tuple-element.330), channel_id=1, source_target_pairs={{0,1},{1,0},{2,3},{3,2},{4,5},{5,4},{6,7},{7,6},{8,9},{9,8},{10,11... | collective-permute-start | bytes 2359304 | tf_op jit(solution)/shard_map/ppermute | solution.py:919
  421.7 18.0 %collective-permute-start.73 = (bf16[3072,128]{1,0:T(8,128)(2,1)}, bf16[3072,128]{1,0:T(8,128)(2,1)S(1)}, u32[]{:S(2)}, u32[]{:S(2)}) collective-permute-start(bf16[3072,128]{1,0:T(8,128)(2,1)} %get-tuple-element.331), channel_id=1, source_target_pairs={{0,1},{1,0},{2,3},{3,2},{4,5},{5,4},{6,7},{7,6},{8,9},{9,8},{10,11... | collective-permute-start | bytes 2359304 | tf_op jit(solution)/shard_map/ppermute | solution.py:919
  422.1 17.5 %collective-permute-start.72 = (bf16[3072,128]{1,0:T(8,128)(2,1)}, bf16[3072,128]{1,0:T(8,128)(2,1)S(1)}, u32[]{:S(2)}, u32[]{:S(2)}) collective-permute-start(bf16[3072,128]{1,0:T(8,128)(2,1)} %get-tuple-element.332), channel_id=1, source_target_pairs={{0,1},{1,0},{2,3},{3,2},{4,5},{5,4},{6,7},{7,6},{8,9},{9,8},{10,11... | collective-permute-start | bytes 2359304 | tf_op jit(solution)/shard_map/ppermute | solution.py:919
  422.2 17.5 %collective-permute-start.69 = (bf16[3072,128]{1,0:T(8,128)(2,1)}, bf16[3072,128]{1,0:T(8,128)(2,1)S(1)}, u32[]{:S(2)}, u32[]{:S(2)}) collective-permute-start(bf16[3072,128]{1,0:T(8,128)(2,1)} %get-tuple-element.333), channel_id=1, source_target_pairs={{0,1},{1,0},{2,3},{3,2},{4,5},{5,4},{6,7},{7,6},{8,9},{9,8},{10,11... | collective-permute-start | bytes 2359304 | tf_op jit(solution)/shard_map/ppermute | solution.py:919
  439.6 19.2 %collective-permute-start.49 = (bf16[200,1024]{1,0:T(8,128)(2,1)S(1)}, bf16[200,1024]{1,0:T(8,128)(2,1)S(1)}, u32[]{:S(2)}, u32[]{:S(2)}) collective-permute-start(bf16[200,1024]{1,0:T(8,128)(2,1)S(1)} %get-tuple-element.149.own_ref), channel_id=1, source_target_pairs={{0,2},{1,3},{2,0},{3,1},{4,6},{5,7},{6,4},{7,5},{8,10},{9,11},{10,... | collective-permute-start | bytes 1228808 | tf_op jit(solution)/shard_map/ppermute | solution.py:957
  450.1 58.2 %collective-permute-start.76 = (bf16[1536,128]{1,0:T(8,128)(2,1)}, bf16[1536,128]{1,0:T(8,128)(2,1)}, u32[]{:S(2)}, u32[]{:S(2)}) collective-permute-start(bf16[1536,128]{1,0:T(8,128)(2,1)} %slice.831), channel_id=1, source_target_pairs={{0,8},{8,16},{16,24},{24,28},{28,20},{20,12},{12,4},{4,0},{1,9},{9... | collective-permute-start | bytes 1179656 | tf_op jit(solution)/shard_map/ppermute | solution.py:691
  469.2 42.2 %collective-permute-start.50 = (bf16[200,1024]{1,0:T(8,128)(2,1)}, bf16[200,1024]{1,0:T(8,128)(2,1)}, u32[]{:S(2)}, u32[]{:S(2)}) collective-permute-start(bf16[200,1024]{1,0:T(8,128)(2,1)} %broadcast_select_fusion.6), channel_id=1, source_target_pairs={{0,2},{1,3},{2,0},{3,1},{4,6},{5,7},{6,4},{7,5},{8,10},{9,11},{10,... | collective-permute-start | bytes 1228808 | tf_op jit(solution)/shard_map/ppermute | solution.py:957
  473.5 29.8 %collective-permute-start.70 = (f32[8,2,384]{2,0,1:T(8,128)S(1)}, f32[8,2,384]{2,0,1:T(8,128)S(1)}, u32[]{:S(2)}, u32[]{:S(2)}) collective-permute-start(f32[8,2,384]{2,0,1:T(8,128)S(1)} %slice.827), channel_id=1, source_target_pairs={{0,2},{1,3},{2,0},{3,1},{4,6},{5,7},{6,4},{7,5},{8,10},{9,11},{10,... | collective-permute-start | bytes 73736 | tf_op jit(solution)/shard_map/ppermute | solution.py:957
  473.8 30.0 %collective-permute-start.52 = (f32[8,2,384]{2,0,1:T(8,128)S(1)}, f32[8,2,384]{2,0,1:T(8,128)S(1)}, u32[]{:S(2)}, u32[]{:S(2)}) collective-permute-start(f32[8,2,384]{2,0,1:T(8,128)S(1)} %slice.807), channel_id=1, source_target_pairs={{0,2},{1,3},{2,0},{3,1},{4,6},{5,7},{6,4},{7,5},{8,10},{9,11},{10,... | collective-permute-start | bytes 73736 | tf_op jit(solution)/shard_map/ppermute | solution.py:957
  503.2 16.8 %collective-permute-start.56 = (bf16[3072,128]{1,0:T(8,128)(2,1)S(1)}, bf16[3072,128]{1,0:T(8,128)(2,1)S(1)}, u32[]{:S(2)}, u32[]{:S(2)}) collective-permute-start(bf16[3072,128]{1,0:T(8,128)(2,1)S(1)} %get-tuple-element.311), channel_id=1, source_target_pairs={{0,1},{1,0},{2,3},{3,2},{4,5},{5,4},{6,7},{7,6},{8,9},{9,8},{10,11... | collective-permute-start | bytes 2359304 | tf_op jit(solution)/shard_map/ppermute | solution.py:919
  503.3 17.2 %collective-permute-start.64 = (bf16[3072,128]{1,0:T(8,128)(2,1)S(1)}, bf16[3072,128]{1,0:T(8,128)(2,1)S(1)}, u32[]{:S(2)}, u32[]{:S(2)}) collective-permute-start(bf16[3072,128]{1,0:T(8,128)(2,1)S(1)} %get-tuple-element.312), channel_id=1, source_target_pairs={{0,1},{1,0},{2,3},{3,2},{4,5},{5,4},{6,7},{7,6},{8,9},{9,8},{10,11... | collective-permute-start | bytes 2359304 | tf_op jit(solution)/shard_map/ppermute | solution.py:919
  521.2 20.6 %collective-permute-start.77 = (bf16[3088,128]{1,0:T(8,128)(2,1)S(1)}, bf16[3088,128]{1,0:T(8,128)(2,1)S(1)}, u32[]{:S(2)}, u32[]{:S(2)}) collective-permute-start(bf16[3088,128]{1,0:T(8,128)(2,1)S(1)} %fusion.30), channel_id=1, source_target_pairs={{0,8},{8,16},{16,24},{24,28},{28,20},{20,12},{12,4},{4,0},{1,9},{9... | collective-permute-start | bytes 2371592 | tf_op jit(solution)/shard_map/ppermute | solution.py:691
  522.3 30.3 %collective-permute-start.84 = (bf16[3088,128]{1,0:T(8,128)(2,1)S(1)}, bf16[3088,128]{1,0:T(8,128)(2,1)S(1)}, u32[]{:S(2)}, u32[]{:S(2)}) collective-permute-start(bf16[3088,128]{1,0:T(8,128)(2,1)S(1)} %pad_maximum_fusion.4), channel_id=1, source_target_pairs={{8,0},{16,8},{24,16},{28,24},{20,28},{12,20},{4,12},{0,4},{9,1},{1... | collective-permute-start | bytes 2371592 | tf_op jit(solution)/shard_map/ppermute | solution.py:691
  527.2 24.2 %collective-permute-start.65 = (bf16[1552,128]{1,0:T(8,128)(2,1)S(1)}, bf16[1552,128]{1,0:T(8,128)(2,1)S(1)}, u32[]{:S(2)}, u32[]{:S(2)}) collective-permute-start(bf16[1552,128]{1,0:T(8,128)(2,1)S(1)} %pad_maximum_fusion.6), channel_id=1, source_target_pairs={{8,0},{16,8},{24,16},{28,24},{20,28},{12,20},{4,12},{0,4},{9,1},{1... | collective-permute-start | bytes 1191944 | tf_op jit(solution)/shard_map/ppermute | solution.py:691
  528.9 21.3 %collective-permute-start.58 = (bf16[1536,128]{1,0:T(8,128)(2,1)S(1)}, bf16[1536,128]{1,0:T(8,128)(2,1)S(1)}, u32[]{:S(2)}, u32[]{:S(2)}) collective-permute-start(bf16[1536,128]{1,0:T(8,128)(2,1)S(1)} %slice.811), channel_id=1, source_target_pairs={{0,8},{8,16},{16,24},{24,28},{28,20},{20,12},{12,4},{4,0},{1,9},{9... | collective-permute-start | bytes 1179656 | tf_op jit(solution)/shard_map/ppermute | solution.py:691
  542.0 25.2 %collective-permute-start.78 = (bf16[3088,128]{1,0:T(8,128)(2,1)S(1)}, bf16[3088,128]{1,0:T(8,128)(2,1)S(1)}, u32[]{:S(2)}, u32[]{:S(2)}) collective-permute-start(bf16[3088,128]{1,0:T(8,128)(2,1)S(1)} %fusion.9), channel_id=1, source_target_pairs={{0,8},{8,16},{16,24},{24,28},{28,20},{20,12},{12,4},{4,0},{1,9},{9... | collective-permute-start | bytes 2371592 | tf_op jit(solution)/shard_map/ppermute | solution.py:691
  550.4 33.7 %collective-permute-start.59 = (bf16[3088,128]{1,0:T(8,128)(2,1)S(1)}, bf16[3088,128]{1,0:T(8,128)(2,1)S(1)}, u32[]{:S(2)}, u32[]{:S(2)}) collective-permute-start(bf16[3088,128]{1,0:T(8,128)(2,1)S(1)} %fusion.28), channel_id=1, source_target_pairs={{0,8},{8,16},{16,24},{24,28},{28,20},{20,12},{12,4},{4,0},{1,9},{9... | collective-permute-start | bytes 2371592 | tf_op jit(solution)/shard_map/ppermute | solution.py:691
  551.6 33.7 %collective-permute-start.66 = (bf16[3088,128]{1,0:T(8,128)(2,1)S(1)}, bf16[3088,128]{1,0:T(8,128)(2,1)S(1)}, u32[]{:S(2)}, u32[]{:S(2)}) collective-permute-start(bf16[3088,128]{1,0:T(8,128)(2,1)S(1)} %pad_maximum_fusion.3), channel_id=1, source_target_pairs={{8,0},{16,8},{24,16},{28,24},{20,28},{12,20},{4,12},{0,4},{9,1},{1... | collective-permute-start | bytes 2371592 | tf_op jit(solution)/shard_map/ppermute | solution.py:691
  553.0 33.6 %collective-permute-start.85 = (bf16[3088,128]{1,0:T(8,128)(2,1)S(1)}, bf16[3088,128]{1,0:T(8,128)(2,1)S(1)}, u32[]{:S(2)}, u32[]{:S(2)}) collective-permute-start(bf16[3088,128]{1,0:T(8,128)(2,1)S(1)} %fusion.11), channel_id=1, source_target_pairs={{8,0},{16,8},{24,16},{28,24},{20,28},{12,20},{4,12},{0,4},{9,1},{1... | collective-permute-start | bytes 2371592 | tf_op jit(solution)/shard_map/ppermute | solution.py:691
  567.4 52.3 %collective-permute-start.79 = (bf16[3088,128]{1,0:T(8,128)(2,1)S(1)}, bf16[3088,128]{1,0:T(8,128)(2,1)S(1)}, u32[]{:S(2)}, u32[]{:S(2)}) collective-permute-start(bf16[3088,128]{1,0:T(8,128)(2,1)S(1)} %fusion.8), channel_id=1, source_target_pairs={{0,8},{8,16},{16,24},{24,28},{28,20},{20,12},{12,4},{4,0},{1,9},{9... | collective-permute-start | bytes 2371592 | tf_op jit(solution)/shard_map/ppermute | solution.py:691
  584.3 32.8 %collective-permute-start.60 = (bf16[3088,128]{1,0:T(8,128)(2,1)S(1)}, bf16[3088,128]{1,0:T(8,128)(2,1)S(1)}, u32[]{:S(2)}, u32[]{:S(2)}) collective-permute-start(bf16[3088,128]{1,0:T(8,128)(2,1)S(1)} %fusion.4), channel_id=1, source_target_pairs={{0,8},{8,16},{16,24},{24,28},{28,20},{20,12},{12,4},{4,0},{1,9},{9... | collective-permute-start | bytes 2371592 | tf_op jit(solution)/shard_map/ppermute | solution.py:691
  585.5 32.9 %collective-permute-start.67 = (bf16[3088,128]{1,0:T(8,128)(2,1)S(1)}, bf16[3088,128]{1,0:T(8,128)(2,1)S(1)}, u32[]{:S(2)}, u32[]{:S(2)}) collective-permute-start(bf16[3088,128]{1,0:T(8,128)(2,1)S(1)} %fusion.6), channel_id=1, source_target_pairs={{8,0},{16,8},{24,16},{28,24},{20,28},{12,20},{4,12},{0,4},{9,1},{1... | collective-permute-start | bytes 2371592 | tf_op jit(solution)/shard_map/ppermute | solution.py:691
  586.9 33.5 %collective-permute-start.86 = (bf16[3088,128]{1,0:T(8,128)(2,1)S(1)}, bf16[3088,128]{1,0:T(8,128)(2,1)S(1)}, u32[]{:S(2)}, u32[]{:S(2)}) collective-permute-start(bf16[3088,128]{1,0:T(8,128)(2,1)S(1)} %fusion.10), channel_id=1, source_target_pairs={{8,0},{16,8},{24,16},{28,24},{20,28},{12,20},{4,12},{0,4},{9,1},{1... | collective-permute-start | bytes 2371592 | tf_op jit(solution)/shard_map/ppermute | solution.py:691
  617.3 18.8 %collective-permute-start.61 = (bf16[3088,128]{1,0:T(8,128)(2,1)S(1)}, bf16[3088,128]{1,0:T(8,128)(2,1)S(1)}, u32[]{:S(2)}, u32[]{:S(2)}) collective-permute-start(bf16[3088,128]{1,0:T(8,128)(2,1)S(1)} %fusion.3), channel_id=1, source_target_pairs={{0,8},{8,16},{16,24},{24,28},{28,20},{20,12},{12,4},{4,0},{1,9},{9... | collective-permute-start | bytes 2371592 | tf_op jit(solution)/shard_map/ppermute | solution.py:691
  618.6 18.7 %collective-permute-start.68 = (bf16[3088,128]{1,0:T(8,128)(2,1)S(1)}, bf16[3088,128]{1,0:T(8,128)(2,1)S(1)}, u32[]{:S(2)}, u32[]{:S(2)}) collective-permute-start(bf16[3088,128]{1,0:T(8,128)(2,1)S(1)} %fusion.5), channel_id=1, source_target_pairs={{8,0},{16,8},{24,16},{28,24},{20,28},{12,20},{4,12},{0,4},{9,1},{1... | collective-permute-start | bytes 2371592 | tf_op jit(solution)/shard_map/ppermute | solution.py:691
  (257 other events, 2036.1 us)

commit v2 on v1

--- a/solution.py
+++ b/solution.py
@@ -29,9 +29,10 @@
 ANY = pl.BlockSpec(memory_space=pl.ANY)
 SMEM = pl.BlockSpec(memory_space=pltpu.SMEM)
 VMEM = pl.BlockSpec(memory_space=pltpu.VMEM)
-
-
-def params(mib):
+HBM = pl.BlockSpec(memory_space=pltpu.HBM)
+
+
+def params(mib=30):
     return pltpu.CompilerParams(vmem_limit_bytes=mib << 20)
 
 
@@ -141,9 +142,9 @@
         functools.partial(attention_forward, first),
         out_shape=outs,
         grid=(1,),
-        in_specs=[full(*a.shape) for a in args[:-1]] + [full(ATT_ROWS, D)],
+        in_specs=[full(*a.shape) for a in args[:-1]] + [VMEM],
         out_specs=[full(*o.shape) for o in outs],
-        compiler_params=params(32),
+        compiler_params=params(),
         cost_estimate=cost(2 * rows * D * 4 * WID * 2, 6 << 20),
         name="attention_forward",
     )(*args)
@@ -153,7 +154,7 @@
 STEP_HID = HID // STEPS
 
 
-def mlp_forward(hid_ref, own_ref, got_ref, vecs, up_ref, down_ref, *rest):
+def mlp_forward(hid_ref, own_ref, got_ref, vecs, weights, *rest):
     mid_ref, n2_ref, act_ref, slope_ref, part_ref, total = rest
     step = pl.program_id(0)
 
@@ -170,14 +171,14 @@
     bias = jnp.where(
         step % 2 == 0, vecs[pl.ds(row, 1), 0:STEP_HID], vecs[pl.ds(row, 1), STEP_HID:D]
     )
-    upward = dot(n2_ref[...], up_ref[...]) + bias
+    upward = dot(n2_ref[...], up_part(weights, step)) + bias
     cdf = 0.5 + 0.5 * lax.erf(upward * 0.7071067811865476)
     act = (upward * cdf).astype(BF)
     act_ref[...] = act
     slope_ref[...] = (
         cdf + upward * (jnp.exp(-0.5 * upward * upward) * 0.3989422804014327)
     ).astype(BF)
-    term = dot(act, down_ref[...])
+    term = dot(act, down_part(weights, step))
 
     @pl.when(step == 0)
     def _():
@@ -196,11 +197,13 @@
     return pl.BlockSpec((rows, cols), lambda s: (0, 0))
 
 
-def mlp_weight_specs():
-    return [
-        pl.BlockSpec((D, STEP_HID), lambda s: (2 + s // 2, s % 2)),
-        pl.BlockSpec((STEP_HID, D), lambda s: (2 * STEPS + s, 0)),
-    ]
+def up_part(weights, step):
+    rows = pl.ds(pl.multiple_of(2 * D + step // 2 * D, D), D)
+    return weights[rows, pl.ds(pl.multiple_of(step % 2 * STEP_HID, STEP_HID), STEP_HID)]
+
+
+def down_part(weights, step):
+    return weights[pl.ds(pl.multiple_of(4 * D + step * STEP_HID, STEP_HID), STEP_HID), :]
 
 
 def call_mlp_forward(hidden, own, got, vecs, weights):
@@ -215,7 +218,7 @@
             jax.ShapeDtypeStruct((rows, HID), BF),
             jax.ShapeDtypeStruct((rows, D), BF),
         ],
-        in_specs=[full(rows, D), full(rows, D), full(rows, D), full(16, D)] + mlp_weight_specs(),
+        in_specs=[full(rows, D), full(rows, D), full(rows, D), full(16, D), VMEM],
         out_specs=[
             full(rows, D),
             full(rows, D),
@@ -224,20 +227,20 @@
             full(rows, D),
         ],
         scratch_shapes=[pltpu.VMEM((rows, D), F32)],
-        compiler_params=params(32),
+        compiler_params=params(),
         cost_estimate=cost(2 * rows * D * 2 * HID * 2, 12 << 20),
         name="mlp_forward",
-    )(hidden, own, got, vecs, weights, weights)
+    )(hidden, own, got, vecs, weights)
 
 
 def mlp_backward(first, *refs):
     if first:
-        grad_ref, mid_ref, slope_ref, vecs, down_ref, up_ref = refs[:6]
-        gd_ref, gu_ref, part_ref, sums_ref, total = refs[6:]
+        grad_ref, mid_ref, slope_ref, vecs, weights = refs[:5]
+        gd_ref, gu_ref, part_ref, sums_ref, total = refs[5:]
     else:
         (gm_ref, own_ref, got_ref, hid_ref, above) = refs[:5]
-        mid_ref, slope_ref, vecs, down_ref, up_ref = refs[5:10]
-        grad_out_ref, gd_ref, gu_ref, part_ref, sums_ref, total = refs[10:]
+        mid_ref, slope_ref, vecs, weights = refs[5:9]
+        grad_out_ref, gd_ref, gu_ref, part_ref, sums_ref, total = refs[9:]
     step = pl.program_id(0)
 
     @pl.when(step == 0)
@@ -253,7 +256,7 @@
         sums_ref[...] = jnp.zeros_like(sums_ref)
         sums_ref[2:3, :] = jnp.sum(gd_ref[...].astype(F32), axis=0, keepdims=True)
 
-    grad_up = (slope_ref[...].astype(F32) * dot_nt(gd_ref[...], down_ref[...])).astype(BF)
+    grad_up = (slope_ref[...].astype(F32) * dot_nt(gd_ref[...], down_part(weights, step))).astype(BF)
     gu_ref[...] = grad_up
     sums = jnp.sum(grad_up.astype(F32), axis=0, keepdims=True)
     for at in range(STEPS):
@@ -264,7 +267,7 @@
                 sums
             )
 
-    term = dot_nt(grad_up, up_ref[...])
+    term = dot_nt(grad_up, up_part(weights, step))
 
     @pl.when(step == 0)
     def _():
@@ -306,14 +309,13 @@
         grid=(STEPS,),
         out_shape=outs,
         in_specs=specs
-        + [full(rows, D), pl.BlockSpec((rows, STEP_HID), lambda s: (0, s)), full(16, D)]
-        + mlp_weight_specs()[::-1],
+        + [full(rows, D), pl.BlockSpec((rows, STEP_HID), lambda s: (0, s)), full(16, D), VMEM],
         out_specs=out_specs,
         scratch_shapes=[pltpu.VMEM((rows, D), F32)],
-        compiler_params=params(36),
+        compiler_params=params(),
         cost_estimate=cost(2 * rows * D * 2 * HID * 2, 12 << 20),
         name="mlp_backward",
-    )(*operands, middle, slope, vecs, weights, weights)
+    )(*operands, middle, slope, vecs, weights)
 
 
 def attention_backward(
@@ -395,9 +397,9 @@
         attention_backward,
         grid=(1,),
         out_shape=outs,
-        in_specs=[full(*a.shape) for a in args[:-1]] + [full(ATT_ROWS, D)],
+        in_specs=[full(*a.shape) for a in args[:-1]] + [VMEM],
         out_specs=[full(*o.shape) for o in outs],
-        compiler_params=params(40),
+        compiler_params=params(),
         cost_estimate=cost(2 * rows * D * 4 * WID * 3, 8 << 20),
         name="attention_backward",
     )(*args)
@@ -481,7 +483,7 @@
             ],
         ),
         out_shape=[buffer, buffer],
-        compiler_params=params(32),
+        compiler_params=params(),
         cost_estimate=cost(2 * 2 * rows * D * 2 * HID * 2, 16 << 20),
         name="mlp_grads",
     )(*slots, *acts, *gds, *n2s, *gus)
@@ -571,7 +573,7 @@
         ),
         out_shape=[jax.ShapeDtypeStruct(own.shape, BF)] * 2,
         input_output_aliases={14: 0, 15: 1},
-        compiler_params=params(24),
+        compiler_params=params(),
         cost_estimate=cost(2 * 2 * rows * D * 4 * WID, 8 << 20),
         name="attention_grads",
     )(*slots, *atts, *gbs, *n1s, *gps, *gps, *gps, own, par)
@@ -599,16 +601,7 @@
 
 def assemble_kernel(plan, rows, cols, *refs):
     sources = refs[: len(plan)]
-    out_ref, held, in_sems, out_sem = refs[-4:]
-    loads, base = [], 0
-    for at, (src, (share, first, count)) in enumerate(zip(sources, plan)):
-        size = count * BLK
-        load = pltpu.make_async_copy(
-            src.at[pl.ds(0, size), :], held.at[pl.ds(base * BLK, size), :], in_sems.at[at]
-        )
-        load.start()
-        loads.append((load, base))
-        base += count
+    out_ref, sem = refs[-2:]
 
     def run(at, act_on):
         share, first, count = plan[at]
@@ -616,12 +609,12 @@
         def one(i, carry):
             row = pl.multiple_of(rows[share, first + i], BLK)
             col = pl.multiple_of(cols[share, first + i], BLK)
-            from_row = pl.multiple_of((loads[at][1] + i) * BLK, BLK)
+            from_row = pl.multiple_of(i * BLK, BLK)
             act_on(
                 pltpu.make_async_copy(
-                    held.at[pl.ds(from_row, BLK), :],
+                    sources[at].at[pl.ds(from_row, BLK), :],
                     out_ref.at[pl.ds(row, BLK), pl.ds(col, BLK)],
-                    out_sem,
+                    sem,
                 )
             )
             return carry
@@ -629,7 +622,6 @@
         lax.fori_loop(0, count, one, 0)
 
     for at in range(len(plan)):
-        loads[at][0].wait()
         run(at, lambda c: c.start())
     for at in range(len(plan)):
         run(at, lambda c: c.wait())
@@ -638,23 +630,17 @@
 def assemble(table, pieces, weights):
     plan = [piece[:3] for piece in pieces]
     arrays = [piece[3] for piece in pieces]
-    total = sum(piece[2] for piece in pieces)
-    shape = jax.ShapeDtypeStruct((6 * D, D), BF)
     alias = {} if weights is None else {2 + len(arrays): 0}
     args = list(table) + arrays + ([] if weights is None else [weights])
     return pl.pallas_call(
         functools.partial(assemble_kernel, plan),
-        out_shape=shape,
-        in_specs=[SMEM, SMEM] + [ANY] * (len(args) - 2),
-        out_specs=ANY,
-        scratch_shapes=[
-            pltpu.VMEM((total * BLK, BLK), BF),
-            pltpu.SemaphoreType.DMA((len(arrays),)),
-            pltpu.SemaphoreType.DMA,
-        ],
+        out_shape=jax.ShapeDtypeStruct((6 * D, D), BF),
+        in_specs=[SMEM, SMEM] + [HBM] * len(arrays) + ([] if weights is None else [VMEM]),
+        out_specs=VMEM,
+        scratch_shapes=[pltpu.SemaphoreType.DMA],
         input_output_aliases=alias,
-        compiler_params=params(16),
-        cost_estimate=cost(0, total * BLK * BLK * 8),
+        compiler_params=params(),
+        cost_estimate=cost(0, BLK),
         name="assemble",
     )(*args)
 
@@ -666,42 +652,83 @@
     return order, position, ahead, [(b, a) for a, b in ahead]
 
 
-def ring_gather(unit, size, per_device):
-    _, _, ahead, behind = ring(size)
+def after(value, *earlier):
+    return lax.optimization_barrier((value, *earlier))[0]
+
+
+def need_order(size):
     far = size // 2
-    front = per_device // 2
-    pieces = []
-    up = down = unit
-    for step in range(1, far):
-        up, down = lax.ppermute(up, "wide", ahead), lax.ppermute(down, "wide", behind)
-        pieces.append((size - step, 0, per_device, up))
-        pieces.append((step, 0, per_device, down))
-    up = lax.ppermute(up[: front * BLK], "wide", ahead)
-    down = lax.ppermute(down[front * BLK :], "wide", behind)
-    pieces.append((far, 0, front, up))
-    pieces.append((far, front, per_device - front, down))
-    return pieces
-
-
-def ring_scatter(unit_of, size, cut):
-    _, _, ahead, behind = ring(size)
-    far = size // 2
-
-    def send(value, perm):
-        return lax.ppermute(value.astype(BF), "wide", perm)
-
-    last = unit_of(far)
-    up = send(last[:cut], ahead).astype(F32)
-    down = send(last[cut:], behind).astype(F32)
+    order = [far]
     for step in range(far - 1, 0, -1):
-        term_up, term_down = unit_of(step), unit_of(size - step)
-        if step == far - 1:
-            up = jnp.concatenate([term_up[:cut] + up, term_up[cut:]])
-            down = jnp.concatenate([term_down[:cut], term_down[cut:] + down])
+        order += [step, size - step]
+    return order + [0]
+
+
+class Gather:
+    def __init__(self, unit, size, per_device):
+        _, _, self.ahead, self.behind = ring(size)
+        self.size, self.per_device, self.step_count = size, per_device, 0
+        self.up = self.down = unit
+
+    def step(self, *earlier):
+        self.step_count += 1
+        step, far, front = self.step_count, self.size // 2, self.per_device // 2
+        up, down = self.up, self.down
+        if step == far:
+            up, down = up[: front * BLK], down[front * BLK :]
+        up, down, *_ = lax.optimization_barrier((up, down, *earlier))
+        self.sent = (up, down)
+        self.up = lax.ppermute(up, "wide", self.ahead)
+        self.down = lax.ppermute(down, "wide", self.behind)
+        if step < far:
+            return [
+                (self.size - step, 0, self.per_device, self.up),
+                (step, 0, self.per_device, self.down),
+            ]
+        return [
+            (far, 0, front, self.up),
+            (far, front, self.per_device - front, self.down),
+        ]
+
+
+class Scatter:
+    def __init__(self, unit_of, size, cut):
+        _, _, self.ahead, self.behind = ring(size)
+        self.unit_of, self.size, self.cut, self.left = unit_of, size, cut, size // 2
+
+    def step(self, *earlier):
+        cut = self.cut
+        if self.left == self.size // 2:
+            last = self.unit_of(self.left)
+            up, down = last[:cut], last[cut:]
         else:
-            up, down = term_up + up, term_down + down
-        up, down = send(up, ahead).astype(F32), send(down, behind).astype(F32)
-    return unit_of(0) + up + down
+            up, down = self.unit_of(self.left), self.unit_of(self.size - self.left)
+            got_up, got_down = self.up.astype(F32), self.down.astype(F32)
+            if self.left == self.size // 2 - 1:
+                up = jnp.concatenate([up[:cut] + got_up, up[cut:]])
+                down = jnp.concatenate([down[:cut], down[cut:] + got_down])
+            else:
+                up, down = up + got_up, down + got_down
+        up, down = up.astype(BF), down.astype(BF)
+        up, down, *_ = lax.optimization_barrier((up, down, *earlier))
+        self.sent = (up, down)
+        self.up = lax.ppermute(up, "wide", self.ahead)
+        self.down = lax.ppermute(down, "wide", self.behind)
+        self.left -= 1
+
+    def result(self):
+        return self.unit_of(0) + self.up.astype(F32) + self.down.astype(F32)
+
+
+def mesh_bits():
+    out, base = [], 1
+    for axis in ("narrow", "wide"):
+        size, bit = lax.axis_size(axis), 1
+        while bit < size:
+            out.append((base * bit, axis, [(i, i ^ bit) for i in range(size)]))
+            bit *= 2
+        base *= size
+    return out
 
 
 def tile_ids(share):
@@ -779,12 +806,8 @@
 
 def total_over_mesh(value):
     value = jnp.broadcast_to(value.reshape(1, 1), (8, BLK))
-    for axis in ("narrow", "wide"):
-        size = lax.axis_size(axis)
-        bit = 1
-        while bit < size:
-            value = value + lax.ppermute(value, axis, [(i, i ^ bit) for i in range(size)])
-            bit *= 2
+    for _, axis, perm in mesh_bits():
+        value = value + lax.ppermute(value, axis, perm)
     return value[0, 0]
 
 
@@ -807,7 +830,7 @@
         out_shape=jax.ShapeDtypeStruct((count, BLK, BLK), F32),
         in_specs=[flat, basis, basis],
         out_specs=spec,
-        compiler_params=params(16),
+        compiler_params=params(10),
         cost_estimate=cost(count * 4 * BLK**3, count * BLK * BLK * 14),
         name="rotate_in",
     )(grads, left_basis, right_basis)
@@ -846,7 +869,7 @@
         out_shape=[shape, shape, shape, jax.ShapeDtypeStruct(master.shape, BF)],
         in_specs=[SMEM, low, high] + [spec] * 5,
         out_specs=[spec] * 4,
-        compiler_params=params(24),
+        compiler_params=params(10),
         cost_estimate=cost(count * 8 * BLK**3, count * BLK * BLK * 2 * 38),
         name="update",
     )(clip, *rots, left, right, first, second, master)
@@ -874,18 +897,13 @@
     own_images = images.shape[0]
     rows = own_images * S
 
-    small_bf = small_params.astype(BF)
-    small_pair = jnp.stack([small_bf, lax.ppermute(small_bf, "narrow", ACROSS)])
-    small_rows = -(-small_pair.size // (16 * BLK)) * 16
-    small_pad = jnp.pad(small_pair.reshape(-1), (0, small_rows * BLK - small_pair.size))
-    small_pad = small_pad.reshape(small_rows, BLK)
+    device = lax.axis_index("wide") * NARROW + me
+    by_distance = jnp.arange(wide * NARROW) ^ device
 
     def chunks(own):
         other = lax.ppermute(own, "narrow", ACROSS)
         return [jnp.where(half == t, own, other) for t in range(2)]
 
-    hidden_in = chunks(images.reshape(rows, D))
-    cot = chunks(cotangent.reshape(rows, D))
     kept = [
         lax.dynamic_slice_in_dim(kept_tokens, (2 * t + core) * own_images, own_images, 0)
         .reshape(1, rows)
@@ -897,6 +915,8 @@
     place = jnp.take(jnp.asarray(position, jnp.int32), lax.axis_index("wide"))
     around = jnp.take(jnp.asarray(order, jnp.int32), (place + jnp.arange(wide)) % wide)
 
+    needed = need_order(wide)
+    turns = [needed.index(distance) for distance in range(wide)]
     slots, tables = [], []
     for layer in range(LAYERS):
         owners = owner_slots[layer]
@@ -906,7 +926,8 @@
             at_wide, at_pos = slot // per_device // NARROW, slot % per_device
             distance = (jnp.take(jnp.asarray(position, jnp.int32), at_wide) - place) % wide
             relative = distance * per_device + at_pos
-            layer_slots.append(relative)
+            turn = jnp.take(jnp.asarray(turns, jnp.int32), distance)
+            layer_slots.append(turn * per_device + at_pos)
             here = relative[None, :] == jnp.arange(SHARE_TILES)[:, None]
             tile = jnp.sum(jnp.where(here, jnp.arange(SHARE_TILES)[None, :], 0), axis=1)
             row, col = place_of(tile, at)
@@ -918,43 +939,65 @@
     def core_swap(value):
         return lax.ppermute(value, "narrow", CORE)
 
-    weights, units = [], []
-    for layer in range(LAYERS):
-        unit = master_blocks[layer].astype(BF).reshape(per_device * BLK, BLK)
-        if layer == 0:
-            unit = jnp.concatenate([unit, small_pad], axis=0)
-        pieces = [(0, 0, per_device, unit)] + ring_gather(unit, wide, per_device)
-        pieces = [piece + (core_swap(piece[3]),) for piece in pieces]
-        matrix = None
-        for group in (pieces[: wide - 3], pieces[wide - 3 : wide - 1], pieces[wide - 1 :]):
-            group = [
-                (share, distance * per_device + first, count, pair[share])
-                for distance, first, count, *pair in group
-                for share in range(2)
-            ]
-            matrix = assemble(tables[layer], group, matrix)
-        weights.append(matrix)
-        units.append(pieces)
-
-    tails = [[None] * wide, [None] * wide]
-    for distance, first, count, *pair in units[0]:
-        if first + count == per_device:
-            for share in range(2):
-                tails[share][distance] = pair[share][count * BLK :]
-    tails = [
-        jnp.stack(t).reshape(wide, small_rows * BLK)[:, : small_pair.size]
-        .reshape(wide, 2, LAYERS, own_small)
-        for t in tails
-    ]
-    by_distance = jnp.stack([tails[0][:, 0], tails[1][:, 0], tails[0][:, 1], tails[1][:, 1]], axis=1)
-    to_order = (jnp.asarray(position, jnp.int32) - place) % wide
-    in_order = jnp.take(by_distance, to_order, axis=0)
-    in_order = jnp.take(in_order, jnp.arange(NARROW) ^ me, axis=1).astype(F32)
-    small_all = in_order.transpose(2, 0, 1, 3).reshape(LAYERS, -1)
-    vecs = [share_vectors(small_all[layer], me) for layer in range(LAYERS)]
-
     def exchange(part):
         return lax.ppermute(part, "narrow", ACROSS)
+
+    units = [
+        master_blocks[layer].astype(BF).reshape(per_device * BLK, BLK) for layer in range(LAYERS)
+    ]
+
+    def swapped(pieces):
+        return [piece + (core_swap(piece[3]),) for piece in pieces]
+
+    def place_pieces(layer, pieces, matrix):
+        group = [
+            (share, distance * per_device + first, count, pair[share])
+            for distance, first, count, *pair in pieces
+            for share in range(2)
+        ]
+        return assemble(tables[layer], group, matrix)
+
+    steps = wide // 2
+    own_small_rows = small_params.astype(BF).reshape(1, -1)
+    small_rows = own_small_rows
+    bits = mesh_bits()
+    near_bits, far_bits = bits[:2], bits[2:]
+    per_window = -(-len(far_bits) // max(steps - 1, 1))
+
+    def grow(rows, some_bits):
+        for _, axis, perm in some_bits:
+            rows = jnp.concatenate([rows, lax.ppermute(rows, axis, perm)])
+        return rows
+
+    gather = Gather(units[0], wide, per_device)
+    arrived = [(0, 0, per_device, units[0])] + gather.step()
+    small_rows = grow(small_rows, near_bits)
+    placed, inputs, extra = [], [images, cotangent], [small_rows]
+    brought = []
+    for step in range(2, steps + 1):
+        latest = swapped(arrived)
+        arrived = gather.step(*extra)
+        extra = [piece[4] for piece in latest]
+        placed = placed + latest
+        if inputs:
+            brought.append(chunks(after(inputs.pop(0).reshape(rows, D), *gather.sent)))
+            extra += brought[-1]
+        at = (step - 2) * per_window
+        small_rows = grow(small_rows, far_bits[at : at + per_window])
+        if step < steps:
+            extra.append(small_rows)
+    while inputs:
+        brought.append(chunks(inputs.pop(0).reshape(rows, D)))
+    hidden_in, cot = brought
+    next_unit = after(units[1], gather.up, gather.down)
+    gather_next = Gather(next_unit, wide, per_device)
+    arrived_next = [(0, 0, per_device, next_unit)] + gather_next.step()
+    last = [piece[:3] + (after(piece[3], *gather_next.sent),) for piece in arrived]
+    weights = [place_pieces(0, placed + swapped(last), None)]
+
+    in_order = jnp.take(small_rows, by_distance, axis=0).astype(F32)
+    small_all = in_order.reshape(-1, LAYERS, own_small).transpose(1, 0, 2).reshape(LAYERS, -1)
+    vecs = [share_vectors(small_all[layer], me) for layer in range(LAYERS)]
 
     saved = []
     state = None
@@ -971,9 +1014,14 @@
                 )
             n1, qkv, lse, att, part = out
             kept_layer.append([hidden, n1, qkv, lse, att, part, exchange(part)])
+        kept_layer[0][5] = after(kept_layer[0][5], kept_layer[1][5])
         state = []
         for t in range(2):
             hidden, n1, qkv, lse, att, part, got = kept_layer[t]
+            if layer == 0 and t == 0:
+                placed = swapped(arrived_next)
+                arrived_next = gather_next.step(part)
+                part = after(part, *gather_next.sent)
             middle, n2, act, slope, down_part = call_mlp_forward(
                 hidden, part, got, vecs[layer], mlp_w
             )
@@ -983,6 +1031,14 @@
             else:
                 state.append((middle, down_part))
         saved.append((att_w, mlp_w, kept_layer))
+        if layer == 0:
+            gates = [down_part] + [piece[4] for piece in placed]
+            for step in range(3, steps + 1):
+                latest = swapped(arrived_next)
+                arrived_next = gather_next.step(*gates)
+                gates = [piece[4] for piece in latest]
+                placed = placed + latest
+            weights.append(place_pieces(1, placed + swapped(arrived_next), None))
 
     def mine(pair):
         return jnp.where(half == 0, pair[0], pair[1])
@@ -1002,6 +1058,7 @@
     upstream = None
     reduced = [None] * LAYERS
     small_terms = [None] * LAYERS
+    pending = None
     for layer in reversed(range(LAYERS)):
         att_w, mlp_w, kept_layer = saved[layer]
         top = layer == LAYERS - 1
@@ -1014,25 +1071,43 @@
                     True, (grad,), middle, slope, vecs[layer], mlp_w
                 )
             else:
+                state = upstream[t]
+                state = (after(state[0], *pending.sent),) + state[1:]
                 grad, gd, gu, part, sums = call_mlp_backward(
-                    False, upstream[t] + (vecs[layer + 1],), middle, slope, vecs[layer], mlp_w
+                    False, state + (vecs[layer + 1],), middle, slope, vecs[layer], mlp_w
                 )
+                if t == 0:
+                    pending.step(part)
             work.append([grad, gd, gu, part, sums, exchange(part)])
+        gds = [w[1] for w in work]
+        if pending is not None:
+            gds[0] = after(gds[0], *pending.sent)
         own, par = call_mlp_grads(
             slots[layer],
             [k[7] for k in kept_layer],
-            [w[1] for w in work],
+            gds,
             [k[6] for k in kept_layer],
             [w[2] for w in work],
         )
+        if pending is not None:
+            pending.step(own)
         back = []
         for t in range(2):
             hidden, n1, qkv, lse, att, middle, n2, act, slope = kept_layer[t]
             grad, gd, gu, part, sums, got = work[t]
+            if pending is not None:
+                part = after(part, *pending.sent)
             gm, gb, gp, att_part, att_sums = call_attention_backward(
                 grad, part, got, middle, hidden, qkv, lse, vecs[layer], kept[t], att_w
             )
             back.append((gm, gb, gp, att_part, att_sums))
+        if pending is not None:
+            pending.step(back[1][3])
+            while pending.left > 0:
+                pending.step()
+            own = after(own, *pending.sent)
+            reduced[layer + 1] = pending.result()
+            arrivals = [pending.up, pending.down]
         if layer > 0:
             upstream = [
                 (back[t][0], back[t][3], exchange(back[t][3]), kept_layer[t][0]) for t in range(2)
@@ -1047,34 +1122,49 @@
             par,
         )
         terms = small_vector([w[4] for w in work], [b[4] for b in back], me)
-        terms = jnp.take(terms.reshape(wide, NARROW, own_small), around, axis=0)
-        terms = jnp.take(terms, jnp.arange(NARROW) ^ me, axis=1)
-        near = terms[:, 0:2] + exchange(terms[:, 2:4])
-        small_sum = near[:, 0] + core_swap(near[:, 1])
-        tail_rows = -(-own_small // (16 * BLK)) * 16
-        small_tail = jnp.pad(small_sum, ((0, 0), (0, tail_rows * BLK - own_small)))
-        small_tail = small_tail.reshape(wide, tail_rows, BLK)
+        small_terms[layer] = terms.reshape(-1, own_small)
         unit_len = per_device * BLK
 
-        def unit_of(distance, own=own, par=par, small_tail=small_tail, unit_len=unit_len):
-            at = slice(distance * unit_len, (distance + 1) * unit_len)
-            term = own[at].astype(F32) + core_swap(par[at]).astype(F32)
-            return jnp.concatenate([term, small_tail[distance]])
-
-        reduced[layer] = ring_scatter(unit_of, wide, (per_device // 2) * BLK)
-        if layer == 0:
-            parts = [b[3] for b in back]
-            hidden = mine([k[0] for k in kept_layer]).astype(F32)
-            centre, rstd = stats(hidden)
-            grad = mine(parts).astype(F32) + exchange(theirs(parts)).astype(F32)
-            lower = norm_back(grad, centre * rstd, rstd, vecs[0][0:1])
-            input_grad = (mine([b[0] for b in back]) + lower).reshape(images.shape)
-
-    tail = per_device * BLK
-    grad_small = jnp.stack([r[tail:].reshape(-1)[:own_small] for r in reduced])
+        first_got = core_swap(par[:unit_len])
+        earlier = pending
+        pending = Scatter(None, wide, (per_device // 2) * BLK)
+
+        def first_unit(distance, own=own, got=first_got, unit_len=unit_len):
+            return own[:unit_len].astype(F32) + got.astype(F32)
+
+        pending.unit_of = first_unit
+        pending.step()
+        rest = core_swap(after(par, *pending.sent))
+
+        def unit_of(distance, own=own, rest=rest, unit_len=unit_len):
+            at = turns[distance] * unit_len
+            return own[at : at + unit_len].astype(F32) + rest[at : at + unit_len].astype(F32)
+
+        pending.unit_of = unit_of
+
+    parts = [b[3] for b in back]
+    last_part = exchange(after(theirs(parts), *pending.sent)).astype(F32)
+    small_rows = jnp.take(jnp.concatenate(small_terms, axis=1), by_distance, axis=0)
+    small_rows = after(small_rows, *pending.sent)
+    backward_bits = mesh_bits()[::-1]
+    while pending.left > 0:
+        for bit, axis, perm in backward_bits[:per_window]:
+            small_rows = small_rows[:bit] + lax.ppermute(small_rows[bit:], axis, perm)
+        backward_bits = backward_bits[per_window:]
+        pending.step(small_rows, last_part, *arrivals)
+        small_rows = after(small_rows, *pending.sent)
+    for bit, axis, perm in backward_bits:
+        small_rows = small_rows[:bit] + lax.ppermute(small_rows[bit:], axis, perm)
+    reduced[0] = pending.result()
+    hidden = mine([k[0] for k in saved[0][2]]).astype(F32)
+    centre, rstd = stats(hidden)
+    lower = norm_back(mine(parts).astype(F32) + last_part, centre * rstd, rstd, vecs[0][0:1])
+    input_grad = (mine([b[0] for b in back]) + lower).reshape(images.shape)
+
+    grad_small = small_rows.reshape(LAYERS, own_small)
     local_sum = jnp.sum(grad_small * grad_small)
-    for grads in reduced:
-        local_sum = local_sum + jnp.sum(grads[:tail] * grads[:tail])
+    for grads in reduced[::-1]:
+        local_sum = local_sum + jnp.sum(grads * grads)
     grad_norm = jnp.sqrt(total_over_mesh(local_sum))
     clip_factor = 1.0 / jnp.maximum(grad_norm, 1.0)
     rots = [

time: 688 us -> 559 us (0.81)
  local copies, waits for them, and re-layouts: 187 us -> 115 us
  waiting for transfers between devices: 193 us -> 141 us
  Pallas kernels: 177 us -> 161 us
  other arithmetic: 45.8 us -> 53 us
    ppermute x38 -> x47, waiting for transfers between devices: 175 us -> 104 us  [the longest x16 52.6 us: step(): self.up = lax.ppermute(up, 'wide', self.ahead)]
    unnamed x512 -> x421, local copies, waits for them, and re-layouts: 149 us -> 89.1 us
    convert_element_type x10 -> x4, other arithmetic: 1.55 us -> 12.2 us  [step(): up, down = (up.astype(BF), down.astype(BF))]
    ppermute x16 -> x14, waiting for transfers between devices: 3.98 us -> 14.5 us  [exchange(): return lax.ppermute(part, 'narrow', ACROSS)]
    ppermute x38 -> x47, starting transfers between devices: 42.7 us -> 49.9 us  [the longest x16 18 us: step(): self.up = lax.ppermute(up, 'wide', self.ahead)]
    ppermute x2, waiting for transfers between devices: 8.49 us -> 15.6 us  [chunks(): other = lax.ppermute(own, 'narrow', ACROSS)]
    slice x21 -> x18, local copies, waits for them, and re-layouts: 14.8 us -> 7.9 us  [the longest x4 4.09 us: step(): up, down = (up[:front * BLK], down[front * BLK:])]
    ppermute x16 -> x14, starting transfers between devices: 16.4 us -> 14.4 us  [exchange(): return lax.ppermute(part, 'narrow', ACROSS)]
  transfers between devices with their start and end apart: 92 -> 85, of which waited for: 28 -> 29; matrix products, arithmetic and copies ran while one was open for 12% -> 12% of each run, Pallas kernels for 23% -> 22%
where the time goes in v2:
time: 559 us; the launch traced here: 548 us
  Pallas kernels  161 us (29%)
  waiting for transfers between devices  141 us (25%)
  local copies, waits for them, and re-layouts  115 us (21%)
  starting transfers between devices  70.8 us (13%)
  other arithmetic  53 us (9%)
  between operations  8.16 us (1%)
    unnamed x421, local copies, waits for them, and re-layouts  89.1 us
    ppermute x16, waiting for transfers between devices, step(): self.up = lax.ppermute(up, 'wide', self.ahead)  52.6 us
    ppermute x5, waiting for transfers between devices, shards(): small_rows = small_rows[:bit] + lax.ppermute(small_rows[bit:], axis, perm)  33.2 us
    pallas_call x2, Pallas kernels, call_mlp_grads(): pl.pallas_call(mlp_grads, grid_spec=pltpu.PrefetchScalarGridSpec(num_scal...  26.4 us
    pallas_call x2, Pallas kernels, assemble(): pl.pallas_call(functools.partial(assemble_kernel, plan), out_shape=jax.Sh...  24.8 us
    pallas_call x4, Pallas kernels, call_attention_backward(): pl.pallas_call(attention_backward, grid=(1,), out_shape=outs, in_specs=[f...  23.9 us
    pallas_call x4, Pallas kernels, call_mlp_backward(): pl.pallas_call(functools.partial(mlp_backward, first), grid=(STEPS,), out...  23 us
    pallas_call x2, Pallas kernels, call_attention_grads(): pl.pallas_call(attention_grads, grid_spec=pltpu.PrefetchScalarGridSpec(nu...  21.7 us
  transfers between devices with their start and end apart: 85, of which 29 were waited for; matrix products, arithmetic and copies ran while one was open for 12% of the time, Pallas kernels for 22%

profile of v2, /device:TPU:0, one launch (start us, length us, event | category | flops | bytes accessed | tf_op | source)
XLA Modules:
  0.0 548.4 jit_solution(1053324267836854980)
XLA Ops:
  0.6 2.1 convert.41
  3.5 2.6 collective-permute-start
  31.2 5.3 collective-permute-done.4
  38.0 2.7 convert_reduce_fusion
  40.7 2.6 collective-permute-start.7
  43.3 4.4 collective-permute-done.11.refs_6_
  49.0 2.3 collective-permute-start.15
  57.0 10.3 %collective-permute-done.19 = bf16[200,1024]{1,0:T(8,128)(2,1)} collective-permute-done((bf16[200,1024]{1,0:T(8,128)(2,1)}, bf16[200,1024]{1,0:T(8,128)(2,1)}, u32[]{:S(2)}, u32[]{:S(2)}) %collective-permute-start.19) | collective-permute-done | bytes 409632 | tf_op jit(solution)/shard_map/ppermute | solution.py:904
  70.6 2.1 collective-permute-start.20
  73.5 7.5 %collective-permute-done.20.refs_14_ = bf16[1536,128]{1,0:T(8,128)(2,1)} collective-permute-done((bf16[1536,128]{1,0:T(8,128)(2,1)S(1)}, bf16[1536,128]{1,0:T(8,128)(2,1)}, u32[]{:S(2)}, u32[]{:S(2)}) %collective-permute-start.20) | collective-permute-done | bytes 393248 | tf_op jit(solution)/shard_map/ppermute | solution.py:681
  89.2 11.8 %assemble.2.refs_3_.weights.refs_8_ = bf16[6144,1024]{1,0:T(8,128)(2,1)} custom-call(s32[2,192]{1,0:T(2,128)S(1)} %pad_add_fusion.rows, s32[2,192]{1,0:T(2,128)S(1)} %pad_add_fusion.1.cols, bf16[3072,128]{1,0:T(8,128)(2,1)S(1)} %bitcast.81, bf16[3072,128]{1,0:T(8,128)(2,1)S(1)} %copy-done.52, bf16[3072,128]{1,0:T(8,128)(2,1)} %collective-permute-done.refs_2_, ...), custom_call_target="tpu_custom_call" | custom-call | bytes 128 | tf_op jit(solution)/shard_map/assemble/pallas_call | solution.py:635
  101.1 4.6 copy-done.2
  105.6 2.4 attention_forward.5
  111.6 4.6 copy-done.3
  116.2 2.4 attention_forward.4
  121.9 2.1 collective-permute-start.33
  127.4 4.1 mlp_forward.5
  134.2 7.4 %collective-permute-done.31.refs_6_ = bf16[3072,128]{1,0:T(8,128)(2,1)S(1)} collective-permute-done((bf16[3072,128]{1,0:T(8,128)(2,1)}, bf16[3072,128]{1,0:T(8,128)(2,1)S(1)}, u32[]{:S(2)}, u32[]{:S(2)}) %collective-permute-start.31) | collective-permute-done | bytes 786464 | tf_op jit(solution)/shard_map/ppermute | solution.py:681
  147.6 13.5 %collective-permute-done.36.refs_10_ = bf16[3072,128]{1,0:T(8,128)(2,1)} collective-permute-done((bf16[3072,128]{1,0:T(8,128)(2,1)S(1)}, bf16[3072,128]{1,0:T(8,128)(2,1)}, u32[]{:S(2)}, u32[]{:S(2)}) %collective-permute-start.36) | collective-permute-done | bytes 786464 | tf_op jit(solution)/shard_map/ppermute | solution.py:681
  168.1 4.9 mlp_forward.4
  179.0 2.7 stack.163
  195.3 13.0 %assemble.3.refs_6_.weights.refs_4_ = bf16[6144,1024]{1,0:T(8,128)(2,1)} custom-call(s32[2,192]{1,0:T(2,128)S(1)} %copy-done.125, s32[2,192]{1,0:T(2,128)S(1)} %copy-done.126, bf16[3072,128]{1,0:T(8,128)(2,1)S(1)} %bitcast.77, bf16[3072,128]{1,0:T(8,128)(2,1)S(1)} %copy-done.54, bf16[3072,128]{1,0:T(8,128)(2,1)} %collective-permute-done.24.refs_2_, ...), custom_call_target="tpu_custom_call" | custom-call | bytes 128 | tf_op jit(solution)/shard_map/assemble/pallas_call | solution.py:635
  208.3 4.6 copy-done
  212.8 3.7 attention_forward.6
  218.2 2.5 attention_forward.7
  224.4 4.6 collective-permute-done.45.got_ref
  229.0 4.1 mlp_forward.6
  233.2 5.1 mlp_backward.4
  241.3 4.1 mlp_forward.7
  246.4 6.0 %mlp_backward.5 = (bf16[200,1024]{1,0:T(8,128)(2,1)S(1)}, bf16[200,2048]{1,0:T(8,128)(2,1)S(1)}, bf16[200,1024]{1,0:T(8,128)(2,1)}, f32[8,1024]{1,0:T(8,128)S(1)}) custom-call(bf16[200,1024]{1,0:T(8,128)(2,1)S(1)} %get-tuple-element.412.refs_0_.grad_ref, f32[200,1024]{1,0:T(8,128)S(1)} %get-tuple-element.201.refs_1_.mid_ref, ...), custom_call_target="tpu_custom_call" | custom-call | flops 3355443200 | bytes 12582912 | tf_op jit(solution)/shard_map/mlp_backward/pallas_call | solution.py:307
  258.9 13.3 %mlp_grads.2 = (bf16[24576,128]{1,0:T(8,128)(2,1)S(1)}, bf16[24576,128]{1,0:T(8,128)(2,1)S(1)}) custom-call(s32[192]{0:T(256)S(1)} %copy-done.130, s32[192]{0:T(256)S(1)} %copy-done.129, bf16[200,2048]{1,0:T(8,128)(2,1)S(1)} %copy-done.138, bf16[200,2048]{1,0:T(8,128)(2,1)S(1)} %copy-done.142, bf16[200,1024]{1,0:T(8,128)(2,1)S(1)} %get-tuple-element.223.refs_2_, ...), custom_call_target="tpu_custom_call" | custom-call | flops 6710886400 | bytes 16777216 | tf_op jit(solution)/shard_map/mlp_grads/pallas_call | solution.py:472
  272.3 2.6 copy-done.11
  276.0 6.2 %attention_backward.4 = (f32[200,1024]{1,0:T(8,128)S(1)}, bf16[200,1024]{1,0:T(8,128)(2,1)S(1)}, bf16[200,1536]{1,0:T(8,128)(2,1)S(1)}, bf16[200,1024]{1,0:T(8,128)(2,1)S(1)}, f32[8,1024]{1,0:T(8,128)S(1)}) custom-call(bf16[200,1024]{1,0:T(8,128)(2,1)S(1)} %get-tuple-element.413.refs_0_.grad_ref, bf16[200,1024]{1,0:T(8,128)(2,1)S(1)} %get-tuple-element.205.own_ref, ...), custom_call_target="tpu_custom_call" | custom-call | flops 2516582400 | bytes 8388608 | tf_op jit(solution)/shard_map/attention_backward/pallas_call | solution.py:396
  284.0 6.4 %attention_backward.5 = (f32[200,1024]{1,0:T(8,128)S(1)}, bf16[200,1024]{1,0:T(8,128)(2,1)S(1)}, bf16[200,1536]{1,0:T(8,128)(2,1)S(1)}, bf16[200,1024]{1,0:T(8,128)(2,1)S(1)}, f32[8,1024]{1,0:T(8,128)S(1)}) custom-call(bf16[200,1024]{1,0:T(8,128)(2,1)S(1)} %get-tuple-element.412.refs_0_.grad_ref, bf16[200,1024]{1,0:T(8,128)(2,1)} %get-tuple-element.213.own_ref, ...), custom_call_target="tpu_custom_call" | custom-call | flops 2516582400 | bytes 8388608 | tf_op jit(solution)/shard_map/attention_backward/pallas_call | solution.py:396
  290.5 11.7 %attention_grads.2 = (bf16[24576,128]{1,0:T(8,128)(2,1)S(1)}, bf16[24576,128]{1,0:T(8,128)(2,1)S(1)}) custom-call(s32[192]{0:T(256)S(1)} %copy-done.130, s32[192]{0:T(256)S(1)} %copy-done.129, bf16[200,512]{1,0:T(8,128)(2,1)S(1)} %copy-done.102, bf16[200,512]{1,0:T(8,128)(2,1)S(1)} %copy-done.104, ...), custom_call_target="tpu_custom_call", output_to_operand_aliasing={{0}: (14, {}), {1}: (15, {})} | custom-call | flops 1677721600 | bytes 8388608 | tf_op jit(solution)/shard_map/attention_grads/pallas_call | solution.py:556
  302.4 2.3 collective-permute-done.50
  310.1 8.3 %collective-permute-done.51.refs_2_ = bf16[200,1024]{1,0:T(8,128)(2,1)S(1)} collective-permute-done((bf16[200,1024]{1,0:T(8,128)(2,1)S(1)}, bf16[200,1024]{1,0:T(8,128)(2,1)S(1)}, u32[]{:S(2)}, u32[]{:S(2)}) %collective-permute-start.51) | collective-permute-done | bytes 409632 | tf_op jit(solution)/shard_map/ppermute | solution.py:943
  319.4 6.3 %mlp_backward.6 = (f32[200,1024]{1,0:T(8,128)S(1)}, bf16[200,1024]{1,0:T(8,128)(2,1)S(1)}, bf16[200,2048]{1,0:T(8,128)(2,1)S(1)}, bf16[200,1024]{1,0:T(8,128)(2,1)}, f32[8,1024]{1,0:T(8,128)S(1)}) custom-call(f32[200,1024]{1,0:T(8,128)S(1)} %copy-done.50, bf16[200,1024]{1,0:T(8,128)(2,1)S(1)} %copy-done.90, ...), custom_call_target="tpu_custom_call" | custom-call | flops 3355443200 | bytes 12582912 | tf_op jit(solution)/shard_map/mlp_backward/pallas_call | solution.py:307
  327.3 2.8 convert_add_fusion.4
  336.4 5.6 %mlp_backward.7 = (f32[200,1024]{1,0:T(8,128)S(1)}, bf16[200,1024]{1,0:T(8,128)(2,1)S(1)}, bf16[200,2048]{1,0:T(8,128)(2,1)S(1)}, bf16[200,1024]{1,0:T(8,128)(2,1)S(1)}, f32[8,1024]{1,0:T(8,128)S(1)}) custom-call(f32[200,1024]{1,0:T(8,128)S(1)} %get-tuple-element.248.refs_0_, bf16[200,1024]{1,0:T(8,128)(2,1)S(1)} %get-tuple-element.249.refs_1_, ...), custom_call_target="tpu_custom_call" | custom-call | flops 3355443200 | bytes 12582912 | tf_op jit(solution)/shard_map/mlp_backward/pallas_call | solution.py:307
  345.5 13.1 %mlp_grads.3 = (bf16[24576,128]{1,0:T(8,128)(2,1)S(1)}, bf16[24576,128]{1,0:T(8,128)(2,1)}) custom-call(s32[192]{0:T(256)S(1)} %copy-done.128, s32[192]{0:T(256)S(1)} %copy-done.127, bf16[200,2048]{1,0:T(8,128)(2,1)S(1)} %copy-done.134, bf16[200,2048]{1,0:T(8,128)(2,1)S(1)} %copy-done.132, bf16[200,1024]{1,0:T(8,128)(2,1)S(1)} %copy-done.152, ...), custom_call_target="tpu_custom_call" | custom-call | flops 6710886400 | bytes 16777216 | tf_op jit(solution)/shard_map/mlp_grads/pallas_call | solution.py:472
  358.7 3.1 add_convert_fusion.7
  364.7 6.3 %attention_backward.6 = (f32[200,1024]{1,0:T(8,128)S(1)}, bf16[200,1024]{1,0:T(8,128)(2,1)S(1)}, bf16[200,1536]{1,0:T(8,128)(2,1)S(1)}, bf16[200,1024]{1,0:T(8,128)(2,1)S(1)}, f32[8,1024]{1,0:T(8,128)S(1)}) custom-call(f32[200,1024]{1,0:T(8,128)S(1)} %get-tuple-element.238.grad_ref, bf16[200,1024]{1,0:T(8,128)(2,1)} %get-tuple-element.259.own_ref, ...), custom_call_target="tpu_custom_call" | custom-call | flops 2516582400 | bytes 8388608 | tf_op jit(solution)/shard_map/attention_backward/pallas_call | solution.py:396
  373.5 5.1 attention_backward.7
  381.5 3.8 add_convert_fusion.5
  385.4 10.1 %attention_grads.3 = (bf16[24576,128]{1,0:T(8,128)(2,1)S(1)}, bf16[24576,128]{1,0:T(8,128)(2,1)}) custom-call(s32[192]{0:T(256)S(1)} %copy-done.128, s32[192]{0:T(256)S(1)} %copy-done.127, bf16[200,512]{1,0:T(8,128)(2,1)S(1)} %copy-done.100, bf16[200,512]{1,0:T(8,128)(2,1)S(1)} %get-tuple-element.272.refs_1_, ...), custom_call_target="tpu_custom_call", output_to_operand_aliasing={{0}: (14, {}), {1}: (15, {})} | custom-call | flops 1677721600 | bytes 8388608 | tf_op jit(solution)/shard_map/attention_grads/pallas_call | solution.py:556
  397.3 2.3 collective-permute-done.62
  406.2 2.1 collective-permute-done.64
  411.7 2.3 convert_add_fusion.2
  414.0 17.0 %collective-permute-done.66 = bf16[1536,128]{1,0:T(8,128)(2,1)S(1)} collective-permute-done((bf16[1536,128]{1,0:T(8,128)(2,1)}, bf16[1536,128]{1,0:T(8,128)(2,1)S(1)}, u32[]{:S(2)}, u32[]{:S(2)}) %collective-permute-start.66) | collective-permute-done | bytes 393248 | tf_op jit(solution)/shard_map/ppermute | solution.py:715
  436.6 16.3 %collective-permute-done.70 = f32[8,768]{1,0:T(8,128)S(1)} collective-permute-done((f32[8,768]{1,0:T(8,128)S(1)}, f32[8,768]{1,0:T(8,128)S(1)}, u32[]{:S(2)}, u32[]{:S(2)}) %collective-permute-start.70) | collective-permute-done | bytes 24608 | tf_op jit(solution)/shard_map/ppermute | solution.py:1152
  452.9 2.0 add_convert_fusion.2
  455.0 2.2 collective-permute-start.75
  460.7 14.8 %collective-permute-done.73 = f32[4,768]{1,0:T(4,128)S(1)} collective-permute-done((f32[4,768]{1,0:T(4,128)S(1)}, f32[4,768]{1,0:T(4,128)S(1)}, u32[]{:S(2)}, u32[]{:S(2)}) %collective-permute-start.73) | collective-permute-done | bytes 12320 | tf_op jit(solution)/shard_map/ppermute | solution.py:1152
  475.5 3.3 add_convert_fusion
  483.0 3.2 multiply_reduce_fusion.1
  492.9 3.4 collective-permute-done.79
  496.6 4.0 multiply_reduce_fusion
  503.9 2.9 collective-permute-done.81
  507.2 3.2 collective-permute-done.82
  512.5 2.4 fusion.7
  514.9 2.2 reshape.580
  517.0 2.7 copy.47
  537.4 9.6 %update.1 = (f32[2,24,128,128]{3,2,1,0:T(8,128)}, f32[2,24,128,128]{3,2,1,0:T(8,128)}, f32[2,24,128,128]{3,2,1,0:T(8,128)}, bf16[2,24,128,128]{3,2,1,0:T(8,128)(2,1)}) custom-call(f32[1]{0:T(128)} %bitcast.59.clip_ref, f32[24,128,128]{2,1,0:T(8,128)S(1)} %copy-done.33, f32[24,128,128]{2,1,0:T(8,128)S(1)} %copy-done.31, f32[2,24,128,128]{3,2,1,0:T(8,128)S(1)} %copy-done.4, ...), custom_call_target="tpu_custom_call" | custom-call | flops 402653184 | bytes 29884416 | tf_op jit(solution)/shard_map/update/pallas_call | solution.py:866
  (760 shorter events, 187.4 us)
Async XLA Ops:
  2.9 37.7 %collective-permute-start.8 = (bf16[3072,128]{1,0:T(8,128)(2,1)S(1)}, bf16[3072,128]{1,0:T(8,128)(2,1)S(1)}, u32[]{:S(2)}, u32[]{:S(2)}) collective-permute-start(bf16[3072,128]{1,0:T(8,128)(2,1)S(1)} %bitcast.78), channel_id=1, source_target_pairs={{0,1},{1,0},{2,3},{3,2},{4,5},{5,4},{6,7},{7,6},{8,9},{9,8},{10,11... | collective-permute-start | bytes 2359304 | tf_op jit(solution)/shard_map/ppermute | solution.py:940
  3.5 20.8 %collective-permute-start = (bf16[3072,128]{1,0:T(8,128)(2,1)S(1)}, bf16[3072,128]{1,0:T(8,128)(2,1)}, u32[]{:S(2)}, u32[]{:S(2)}) collective-permute-start(bf16[3072,128]{1,0:T(8,128)(2,1)S(1)} %bitcast.79), channel_id=1, source_target_pairs={{0,8},{8,16},{16,24},{24,28},{28,20},{20,12},{12,4},{4,0},{1,9},{9... | collective-permute-start | bytes 2359304 | tf_op jit(solution)/shard_map/ppermute | solution.py:681
  6.1 19.7 %collective-permute-start.1 = (bf16[3072,128]{1,0:T(8,128)(2,1)S(1)}, bf16[3072,128]{1,0:T(8,128)(2,1)}, u32[]{:S(2)}, u32[]{:S(2)}) collective-permute-start(bf16[3072,128]{1,0:T(8,128)(2,1)S(1)} %bitcast.80), channel_id=1, source_target_pairs={{8,0},{16,8},{24,16},{28,24},{20,28},{12,20},{4,12},{0,4},{9,1},{1... | collective-permute-start | bytes 2359304 | tf_op jit(solution)/shard_map/ppermute | solution.py:682
  6.2 11.9 %collective-permute-start.2 = (bf16[1,768]{1,0:T(2,128)(2,1)S(1)}, bf16[1,768]{1,0:T(2,128)(2,1)S(1)}, u32[]{:S(2)}, u32[]{:S(2)}) collective-permute-start(bf16[1,768]{1,0:T(2,128)(2,1)S(1)} %bitcast.86), channel_id=1, source_target_pairs={{0,1},{1,0},{2,3},{3,2},{4,5},{5,4},{6,7},{7,6},{8,9},{9,8},{10,11... | collective-permute-start | bytes 4616 | tf_op jit(solution)/shard_map/ppermute | solution.py:969
  25.8 10.7 %collective-permute-start.4 = (bf16[200,1024]{1,0:T(8,128)(2,1)S(1)}, bf16[200,1024]{1,0:T(8,128)(2,1)S(1)}, u32[]{:S(2)}, u32[]{:S(2)}) collective-permute-start(bf16[200,1024]{1,0:T(8,128)(2,1)S(1)} %reshape.576), channel_id=1, source_target_pairs={{0,2},{1,3},{2,0},{3,1},{4,6},{5,7},{6,4},{7,5},{8,10},{9,11},{10,... | collective-permute-start | bytes 1228808 | tf_op jit(solution)/shard_map/ppermute | solution.py:904
  29.1 18.6 %collective-permute-start.11 = (bf16[3072,128]{1,0:T(8,128)(2,1)}, bf16[3072,128]{1,0:T(8,128)(2,1)}, u32[]{:S(2)}, u32[]{:S(2)}) collective-permute-start(bf16[3072,128]{1,0:T(8,128)(2,1)} %collective-permute-done.refs_2_), channel_id=1, source_target_pairs={{0,8},{8,16},{16,24},{24,28},{28,20},{20,12},{12,4},{4,0},{1,9},{9... | collective-permute-start | bytes 2359304 | tf_op jit(solution)/shard_map/ppermute | solution.py:681
  29.6 19.4 %collective-permute-start.13 = (bf16[3072,128]{1,0:T(8,128)(2,1)}, bf16[3072,128]{1,0:T(8,128)(2,1)}, u32[]{:S(2)}, u32[]{:S(2)}) collective-permute-start(bf16[3072,128]{1,0:T(8,128)(2,1)} %collective-permute-done.1.refs_4_), channel_id=1, source_target_pairs={{8,0},{16,8},{24,16},{28,24},{20,28},{12,20},{4,12},{0,4},{9,1},{1... | collective-permute-start | bytes 2359304 | tf_op jit(solution)/shard_map/ppermute | solution.py:682
  31.2 12.1 %collective-permute-start.9 = (bf16[3072,128]{1,0:T(8,128)(2,1)}, bf16[3072,128]{1,0:T(8,128)(2,1)}, u32[]{:S(2)}, u32[]{:S(2)}) collective-permute-start(bf16[3072,128]{1,0:T(8,128)(2,1)} %collective-permute-done.refs_2_), channel_id=1, source_target_pairs={{0,1},{1,0},{2,3},{3,2},{4,5},{5,4},{6,7},{7,6},{8,9},{9,8},{10,11... | collective-permute-start | bytes 2359304 | tf_op jit(solution)/shard_map/ppermute | solution.py:940
  40.7 15.0 %collective-permute-start.7 = (bf16[16,768]{1,0:T(8,128)(2,1)S(1)}, bf16[16,768]{1,0:T(8,128)(2,1)S(1)}, u32[]{:S(2)}, u32[]{:S(2)}) collective-permute-start(bf16[16,768]{1,0:T(8,128)(2,1)S(1)} %concatenate.97), channel_id=1, source_target_pairs={{0,16},{4,20},{8,24},{12,28},{16,0},{20,4},{24,8},{28,12},{1,17},{... | collective-permute-start | bytes 73736 | tf_op jit(solution)/shard_map/ppermute | solution.py:969
  49.0 19.5 %collective-permute-start.15 = (bf16[3072,128]{1,0:T(8,128)(2,1)}, bf16[3072,128]{1,0:T(8,128)(2,1)}, u32[]{:S(2)}, u32[]{:S(2)}) collective-permute-start(bf16[3072,128]{1,0:T(8,128)(2,1)} %collective-permute-done.11.refs_6_), channel_id=1, source_target_pairs={{0,8},{8,16},{16,24},{24,28},{28,20},{20,12},{12,4},{4,0},{1,9},{9... | collective-permute-start | bytes 2359304 | tf_op jit(solution)/shard_map/ppermute | solution.py:681
  51.2 18.3 %collective-permute-start.17 = (bf16[3072,128]{1,0:T(8,128)(2,1)}, bf16[3072,128]{1,0:T(8,128)(2,1)}, u32[]{:S(2)}, u32[]{:S(2)}) collective-permute-start(bf16[3072,128]{1,0:T(8,128)(2,1)} %collective-permute-done.13.refs_8_), channel_id=1, source_target_pairs={{8,0},{16,8},{24,16},{28,24},{20,28},{12,20},{4,12},{0,4},{9,1},{1... | collective-permute-start | bytes 2359304 | tf_op jit(solution)/shard_map/ppermute | solution.py:682
  51.2 19.4 %collective-permute-start.12 = (bf16[3072,128]{1,0:T(8,128)(2,1)}, bf16[3072,128]{1,0:T(8,128)(2,1)}, u32[]{:S(2)}, u32[]{:S(2)}) collective-permute-start(bf16[3072,128]{1,0:T(8,128)(2,1)} %collective-permute-done.11.refs_6_), channel_id=1, source_target_pairs={{0,1},{1,0},{2,3},{3,2},{4,5},{5,4},{6,7},{7,6},{8,9},{9,8},{10,11... | collective-permute-start | bytes 2359304 | tf_op jit(solution)/shard_map/ppermute | solution.py:940
  51.3 19.4 %collective-permute-start.14 = (bf16[3072,128]{1,0:T(8,128)(2,1)}, bf16[3072,128]{1,0:T(8,128)(2,1)}, u32[]{:S(2)}, u32[]{:S(2)}) collective-permute-start(bf16[3072,128]{1,0:T(8,128)(2,1)} %collective-permute-done.13.refs_8_), channel_id=1, source_target_pairs={{0,1},{1,0},{2,3},{3,2},{4,5},{5,4},{6,7},{7,6},{8,9},{9,8},{10,11... | collective-permute-start | bytes 2359304 | tf_op jit(solution)/shard_map/ppermute | solution.py:940
  55.6 11.7 %collective-permute-start.19 = (bf16[200,1024]{1,0:T(8,128)(2,1)}, bf16[200,1024]{1,0:T(8,128)(2,1)}, u32[]{:S(2)}, u32[]{:S(2)}) collective-permute-start(bf16[200,1024]{1,0:T(8,128)(2,1)} %reshape.578), channel_id=1, source_target_pairs={{0,2},{1,3},{2,0},{3,1},{4,6},{5,7},{6,4},{7,5},{8,10},{9,11},{10,... | collective-permute-start | bytes 1228808 | tf_op jit(solution)/shard_map/ppermute | solution.py:904
  70.6 10.3 %collective-permute-start.20 = (bf16[1536,128]{1,0:T(8,128)(2,1)S(1)}, bf16[1536,128]{1,0:T(8,128)(2,1)}, u32[]{:S(2)}, u32[]{:S(2)}) collective-permute-start(bf16[1536,128]{1,0:T(8,128)(2,1)S(1)} %slice.602), channel_id=1, source_target_pairs={{0,8},{8,16},{16,24},{24,28},{28,20},{20,12},{12,4},{4,0},{1,9},{9... | collective-permute-start | bytes 1179656 | tf_op jit(solution)/shard_map/ppermute | solution.py:681
  72.7 11.6 %collective-permute-start.16 = (bf16[3072,128]{1,0:T(8,128)(2,1)}, bf16[3072,128]{1,0:T(8,128)(2,1)S(1)}, u32[]{:S(2)}, u32[]{:S(2)}) collective-permute-start(bf16[3072,128]{1,0:T(8,128)(2,1)} %collective-permute-done.15.refs_10_), channel_id=1, source_target_pairs={{0,1},{1,0},{2,3},{3,2},{4,5},{5,4},{6,7},{7,6},{8,9},{9,8},{10,11... | collective-permute-start | bytes 2359304 | tf_op jit(solution)/shard_map/ppermute | solution.py:940
  72.8 14.1 %collective-permute-start.18 = (bf16[3072,128]{1,0:T(8,128)(2,1)}, bf16[3072,128]{1,0:T(8,128)(2,1)}, u32[]{:S(2)}, u32[]{:S(2)}) collective-permute-start(bf16[3072,128]{1,0:T(8,128)(2,1)} %collective-permute-done.17.refs_12_), channel_id=1, source_target_pairs={{0,1},{1,0},{2,3},{3,2},{4,5},{5,4},{6,7},{7,6},{8,9},{9,8},{10,11... | collective-permute-start | bytes 2359304 | tf_op jit(solution)/shard_map/ppermute | solution.py:940
  83.9 37.6 %collective-permute-start.24 = (bf16[3072,128]{1,0:T(8,128)(2,1)S(1)}, bf16[3072,128]{1,0:T(8,128)(2,1)}, u32[]{:S(2)}, u32[]{:S(2)}) collective-permute-start(bf16[3072,128]{1,0:T(8,128)(2,1)S(1)} %bitcast.74), channel_id=1, source_target_pairs={{0,8},{8,16},{16,24},{24,28},{28,20},{20,12},{12,4},{4,0},{1,9},{9... | collective-permute-start | bytes 2359304 | tf_op jit(solution)/shard_map/ppermute | solution.py:681
  85.1 36.4 %collective-permute-start.25 = (bf16[3072,128]{1,0:T(8,128)(2,1)S(1)}, bf16[3072,128]{1,0:T(8,128)(2,1)}, u32[]{:S(2)}, u32[]{:S(2)}) collective-permute-start(bf16[3072,128]{1,0:T(8,128)(2,1)S(1)} %bitcast.75), channel_id=1, source_target_pairs={{8,0},{16,8},{24,16},{28,24},{20,28},{12,20},{4,12},{0,4},{9,1},{1... | collective-permute-start | bytes 2359304 | tf_op jit(solution)/shard_map/ppermute | solution.py:682
  110.3 13.7 %collective-permute-start.35 = (bf16[200,1024]{1,0:T(8,128)(2,1)S(1)}, bf16[200,1024]{1,0:T(8,128)(2,1)S(1)}, u32[]{:S(2)}, u32[]{:S(2)}) collective-permute-start(bf16[200,1024]{1,0:T(8,128)(2,1)S(1)} %get-tuple-element.180.own_ref), channel_id=1, source_target_pairs={{0,2},{1,3},{2,0},{3,1},{4,6},{5,7},{6,4},{7,5},{8,10},{9,11},{10,... | collective-permute-start | bytes 1228808 | tf_op jit(solution)/shard_map/ppermute | solution.py:943
  111.6 22.6 %collective-permute-start.28 = (bf16[3072,128]{1,0:T(8,128)(2,1)S(1)}, bf16[3072,128]{1,0:T(8,128)(2,1)S(1)}, u32[]{:S(2)}, u32[]{:S(2)}) collective-permute-start(bf16[3072,128]{1,0:T(8,128)(2,1)S(1)} %bitcast.76), channel_id=1, source_target_pairs={{0,1},{1,0},{2,3},{3,2},{4,5},{5,4},{6,7},{7,6},{8,9},{9,8},{10,11... | collective-permute-start | bytes 2359304 | tf_op jit(solution)/shard_map/ppermute | solution.py:940
  121.5 20.2 %collective-permute-start.31 = (bf16[3072,128]{1,0:T(8,128)(2,1)}, bf16[3072,128]{1,0:T(8,128)(2,1)S(1)}, u32[]{:S(2)}, u32[]{:S(2)}) collective-permute-start(bf16[3072,128]{1,0:T(8,128)(2,1)} %collective-permute-done.24.refs_2_), channel_id=1, source_target_pairs={{0,8},{8,16},{16,24},{24,28},{28,20},{20,12},{12,4},{4,0},{1,9},{9... | collective-permute-start | bytes 2359304 | tf_op jit(solution)/shard_map/ppermute | solution.py:681
  121.9 20.3 %collective-permute-start.33 = (bf16[3072,128]{1,0:T(8,128)(2,1)}, bf16[3072,128]{1,0:T(8,128)(2,1)S(1)}, u32[]{:S(2)}, u32[]{:S(2)}) collective-permute-start(bf16[3072,128]{1,0:T(8,128)(2,1)} %collective-permute-done.25.refs_4_), channel_id=1, source_target_pairs={{8,0},{16,8},{24,16},{28,24},{20,28},{12,20},{4,12},{0,4},{9,1},{1... | collective-permute-start | bytes 2359304 | tf_op jit(solution)/shard_map/ppermute | solution.py:682
  124.0 10.2 %collective-permute-start.29 = (bf16[3072,128]{1,0:T(8,128)(2,1)}, bf16[3072,128]{1,0:T(8,128)(2,1)S(1)}, u32[]{:S(2)}, u32[]{:S(2)}) collective-permute-start(bf16[3072,128]{1,0:T(8,128)(2,1)} %collective-permute-done.24.refs_2_), channel_id=1, source_target_pairs={{0,1},{1,0},{2,3},{3,2},{4,5},{5,4},{6,7},{7,6},{8,9},{9,8},{10,11... | collective-permute-start | bytes 2359304 | tf_op jit(solution)/shard_map/ppermute | solution.py:940
  142.2 18.9 %collective-permute-start.36 = (bf16[3072,128]{1,0:T(8,128)(2,1)S(1)}, bf16[3072,128]{1,0:T(8,128)(2,1)}, u32[]{:S(2)}, u32[]{:S(2)}) collective-permute-start(bf16[3072,128]{1,0:T(8,128)(2,1)S(1)} %collective-permute-done.31.refs_6_), channel_id=1, source_target_pairs={{0,8},{8,16},{16,24},{24,28},{28,20},{20,12},{12,4},{4,0},{1,9},{9... | collective-permute-start | bytes 2359304 | tf_op jit(solution)/shard_map/ppermute | solution.py:681
  142.6 19.5 %collective-permute-start.38 = (bf16[3072,128]{1,0:T(8,128)(2,1)S(1)}, bf16[3072,128]{1,0:T(8,128)(2,1)}, u32[]{:S(2)}, u32[]{:S(2)}) collective-permute-start(bf16[3072,128]{1,0:T(8,128)(2,1)S(1)} %collective-permute-done.33.refs_8_), channel_id=1, source_target_pairs={{8,0},{16,8},{24,16},{28,24},{20,28},{12,20},{4,12},{0,4},{9,1},{1... | collective-permute-start | bytes 2359304 | tf_op jit(solution)/shard_map/ppermute | solution.py:682
  144.2 19.0 %collective-permute-start.32 = (bf16[3072,128]{1,0:T(8,128)(2,1)S(1)}, bf16[3072,128]{1,0:T(8,128)(2,1)S(1)}, u32[]{:S(2)}, u32[]{:S(2)}) collective-permute-start(bf16[3072,128]{1,0:T(8,128)(2,1)S(1)} %collective-permute-done.31.refs_6_), channel_id=1, source_target_pairs={{0,1},{1,0},{2,3},{3,2},{4,5},{5,4},{6,7},{7,6},{8,9},{9,8},{10,11... | collective-permute-start | bytes 2359304 | tf_op jit(solution)/shard_map/ppermute | solution.py:940
  144.2 19.9 %collective-permute-start.34 = (bf16[3072,128]{1,0:T(8,128)(2,1)S(1)}, bf16[3072,128]{1,0:T(8,128)(2,1)S(1)}, u32[]{:S(2)}, u32[]{:S(2)}) collective-permute-start(bf16[3072,128]{1,0:T(8,128)(2,1)S(1)} %collective-permute-done.33.refs_8_), channel_id=1, source_target_pairs={{0,1},{1,0},{2,3},{3,2},{4,5},{5,4},{6,7},{7,6},{8,9},{9,8},{10,11... | collective-permute-start | bytes 2359304 | tf_op jit(solution)/shard_map/ppermute | solution.py:940
  145.4 22.7 %collective-permute-start.26 = (bf16[200,1024]{1,0:T(8,128)(2,1)S(1)}, bf16[200,1024]{1,0:T(8,128)(2,1)S(1)}, u32[]{:S(2)}, u32[]{:S(2)}) collective-permute-start(bf16[200,1024]{1,0:T(8,128)(2,1)S(1)} %get-tuple-element.184.own_ref), channel_id=1, source_target_pairs={{0,2},{1,3},{2,0},{3,1},{4,6},{5,7},{6,4},{7,5},{8,10},{9,11},{10,... | collective-permute-start | bytes 1228808 | tf_op jit(solution)/shard_map/ppermute | solution.py:943
  165.0 12.2 %collective-permute-start.40 = (bf16[1536,128]{1,0:T(8,128)(2,1)S(1)}, bf16[1536,128]{1,0:T(8,128)(2,1)}, u32[]{:S(2)}, u32[]{:S(2)}) collective-permute-start(bf16[1536,128]{1,0:T(8,128)(2,1)S(1)} %slice.615), channel_id=1, source_target_pairs={{0,8},{8,16},{16,24},{24,28},{28,20},{20,12},{12,4},{4,0},{1,9},{9... | collective-permute-start | bytes 1179656 | tf_op jit(solution)/shard_map/ppermute | solution.py:681
  165.8 11.4 %collective-permute-start.42 = (bf16[1536,128]{1,0:T(8,128)(2,1)S(1)}, bf16[1536,128]{1,0:T(8,128)(2,1)}, u32[]{:S(2)}, u32[]{:S(2)}) collective-permute-start(bf16[1536,128]{1,0:T(8,128)(2,1)S(1)} %slice.616), channel_id=1, source_target_pairs={{8,0},{16,8},{24,16},{28,24},{20,28},{12,20},{4,12},{0,4},{9,1},{1... | collective-permute-start | bytes 1179656 | tf_op jit(solution)/shard_map/ppermute | solution.py:682
  167.0 15.5 %collective-permute-start.37 = (bf16[3072,128]{1,0:T(8,128)(2,1)}, bf16[3072,128]{1,0:T(8,128)(2,1)}, u32[]{:S(2)}, u32[]{:S(2)}) collective-permute-start(bf16[3072,128]{1,0:T(8,128)(2,1)} %collective-permute-done.36.refs_10_), channel_id=1, source_target_pairs={{0,1},{1,0},{2,3},{3,2},{4,5},{5,4},{6,7},{7,6},{8,9},{9,8},{10,11... | collective-permute-start | bytes 2359304 | tf_op jit(solution)/shard_map/ppermute | solution.py:940
  167.0 16.1 %collective-permute-start.39 = (bf16[3072,128]{1,0:T(8,128)(2,1)}, bf16[3072,128]{1,0:T(8,128)(2,1)}, u32[]{:S(2)}, u32[]{:S(2)}) collective-permute-start(bf16[3072,128]{1,0:T(8,128)(2,1)} %collective-permute-done.38.refs_12_), channel_id=1, source_target_pairs={{0,1},{1,0},{2,3},{3,2},{4,5},{5,4},{6,7},{7,6},{8,9},{9,8},{10,11... | collective-permute-start | bytes 2359304 | tf_op jit(solution)/shard_map/ppermute | solution.py:940
  175.7 32.6 %collective-permute-start.27 = (bf16[200,1024]{1,0:T(8,128)(2,1)}, bf16[200,1024]{1,0:T(8,128)(2,1)}, u32[]{:S(2)}, u32[]{:S(2)}) collective-permute-start(bf16[200,1024]{1,0:T(8,128)(2,1)} %get-tuple-element.186.refs_1_), channel_id=1, source_target_pairs={{0,2},{1,3},{2,0},{3,1},{4,6},{5,7},{6,4},{7,5},{8,10},{9,11},{10,... | collective-permute-start | bytes 1228808 | tf_op jit(solution)/shard_map/ppermute | solution.py:943
  182.5 35.7 %collective-permute-start.44 = (bf16[200,1024]{1,0:T(8,128)(2,1)}, bf16[200,1024]{1,0:T(8,128)(2,1)S(1)}, u32[]{:S(2)}, u32[]{:S(2)}) collective-permute-start(bf16[200,1024]{1,0:T(8,128)(2,1)} %copy-done.81), channel_id=1, source_target_pairs={{0,2},{1,3},{2,0},{3,1},{4,6},{5,7},{6,4},{7,5},{8,10},{9,11},{10,... | collective-permute-start | bytes 1228808 | tf_op jit(solution)/shard_map/ppermute | solution.py:943
  216.6 12.4 %collective-permute-start.45 = (bf16[200,1024]{1,0:T(8,128)(2,1)S(1)}, bf16[200,1024]{1,0:T(8,128)(2,1)S(1)}, u32[]{:S(2)}, u32[]{:S(2)}) collective-permute-start(bf16[200,1024]{1,0:T(8,128)(2,1)S(1)} %get-tuple-element.198.own_ref), channel_id=1, source_target_pairs={{0,2},{1,3},{2,0},{3,1},{4,6},{5,7},{6,4},{7,5},{8,10},{9,11},{10,... | collective-permute-start | bytes 1228808 | tf_op jit(solution)/shard_map/ppermute | solution.py:943
  223.0 18.3 %collective-permute-start.46 = (bf16[200,1024]{1,0:T(8,128)(2,1)S(1)}, bf16[200,1024]{1,0:T(8,128)(2,1)S(1)}, u32[]{:S(2)}, u32[]{:S(2)}) collective-permute-start(bf16[200,1024]{1,0:T(8,128)(2,1)S(1)} %get-tuple-element.197.own_ref), channel_id=1, source_target_pairs={{0,2},{1,3},{2,0},{3,1},{4,6},{5,7},{6,4},{7,5},{8,10},{9,11},{10,... | collective-permute-start | bytes 1228808 | tf_op jit(solution)/shard_map/ppermute | solution.py:943
  239.8 35.1 %collective-permute-start.48 = (bf16[200,1024]{1,0:T(8,128)(2,1)S(1)}, bf16[200,1024]{1,0:T(8,128)(2,1)}, u32[]{:S(2)}, u32[]{:S(2)}) collective-permute-start(bf16[200,1024]{1,0:T(8,128)(2,1)S(1)} %get-tuple-element.205.own_ref), channel_id=1, source_target_pairs={{0,2},{1,3},{2,0},{3,1},{4,6},{5,7},{6,4},{7,5},{8,10},{9,11},{10,... | collective-permute-start | bytes 1228808 | tf_op jit(solution)/shard_map/ppermute | solution.py:943
  254.0 29.9 %collective-permute-start.49 = (bf16[200,1024]{1,0:T(8,128)(2,1)}, bf16[200,1024]{1,0:T(8,128)(2,1)}, u32[]{:S(2)}, u32[]{:S(2)}) collective-permute-start(bf16[200,1024]{1,0:T(8,128)(2,1)} %get-tuple-element.213.own_ref), channel_id=1, source_target_pairs={{0,2},{1,3},{2,0},{3,1},{4,6},{5,7},{6,4},{7,5},{8,10},{9,11},{10,... | collective-permute-start | bytes 1228808 | tf_op jit(solution)/shard_map/ppermute | solution.py:943
  306.0 21.3 %collective-permute-start.52 = (bf16[24576,128]{1,0:T(8,128)(2,1)S(1)}, bf16[24576,128]{1,0:T(8,128)(2,1)S(1)}, u32[]{:S(2)}, u32[]{:S(2)}) collective-permute-start(bf16[24576,128]{1,0:T(8,128)(2,1)S(1)} %get-tuple-element.240), channel_id=1, source_target_pairs={{0,1},{1,0},{2,3},{3,2},{4,5},{5,4},{6,7},{7,6},{8,9},{9,8},{10,11... | collective-permute-start | bytes 18874376 | tf_op jit(solution)/shard_map/ppermute | solution.py:940
  306.0 12.3 %collective-permute-start.51 = (bf16[200,1024]{1,0:T(8,128)(2,1)S(1)}, bf16[200,1024]{1,0:T(8,128)(2,1)S(1)}, u32[]{:S(2)}, u32[]{:S(2)}) collective-permute-start(bf16[200,1024]{1,0:T(8,128)(2,1)S(1)} %get-tuple-element.236.refs_1_), channel_id=1, source_target_pairs={{0,2},{1,3},{2,0},{3,1},{4,6},{5,7},{6,4},{7,5},{8,10},{9,11},{10,... | collective-permute-start | bytes 1228808 | tf_op jit(solution)/shard_map/ppermute | solution.py:943
  307.6 28.8 %collective-permute-start.57 = (bf16[200,1024]{1,0:T(8,128)(2,1)S(1)}, bf16[200,1024]{1,0:T(8,128)(2,1)S(1)}, u32[]{:S(2)}, u32[]{:S(2)}) collective-permute-start(bf16[200,1024]{1,0:T(8,128)(2,1)S(1)} %get-tuple-element.249.refs_1_), channel_id=1, source_target_pairs={{0,2},{1,3},{2,0},{3,1},{4,6},{5,7},{6,4},{7,5},{8,10},{9,11},{10,... | collective-permute-start | bytes 1228808 | tf_op jit(solution)/shard_map/ppermute | solution.py:943
  308.1 22.1 %collective-permute-start.53 = (bf16[1536,128]{1,0:T(8,128)(2,1)}, bf16[1536,128]{1,0:T(8,128)(2,1)}, u32[]{:S(2)}, u32[]{:S(2)}) collective-permute-start(bf16[1536,128]{1,0:T(8,128)(2,1)} %get-tuple-element.233), channel_id=1, source_target_pairs={{0,8},{8,16},{16,24},{24,28},{28,20},{20,12},{12,4},{4,0},{1,9},{9... | collective-permute-start | bytes 1179656 | tf_op jit(solution)/shard_map/ppermute | solution.py:715
  308.9 22.4 %collective-permute-start.54 = (bf16[1536,128]{1,0:T(8,128)(2,1)}, bf16[1536,128]{1,0:T(8,128)(2,1)}, u32[]{:S(2)}, u32[]{:S(2)}) collective-permute-start(bf16[1536,128]{1,0:T(8,128)(2,1)} %get-tuple-element.234), channel_id=1, source_target_pairs={{8,0},{16,8},{24,16},{28,24},{20,28},{12,20},{4,12},{0,4},{9,1},{1... | collective-permute-start | bytes 1179656 | tf_op jit(solution)/shard_map/ppermute | solution.py:716
  325.8 38.9 %collective-permute-start.58 = (bf16[200,1024]{1,0:T(8,128)(2,1)}, bf16[200,1024]{1,0:T(8,128)(2,1)}, u32[]{:S(2)}, u32[]{:S(2)}) collective-permute-start(bf16[200,1024]{1,0:T(8,128)(2,1)} %get-tuple-element.259.own_ref), channel_id=1, source_target_pairs={{0,2},{1,3},{2,0},{3,1},{4,6},{5,7},{6,4},{7,5},{8,10},{9,11},{10,... | collective-permute-start | bytes 1228808 | tf_op jit(solution)/shard_map/ppermute | solution.py:943
  334.3 24.3 %collective-permute-start.56 = (bf16[3072,128]{1,0:T(8,128)(2,1)}, bf16[3072,128]{1,0:T(8,128)(2,1)}, u32[]{:S(2)}, u32[]{:S(2)}) collective-permute-start(bf16[3072,128]{1,0:T(8,128)(2,1)} %pad_maximum_fusion.1), channel_id=1, source_target_pairs={{8,0},{16,8},{24,16},{28,24},{20,28},{12,20},{4,12},{0,4},{9,1},{1... | collective-permute-start | bytes 2359304 | tf_op jit(solution)/shard_map/ppermute | solution.py:716
  335.9 22.7 %collective-permute-start.55 = (bf16[3072,128]{1,0:T(8,128)(2,1)}, bf16[3072,128]{1,0:T(8,128)(2,1)}, u32[]{:S(2)}, u32[]{:S(2)}) collective-permute-start(bf16[3072,128]{1,0:T(8,128)(2,1)} %pad_maximum_fusion), channel_id=1, source_target_pairs={{0,8},{8,16},{16,24},{24,28},{28,20},{20,12},{12,4},{4,0},{1,9},{9... | collective-permute-start | bytes 2359304 | tf_op jit(solution)/shard_map/ppermute | solution.py:715
  361.7 17.9 %collective-permute-start.61 = (bf16[3072,128]{1,0:T(8,128)(2,1)S(1)}, bf16[3072,128]{1,0:T(8,128)(2,1)S(1)}, u32[]{:S(2)}, u32[]{:S(2)}) collective-permute-start(bf16[3072,128]{1,0:T(8,128)(2,1)S(1)} %get-tuple-element.258), channel_id=1, source_target_pairs={{8,0},{16,8},{24,16},{28,24},{20,28},{12,20},{4,12},{0,4},{9,1},{1... | collective-permute-start | bytes 2359304 | tf_op jit(solution)/shard_map/ppermute | solution.py:716
  363.4 18.1 %collective-permute-start.60 = (bf16[3072,128]{1,0:T(8,128)(2,1)S(1)}, bf16[3072,128]{1,0:T(8,128)(2,1)}, u32[]{:S(2)}, u32[]{:S(2)}) collective-permute-start(bf16[3072,128]{1,0:T(8,128)(2,1)S(1)} %get-tuple-element.257), channel_id=1, source_target_pairs={{0,8},{8,16},{16,24},{24,28},{28,20},{20,12},{12,4},{4,0},{1,9},{9... | collective-permute-start | bytes 2359304 | tf_op jit(solution)/shard_map/ppermute | solution.py:715
  400.6 10.5 %collective-permute-start.65 = (bf16[24576,128]{1,0:T(8,128)(2,1)}, bf16[24576,128]{1,0:T(8,128)(2,1)}, u32[]{:S(2)}, u32[]{:S(2)}) collective-permute-start(bf16[24576,128]{1,0:T(8,128)(2,1)} %get-tuple-element.297), channel_id=1, source_target_pairs={{0,1},{1,0},{2,3},{3,2},{4,5},{5,4},{6,7},{7,6},{8,9},{9,8},{10,11... | collective-permute-start | bytes 18874376 | tf_op jit(solution)/shard_map/ppermute | solution.py:940
  402.8 30.5 %collective-permute-start.68 = (bf16[3072,128]{1,0:T(8,128)(2,1)}, bf16[3072,128]{1,0:T(8,128)(2,1)S(1)}, u32[]{:S(2)}, u32[]{:S(2)}) collective-permute-start(bf16[3072,128]{1,0:T(8,128)(2,1)} %get-tuple-element.279), channel_id=1, source_target_pairs={{0,8},{8,16},{16,24},{24,28},{28,20},{20,12},{12,4},{4,0},{1,9},{9... | collective-permute-start | bytes 2359304 | tf_op jit(solution)/shard_map/ppermute | solution.py:715
  404.2 29.1 %collective-permute-start.69 = (bf16[3072,128]{1,0:T(8,128)(2,1)S(1)}, bf16[3072,128]{1,0:T(8,128)(2,1)S(1)}, u32[]{:S(2)}, u32[]{:S(2)}) collective-permute-start(bf16[3072,128]{1,0:T(8,128)(2,1)S(1)} %copy-done.160), channel_id=1, source_target_pairs={{8,0},{16,8},{24,16},{28,24},{20,28},{12,20},{4,12},{0,4},{9,1},{1... | collective-permute-start | bytes 2359304 | tf_op jit(solution)/shard_map/ppermute | solution.py:716
  404.9 26.1 %collective-permute-start.66 = (bf16[1536,128]{1,0:T(8,128)(2,1)}, bf16[1536,128]{1,0:T(8,128)(2,1)S(1)}, u32[]{:S(2)}, u32[]{:S(2)}) collective-permute-start(bf16[1536,128]{1,0:T(8,128)(2,1)} %get-tuple-element.285), channel_id=1, source_target_pairs={{0,8},{8,16},{16,24},{24,28},{28,20},{20,12},{12,4},{4,0},{1,9},{9... | collective-permute-start | bytes 1179656 | tf_op jit(solution)/shard_map/ppermute | solution.py:715
  408.3 24.6 %collective-permute-start.67 = (bf16[1536,128]{1,0:T(8,128)(2,1)S(1)}, bf16[1536,128]{1,0:T(8,128)(2,1)S(1)}, u32[]{:S(2)}, u32[]{:S(2)}) collective-permute-start(bf16[1536,128]{1,0:T(8,128)(2,1)S(1)} %get-tuple-element.286), channel_id=1, source_target_pairs={{8,0},{16,8},{24,16},{28,24},{20,28},{12,20},{4,12},{0,4},{9,1},{1... | collective-permute-start | bytes 1179656 | tf_op jit(solution)/shard_map/ppermute | solution.py:716
  411.1 22.2 %collective-permute-start.63 = (bf16[200,1024]{1,0:T(8,128)(2,1)S(1)}, bf16[200,1024]{1,0:T(8,128)(2,1)S(1)}, u32[]{:S(2)}, u32[]{:S(2)}) collective-permute-start(bf16[200,1024]{1,0:T(8,128)(2,1)S(1)} %broadcast_select_fusion.4), channel_id=1, source_target_pairs={{0,2},{1,3},{2,0},{3,1},{4,6},{5,7},{6,4},{7,5},{8,10},{9,11},{10,... | collective-permute-start | bytes 1228808 | tf_op jit(solution)/shard_map/ppermute | solution.py:943
  433.3 19.6 %collective-permute-start.72 = (bf16[3072,128]{1,0:T(8,128)(2,1)S(1)}, bf16[3072,128]{1,0:T(8,128)(2,1)S(1)}, u32[]{:S(2)}, u32[]{:S(2)}) collective-permute-start(bf16[3072,128]{1,0:T(8,128)(2,1)S(1)} %pad_maximum_fusion.3), channel_id=1, source_target_pairs={{8,0},{16,8},{24,16},{28,24},{20,28},{12,20},{4,12},{0,4},{9,1},{1... | collective-permute-start | bytes 2359304 | tf_op jit(solution)/shard_map/ppermute | solution.py:716
  433.4 19.5 %collective-permute-start.71 = (bf16[3072,128]{1,0:T(8,128)(2,1)S(1)}, bf16[3072,128]{1,0:T(8,128)(2,1)S(1)}, u32[]{:S(2)}, u32[]{:S(2)}) collective-permute-start(bf16[3072,128]{1,0:T(8,128)(2,1)S(1)} %pad_maximum_fusion.2), channel_id=1, source_target_pairs={{0,8},{8,16},{16,24},{24,28},{28,20},{20,12},{12,4},{4,0},{1,9},{9... | collective-permute-start | bytes 2359304 | tf_op jit(solution)/shard_map/ppermute | solution.py:715
  435.4 17.5 %collective-permute-start.70 = (f32[8,768]{1,0:T(8,128)S(1)}, f32[8,768]{1,0:T(8,128)S(1)}, u32[]{:S(2)}, u32[]{:S(2)}) collective-permute-start(f32[8,768]{1,0:T(8,128)S(1)} %slice.482), channel_id=1, source_target_pairs={{0,8},{4,12},{8,0},{12,4},{16,24},{20,28},{24,16},{28,20},{1,9},{5... | collective-permute-start | bytes 73736 | tf_op jit(solution)/shard_map/ppermute | solution.py:1152
  455.0 20.5 %collective-permute-start.75 = (bf16[3072,128]{1,0:T(8,128)(2,1)S(1)}, bf16[3072,128]{1,0:T(8,128)(2,1)S(1)}, u32[]{:S(2)}, u32[]{:S(2)}) collective-permute-start(bf16[3072,128]{1,0:T(8,128)(2,1)S(1)} %get-tuple-element.302), channel_id=1, source_target_pairs={{8,0},{16,8},{24,16},{28,24},{20,28},{12,20},{4,12},{0,4},{9,1},{1... | collective-permute-start | bytes 2359304 | tf_op jit(solution)/shard_map/ppermute | solution.py:716
  457.2 18.4 %collective-permute-start.74 = (bf16[3072,128]{1,0:T(8,128)(2,1)S(1)}, bf16[3072,128]{1,0:T(8,128)(2,1)S(1)}, u32[]{:S(2)}, u32[]{:S(2)}) collective-permute-start(bf16[3072,128]{1,0:T(8,128)(2,1)S(1)} %get-tuple-element.301), channel_id=1, source_target_pairs={{0,8},{8,16},{16,24},{24,28},{28,20},{20,12},{12,4},{4,0},{1,9},{9... | collective-permute-start | bytes 2359304 | tf_op jit(solution)/shard_map/ppermute | solution.py:715
  458.0 17.5 %collective-permute-start.73 = (f32[4,768]{1,0:T(4,128)S(1)}, f32[4,768]{1,0:T(4,128)S(1)}, u32[]{:S(2)}, u32[]{:S(2)}) collective-permute-start(f32[4,768]{1,0:T(4,128)S(1)} %slice.488), channel_id=1, source_target_pairs={{0,4},{4,0},{8,12},{12,8},{16,20},{20,16},{24,28},{28,24},{1,5},{5... | collective-permute-start | bytes 36872 | tf_op jit(solution)/shard_map/ppermute | solution.py:1152
  460.1 20.7 %collective-permute-start.47 = (bf16[200,1024]{1,0:T(8,128)(2,1)S(1)}, bf16[200,1024]{1,0:T(8,128)(2,1)S(1)}, u32[]{:S(2)}, u32[]{:S(2)}) collective-permute-start(bf16[200,1024]{1,0:T(8,128)(2,1)S(1)} %broadcast_select_fusion.3), channel_id=1, source_target_pairs={{0,2},{1,3},{2,0},{3,1},{4,6},{5,7},{6,4},{7,5},{8,10},{9,11},{10,... | collective-permute-start | bytes 1228808 | tf_op jit(solution)/shard_map/ppermute | solution.py:943
  478.8 17.5 %collective-permute-start.79 = (bf16[3072,128]{1,0:T(8,128)(2,1)}, bf16[3072,128]{1,0:T(8,128)(2,1)}, u32[]{:S(2)}, u32[]{:S(2)}) collective-permute-start(bf16[3072,128]{1,0:T(8,128)(2,1)} %get-tuple-element.305), channel_id=1, source_target_pairs={{8,0},{16,8},{24,16},{28,24},{20,28},{12,20},{4,12},{0,4},{9,1},{1... | collective-permute-start | bytes 2359304 | tf_op jit(solution)/shard_map/ppermute | solution.py:716
  479.1 17.5 %collective-permute-start.78 = (bf16[3072,128]{1,0:T(8,128)(2,1)}, bf16[3072,128]{1,0:T(8,128)(2,1)}, u32[]{:S(2)}, u32[]{:S(2)}) collective-permute-start(bf16[3072,128]{1,0:T(8,128)(2,1)} %get-tuple-element.304), channel_id=1, source_target_pairs={{0,8},{8,16},{16,24},{24,28},{28,20},{20,12},{12,4},{4,0},{1,9},{9... | collective-permute-start | bytes 2359304 | tf_op jit(solution)/shard_map/ppermute | solution.py:715
  (223 other events, 1995.1 us)

commit v3 on v2

--- a/solution.py
+++ b/solution.py
@@ -29,10 +29,9 @@
 ANY = pl.BlockSpec(memory_space=pl.ANY)
 SMEM = pl.BlockSpec(memory_space=pltpu.SMEM)
 VMEM = pl.BlockSpec(memory_space=pltpu.VMEM)
-HBM = pl.BlockSpec(memory_space=pltpu.HBM)
-
-
-def params(mib=30):
+
+
+def params(mib=16):
     return pltpu.CompilerParams(vmem_limit_bytes=mib << 20)
 
 
@@ -69,11 +68,7 @@
 
 def key_bias(kept_row, rows):
     def image_of(dim):
-        pos = lax.broadcasted_iota(jnp.int32, (rows, rows), dim)
-        image = jnp.zeros((rows, rows), jnp.int32)
-        for edge in range(S, rows, S):
-            image = image + (pos >= edge).astype(jnp.int32)
-        return image
+        return lax.rem(lax.broadcasted_iota(jnp.int32, (rows, rows), dim), rows // S)
 
     allowed = (image_of(0) == image_of(1)) & (kept_row > 0.0)
     return jnp.where(allowed, 0.0, -1e30)
@@ -87,11 +82,11 @@
 
 def attention_forward(first, *refs):
     if first:
-        x_ref, vecs, kept, weights, n1_ref, qkv_ref, lse_ref, att_ref, part_ref = refs
+        x_ref, vecs, kept, weights, n1_ref, qkv_ref, lse_ref, att_ref, part_ref, _ = refs
         hidden = x_ref[...].astype(F32)
     else:
         (mid_ref, own_ref, got_ref, prev, vecs, kept, weights) = refs[:7]
-        hidden_ref, n1_ref, qkv_ref, lse_ref, att_ref, part_ref = refs[7:]
+        hidden_ref, n1_ref, qkv_ref, lse_ref, att_ref, part_ref, _ = refs[7:]
         hidden = mid_ref[...] + (
             own_ref[...].astype(F32) + got_ref[...].astype(F32) + prev[6:7, :]
         )
@@ -140,10 +135,11 @@
     args = list(operands) + [vecs, kept, weights]
     return pl.pallas_call(
         functools.partial(attention_forward, first),
-        out_shape=outs,
+        out_shape=outs + [jax.ShapeDtypeStruct(weights.shape, BF)],
         grid=(1,),
         in_specs=[full(*a.shape) for a in args[:-1]] + [VMEM],
-        out_specs=[full(*o.shape) for o in outs],
+        out_specs=[full(*o.shape) for o in outs] + [VMEM],
+        input_output_aliases={len(args) - 1: len(outs)},
         compiler_params=params(),
         cost_estimate=cost(2 * rows * D * 4 * WID * 2, 6 << 20),
         name="attention_forward",
@@ -155,7 +151,7 @@
 
 
 def mlp_forward(hid_ref, own_ref, got_ref, vecs, weights, *rest):
-    mid_ref, n2_ref, act_ref, slope_ref, part_ref, total = rest
+    mid_ref, n2_ref, act_ref, slope_ref, part_ref, _, total = rest
     step = pl.program_id(0)
 
     @pl.when(step == 0)
@@ -217,7 +213,9 @@
             jax.ShapeDtypeStruct((rows, HID), BF),
             jax.ShapeDtypeStruct((rows, HID), BF),
             jax.ShapeDtypeStruct((rows, D), BF),
+            jax.ShapeDtypeStruct(weights.shape, BF),
         ],
+        input_output_aliases={4: 5},
         in_specs=[full(rows, D), full(rows, D), full(rows, D), full(16, D), VMEM],
         out_specs=[
             full(rows, D),
@@ -225,6 +223,7 @@
             pl.BlockSpec((rows, STEP_HID), lambda s: (0, s)),
             pl.BlockSpec((rows, STEP_HID), lambda s: (0, s)),
             full(rows, D),
+            VMEM,
         ],
         scratch_shapes=[pltpu.VMEM((rows, D), F32)],
         compiler_params=params(),
@@ -236,11 +235,11 @@
 def mlp_backward(first, *refs):
     if first:
         grad_ref, mid_ref, slope_ref, vecs, weights = refs[:5]
-        gd_ref, gu_ref, part_ref, sums_ref, total = refs[5:]
+        gd_ref, gu_ref, part_ref, sums_ref, _, total = refs[5:]
     else:
         (gm_ref, own_ref, got_ref, hid_ref, above) = refs[:5]
         mid_ref, slope_ref, vecs, weights = refs[5:9]
-        grad_out_ref, gd_ref, gu_ref, part_ref, sums_ref, total = refs[9:]
+        grad_out_ref, gd_ref, gu_ref, part_ref, sums_ref, _, total = refs[9:]
     step = pl.program_id(0)
 
     @pl.when(step == 0)
@@ -307,10 +306,11 @@
     return pl.pallas_call(
         functools.partial(mlp_backward, first),
         grid=(STEPS,),
-        out_shape=outs,
+        out_shape=outs + [jax.ShapeDtypeStruct(weights.shape, BF)],
+        input_output_aliases={len(specs) + 3: len(outs)},
         in_specs=specs
         + [full(rows, D), pl.BlockSpec((rows, STEP_HID), lambda s: (0, s)), full(16, D), VMEM],
-        out_specs=out_specs,
+        out_specs=out_specs + [VMEM],
         scratch_shapes=[pltpu.VMEM((rows, D), F32)],
         compiler_params=params(),
         cost_estimate=cost(2 * rows * D * 2 * HID * 2, 12 << 20),
@@ -334,6 +334,7 @@
     gp_ref,
     part_ref,
     sums_ref,
+    _,
 ):
     rows = grad_ref.shape[0]
     centre, rstd = stats(mid_ref[...])
@@ -396,9 +397,10 @@
     return pl.pallas_call(
         attention_backward,
         grid=(1,),
-        out_shape=outs,
+        out_shape=outs + [jax.ShapeDtypeStruct(args[-1].shape, BF)],
+        input_output_aliases={len(args) - 1: len(outs)},
         in_specs=[full(*a.shape) for a in args[:-1]] + [VMEM],
-        out_specs=[full(*o.shape) for o in outs],
+        out_specs=[full(*o.shape) for o in outs] + [VMEM],
         compiler_params=params(),
         cost_estimate=cost(2 * rows * D * 4 * WID * 3, 8 << 20),
         name="attention_backward",
@@ -412,55 +414,52 @@
     at = lax.rem(step, 2)
     tiles = STEP_HID // 2 // BLK
 
-    def copies(of_step, act_on):
+    def start(of_step):
         part = lax.rem(of_step, 2)
         first = lax.rem(of_step, STEPS) * tiles
 
-        def one(index, carry):
-            tile = lax.div(index, 8)
-            block = lax.rem(index, 8)
-            down_id = 128 + (first + tile) * 8 + block
-            up_id = 64 + block * 8 + first + tile
-            for slots, out in ((slot_own, own_ref), (slot_par, par_ref)):
-                mine = (of_step < STEPS) if out is own_ref else (of_step >= STEPS)
-
-                @pl.when(mine)
-                def _():
-                    down_row = pl.multiple_of(slots[down_id] * BLK, BLK)
-                    up_row = pl.multiple_of(slots[up_id] * BLK, BLK)
-                    tile_row = pl.multiple_of(tile * BLK, BLK)
-                    block_row = pl.multiple_of(block * BLK, BLK)
-                    act_on(
-                        pltpu.make_async_copy(
-                            down_buf.at[part, pl.ds(tile_row, BLK), pl.ds(block_row, BLK)],
-                            out.at[pl.ds(down_row, BLK), :],
-                            sems.at[part],
-                        )
-                    )
-                    act_on(
-                        pltpu.make_async_copy(
-                            up_buf.at[part, pl.ds(block_row, BLK), pl.ds(tile_row, BLK)],
-                            out.at[pl.ds(up_row, BLK), :],
-                            sems.at[part],
-                        )
-                    )
-
-            return carry
-
-        lax.fori_loop(0, tiles * 8, one, 0)
+        def send(slots, out):
+            def one(index, carry):
+                tile = lax.div(index, 8)
+                block = lax.rem(index, 8)
+                down_row = pl.multiple_of(slots[128 + (first + tile) * 8 + block] * BLK, BLK)
+                up_row = pl.multiple_of(slots[64 + block * 8 + first + tile] * BLK, BLK)
+                tile_row = pl.multiple_of(tile * BLK, BLK)
+                block_row = pl.multiple_of(block * BLK, BLK)
+                pltpu.make_async_copy(
+                    down_buf.at[part, pl.ds(tile_row, BLK), pl.ds(block_row, BLK)],
+                    out.at[pl.ds(down_row, BLK), :],
+                    sems.at[part],
+                ).start()
+                pltpu.make_async_copy(
+                    up_buf.at[part, pl.ds(block_row, BLK), pl.ds(tile_row, BLK)],
+                    out.at[pl.ds(up_row, BLK), :],
+                    sems.at[part],
+                ).start()
+                return carry
+
+            lax.fori_loop(0, tiles * 8, one, 0)
+
+        pl.when(of_step < STEPS)(lambda: send(slot_own, own_ref))
+        pl.when(of_step >= STEPS)(lambda: send(slot_par, par_ref))
+
+    def wait(of_step):
+        part = lax.rem(of_step, 2)
+        for buf in (down_buf, up_buf):
+            pltpu.make_async_copy(buf.at[part], buf.at[part], sems.at[part]).wait()
 
     @pl.when(step >= 2)
     def _():
-        copies(step - 2, lambda c: c.wait())
+        wait(step - 2)
 
     down_buf[at] = sum(dot_tn(a[...], g[...]) for a, g in zip(acts, gds)).astype(BF)
     up_buf[at] = sum(dot_tn(n[...], g[...]) for n, g in zip(n2s, gus)).astype(BF)
-    copies(step, lambda c: c.start())
+    start(step)
 
     @pl.when(step == 2 * STEPS - 1)
     def _():
-        copies(step - 1, lambda c: c.wait())
-        copies(step, lambda c: c.wait())
+        wait(step - 1)
+        wait(step)
 
 
 def call_mlp_grads(slots, acts, gds, n2s, gus):
@@ -492,72 +491,66 @@
 def attention_grads(slot_own, slot_par, *refs):
     atts, gbs, n1s, gqs, gks, gvs = (refs[2 * i : 2 * i + 2] for i in range(6))
     own_ref, par_ref, out_buf, qkv_buf, sems = refs[14:]
-    step = pl.program_id(0)
-    at = lax.rem(step, 2)
+    step = at = pl.program_id(0)
     per_share = D // NARROW // BLK
 
-    def copies(of_step, act_on):
-        part = lax.rem(of_step, 2)
-        column = lax.rem(of_step, per_share)
-
-        def one(block, carry):
-            block_row = pl.multiple_of(block * BLK, BLK)
-            for slots, out in ((slot_own, own_ref), (slot_par, par_ref)):
-                mine = (of_step < per_share) if out is own_ref else (of_step >= per_share)
-
-                @pl.when(mine)
-                def _():
+    def start(of_step):
+        part = of_step
+
+        def send(slots, out):
+            def one(block, carry):
+                block_row = pl.multiple_of(block * BLK, BLK)
+                for column in range(per_share):
+                    cols = pl.ds(column * BLK, BLK)
                     row = pl.multiple_of(slots[48 + column * 8 + block] * BLK, BLK)
-                    act_on(
-                        pltpu.make_async_copy(
-                            out_buf.at[part, :, pl.ds(block_row, BLK)],
-                            out.at[pl.ds(row, BLK), :],
-                            sems.at[part],
-                        )
-                    )
+                    pltpu.make_async_copy(
+                        out_buf.at[part, cols, pl.ds(block_row, BLK)],
+                        out.at[pl.ds(row, BLK), :],
+                        sems.at[part],
+                    ).start()
                     for third in range(3):
                         tile = block * 6 + third * 2 + column
                         row = pl.multiple_of(slots[tile] * BLK, BLK)
-                        act_on(
-                            pltpu.make_async_copy(
-                                qkv_buf.at[part, third, pl.ds(block_row, BLK), :],
-                                out.at[pl.ds(row, BLK), :],
-                                sems.at[part],
-                            )
-                        )
-
-            return carry
-
-        lax.fori_loop(0, 8, one, 0)
-
-    @pl.when(step >= 2)
-    def _():
-        copies(step - 2, lambda c: c.wait())
+                        pltpu.make_async_copy(
+                            qkv_buf.at[part, third, pl.ds(block_row, BLK), cols],
+                            out.at[pl.ds(row, BLK), :],
+                            sems.at[part],
+                        ).start()
+                return carry
+
+            lax.fori_loop(0, 8, one, 0)
+
+        pl.when(of_step == 0)(lambda: send(slot_own, own_ref))
+        pl.when(of_step == 1)(lambda: send(slot_par, par_ref))
+
+    def wait(part):
+        for buf in (out_buf, qkv_buf):
+            pltpu.make_async_copy(buf.at[part], buf.at[part], sems.at[part]).wait()
 
     out_buf[at] = sum(dot_tn(a[...], g[...]) for a, g in zip(atts, gbs)).astype(BF)
     for third, grads in enumerate((gqs, gks, gvs)):
         qkv_buf[at, third] = sum(dot_tn(n[...], g[...]) for n, g in zip(n1s, grads)).astype(BF)
-    copies(step, lambda c: c.start())
-
-    @pl.when(step == 2 * per_share - 1)
+    start(step)
+
+    @pl.when(step == 1)
     def _():
-        copies(step - 1, lambda c: c.wait())
-        copies(step, lambda c: c.wait())
+        wait(0)
+        wait(1)
 
 
 def call_attention_grads(slots, atts, gbs, n1s, gps, own, par):
     rows = gbs[0].shape[0]
-    steps = WID // BLK
+    width = WID // 2
     whole = pl.BlockSpec((rows, D), lambda s, a, b: (0, 0))
 
     def by_column(third):
-        return pl.BlockSpec((rows, BLK), lambda s, a, b: (0, third * steps + s))
+        return pl.BlockSpec((rows, width), lambda s, a, b: (0, third * 2 + s))
 
     return pl.pallas_call(
         attention_grads,
         grid_spec=pltpu.PrefetchScalarGridSpec(
             num_scalar_prefetch=2,
-            grid=(steps,),
+            grid=(2,),
             in_specs=[by_column(0)] * 2
             + [whole] * 4
             + [by_column(0)] * 2
@@ -566,8 +559,8 @@
             + [ANY, ANY],
             out_specs=[ANY, ANY],
             scratch_shapes=[
-                pltpu.VMEM((2, BLK, D), BF),
-                pltpu.VMEM((2, 3, D, BLK), BF),
+                pltpu.VMEM((2, width, D), BF),
+                pltpu.VMEM((2, 3, D, width), BF),
                 pltpu.SemaphoreType.DMA((2,)),
             ],
         ),
@@ -602,43 +595,33 @@
 def assemble_kernel(plan, rows, cols, *refs):
     sources = refs[: len(plan)]
     out_ref, sem = refs[-2:]
-
-    def run(at, act_on):
-        share, first, count = plan[at]
-
-        def one(i, carry):
+    for source, (share, first, count) in zip(sources, plan):
+
+        def one(i, carry, source=source, share=share, first=first):
             row = pl.multiple_of(rows[share, first + i], BLK)
             col = pl.multiple_of(cols[share, first + i], BLK)
-            from_row = pl.multiple_of(i * BLK, BLK)
-            act_on(
-                pltpu.make_async_copy(
-                    sources[at].at[pl.ds(from_row, BLK), :],
-                    out_ref.at[pl.ds(row, BLK), pl.ds(col, BLK)],
-                    sem,
-                )
-            )
+            pltpu.make_async_copy(
+                source.at[pl.ds(pl.multiple_of(i * BLK, BLK), BLK), :],
+                out_ref.at[pl.ds(row, BLK), pl.ds(col, BLK)],
+                sem,
+            ).start()
             return carry
 
-        lax.fori_loop(0, count, one, 0)
-
-    for at in range(len(plan)):
-        run(at, lambda c: c.start())
-    for at in range(len(plan)):
-        run(at, lambda c: c.wait())
-
-
-def assemble(table, pieces, weights):
+        lax.fori_loop(0, count, one, 0, unroll=4 if count % 4 == 0 else 1)
+    for source, (_, _, count) in zip(sources, plan):
+        tiles = source.at[pl.ds(0, count * BLK), :]
+        pltpu.make_async_copy(tiles, tiles, sem).wait()
+
+
+def assemble(table, pieces):
     plan = [piece[:3] for piece in pieces]
-    arrays = [piece[3] for piece in pieces]
-    alias = {} if weights is None else {2 + len(arrays): 0}
-    args = list(table) + arrays + ([] if weights is None else [weights])
+    args = list(table) + [piece[3] for piece in pieces]
     return pl.pallas_call(
         functools.partial(assemble_kernel, plan),
         out_shape=jax.ShapeDtypeStruct((6 * D, D), BF),
-        in_specs=[SMEM, SMEM] + [HBM] * len(arrays) + ([] if weights is None else [VMEM]),
-        out_specs=VMEM,
+        in_specs=[SMEM, SMEM] + [ANY] * len(pieces),
+        out_specs=ANY,
         scratch_shapes=[pltpu.SemaphoreType.DMA],
-        input_output_aliases=alias,
         compiler_params=params(),
         cost_estimate=cost(0, BLK),
         name="assemble",
@@ -811,57 +794,43 @@
     return value[0, 0]
 
 
-def rotate_in_kernel(grad_ref, left_ref, right_ref, out_ref):
-    for block in range(out_ref.shape[0]):
-        grad = grad_ref[block * BLK : (block + 1) * BLK, :].astype(BF)
-        inner = dot_tn(left_ref[0, block].astype(BF), grad)
-        out_ref[block] = dot(inner.astype(BF), right_ref[0, block].astype(BF))
-
-
-def rotate_in(layer, grads, left_basis, right_basis):
-    count = left_basis.shape[1]
-    group = 6
-    spec = pl.BlockSpec((group, BLK, BLK), lambda i: (i, 0, 0))
-    flat = pl.BlockSpec((group * BLK, BLK), lambda i: (i, 0))
-    basis = pl.BlockSpec((1, group, BLK, BLK), lambda i: (layer, i, 0, 0))
-    return pl.pallas_call(
-        rotate_in_kernel,
-        grid=(count // group,),
-        out_shape=jax.ShapeDtypeStruct((count, BLK, BLK), F32),
-        in_specs=[flat, basis, basis],
-        out_specs=spec,
-        compiler_params=params(10),
-        cost_estimate=cost(count * 4 * BLK**3, count * BLK * BLK * 14),
-        name="rotate_in",
-    )(grads, left_basis, right_basis)
-
-
-def update_kernel(clip_ref, rot0, rot1, left, right, first, second, master, *outs):
+def update_kernel(clip_ref, grad0, grad1, left, right, first, second, master, *outs):
     new_first, new_second, new_master, new_weights = outs
     step = pl.program_id(0)
     half = pl.num_programs(0) // 2
     clip = clip_ref[0]
-    for block in range(rot0.shape[0]):
-        rotated = clip * jnp.where(step < half, rot0[block], rot1[block])
-        one = 0.5 * first[0, block] + 0.5 * rotated
-        two = 0.5 * second[0, block] + 0.5 * rotated * rotated
-        new_first[0, block] = one
-        new_second[0, block] = two
-        direction = one / (jnp.sqrt(two) + 1e-08)
-        inner = dot(left[0, block].astype(BF), direction.astype(BF))
-        turned = dot_nt(inner.astype(BF), right[0, block].astype(BF))
-        weights = master[0, block] - 0.02 * turned
-        new_master[0, block] = weights
-        new_weights[0, block] = weights.astype(BF)
-
-
-def update(clip, rots, left, right, first, second, master):
-    count = rots[0].shape[0]
-    group = 3
+    grads = (grad0, grad1)
+    count = left.shape[1]
+    for base in range(0, count, 4):
+        blocks = range(base, min(base + 4, count))
+        lefts = [left[0, b].astype(BF) for b in blocks]
+        rights = [right[0, b].astype(BF) for b in blocks]
+        terms = [
+            jnp.where(step < half, *(g[b * BLK : (b + 1) * BLK, :] for g in grads)).astype(BF)
+            for b in blocks
+        ]
+        terms = [dot_tn(a, x).astype(BF) for a, x in zip(lefts, terms)]
+        terms = [clip * dot(x, b) for x, b in zip(terms, rights)]
+        ones = [0.5 * first[0, b] + 0.5 * x for b, x in zip(blocks, terms)]
+        twos = [0.5 * second[0, b] + 0.5 * x * x for b, x in zip(blocks, terms)]
+        terms = [(a / (jnp.sqrt(b) + 1e-08)).astype(BF) for a, b in zip(ones, twos)]
+        terms = [dot(a, x).astype(BF) for a, x in zip(lefts, terms)]
+        terms = [dot_nt(x, b) for x, b in zip(terms, rights)]
+        for b, one, two, turned in zip(blocks, ones, twos, terms):
+            new_first[0, b] = one
+            new_second[0, b] = two
+            weights = master[0, b] - 0.02 * turned
+            new_master[0, b] = weights
+            new_weights[0, b] = weights.astype(BF)
+
+
+def update(clip, grads, left, right, first, second, master):
+    count = left.shape[1]
+    group = 8 if count % 8 == 0 else 1
     steps = count // group
     spec = pl.BlockSpec((1, group, BLK, BLK), lambda i: (i // steps, i % steps, 0, 0))
-    low = pl.BlockSpec((group, BLK, BLK), lambda i: (jnp.minimum(i, steps - 1), 0, 0))
-    high = pl.BlockSpec((group, BLK, BLK), lambda i: (jnp.maximum(i - steps, 0), 0, 0))
+    low = pl.BlockSpec((group * BLK, BLK), lambda i: (jnp.minimum(i, steps - 1), 0))
+    high = pl.BlockSpec((group * BLK, BLK), lambda i: (jnp.maximum(i - steps, 0), 0))
     shape = jax.ShapeDtypeStruct(master.shape, F32)
     return pl.pallas_call(
         update_kernel,
@@ -869,10 +838,10 @@
         out_shape=[shape, shape, shape, jax.ShapeDtypeStruct(master.shape, BF)],
         in_specs=[SMEM, low, high] + [spec] * 5,
         out_specs=[spec] * 4,
-        compiler_params=params(10),
-        cost_estimate=cost(count * 8 * BLK**3, count * BLK * BLK * 2 * 38),
+        compiler_params=params(56),
+        cost_estimate=cost(count * 16 * BLK**3, count * BLK * BLK * 2 * 38),
         name="update",
-    )(clip, *rots, left, right, first, second, master)
+    )(clip, *grads, left, right, first, second, master)
 
 
 def shards(
@@ -906,7 +875,7 @@
 
     kept = [
         lax.dynamic_slice_in_dim(kept_tokens, (2 * t + core) * own_images, own_images, 0)
-        .reshape(1, rows)
+        .T.reshape(1, rows)
         .astype(F32)
         for t in range(2)
     ]
@@ -936,6 +905,12 @@
         slots.append(layer_slots)
         tables.append((jnp.stack(layer_rows), jnp.stack(layer_cols)))
 
+    def by_token(value):
+        return value.transpose(1, 0, 2).reshape(rows, D)
+
+    def by_image(value):
+        return value.reshape(S, own_images, D).transpose(1, 0, 2)
+
     def core_swap(value):
         return lax.ppermute(value, "narrow", CORE)
 
@@ -949,13 +924,13 @@
     def swapped(pieces):
         return [piece + (core_swap(piece[3]),) for piece in pieces]
 
-    def place_pieces(layer, pieces, matrix):
+    def place_pieces(layer, pieces):
         group = [
             (share, distance * per_device + first, count, pair[share])
             for distance, first, count, *pair in pieces
             for share in range(2)
         ]
-        return assemble(tables[layer], group, matrix)
+        return assemble(tables[layer], group)
 
     steps = wide // 2
     own_small_rows = small_params.astype(BF).reshape(1, -1)
@@ -972,28 +947,30 @@
     gather = Gather(units[0], wide, per_device)
     arrived = [(0, 0, per_device, units[0])] + gather.step()
     small_rows = grow(small_rows, near_bits)
-    placed, inputs, extra = [], [images, cotangent], [small_rows]
+    inputs = [by_token(images), by_token(cotangent)]
+    placed, extra = [], [small_rows]
     brought = []
     for step in range(2, steps + 1):
         latest = swapped(arrived)
         arrived = gather.step(*extra)
+        placed += latest
         extra = [piece[4] for piece in latest]
-        placed = placed + latest
-        if inputs:
-            brought.append(chunks(after(inputs.pop(0).reshape(rows, D), *gather.sent)))
-            extra += brought[-1]
+        if step == 2:
+            brought = chunks(after(inputs[0], *gather.sent))
+            extra += brought
+        elif step == 3:
+            late = exchange(after(inputs[1], *gather.sent))
         at = (step - 2) * per_window
         small_rows = grow(small_rows, far_bits[at : at + per_window])
         if step < steps:
             extra.append(small_rows)
-    while inputs:
-        brought.append(chunks(inputs.pop(0).reshape(rows, D)))
-    hidden_in, cot = brought
-    next_unit = after(units[1], gather.up, gather.down)
+    hidden_in = brought
+    next_unit = after(units[1], gather.up, gather.down, late)
     gather_next = Gather(next_unit, wide, per_device)
     arrived_next = [(0, 0, per_device, next_unit)] + gather_next.step()
     last = [piece[:3] + (after(piece[3], *gather_next.sent),) for piece in arrived]
-    weights = [place_pieces(0, placed + swapped(last), None)]
+    weights = [place_pieces(0, placed + swapped(last))]
+    cot = [jnp.where(half == t, inputs[1], late) for t in range(2)]
 
     in_order = jnp.take(small_rows, by_distance, axis=0).astype(F32)
     small_all = in_order.reshape(-1, LAYERS, own_small).transpose(1, 0, 2).reshape(LAYERS, -1)
@@ -1002,15 +979,20 @@
     saved = []
     state = None
     for layer in range(LAYERS):
-        att_w = mlp_w = weights[layer]
         kept_layer = []
         for t in range(2):
             if layer == 0:
-                out = call_attention_forward(True, (hidden_in[t],), vecs[0], kept[t], att_w)
                 hidden = hidden_in[t]
+                if t == 1:
+                    placed = swapped(arrived_next)
+                    arrived_next = gather_next.step(part)
+                    hidden = after(hidden, *gather_next.sent)
+                *out, weights[layer] = call_attention_forward(
+                    True, (hidden,), vecs[0], kept[t], weights[layer]
+                )
             else:
-                hidden, *out = call_attention_forward(
-                    False, state[t] + (vecs[layer - 1],), vecs[layer], kept[t], att_w
+                hidden, *out, weights[layer] = call_attention_forward(
+                    False, state[t] + (vecs[layer - 1],), vecs[layer], kept[t], weights[layer]
                 )
             n1, qkv, lse, att, part = out
             kept_layer.append([hidden, n1, qkv, lse, att, part, exchange(part)])
@@ -1018,27 +1000,27 @@
         state = []
         for t in range(2):
             hidden, n1, qkv, lse, att, part, got = kept_layer[t]
-            if layer == 0 and t == 0:
-                placed = swapped(arrived_next)
-                arrived_next = gather_next.step(part)
-                part = after(part, *gather_next.sent)
-            middle, n2, act, slope, down_part = call_mlp_forward(
-                hidden, part, got, vecs[layer], mlp_w
+            if layer == 0 and t == 1:
+                placed += swapped(arrived_next)
+                arrived_next = gather_next.step(down_part)
+                part = after(part, *gather_next.sent, *vecs[1:])
+            middle, n2, act, slope, down_part, weights[layer] = call_mlp_forward(
+                hidden, part, got, vecs[layer], weights[layer]
             )
             kept_layer[t] = (hidden, n1, qkv, lse, att, middle, n2, act, slope)
             if layer < LAYERS - 1:
                 state.append((middle, down_part, exchange(down_part)))
             else:
                 state.append((middle, down_part))
-        saved.append((att_w, mlp_w, kept_layer))
+        saved.append(kept_layer)
         if layer == 0:
-            gates = [down_part] + [piece[4] for piece in placed]
-            for step in range(3, steps + 1):
+            gates = [down_part]
+            for step in range(4, steps + 1):
                 latest = swapped(arrived_next)
                 arrived_next = gather_next.step(*gates)
+                placed += latest
                 gates = [piece[4] for piece in latest]
-                placed = placed + latest
-            weights.append(place_pieces(1, placed + swapped(arrived_next), None))
+            weights.append(place_pieces(1, placed + swapped(arrived_next)))
 
     def mine(pair):
         return jnp.where(half == 0, pair[0], pair[1])
@@ -1048,33 +1030,26 @@
 
     down_parts = [state[t][1] for t in range(2)]
     middles = [state[t][0] for t in range(2)]
-    final = mine(middles) + (
-        mine(down_parts).astype(F32)
-        + exchange(theirs(down_parts)).astype(F32)
-        + vecs[LAYERS - 1][6]
-    )
-    block_output = final.astype(BF).reshape(images.shape)
-
     upstream = None
     reduced = [None] * LAYERS
     small_terms = [None] * LAYERS
     pending = None
     for layer in reversed(range(LAYERS)):
-        att_w, mlp_w, kept_layer = saved[layer]
+        kept_layer = saved[layer]
         top = layer == LAYERS - 1
         work = []
         for t in range(2):
             hidden, n1, qkv, lse, att, middle, n2, act, slope = kept_layer[t]
             if top:
                 grad = cot[t]
-                gd, gu, part, sums = call_mlp_backward(
-                    True, (grad,), middle, slope, vecs[layer], mlp_w
+                gd, gu, part, sums, weights[layer] = call_mlp_backward(
+                    True, (grad,), middle, slope, vecs[layer], weights[layer]
                 )
             else:
                 state = upstream[t]
                 state = (after(state[0], *pending.sent),) + state[1:]
-                grad, gd, gu, part, sums = call_mlp_backward(
-                    False, state + (vecs[layer + 1],), middle, slope, vecs[layer], mlp_w
+                grad, gd, gu, part, sums, weights[layer] = call_mlp_backward(
+                    False, state + (vecs[layer + 1],), middle, slope, vecs[layer], weights[layer]
                 )
                 if t == 0:
                     pending.step(part)
@@ -1097,8 +1072,8 @@
             grad, gd, gu, part, sums, got = work[t]
             if pending is not None:
                 part = after(part, *pending.sent)
-            gm, gb, gp, att_part, att_sums = call_attention_backward(
-                grad, part, got, middle, hidden, qkv, lse, vecs[layer], kept[t], att_w
+            gm, gb, gp, att_part, att_sums, weights[layer] = call_attention_backward(
+                grad, part, got, middle, hidden, qkv, lse, vecs[layer], kept[t], weights[layer]
             )
             back.append((gm, gb, gp, att_part, att_sums))
         if pending is not None:
@@ -1106,11 +1081,12 @@
             while pending.left > 0:
                 pending.step()
             own = after(own, *pending.sent)
-            reduced[layer + 1] = pending.result()
-            arrivals = [pending.up, pending.down]
         if layer > 0:
+            got = [exchange(back[t][3]) for t in range(2)]
+            own = after(own, got[0])
             upstream = [
-                (back[t][0], back[t][3], exchange(back[t][3]), kept_layer[t][0]) for t in range(2)
+                (after(back[0][0], got[1]), back[0][3], got[0], kept_layer[0][0]),
+                (back[1][0], back[1][3], got[1], kept_layer[1][0]),
             ]
         own, par = call_attention_grads(
             slots[layer],
@@ -1135,6 +1111,9 @@
         pending.unit_of = first_unit
         pending.step()
         rest = core_swap(after(par, *pending.sent))
+        if earlier is not None:
+            earlier.up = after(earlier.up, *pending.sent)
+            reduced[layer + 1] = earlier.result()
 
         def unit_of(distance, own=own, rest=rest, unit_len=unit_len):
             at = turns[distance] * unit_len
@@ -1142,37 +1121,50 @@
 
         pending.unit_of = unit_of
 
+    final = mine(middles) + (
+        mine(down_parts).astype(F32)
+        + exchange(after(theirs(down_parts), rest)).astype(F32)
+        + vecs[LAYERS - 1][6]
+    )
+    block_output = by_image(final.astype(BF))
     parts = [b[3] for b in back]
-    last_part = exchange(after(theirs(parts), *pending.sent)).astype(F32)
+    last_part = exchange(after(theirs(parts), rest)).astype(F32)
     small_rows = jnp.take(jnp.concatenate(small_terms, axis=1), by_distance, axis=0)
-    small_rows = after(small_rows, *pending.sent)
+    small_rows = after(small_rows, rest)
     backward_bits = mesh_bits()[::-1]
+    local_sum = input_grad = None
     while pending.left > 0:
         for bit, axis, perm in backward_bits[:per_window]:
             small_rows = small_rows[:bit] + lax.ppermute(small_rows[bit:], axis, perm)
         backward_bits = backward_bits[per_window:]
-        pending.step(small_rows, last_part, *arrivals)
-        small_rows = after(small_rows, *pending.sent)
+        pending.step(small_rows)
+        early = list(pending.sent)
+        if local_sum is None:
+            upper = [after(grads, *pending.sent) for grads in reduced[1:]]
+            local_sum = sum(jnp.sum(grads * grads) for grads in upper)
+            early.append(local_sum)
+        elif input_grad is None:
+            hidden = mine([k[0] for k in saved[0]]).astype(F32)
+            centre, rstd = stats(hidden)
+            lower = norm_back(
+                mine(parts).astype(F32) + after(last_part, *pending.sent),
+                centre * rstd,
+                rstd,
+                vecs[0][0:1],
+            )
+            input_grad = by_image(mine([b[0] for b in back]) + lower)
+            early += [input_grad, block_output]
+        small_rows = after(small_rows, *early)
     for bit, axis, perm in backward_bits:
         small_rows = small_rows[:bit] + lax.ppermute(small_rows[bit:], axis, perm)
     reduced[0] = pending.result()
-    hidden = mine([k[0] for k in saved[0][2]]).astype(F32)
-    centre, rstd = stats(hidden)
-    lower = norm_back(mine(parts).astype(F32) + last_part, centre * rstd, rstd, vecs[0][0:1])
-    input_grad = (mine([b[0] for b in back]) + lower).reshape(images.shape)
-
     grad_small = small_rows.reshape(LAYERS, own_small)
-    local_sum = jnp.sum(grad_small * grad_small)
-    for grads in reduced[::-1]:
-        local_sum = local_sum + jnp.sum(grads * grads)
+    local_sum = local_sum + jnp.sum(grad_small * grad_small) + jnp.sum(reduced[0] * reduced[0])
     grad_norm = jnp.sqrt(total_over_mesh(local_sum))
     clip_factor = 1.0 / jnp.maximum(grad_norm, 1.0)
-    rots = [
-        rotate_in(layer, reduced[layer], left_basis, right_basis) for layer in range(LAYERS)
-    ]
     new_first, new_second, new_master, new_weights = update(
         clip_factor.reshape(1),
-        rots,
+        reduced,
         left_basis,
         right_basis,
         first_moment,

time: 559 us -> 503 us (0.90)
  local copies, waits for them, and re-layouts: 115 us -> 77.7 us
  Pallas kernels: 161 us -> 127 us
  waiting for transfers between devices: 141 us -> 169 us
  other arithmetic: 53 us -> 40.9 us
    unnamed x421 -> x247, local copies, waits for them, and re-layouts: 89.1 us -> 58 us
    ppermute x14 -> x15, waiting for transfers between devices: 14.5 us -> 33.8 us  [exchange(): return lax.ppermute(part, 'narrow', ACROSS)]
    ppermute x5, waiting for transfers between devices: 0.91 us -> 16.6 us  [grow(): rows = jnp.concatenate([rows, lax.ppermute(rows, axis, perm)])]
    pallas_call x2, Pallas kernels: 24.8 us -> 10.1 us  [assemble(): pl.pallas_call(functools.partial(assemble_kernel, plan), out_shape=jax.Sh...]
    pallas_call x2, Pallas kernels: 21.7 us -> 9.6 us  [call_attention_grads(): pl.pallas_call(attention_grads, grid_spec=pltpu.PrefetchScalarGridSpec(nu...]
    ppermute x2 -> x1, waiting for transfers between devices: 15.6 us -> 5.24 us  [chunks(): other = lax.ppermute(own, 'narrow', ACROSS)]
    ppermute x16, starting transfers between devices: 16.6 us -> 23.2 us  [step(): self.down = lax.ppermute(down, 'wide', self.behind)]
    ppermute x5, waiting for transfers between devices: 6.1 us -> 12.7 us  [total_over_mesh(): value = value + lax.ppermute(value, axis, perm)]
  transfers between devices with their start and end apart: 85 -> 85, of which waited for: 29 -> 41; matrix products, arithmetic and copies ran while one was open for 12% -> 9% of each run, Pallas kernels for 22% -> 19%
where the time goes in v3:
time: 503 us; the launch traced here: 495 us
  waiting for transfers between devices  169 us (34%)
  Pallas kernels  127 us (25%)
  local copies, waits for them, and re-layouts  77.7 us (15%)
  starting transfers between devices  73.7 us (15%)
  other arithmetic  40.9 us (8%)
  between operations  7.58 us (2%)
    unnamed x247, local copies, waits for them, and re-layouts  58 us
    ppermute x16, waiting for transfers between devices, step(): self.up = lax.ppermute(up, 'wide', self.ahead)  53.3 us
    ppermute x15, waiting for transfers between devices, exchange(): return lax.ppermute(part, 'narrow', ACROSS)  33.8 us
    ppermute x5, waiting for transfers between devices, shards(): small_rows = small_rows[:bit] + lax.ppermute(small_rows[bit:], axis, perm)  27.5 us
    ppermute x16, starting transfers between devices, step(): self.down = lax.ppermute(down, 'wide', self.behind)  23.2 us
    pallas_call x2, Pallas kernels, call_mlp_grads(): pl.pallas_call(mlp_grads, grid_spec=pltpu.PrefetchScalarGridSpec(num_scal...  22.8 us
    pallas_call x4, Pallas kernels, call_mlp_backward(): pl.pallas_call(functools.partial(mlp_backward, first), grid=(STEPS,), out...  22.3 us
    pallas_call x4, Pallas kernels, call_attention_backward(): pl.pallas_call(attention_backward, grid=(1,), out_shape=outs + [jax.Shape...  21.7 us
  transfers between devices with their start and end apart: 85, of which 41 were waited for; matrix products, arithmetic and copies ran while one was open for 9% of the time, Pallas kernels for 19%

profile of v3, /device:TPU:0, one launch (start us, length us, event | category | flops | bytes accessed | tf_op | source)
XLA Modules:
  0.0 495.3 jit_solution(17432771357879622832)
XLA Ops:
  3.5 2.6 collective-permute-start
  21.8 2.4 collective-permute-done.refs_2_
  31.3 5.2 %collective-permute-done.4 = bf16[200,1024]{1,0:T(8,128)(2,1)S(1)} collective-permute-done((bf16[200,1024]{1,0:T(8,128)(2,1)S(1)}, bf16[200,1024]{1,0:T(8,128)(2,1)S(1)}, u32[]{:S(2)}, u32[]{:S(2)}) %collective-permute-start.4) | collective-permute-done | bytes 409632 | tf_op jit(solution)/shard_map/ppermute | solution.py:873
  39.4 7.3 %collective-permute-done.11.refs_6_ = bf16[3072,128]{1,0:T(8,128)(2,1)} collective-permute-done((bf16[3072,128]{1,0:T(8,128)(2,1)}, bf16[3072,128]{1,0:T(8,128)(2,1)}, u32[]{:S(2)}, u32[]{:S(2)}) %collective-permute-start.11) | collective-permute-done | bytes 786464 | tf_op jit(solution)/shard_map/ppermute | solution.py:664
  55.0 13.7 %collective-permute-done.6 = bf16[8,768]{1,0:T(8,128)(2,1)S(1)} collective-permute-done((bf16[8,768]{1,0:T(8,128)(2,1)S(1)}, bf16[8,768]{1,0:T(8,128)(2,1)S(1)}, u32[]{:S(2)}, u32[]{:S(2)}) %collective-permute-start.6) | collective-permute-done | bytes 12320 | tf_op jit(solution)/shard_map/ppermute | solution.py:944
  68.8 2.8 collective-permute-start.7
  79.1 7.5 %collective-permute-done.21 = bf16[200,1024]{1,0:T(8,128)(2,1)S(1)} collective-permute-done((bf16[200,1024]{1,0:T(8,128)(2,1)}, bf16[200,1024]{1,0:T(8,128)(2,1)S(1)}, u32[]{:S(2)}, u32[]{:S(2)}) %collective-permute-start.21) | collective-permute-done | bytes 409632 | tf_op jit(solution)/shard_map/ppermute | solution.py:918
  96.8 5.6 %assemble.2.refs_3_ = bf16[6144,1024]{1,0:T(8,128)(2,1)S(1)} custom-call(s32[2,192]{1,0:T(2,128)S(1)} %pad_add_fusion.rows, s32[2,192]{1,0:T(2,128)S(1)} %pad_add_fusion.1.cols, bf16[3072,128]{1,0:T(8,128)(2,1)S(1)} %bitcast.85, bf16[3072,128]{1,0:T(8,128)(2,1)S(1)} %copy-done.25, bf16[3072,128]{1,0:T(8,128)(2,1)} %collective-permute-done.refs_2_, ...), custom_call_target="tpu_custom_call" | custom-call | bytes 128 | tf_op jit(solution)/shard_map/assemble/pallas_call | solution.py:619
  102.4 2.4 attention_forward.4
  104.8 4.6 copy-done
  116.3 4.6 copy-done.1
  120.9 2.4 attention_forward.5
  129.5 4.1 mlp_forward.4
  133.7 4.6 copy-done.2
  147.0 14.0 %collective-permute-done.35.refs_10_ = bf16[3072,128]{1,0:T(8,128)(2,1)S(1)} collective-permute-done((bf16[3072,128]{1,0:T(8,128)(2,1)}, bf16[3072,128]{1,0:T(8,128)(2,1)S(1)}, u32[]{:S(2)}, u32[]{:S(2)}) %collective-permute-start.35) | collective-permute-done | bytes 786464 | tf_op jit(solution)/shard_map/ppermute | solution.py:664
  163.6 4.6 copy-done.3
  170.1 4.2 mlp_forward.5
  174.3 4.6 copy-done.4
  180.5 2.1 collective-permute-start.42
  184.4 7.0 %collective-permute-done.40.refs_14_ = bf16[1536,128]{1,0:T(8,128)(2,1)S(1)} collective-permute-done((bf16[1536,128]{1,0:T(8,128)(2,1)S(1)}, bf16[1536,128]{1,0:T(8,128)(2,1)S(1)}, u32[]{:S(2)}, u32[]{:S(2)}) %collective-permute-start.40) | collective-permute-done | bytes 393248 | tf_op jit(solution)/shard_map/ppermute | solution.py:664
  195.1 4.5 assemble.3.refs_6_
  199.6 2.5 attention_forward.6
  203.5 2.5 attention_forward.7
  207.6 6.9 %collective-permute-done.45.got_ref = bf16[200,1024]{1,0:T(8,128)(2,1)S(1)} collective-permute-done((bf16[200,1024]{1,0:T(8,128)(2,1)S(1)}, bf16[200,1024]{1,0:T(8,128)(2,1)S(1)}, u32[]{:S(2)}, u32[]{:S(2)}) %collective-permute-start.45) | collective-permute-done | bytes 409632 | tf_op jit(solution)/shard_map/ppermute | solution.py:918
  214.6 4.2 mlp_forward.6
  218.8 3.7 collective-permute-done.46.got_ref
  222.5 4.2 mlp_forward.7
  226.7 5.1 %mlp_backward.4 = (bf16[200,1024]{1,0:T(8,128)(2,1)S(1)}, bf16[200,2048]{1,0:T(8,128)(2,1)S(1)}, bf16[200,1024]{1,0:T(8,128)(2,1)S(1)}, f32[8,1024]{1,0:T(8,128)S(1)}, bf16[6144,1024]{1,0:T(8,128)(2,1)S(1)}) custom-call(bf16[200,1024]{1,0:T(8,128)(2,1)S(1)} %get-tuple-element.419.refs_0_.grad_ref, ...), custom_call_target="tpu_custom_call", output_to_operand_aliasing={{4}: (4, {})} | custom-call | flops 3355443200 | bytes 12582912 | tf_op jit(solution)/shard_map/mlp_backward/pallas_call | solution.py:306
  232.5 5.3 %mlp_backward.5 = (bf16[200,1024]{1,0:T(8,128)(2,1)S(1)}, bf16[200,2048]{1,0:T(8,128)(2,1)S(1)}, bf16[200,1024]{1,0:T(8,128)(2,1)S(1)}, f32[8,1024]{1,0:T(8,128)S(1)}, bf16[6144,1024]{1,0:T(8,128)(2,1)S(1)}) custom-call(bf16[200,1024]{1,0:T(8,128)(2,1)S(1)} %get-tuple-element.418.refs_0_.grad_ref, ...), custom_call_target="tpu_custom_call", output_to_operand_aliasing={{4}: (4, {})} | custom-call | flops 3355443200 | bytes 12582912 | tf_op jit(solution)/shard_map/mlp_backward/pallas_call | solution.py:306
  239.8 4.4 collective-permute-done.47.got_ref
  244.3 5.1 %attention_backward.4 = (f32[200,1024]{1,0:T(8,128)S(1)}, bf16[200,1024]{1,0:T(8,128)(2,1)S(1)}, bf16[200,1536]{1,0:T(8,128)(2,1)S(1)}, bf16[200,1024]{1,0:T(8,1...) custom-call(bf16[200,1024]{1,0:T(8,128)(2,1)S(1)} %get-tuple-element.419.refs, ...), custom_call_target="tpu_custom_call", output_to_operand_aliasing={{5}: (9, {})} | custom-call | flops 2516582400 | bytes 8388608 | tf_op jit(solution)/shard_map/attention_backward/pallas_call | solution.py:397
  250.1 11.4 %mlp_grads.2 = (bf16[24576,128]{1,0:T(8,128)(2,1)S(1)}, bf16[24576,128]{1,0:T(8,128)(2,1)S(1)}) custom-call(s32[192]{0:T(256)S(1)} %copy-done.75, s32[192]{0:T(256)S(1)} %copy-done.74, bf16[200,2048]{1,0:T(8,128)(2,1)S(1)} %get-tuple-element.257.refs_0_, bf16[200,2048]{1,0:T(8,128)(2,1)S(1)} %get-tuple-element.258.refs_1_, ...), custom_call_target="tpu_custom_call" | custom-call | flops 6710886400 | bytes 16777216 | tf_op jit(solution)/shard_map/mlp_grads/pallas_call | solution.py:471
  261.5 5.1 %attention_backward.5 = (f32[200,1024]{1,0:T(8,128)S(1)}, bf16[200,1024]{1,0:T(8,128)(2,1)S(1)}, bf16[200,1536]{1,0:T(8,128)(2,1)S(1)}, bf16[200,1024]{1,0:T(8,1...) custom-call(bf16[200,1024]{1,0:T(8,128)(2,1)S(1)} %get-tuple-element.418.refs, ...), custom_call_target="tpu_custom_call", output_to_operand_aliasing={{5}: (9, {})} | custom-call | flops 2516582400 | bytes 8388608 | tf_op jit(solution)/shard_map/attention_backward/pallas_call | solution.py:397
  266.7 4.8 attention_grads.2
  271.6 2.3 collective-permute-done.51
  275.8 10.3 %collective-permute-done.49.refs_2_ = bf16[200,1024]{1,0:T(8,128)(2,1)S(1)} collective-permute-done((bf16[200,1024]{1,0:T(8,128)(2,1)S(1)}, bf16[200,1024]{1,0:T(8,128)(2,1)S(1)}, u32[]{:S(2)}, u32[]{:S(2)}) %collective-permute-start.49) | collective-permute-done | bytes 409632 | tf_op jit(solution)/shard_map/ppermute | solution.py:918
  288.2 5.6 %mlp_backward.6 = (f32[200,1024]{1,0:T(8,128)S(1)}, bf16[200,1024]{1,0:T(8,128)(2,1)S(1)}, bf16[200,2048]{1,0:T(8,128)(2,1)S(1)}, bf16[200,1024]{1,0:T(8,128)(2,...) custom-call(f32[200,1024]{1,0:T(8,128)S(1)} %get-tuple-element.273.refs_0_, ...), custom_call_target="tpu_custom_call", output_to_operand_aliasing={{5}: (8, {})} | custom-call | flops 3355443200 | bytes 12582912 | tf_op jit(solution)/shard_map/mlp_backward/pallas_call | solution.py:306
  300.3 6.4 %mlp_backward.7 = (f32[200,1024]{1,0:T(8,128)S(1)}, bf16[200,1024]{1,0:T(8,128)(2,1)S(1)}, bf16[200,2048]{1,0:T(8,128)(2,1)S(1)}, bf16[200,1024]{1,0:T(8,128)(2,...) custom-call(f32[200,1024]{1,0:T(8,128)S(1)} %get-tuple-element.286.refs_0_, ...), custom_call_target="tpu_custom_call", output_to_operand_aliasing={{5}: (8, {})} | custom-call | flops 3355443200 | bytes 12582912 | tf_op jit(solution)/shard_map/mlp_backward/pallas_call | solution.py:306
  306.7 11.4 %mlp_grads.3 = (bf16[24576,128]{1,0:T(8,128)(2,1)S(1)}, bf16[24576,128]{1,0:T(8,128)(2,1)S(1)}) custom-call(s32[192]{0:T(256)S(1)} %copy-done.73, s32[192]{0:T(256)S(1)} %copy-done.72, bf16[200,2048]{1,0:T(8,128)(2,1)S(1)} %copy-done.77, bf16[200,2048]{1,0:T(8,128)(2,1)S(1)} %get-tuple-element.282.refs_1_, bf16[200,1024]{1,0:T(8,128)(2,1)S(1)} %get-tuple-element.284.refs_2_, ...), custom_call_target="tpu_custom_call" | custom-call | flops 6710886400 | bytes 16777216 | tf_op jit(solution)/shard_map/mlp_grads/pallas_call | solution.py:471
  318.2 3.5 add_convert_fusion.7
  326.4 5.2 %attention_backward.6 = (f32[200,1024]{1,0:T(8,128)S(1)}, bf16[200,1024]{1,0:T(8,128)(2,1)S(1)}, bf16[200,1536]{1,0:T(8,128)(2,1)S(1)}, bf16[200,1024]{1,0:T(8,1...) custom-call(f32[200,1024]{1,0:T(8,128)S(1)} %copy-done.23, ...), custom_call_target="tpu_custom_call", output_to_operand_aliasing={{5}: (9, {})} | custom-call | flops 2516582400 | bytes 8388608 | tf_op jit(solution)/shard_map/attention_backward/pallas_call | solution.py:397
  333.2 6.2 %attention_backward.7 = (f32[200,1024]{1,0:T(8,128)S(1)}, bf16[200,1024]{1,0:T(8,128)(2,1)S(1)}, bf16[200,1536]{1,0:T(8,128)(2,1)S(1)}, bf16[200,1024]{1,0:T(8,1...) custom-call(f32[200,1024]{1,0:T(8,128)S(1)} %get-tuple-element.302.grad_ref, ...), custom_call_target="tpu_custom_call", output_to_operand_aliasing={{5}: (9, {})} | custom-call | flops 2516582400 | bytes 8388608 | tf_op jit(solution)/shard_map/attention_backward/pallas_call | solution.py:397
  342.0 3.6 add_convert_fusion.5
  345.6 4.8 attention_grads.3
  350.4 2.7 copy-done.5
  353.1 2.6 copy-done.7
  355.9 2.4 collective-permute-done.61
  367.3 15.5 %collective-permute-done.70 = bf16[3072,128]{1,0:T(8,128)(2,1)} collective-permute-done((bf16[3072,128]{1,0:T(8,128)(2,1)}, bf16[3072,128]{1,0:T(8,128)(2,1)}, u32[]{:S(2)}, u32[]{:S(2)}) %collective-permute-start.70) | collective-permute-done | bytes 786464 | tf_op jit(solution)/shard_map/ppermute | solution.py:698
  382.8 2.2 convert_add_fusion.2
  386.5 4.0 collective-permute-done.65
  402.8 10.0 %collective-permute-done.72 = f32[8,768]{1,0:T(8,128)S(1)} collective-permute-done((f32[8,768]{1,0:T(8,128)S(1)}, f32[8,768]{1,0:T(8,128)S(1)}, u32[]{:S(2)}, u32[]{:S(2)}) %collective-permute-start.72) | collective-permute-done | bytes 24608 | tf_op jit(solution)/shard_map/ppermute | solution.py:1138
  412.9 3.6 add_convert_fusion.2
  416.5 2.2 collective-permute-start.75
  424.0 12.1 %collective-permute-done.73 = f32[4,768]{1,0:T(4,128)S(1)} collective-permute-done((f32[4,768]{1,0:T(4,128)S(1)}, f32[4,768]{1,0:T(4,128)S(1)}, u32[]{:S(2)}, u32[]{:S(2)}) %collective-permute-start.73) | collective-permute-done | bytes 12320 | tf_op jit(solution)/shard_map/ppermute | solution.py:1138
  436.1 2.9 add_convert_fusion
  439.0 2.3 collective-permute-start.79
  442.8 2.2 collective-permute-done.76
  448.2 7.0 %collective-permute-done.79 = bf16[3072,128]{1,0:T(8,128)(2,1)S(1)} collective-permute-done((bf16[3072,128]{1,0:T(8,128)(2,1)S(1)}, bf16[3072,128]{1,0:T(8,128)(2,1)S(1)}, u32[]{:S(2)}, u32[]{:S(2)}) %collective-permute-start.79) | collective-permute-done | bytes 786464 | tf_op jit(solution)/shard_map/ppermute | solution.py:699
  455.2 2.2 collective-permute-done.78
  457.4 3.6 multiply_reduce_fusion
  464.4 2.2 collective-permute-done.81
  470.4 3.3 collective-permute-done.83
  474.4 3.9 collective-permute-done.84
  480.2 13.8 %update.1 = (f32[2,24,128,128]{3,2,1,0:T(8,128)}, f32[2,24,128,128]{3,2,1,0:T(8,128)}, f32[2,24,128,128]{3,2,1,0:T(8,128)}, bf16[2,24,128,128]{3,2,1,0:T(8,128)(2,1)}) custom-call(f32[1]{0:T(128)} %bitcast.65.clip_ref, f32[3072,128]{1,0:T(8,128)} %get-tuple-element.382.grad0, f32[3072,128]{1,0:T(8,128)} %copy-done.80, f32[2,24,128,128]{3,2,1,0:T(8,128)} %left.1, ...), custom_call_target="tpu_custom_call" | custom-call | flops 805306368 | bytes 29884416 | tf_op jit(solution)/shard_map/update/pallas_call | solution.py:835
  (590 shorter events, 152.0 us)
Async XLA Ops:
  2.9 35.5 %collective-permute-start.8 = (bf16[3072,128]{1,0:T(8,128)(2,1)S(1)}, bf16[3072,128]{1,0:T(8,128)(2,1)S(1)}, u32[]{:S(2)}, u32[]{:S(2)}) collective-permute-start(bf16[3072,128]{1,0:T(8,128)(2,1)S(1)} %bitcast.82), channel_id=1, source_target_pairs={{0,1},{1,0},{2,3},{3,2},{4,5},{5,4},{6,7},{7,6},{8,9},{9,8},{10,11... | collective-permute-start | bytes 2359304 | tf_op jit(solution)/shard_map/ppermute | solution.py:915
  3.5 20.8 %collective-permute-start = (bf16[3072,128]{1,0:T(8,128)(2,1)S(1)}, bf16[3072,128]{1,0:T(8,128)(2,1)}, u32[]{:S(2)}, u32[]{:S(2)}) collective-permute-start(bf16[3072,128]{1,0:T(8,128)(2,1)S(1)} %bitcast.83), channel_id=1, source_target_pairs={{0,8},{8,16},{16,24},{24,28},{28,20},{20,12},{12,4},{4,0},{1,9},{9... | collective-permute-start | bytes 2359304 | tf_op jit(solution)/shard_map/ppermute | solution.py:664
  6.1 19.7 %collective-permute-start.1 = (bf16[3072,128]{1,0:T(8,128)(2,1)S(1)}, bf16[3072,128]{1,0:T(8,128)(2,1)}, u32[]{:S(2)}, u32[]{:S(2)}) collective-permute-start(bf16[3072,128]{1,0:T(8,128)(2,1)S(1)} %bitcast.84), channel_id=1, source_target_pairs={{8,0},{16,8},{24,16},{28,24},{20,28},{12,20},{4,12},{0,4},{9,1},{1... | collective-permute-start | bytes 2359304 | tf_op jit(solution)/shard_map/ppermute | solution.py:665
  6.1 12.0 %collective-permute-start.2 = (bf16[1,768]{1,0:T(2,128)(2,1)S(1)}, bf16[1,768]{1,0:T(2,128)(2,1)S(1)}, u32[]{:S(2)}, u32[]{:S(2)}) collective-permute-start(bf16[1,768]{1,0:T(2,128)(2,1)S(1)} %bitcast.94), channel_id=1, source_target_pairs={{0,1},{1,0},{2,3},{3,2},{4,5},{5,4},{6,7},{7,6},{8,9},{9,8},{10,11... | collective-permute-start | bytes 4616 | tf_op jit(solution)/shard_map/ppermute | solution.py:944
  28.0 18.6 %collective-permute-start.11 = (bf16[3072,128]{1,0:T(8,128)(2,1)}, bf16[3072,128]{1,0:T(8,128)(2,1)}, u32[]{:S(2)}, u32[]{:S(2)}) collective-permute-start(bf16[3072,128]{1,0:T(8,128)(2,1)} %collective-permute-done.refs_2_), channel_id=1, source_target_pairs={{0,8},{8,16},{16,24},{24,28},{28,20},{20,12},{12,4},{4,0},{1,9},{9... | collective-permute-start | bytes 2359304 | tf_op jit(solution)/shard_map/ppermute | solution.py:664
  29.5 18.2 %collective-permute-start.13 = (bf16[3072,128]{1,0:T(8,128)(2,1)}, bf16[3072,128]{1,0:T(8,128)(2,1)S(1)}, u32[]{:S(2)}, u32[]{:S(2)}) collective-permute-start(bf16[3072,128]{1,0:T(8,128)(2,1)} %collective-permute-done.1.refs_4_), channel_id=1, source_target_pairs={{8,0},{16,8},{24,16},{28,24},{20,28},{12,20},{4,12},{0,4},{9,1},{1... | collective-permute-start | bytes 2359304 | tf_op jit(solution)/shard_map/ppermute | solution.py:665
  31.3 16.5 %collective-permute-start.9 = (bf16[3072,128]{1,0:T(8,128)(2,1)}, bf16[3072,128]{1,0:T(8,128)(2,1)S(1)}, u32[]{:S(2)}, u32[]{:S(2)}) collective-permute-start(bf16[3072,128]{1,0:T(8,128)(2,1)} %collective-permute-done.refs_2_), channel_id=1, source_target_pairs={{0,1},{1,0},{2,3},{3,2},{4,5},{5,4},{6,7},{7,6},{8,9},{9,8},{10,11... | collective-permute-start | bytes 2359304 | tf_op jit(solution)/shard_map/ppermute | solution.py:915
  36.5 12.2 %collective-permute-start.10 = (bf16[3072,128]{1,0:T(8,128)(2,1)}, bf16[3072,128]{1,0:T(8,128)(2,1)S(1)}, u32[]{:S(2)}, u32[]{:S(2)}) collective-permute-start(bf16[3072,128]{1,0:T(8,128)(2,1)} %collective-permute-done.1.refs_4_), channel_id=1, source_target_pairs={{0,1},{1,0},{2,3},{3,2},{4,5},{5,4},{6,7},{7,6},{8,9},{9,8},{10,11... | collective-permute-start | bytes 2359304 | tf_op jit(solution)/shard_map/ppermute | solution.py:915
  49.6 22.0 %collective-permute-start.15 = (bf16[3072,128]{1,0:T(8,128)(2,1)}, bf16[3072,128]{1,0:T(8,128)(2,1)S(1)}, u32[]{:S(2)}, u32[]{:S(2)}) collective-permute-start(bf16[3072,128]{1,0:T(8,128)(2,1)} %collective-permute-done.11.refs_6_), channel_id=1, source_target_pairs={{0,8},{8,16},{16,24},{24,28},{28,20},{20,12},{12,4},{4,0},{1,9},{9... | collective-permute-start | bytes 2359304 | tf_op jit(solution)/shard_map/ppermute | solution.py:664
  51.2 23.8 %collective-permute-start.17 = (bf16[3072,128]{1,0:T(8,128)(2,1)}, bf16[3072,128]{1,0:T(8,128)(2,1)}, u32[]{:S(2)}, u32[]{:S(2)}) collective-permute-start(bf16[3072,128]{1,0:T(8,128)(2,1)} %copy-done.26), channel_id=1, source_target_pairs={{8,0},{16,8},{24,16},{28,24},{20,28},{12,20},{4,12},{0,4},{9,1},{1... | collective-permute-start | bytes 2359304 | tf_op jit(solution)/shard_map/ppermute | solution.py:665
  51.7 24.4 %collective-permute-start.12 = (bf16[3072,128]{1,0:T(8,128)(2,1)}, bf16[3072,128]{1,0:T(8,128)(2,1)}, u32[]{:S(2)}, u32[]{:S(2)}) collective-permute-start(bf16[3072,128]{1,0:T(8,128)(2,1)} %collective-permute-done.11.refs_6_), channel_id=1, source_target_pairs={{0,1},{1,0},{2,3},{3,2},{4,5},{5,4},{6,7},{7,6},{8,9},{9,8},{10,11... | collective-permute-start | bytes 2359304 | tf_op jit(solution)/shard_map/ppermute | solution.py:915
  51.7 24.4 %collective-permute-start.14 = (bf16[3072,128]{1,0:T(8,128)(2,1)}, bf16[3072,128]{1,0:T(8,128)(2,1)}, u32[]{:S(2)}, u32[]{:S(2)}) collective-permute-start(bf16[3072,128]{1,0:T(8,128)(2,1)} %copy-done.26), channel_id=1, source_target_pairs={{0,1},{1,0},{2,3},{3,2},{4,5},{5,4},{6,7},{7,6},{8,9},{9,8},{10,11... | collective-permute-start | bytes 2359304 | tf_op jit(solution)/shard_map/ppermute | solution.py:915
  53.4 15.3 %collective-permute-start.6 = (bf16[8,768]{1,0:T(8,128)(2,1)S(1)}, bf16[8,768]{1,0:T(8,128)(2,1)S(1)}, u32[]{:S(2)}, u32[]{:S(2)}) collective-permute-start(bf16[8,768]{1,0:T(8,128)(2,1)S(1)} %pad_maximum_fusion.5), channel_id=1, source_target_pairs={{0,8},{4,12},{8,0},{12,4},{16,24},{20,28},{24,16},{28,20},{1,9},{5... | collective-permute-start | bytes 36872 | tf_op jit(solution)/shard_map/ppermute | solution.py:944
  71.6 18.0 %collective-permute-start.16 = (bf16[3072,128]{1,0:T(8,128)(2,1)S(1)}, bf16[3072,128]{1,0:T(8,128)(2,1)}, u32[]{:S(2)}, u32[]{:S(2)}) collective-permute-start(bf16[3072,128]{1,0:T(8,128)(2,1)S(1)} %collective-permute-done.15.refs_10_), channel_id=1, source_target_pairs={{0,1},{1,0},{2,3},{3,2},{4,5},{5,4},{6,7},{7,6},{8,9},{9,8},{10,11... | collective-permute-start | bytes 2359304 | tf_op jit(solution)/shard_map/ppermute | solution.py:915
  74.4 12.1 %collective-permute-start.21 = (bf16[200,1024]{1,0:T(8,128)(2,1)}, bf16[200,1024]{1,0:T(8,128)(2,1)S(1)}, u32[]{:S(2)}, u32[]{:S(2)}) collective-permute-start(bf16[200,1024]{1,0:T(8,128)(2,1)} %reshape.578), channel_id=1, source_target_pairs={{0,2},{1,3},{2,0},{3,1},{4,6},{5,7},{6,4},{7,5},{8,10},{9,11},{10,... | collective-permute-start | bytes 1228808 | tf_op jit(solution)/shard_map/ppermute | solution.py:918
  76.1 11.4 %collective-permute-start.19 = (bf16[1536,128]{1,0:T(8,128)(2,1)S(1)}, bf16[1536,128]{1,0:T(8,128)(2,1)}, u32[]{:S(2)}, u32[]{:S(2)}) collective-permute-start(bf16[1536,128]{1,0:T(8,128)(2,1)S(1)} %slice.602), channel_id=1, source_target_pairs={{0,8},{8,16},{16,24},{24,28},{28,20},{20,12},{12,4},{4,0},{1,9},{9... | collective-permute-start | bytes 1179656 | tf_op jit(solution)/shard_map/ppermute | solution.py:664
  76.2 11.4 %collective-permute-start.20 = (bf16[1536,128]{1,0:T(8,128)(2,1)S(1)}, bf16[1536,128]{1,0:T(8,128)(2,1)}, u32[]{:S(2)}, u32[]{:S(2)}) collective-permute-start(bf16[1536,128]{1,0:T(8,128)(2,1)S(1)} %slice.603), channel_id=1, source_target_pairs={{8,0},{16,8},{24,16},{28,24},{20,28},{12,20},{4,12},{0,4},{9,1},{1... | collective-permute-start | bytes 1179656 | tf_op jit(solution)/shard_map/ppermute | solution.py:665
  78.3 12.1 %collective-permute-start.18 = (bf16[3072,128]{1,0:T(8,128)(2,1)}, bf16[3072,128]{1,0:T(8,128)(2,1)}, u32[]{:S(2)}, u32[]{:S(2)}) collective-permute-start(bf16[3072,128]{1,0:T(8,128)(2,1)} %collective-permute-done.17.refs_12_), channel_id=1, source_target_pairs={{0,1},{1,0},{2,3},{3,2},{4,5},{5,4},{6,7},{7,6},{8,9},{9,8},{10,11... | collective-permute-start | bytes 2359304 | tf_op jit(solution)/shard_map/ppermute | solution.py:915
  87.6 25.5 %collective-permute-start.24 = (bf16[3072,128]{1,0:T(8,128)(2,1)S(1)}, bf16[3072,128]{1,0:T(8,128)(2,1)}, u32[]{:S(2)}, u32[]{:S(2)}) collective-permute-start(bf16[3072,128]{1,0:T(8,128)(2,1)S(1)} %bitcast.78), channel_id=1, source_target_pairs={{0,8},{8,16},{16,24},{24,28},{28,20},{20,12},{12,4},{4,0},{1,9},{9... | collective-permute-start | bytes 2359304 | tf_op jit(solution)/shard_map/ppermute | solution.py:664
  88.0 25.1 %collective-permute-start.25 = (bf16[3072,128]{1,0:T(8,128)(2,1)S(1)}, bf16[3072,128]{1,0:T(8,128)(2,1)}, u32[]{:S(2)}, u32[]{:S(2)}) collective-permute-start(bf16[3072,128]{1,0:T(8,128)(2,1)S(1)} %bitcast.79), channel_id=1, source_target_pairs={{8,0},{16,8},{24,16},{28,24},{20,28},{12,20},{4,12},{0,4},{9,1},{1... | collective-permute-start | bytes 2359304 | tf_op jit(solution)/shard_map/ppermute | solution.py:665
  111.6 15.2 %collective-permute-start.26 = (bf16[200,1024]{1,0:T(8,128)(2,1)S(1)}, bf16[200,1024]{1,0:T(8,128)(2,1)S(1)}, u32[]{:S(2)}, u32[]{:S(2)}) collective-permute-start(bf16[200,1024]{1,0:T(8,128)(2,1)S(1)} %get-tuple-element.206.own_ref), channel_id=1, source_target_pairs={{0,2},{1,3},{2,0},{3,1},{4,6},{5,7},{6,4},{7,5},{8,10},{9,11},{10,... | collective-permute-start | bytes 1228808 | tf_op jit(solution)/shard_map/ppermute | solution.py:918
  113.1 28.5 %collective-permute-start.31 = (bf16[3072,128]{1,0:T(8,128)(2,1)}, bf16[3072,128]{1,0:T(8,128)(2,1)}, u32[]{:S(2)}, u32[]{:S(2)}) collective-permute-start(bf16[3072,128]{1,0:T(8,128)(2,1)} %collective-permute-done.24.refs_2_), channel_id=1, source_target_pairs={{0,8},{8,16},{16,24},{24,28},{28,20},{20,12},{12,4},{4,0},{1,9},{9... | collective-permute-start | bytes 2359304 | tf_op jit(solution)/shard_map/ppermute | solution.py:664
  113.5 28.1 %collective-permute-start.33 = (bf16[3072,128]{1,0:T(8,128)(2,1)}, bf16[3072,128]{1,0:T(8,128)(2,1)}, u32[]{:S(2)}, u32[]{:S(2)}) collective-permute-start(bf16[3072,128]{1,0:T(8,128)(2,1)} %collective-permute-done.25.refs_4_), channel_id=1, source_target_pairs={{8,0},{16,8},{24,16},{28,24},{20,28},{12,20},{4,12},{0,4},{9,1},{1... | collective-permute-start | bytes 2359304 | tf_op jit(solution)/shard_map/ppermute | solution.py:665
  115.5 28.8 %collective-permute-start.28 = (bf16[3072,128]{1,0:T(8,128)(2,1)S(1)}, bf16[3072,128]{1,0:T(8,128)(2,1)}, u32[]{:S(2)}, u32[]{:S(2)}) collective-permute-start(bf16[3072,128]{1,0:T(8,128)(2,1)S(1)} %bitcast.80), channel_id=1, source_target_pairs={{0,1},{1,0},{2,3},{3,2},{4,5},{5,4},{6,7},{7,6},{8,9},{9,8},{10,11... | collective-permute-start | bytes 2359304 | tf_op jit(solution)/shard_map/ppermute | solution.py:915
  126.2 18.6 %collective-permute-start.39 = (bf16[200,1024]{1,0:T(8,128)(2,1)S(1)}, bf16[200,1024]{1,0:T(8,128)(2,1)S(1)}, u32[]{:S(2)}, u32[]{:S(2)}) collective-permute-start(bf16[200,1024]{1,0:T(8,128)(2,1)S(1)} %get-tuple-element.214.own_ref), channel_id=1, source_target_pairs={{0,2},{1,3},{2,0},{3,1},{4,6},{5,7},{6,4},{7,5},{8,10},{9,11},{10,... | collective-permute-start | bytes 1228808 | tf_op jit(solution)/shard_map/ppermute | solution.py:918
  141.6 19.4 %collective-permute-start.35 = (bf16[3072,128]{1,0:T(8,128)(2,1)}, bf16[3072,128]{1,0:T(8,128)(2,1)S(1)}, u32[]{:S(2)}, u32[]{:S(2)}) collective-permute-start(bf16[3072,128]{1,0:T(8,128)(2,1)} %collective-permute-done.31.refs_6_), channel_id=1, source_target_pairs={{0,8},{8,16},{16,24},{24,28},{28,20},{20,12},{12,4},{4,0},{1,9},{9... | collective-permute-start | bytes 2359304 | tf_op jit(solution)/shard_map/ppermute | solution.py:664
  142.0 19.2 %collective-permute-start.37 = (bf16[3072,128]{1,0:T(8,128)(2,1)}, bf16[3072,128]{1,0:T(8,128)(2,1)}, u32[]{:S(2)}, u32[]{:S(2)}) collective-permute-start(bf16[3072,128]{1,0:T(8,128)(2,1)} %collective-permute-done.33.refs_8_), channel_id=1, source_target_pairs={{8,0},{16,8},{24,16},{28,24},{20,28},{12,20},{4,12},{0,4},{9,1},{1... | collective-permute-start | bytes 2359304 | tf_op jit(solution)/shard_map/ppermute | solution.py:665
  144.3 35.7 %collective-permute-start.29 = (bf16[3072,128]{1,0:T(8,128)(2,1)}, bf16[3072,128]{1,0:T(8,128)(2,1)}, u32[]{:S(2)}, u32[]{:S(2)}) collective-permute-start(bf16[3072,128]{1,0:T(8,128)(2,1)} %collective-permute-done.24.refs_2_), channel_id=1, source_target_pairs={{0,1},{1,0},{2,3},{3,2},{4,5},{5,4},{6,7},{7,6},{8,9},{9,8},{10,11... | collective-permute-start | bytes 2359304 | tf_op jit(solution)/shard_map/ppermute | solution.py:915
  144.3 36.2 %collective-permute-start.30 = (bf16[3072,128]{1,0:T(8,128)(2,1)}, bf16[3072,128]{1,0:T(8,128)(2,1)}, u32[]{:S(2)}, u32[]{:S(2)}) collective-permute-start(bf16[3072,128]{1,0:T(8,128)(2,1)} %collective-permute-done.25.refs_4_), channel_id=1, source_target_pairs={{0,1},{1,0},{2,3},{3,2},{4,5},{5,4},{6,7},{7,6},{8,9},{9,8},{10,11... | collective-permute-start | bytes 2359304 | tf_op jit(solution)/shard_map/ppermute | solution.py:915
  145.6 37.1 %collective-permute-start.32 = (bf16[3072,128]{1,0:T(8,128)(2,1)}, bf16[3072,128]{1,0:T(8,128)(2,1)}, u32[]{:S(2)}, u32[]{:S(2)}) collective-permute-start(bf16[3072,128]{1,0:T(8,128)(2,1)} %collective-permute-done.31.refs_6_), channel_id=1, source_target_pairs={{0,1},{1,0},{2,3},{3,2},{4,5},{5,4},{6,7},{7,6},{8,9},{9,8},{10,11... | collective-permute-start | bytes 2359304 | tf_op jit(solution)/shard_map/ppermute | solution.py:915
  161.0 21.8 %collective-permute-start.34 = (bf16[3072,128]{1,0:T(8,128)(2,1)}, bf16[3072,128]{1,0:T(8,128)(2,1)}, u32[]{:S(2)}, u32[]{:S(2)}) collective-permute-start(bf16[3072,128]{1,0:T(8,128)(2,1)} %collective-permute-done.33.refs_8_), channel_id=1, source_target_pairs={{0,1},{1,0},{2,3},{3,2},{4,5},{5,4},{6,7},{7,6},{8,9},{9,8},{10,11... | collective-permute-start | bytes 2359304 | tf_op jit(solution)/shard_map/ppermute | solution.py:915
  161.2 31.7 %collective-permute-start.36 = (bf16[3072,128]{1,0:T(8,128)(2,1)S(1)}, bf16[3072,128]{1,0:T(8,128)(2,1)}, u32[]{:S(2)}, u32[]{:S(2)}) collective-permute-start(bf16[3072,128]{1,0:T(8,128)(2,1)S(1)} %collective-permute-done.35.refs_10_), channel_id=1, source_target_pairs={{0,1},{1,0},{2,3},{3,2},{4,5},{5,4},{6,7},{7,6},{8,9},{9,8},{10,11... | collective-permute-start | bytes 2359304 | tf_op jit(solution)/shard_map/ppermute | solution.py:915
  180.5 12.4 %collective-permute-start.42 = (bf16[1536,128]{1,0:T(8,128)(2,1)S(1)}, bf16[1536,128]{1,0:T(8,128)(2,1)S(1)}, u32[]{:S(2)}, u32[]{:S(2)}) collective-permute-start(bf16[1536,128]{1,0:T(8,128)(2,1)S(1)} %slice.616), channel_id=1, source_target_pairs={{8,0},{16,8},{24,16},{28,24},{20,28},{12,20},{4,12},{0,4},{9,1},{1... | collective-permute-start | bytes 1179656 | tf_op jit(solution)/shard_map/ppermute | solution.py:665
  182.8 16.9 %collective-permute-start.27 = (bf16[200,1024]{1,0:T(8,128)(2,1)S(1)}, bf16[200,1024]{1,0:T(8,128)(2,1)S(1)}, u32[]{:S(2)}, u32[]{:S(2)}) collective-permute-start(bf16[200,1024]{1,0:T(8,128)(2,1)S(1)} %copy-done.41), channel_id=1, source_target_pairs={{0,2},{1,3},{2,0},{3,1},{4,6},{5,7},{6,4},{7,5},{8,10},{9,11},{10,... | collective-permute-start | bytes 1228808 | tf_op jit(solution)/shard_map/ppermute | solution.py:918
  191.3 12.1 %collective-permute-start.44 = (bf16[200,1024]{1,0:T(8,128)(2,1)S(1)}, bf16[200,1024]{1,0:T(8,128)(2,1)S(1)}, u32[]{:S(2)}, u32[]{:S(2)}) collective-permute-start(bf16[200,1024]{1,0:T(8,128)(2,1)S(1)} %get-tuple-element.216.refs_1_), channel_id=1, source_target_pairs={{0,2},{1,3},{2,0},{3,1},{4,6},{5,7},{6,4},{7,5},{8,10},{9,11},{10,... | collective-permute-start | bytes 1228808 | tf_op jit(solution)/shard_map/ppermute | solution.py:918
  202.2 12.4 %collective-permute-start.45 = (bf16[200,1024]{1,0:T(8,128)(2,1)S(1)}, bf16[200,1024]{1,0:T(8,128)(2,1)S(1)}, u32[]{:S(2)}, u32[]{:S(2)}) collective-permute-start(bf16[200,1024]{1,0:T(8,128)(2,1)S(1)} %get-tuple-element.224.own_ref), channel_id=1, source_target_pairs={{0,2},{1,3},{2,0},{3,1},{4,6},{5,7},{6,4},{7,5},{8,10},{9,11},{10,... | collective-permute-start | bytes 1228808 | tf_op jit(solution)/shard_map/ppermute | solution.py:918
  206.0 16.5 %collective-permute-start.46 = (bf16[200,1024]{1,0:T(8,128)(2,1)S(1)}, bf16[200,1024]{1,0:T(8,128)(2,1)S(1)}, u32[]{:S(2)}, u32[]{:S(2)}) collective-permute-start(bf16[200,1024]{1,0:T(8,128)(2,1)S(1)} %get-tuple-element.223.own_ref), channel_id=1, source_target_pairs={{0,2},{1,3},{2,0},{3,1},{4,6},{5,7},{6,4},{7,5},{8,10},{9,11},{10,... | collective-permute-start | bytes 1228808 | tf_op jit(solution)/shard_map/ppermute | solution.py:918
  231.8 12.4 %collective-permute-start.47 = (bf16[200,1024]{1,0:T(8,128)(2,1)S(1)}, bf16[200,1024]{1,0:T(8,128)(2,1)S(1)}, u32[]{:S(2)}, u32[]{:S(2)}) collective-permute-start(bf16[200,1024]{1,0:T(8,128)(2,1)S(1)} %get-tuple-element.236.own_ref), channel_id=1, source_target_pairs={{0,2},{1,3},{2,0},{3,1},{4,6},{5,7},{6,4},{7,5},{8,10},{9,11},{10,... | collective-permute-start | bytes 1228808 | tf_op jit(solution)/shard_map/ppermute | solution.py:918
  238.4 23.1 %collective-permute-start.48 = (bf16[200,1024]{1,0:T(8,128)(2,1)S(1)}, bf16[200,1024]{1,0:T(8,128)(2,1)S(1)}, u32[]{:S(2)}, u32[]{:S(2)}) collective-permute-start(bf16[200,1024]{1,0:T(8,128)(2,1)S(1)} %get-tuple-element.243.own_ref), channel_id=1, source_target_pairs={{0,2},{1,3},{2,0},{3,1},{4,6},{5,7},{6,4},{7,5},{8,10},{9,11},{10,... | collective-permute-start | bytes 1228808 | tf_op jit(solution)/shard_map/ppermute | solution.py:918
  249.4 17.2 %collective-permute-start.50 = (bf16[200,1024]{1,0:T(8,128)(2,1)S(1)}, bf16[200,1024]{1,0:T(8,128)(2,1)S(1)}, u32[]{:S(2)}, u32[]{:S(2)}) collective-permute-start(bf16[200,1024]{1,0:T(8,128)(2,1)S(1)} %get-tuple-element.266.refs_1_), channel_id=1, source_target_pairs={{0,2},{1,3},{2,0},{3,1},{4,6},{5,7},{6,4},{7,5},{8,10},{9,11},{10,... | collective-permute-start | bytes 1228808 | tf_op jit(solution)/shard_map/ppermute | solution.py:918
  274.2 21.9 %collective-permute-start.52 = (bf16[24576,128]{1,0:T(8,128)(2,1)S(1)}, bf16[24576,128]{1,0:T(8,128)(2,1)}, u32[]{:S(2)}, u32[]{:S(2)}) collective-permute-start(bf16[24576,128]{1,0:T(8,128)(2,1)S(1)} %get-tuple-element.278), channel_id=1, source_target_pairs={{0,1},{1,0},{2,3},{3,2},{4,5},{5,4},{6,7},{7,6},{8,9},{9,8},{10,11... | collective-permute-start | bytes 18874376 | tf_op jit(solution)/shard_map/ppermute | solution.py:915
  274.4 11.7 %collective-permute-start.49 = (bf16[200,1024]{1,0:T(8,128)(2,1)S(1)}, bf16[200,1024]{1,0:T(8,128)(2,1)S(1)}, u32[]{:S(2)}, u32[]{:S(2)}) collective-permute-start(bf16[200,1024]{1,0:T(8,128)(2,1)S(1)} %get-tuple-element.247.refs_1_), channel_id=1, source_target_pairs={{0,2},{1,3},{2,0},{3,1},{4,6},{5,7},{6,4},{7,5},{8,10},{9,11},{10,... | collective-permute-start | bytes 1228808 | tf_op jit(solution)/shard_map/ppermute | solution.py:918
  286.1 11.7 %collective-permute-start.53 = (bf16[1536,128]{1,0:T(8,128)(2,1)S(1)}, bf16[1536,128]{1,0:T(8,128)(2,1)S(1)}, u32[]{:S(2)}, u32[]{:S(2)}) collective-permute-start(bf16[1536,128]{1,0:T(8,128)(2,1)S(1)} %get-tuple-element.271), channel_id=1, source_target_pairs={{0,8},{8,16},{16,24},{24,28},{28,20},{20,12},{12,4},{4,0},{1,9},{9... | collective-permute-start | bytes 1179656 | tf_op jit(solution)/shard_map/ppermute | solution.py:698
  286.7 11.4 %collective-permute-start.54 = (bf16[1536,128]{1,0:T(8,128)(2,1)S(1)}, bf16[1536,128]{1,0:T(8,128)(2,1)S(1)}, u32[]{:S(2)}, u32[]{:S(2)}) collective-permute-start(bf16[1536,128]{1,0:T(8,128)(2,1)S(1)} %get-tuple-element.272), channel_id=1, source_target_pairs={{8,0},{16,8},{24,16},{28,24},{20,28},{12,20},{4,12},{0,4},{9,1},{1... | collective-permute-start | bytes 1179656 | tf_op jit(solution)/shard_map/ppermute | solution.py:699
  294.7 30.0 %collective-permute-start.57 = (bf16[200,1024]{1,0:T(8,128)(2,1)S(1)}, bf16[200,1024]{1,0:T(8,128)(2,1)S(1)}, u32[]{:S(2)}, u32[]{:S(2)}) collective-permute-start(bf16[200,1024]{1,0:T(8,128)(2,1)S(1)} %get-tuple-element.297.own_ref), channel_id=1, source_target_pairs={{0,2},{1,3},{2,0},{3,1},{4,6},{5,7},{6,4},{7,5},{8,10},{9,11},{10,... | collective-permute-start | bytes 1228808 | tf_op jit(solution)/shard_map/ppermute | solution.py:918
  298.2 19.9 %collective-permute-start.56 = (bf16[3072,128]{1,0:T(8,128)(2,1)S(1)}, bf16[3072,128]{1,0:T(8,128)(2,1)S(1)}, u32[]{:S(2)}, u32[]{:S(2)}) collective-permute-start(bf16[3072,128]{1,0:T(8,128)(2,1)S(1)} %pad_maximum_fusion.1), channel_id=1, source_target_pairs={{8,0},{16,8},{24,16},{28,24},{20,28},{12,20},{4,12},{0,4},{9,1},{1... | collective-permute-start | bytes 2359304 | tf_op jit(solution)/shard_map/ppermute | solution.py:699
  299.9 18.2 %collective-permute-start.55 = (bf16[3072,128]{1,0:T(8,128)(2,1)S(1)}, bf16[3072,128]{1,0:T(8,128)(2,1)}, u32[]{:S(2)}, u32[]{:S(2)}) collective-permute-start(bf16[3072,128]{1,0:T(8,128)(2,1)S(1)} %pad_maximum_fusion), channel_id=1, source_target_pairs={{0,8},{8,16},{16,24},{24,28},{28,20},{20,12},{12,4},{4,0},{1,9},{9... | collective-permute-start | bytes 2359304 | tf_op jit(solution)/shard_map/ppermute | solution.py:698
  321.6 19.5 %collective-permute-start.60 = (bf16[3072,128]{1,0:T(8,128)(2,1)}, bf16[3072,128]{1,0:T(8,128)(2,1)S(1)}, u32[]{:S(2)}, u32[]{:S(2)}) collective-permute-start(bf16[3072,128]{1,0:T(8,128)(2,1)} %get-tuple-element.296), channel_id=1, source_target_pairs={{8,0},{16,8},{24,16},{28,24},{20,28},{12,20},{4,12},{0,4},{9,1},{1... | collective-permute-start | bytes 2359304 | tf_op jit(solution)/shard_map/ppermute | solution.py:699
  323.3 18.7 %collective-permute-start.59 = (bf16[3072,128]{1,0:T(8,128)(2,1)}, bf16[3072,128]{1,0:T(8,128)(2,1)}, u32[]{:S(2)}, u32[]{:S(2)}) collective-permute-start(bf16[3072,128]{1,0:T(8,128)(2,1)} %get-tuple-element.295), channel_id=1, source_target_pairs={{0,8},{8,16},{16,24},{24,28},{28,20},{20,12},{12,4},{4,0},{1,9},{9... | collective-permute-start | bytes 2359304 | tf_op jit(solution)/shard_map/ppermute | solution.py:698
  360.7 22.1 %collective-permute-start.62 = (bf16[24576,128]{1,0:T(8,128)(2,1)}, bf16[24576,128]{1,0:T(8,128)(2,1)}, u32[]{:S(2)}, u32[]{:S(2)}) collective-permute-start(bf16[24576,128]{1,0:T(8,128)(2,1)} %copy-done.7), channel_id=1, source_target_pairs={{0,1},{1,0},{2,3},{3,2},{4,5},{5,4},{6,7},{7,6},{8,9},{9,8},{10,11... | collective-permute-start | bytes 18874376 | tf_op jit(solution)/shard_map/ppermute | solution.py:915
  362.0 20.8 %collective-permute-start.70 = (bf16[3072,128]{1,0:T(8,128)(2,1)}, bf16[3072,128]{1,0:T(8,128)(2,1)}, u32[]{:S(2)}, u32[]{:S(2)}) collective-permute-start(bf16[3072,128]{1,0:T(8,128)(2,1)} %get-tuple-element.314), channel_id=1, source_target_pairs={{0,8},{8,16},{16,24},{24,28},{28,20},{20,12},{12,4},{4,0},{1,9},{9... | collective-permute-start | bytes 2359304 | tf_op jit(solution)/shard_map/ppermute | solution.py:698
  363.6 32.9 %collective-permute-start.71 = (bf16[3072,128]{1,0:T(8,128)(2,1)}, bf16[3072,128]{1,0:T(8,128)(2,1)S(1)}, u32[]{:S(2)}, u32[]{:S(2)}) collective-permute-start(bf16[3072,128]{1,0:T(8,128)(2,1)} %get-tuple-element.315), channel_id=1, source_target_pairs={{8,0},{16,8},{24,16},{28,24},{20,28},{12,20},{4,12},{0,4},{9,1},{1... | collective-permute-start | bytes 2359304 | tf_op jit(solution)/shard_map/ppermute | solution.py:699
  365.2 25.3 %collective-permute-start.65 = (bf16[1536,128]{1,0:T(8,128)(2,1)}, bf16[1536,128]{1,0:T(8,128)(2,1)S(1)}, u32[]{:S(2)}, u32[]{:S(2)}) collective-permute-start(bf16[1536,128]{1,0:T(8,128)(2,1)} %get-tuple-element.320), channel_id=1, source_target_pairs={{0,8},{8,16},{16,24},{24,28},{28,20},{20,12},{12,4},{4,0},{1,9},{9... | collective-permute-start | bytes 1179656 | tf_op jit(solution)/shard_map/ppermute | solution.py:698
  365.8 26.2 %collective-permute-start.66 = (bf16[1536,128]{1,0:T(8,128)(2,1)S(1)}, bf16[1536,128]{1,0:T(8,128)(2,1)S(1)}, u32[]{:S(2)}, u32[]{:S(2)}) collective-permute-start(bf16[1536,128]{1,0:T(8,128)(2,1)S(1)} %get-tuple-element.321), channel_id=1, source_target_pairs={{8,0},{16,8},{24,16},{28,24},{20,28},{12,20},{4,12},{0,4},{9,1},{1... | collective-permute-start | bytes 1179656 | tf_op jit(solution)/shard_map/ppermute | solution.py:699
  394.4 18.6 %collective-permute-start.69 = (bf16[3072,128]{1,0:T(8,128)(2,1)S(1)}, bf16[3072,128]{1,0:T(8,128)(2,1)S(1)}, u32[]{:S(2)}, u32[]{:S(2)}) collective-permute-start(bf16[3072,128]{1,0:T(8,128)(2,1)S(1)} %pad_maximum_fusion.3), channel_id=1, source_target_pairs={{8,0},{16,8},{24,16},{28,24},{20,28},{12,20},{4,12},{0,4},{9,1},{1... | collective-permute-start | bytes 2359304 | tf_op jit(solution)/shard_map/ppermute | solution.py:699
  394.9 18.1 %collective-permute-start.68 = (bf16[3072,128]{1,0:T(8,128)(2,1)S(1)}, bf16[3072,128]{1,0:T(8,128)(2,1)S(1)}, u32[]{:S(2)}, u32[]{:S(2)}) collective-permute-start(bf16[3072,128]{1,0:T(8,128)(2,1)S(1)} %pad_maximum_fusion.2), channel_id=1, source_target_pairs={{0,8},{8,16},{16,24},{24,28},{28,20},{20,12},{12,4},{4,0},{1,9},{9... | collective-permute-start | bytes 2359304 | tf_op jit(solution)/shard_map/ppermute | solution.py:698
  398.4 14.4 %collective-permute-start.64 = (bf16[200,1024]{1,0:T(8,128)(2,1)S(1)}, bf16[200,1024]{1,0:T(8,128)(2,1)S(1)}, u32[]{:S(2)}, u32[]{:S(2)}) collective-permute-start(bf16[200,1024]{1,0:T(8,128)(2,1)S(1)} %broadcast_select_fusion.5), channel_id=1, source_target_pairs={{0,2},{1,3},{2,0},{3,1},{4,6},{5,7},{6,4},{7,5},{8,10},{9,11},{10,... | collective-permute-start | bytes 1228808 | tf_op jit(solution)/shard_map/ppermute | solution.py:918
  401.0 11.8 %collective-permute-start.72 = (f32[8,768]{1,0:T(8,128)S(1)}, f32[8,768]{1,0:T(8,128)S(1)}, u32[]{:S(2)}, u32[]{:S(2)}) collective-permute-start(f32[8,768]{1,0:T(8,128)S(1)} %slice.488), channel_id=1, source_target_pairs={{0,8},{4,12},{8,0},{12,4},{16,24},{20,28},{24,16},{28,20},{1,9},{5... | collective-permute-start | bytes 73736 | tf_op jit(solution)/shard_map/ppermute | solution.py:1138
  402.1 17.1 %collective-permute-start.63 = (bf16[200,1024]{1,0:T(8,128)(2,1)S(1)}, bf16[200,1024]{1,0:T(8,128)(2,1)S(1)}, u32[]{:S(2)}, u32[]{:S(2)}) collective-permute-start(bf16[200,1024]{1,0:T(8,128)(2,1)S(1)} %broadcast_select_fusion.4), channel_id=1, source_target_pairs={{0,2},{1,3},{2,0},{3,1},{4,6},{5,7},{6,4},{7,5},{8,10},{9,11},{10,... | collective-permute-start | bytes 1228808 | tf_op jit(solution)/shard_map/ppermute | solution.py:918
  416.5 19.6 %collective-permute-start.75 = (bf16[3072,128]{1,0:T(8,128)(2,1)}, bf16[3072,128]{1,0:T(8,128)(2,1)}, u32[]{:S(2)}, u32[]{:S(2)}) collective-permute-start(bf16[3072,128]{1,0:T(8,128)(2,1)} %get-tuple-element.343), channel_id=1, source_target_pairs={{8,0},{16,8},{24,16},{28,24},{20,28},{12,20},{4,12},{0,4},{9,1},{1... | collective-permute-start | bytes 2359304 | tf_op jit(solution)/shard_map/ppermute | solution.py:699
  418.7 17.4 %collective-permute-start.74 = (bf16[3072,128]{1,0:T(8,128)(2,1)}, bf16[3072,128]{1,0:T(8,128)(2,1)}, u32[]{:S(2)}, u32[]{:S(2)}) collective-permute-start(bf16[3072,128]{1,0:T(8,128)(2,1)} %get-tuple-element.342), channel_id=1, source_target_pairs={{0,8},{8,16},{16,24},{24,28},{28,20},{20,12},{12,4},{4,0},{1,9},{9... | collective-permute-start | bytes 2359304 | tf_op jit(solution)/shard_map/ppermute | solution.py:698
  422.0 14.1 %collective-permute-start.73 = (f32[4,768]{1,0:T(4,128)S(1)}, f32[4,768]{1,0:T(4,128)S(1)}, u32[]{:S(2)}, u32[]{:S(2)}) collective-permute-start(f32[4,768]{1,0:T(4,128)S(1)} %slice.490), channel_id=1, source_target_pairs={{0,4},{4,0},{8,12},{12,8},{16,20},{20,16},{24,28},{28,24},{1,5},{5... | collective-permute-start | bytes 36872 | tf_op jit(solution)/shard_map/ppermute | solution.py:1138
  439.0 16.2 %collective-permute-start.79 = (bf16[3072,128]{1,0:T(8,128)(2,1)S(1)}, bf16[3072,128]{1,0:T(8,128)(2,1)S(1)}, u32[]{:S(2)}, u32[]{:S(2)}) collective-permute-start(bf16[3072,128]{1,0:T(8,128)(2,1)S(1)} %get-tuple-element.347), channel_id=1, source_target_pairs={{8,0},{16,8},{24,16},{28,24},{20,28},{12,20},{4,12},{0,4},{9,1},{1... | collective-permute-start | bytes 2359304 | tf_op jit(solution)/shard_map/ppermute | solution.py:699
  441.3 16.1 %collective-permute-start.78 = (bf16[3072,128]{1,0:T(8,128)(2,1)S(1)}, bf16[3072,128]{1,0:T(8,128)(2,1)S(1)}, u32[]{:S(2)}, u32[]{:S(2)}) collective-permute-start(bf16[3072,128]{1,0:T(8,128)(2,1)S(1)} %get-tuple-element.346), channel_id=1, source_target_pairs={{0,8},{8,16},{16,24},{24,28},{28,20},{20,12},{12,4},{4,0},{1,9},{9... | collective-permute-start | bytes 2359304 | tf_op jit(solution)/shard_map/ppermute | solution.py:698
  (138 other events, 938.5 us)

commit v4 on v3

--- a/solution.py
+++ b/solution.py
@@ -37,6 +37,10 @@
 
 def cost(flops, nbytes):
     return pl.CostEstimate(flops=flops, bytes_accessed=nbytes, transcendentals=0)
+
+
+def output(in_hbm, *shape, dtype=BF):
+    return (pltpu.HBM if in_hbm else jax.ShapeDtypeStruct)(shape, dtype)
 
 
 def dot(a, b):
@@ -124,10 +128,10 @@
 def call_attention_forward(first, operands, vecs, kept, weights):
     rows = operands[0].shape[0]
     outs = [
-        jax.ShapeDtypeStruct((rows, D), BF),
-        jax.ShapeDtypeStruct((rows, 3 * WID), BF),
-        jax.ShapeDtypeStruct((rows, BLK), F32),
-        jax.ShapeDtypeStruct((rows, WID), BF),
+        output(first, rows, D),
+        output(first, rows, 3 * WID),
+        output(first, rows, BLK, dtype=F32),
+        output(first, rows, WID),
         jax.ShapeDtypeStruct((rows, D), BF),
     ]
     if not first:
@@ -202,16 +206,16 @@
     return weights[pl.ds(pl.multiple_of(4 * D + step * STEP_HID, STEP_HID), STEP_HID), :]
 
 
-def call_mlp_forward(hidden, own, got, vecs, weights):
+def call_mlp_forward(first, hidden, own, got, vecs, weights):
     rows = hidden.shape[0]
     return pl.pallas_call(
         mlp_forward,
         grid=(STEPS,),
         out_shape=[
             jax.ShapeDtypeStruct((rows, D), F32),
-            jax.ShapeDtypeStruct((rows, D), BF),
-            jax.ShapeDtypeStruct((rows, HID), BF),
-            jax.ShapeDtypeStruct((rows, HID), BF),
+            output(first, rows, D),
+            output(first, rows, HID),
+            output(first, rows, HID),
             jax.ShapeDtypeStruct((rows, D), BF),
             jax.ShapeDtypeStruct(weights.shape, BF),
         ],
@@ -467,7 +471,7 @@
     wide = STEP_HID // 2
     by_hidden = pl.BlockSpec((rows, wide), lambda s, a, b: (0, s))
     whole = pl.BlockSpec((rows, D), lambda s, a, b: (0, 0))
-    buffer = jax.ShapeDtypeStruct((SHARE_TILES * BLK, BLK), BF)
+    buffer = pltpu.HBM((SHARE_TILES * BLK, BLK), BF)
     return pl.pallas_call(
         mlp_grads,
         grid_spec=pltpu.PrefetchScalarGridSpec(
@@ -564,7 +568,7 @@
                 pltpu.SemaphoreType.DMA((2,)),
             ],
         ),
-        out_shape=[jax.ShapeDtypeStruct(own.shape, BF)] * 2,
+        out_shape=[pltpu.HBM(own.shape, BF)] * 2,
         input_output_aliases={14: 0, 15: 1},
         compiler_params=params(),
         cost_estimate=cost(2 * 2 * rows * D * 4 * WID, 8 << 20),
@@ -615,7 +619,7 @@
 
 def assemble(table, pieces):
     plan = [piece[:3] for piece in pieces]
-    args = list(table) + [piece[3] for piece in pieces]
+    args = list(table) + [pltpu.with_memory_space_constraint(p[3], pltpu.HBM) for p in pieces]
     return pl.pallas_call(
         functools.partial(assemble_kernel, plan),
         out_shape=jax.ShapeDtypeStruct((6 * D, D), BF),
@@ -789,8 +793,19 @@
 
 def total_over_mesh(value):
     value = jnp.broadcast_to(value.reshape(1, 1), (8, BLK))
-    for _, axis, perm in mesh_bits():
-        value = value + lax.ppermute(value, axis, perm)
+    for axis in ("narrow", "wide"):
+        size, bit = lax.axis_size(axis), 1
+
+        def swap(flip, value=None, axis=axis, size=size):
+            return lax.ppermute(value, axis, [(i, i ^ flip) for i in range(size)])
+
+        while bit < size:
+            if 2 * bit < size:
+                near, far, both = (swap(bit * k, value) for k in (1, 2, 3))
+                value = (value + near) + (far + both)
+            else:
+                value = value + swap(bit, value)
+            bit *= 4
     return value[0, 0]
 
 
@@ -957,7 +972,7 @@
         extra = [piece[4] for piece in latest]
         if step == 2:
             brought = chunks(after(inputs[0], *gather.sent))
-            extra += brought
+            extra += brought + [inputs[1]]
         elif step == 3:
             late = exchange(after(inputs[1], *gather.sent))
         at = (step - 2) * per_window
@@ -1003,9 +1018,11 @@
             if layer == 0 and t == 1:
                 placed += swapped(arrived_next)
                 arrived_next = gather_next.step(down_part)
+                placed += swapped(arrived_next)
+                arrived_next = gather_next.step()
                 part = after(part, *gather_next.sent, *vecs[1:])
             middle, n2, act, slope, down_part, weights[layer] = call_mlp_forward(
-                hidden, part, got, vecs[layer], weights[layer]
+                layer == 0, hidden, part, got, vecs[layer], weights[layer]
             )
             kept_layer[t] = (hidden, n1, qkv, lse, att, middle, n2, act, slope)
             if layer < LAYERS - 1:
@@ -1014,12 +1031,9 @@
                 state.append((middle, down_part))
         saved.append(kept_layer)
         if layer == 0:
-            gates = [down_part]
-            for step in range(4, steps + 1):
-                latest = swapped(arrived_next)
-                arrived_next = gather_next.step(*gates)
-                placed += latest
-                gates = [piece[4] for piece in latest]
+            for _ in range(5, steps + 1):
+                placed += swapped(arrived_next)
+                arrived_next = gather_next.step()
             weights.append(place_pieces(1, placed + swapped(arrived_next)))
 
     def mine(pair):
@@ -1085,7 +1099,7 @@
             got = [exchange(back[t][3]) for t in range(2)]
             own = after(own, got[0])
             upstream = [
-                (after(back[0][0], got[1]), back[0][3], got[0], kept_layer[0][0]),
+                (back[0][0], back[0][3], got[0], kept_layer[0][0]),
                 (back[1][0], back[1][3], got[1], kept_layer[1][0]),
             ]
         own, par = call_attention_grads(
@@ -1097,6 +1111,8 @@
             own,
             par,
         )
+        if pending is not None:
+            own = after(own, pending.up, pending.down)
         terms = small_vector([w[4] for w in work], [b[4] for b in back], me)
         small_terms[layer] = terms.reshape(-1, own_small)
         unit_len = per_device * BLK

time: 503 us -> 455 us (0.905)
  local copies, waits for them, and re-layouts: 77.7 us -> 46.1 us
  other arithmetic: 40.9 us -> 32.6 us
    unnamed x247 -> x157, local copies, waits for them, and re-layouts: 58 us -> 26.5 us
    ppermute x16, waiting for transfers between devices: 53.3 us -> 33.1 us  [step(): self.up = lax.ppermute(up, 'wide', self.ahead)]
    ppermute x16, starting transfers between devices: 23.2 us -> 10.2 us  [step(): self.down = lax.ppermute(down, 'wide', self.behind)]
    ppermute x16, starting transfers between devices: 11.9 us -> 24.4 us  [step(): self.up = lax.ppermute(up, 'wide', self.ahead)]
    ppermute x16, waiting for transfers between devices: 11.4 us -> 18.5 us  [step(): self.down = lax.ppermute(down, 'wide', self.behind)]
    ppermute x5 -> x7, waiting for transfers between devices: 12.7 us -> 6.6 us  [swap(): return lax.ppermute(value, axis, [(i, i ^ flip) for i in range(size)])]
    ppermute x15, waiting for transfers between devices: 33.8 us -> 39 us  [exchange(): return lax.ppermute(part, 'narrow', ACROSS)]
  transfers between devices with their start and end apart: 85 -> 87, of which waited for: 41 -> 52; matrix products, arithmetic and copies ran while one was open for 9% -> 8% of each run, Pallas kernels for 19% -> 22%
where the time goes in v4:
time: 455 us; the launch traced here: 448 us
  waiting for transfers between devices  165 us (36%)
  Pallas kernels  126 us (28%)
  starting transfers between devices  71.2 us (16%)
  local copies, waits for them, and re-layouts  46.1 us (10%)
  other arithmetic  32.6 us (7%)
  between operations  7.26 us (2%)
    ppermute x15, waiting for transfers between devices, exchange(): return lax.ppermute(part, 'narrow', ACROSS)  39 us
    ppermute x16, waiting for transfers between devices, step(): self.up = lax.ppermute(up, 'wide', self.ahead)  33.1 us
    ppermute x5, waiting for transfers between devices, shards(): small_rows = small_rows[:bit] + lax.ppermute(small_rows[bit:], axis, perm)  31 us
    unnamed x157, local copies, waits for them, and re-layouts  26.5 us
    ppermute x16, starting transfers between devices, step(): self.up = lax.ppermute(up, 'wide', self.ahead)  24.4 us
    pallas_call x4, Pallas kernels, call_mlp_backward(): pl.pallas_call(functools.partial(mlp_backward, first), grid=(STEPS,), out...  21.5 us
    pallas_call x2, Pallas kernels, call_mlp_grads(): pl.pallas_call(mlp_grads, grid_spec=pltpu.PrefetchScalarGridSpec(num_scal...  20.4 us
    pallas_call x4, Pallas kernels, call_attention_backward(): pl.pallas_call(attention_backward, grid=(1,), out_shape=outs + [jax.Shape...  20.4 us
  transfers between devices with their start and end apart: 87, of which 52 were waited for; matrix products, arithmetic and copies ran while one was open for 8% of the time, Pallas kernels for 22%

profile of v4, /device:TPU:0, one launch (start us, length us, event | category | flops | bytes accessed | tf_op | source)
XLA Modules:
  0.0 447.7 jit_solution(3759108692462979898)
XLA Ops:
  0.6 2.1 convert.41
  4.3 2.6 collective-permute-start
  16.1 1.8 collective-permute-start.3
  19.8 5.3 %collective-permute-done.refs_2_ = bf16[3072,128]{1,0:T(8,128)(2,1)} collective-permute-done((bf16[3072,128]{1,0:T(8,128)(2,1)S(1)}, bf16[3072,128]{1,0:T(8,128)(2,1)}, u32[]{:S(2)}, u32[]{:S(2)}) %collective-permute-start) | collective-permute-done | bytes 786464 | tf_op jit(solution)/shard_map/ppermute | solution.py:668
  32.5 5.0 %collective-permute-done.4 = bf16[200,1024]{1,0:T(8,128)(2,1)} collective-permute-done((bf16[200,1024]{1,0:T(8,128)(2,1)S(1)}, bf16[200,1024]{1,0:T(8,128)(2,1)}, u32[]{:S(2)}, u32[]{:S(2)}) %collective-permute-start.4) | collective-permute-done | bytes 409632 | tf_op jit(solution)/shard_map/ppermute | solution.py:888
  38.7 9.4 %collective-permute-done.11.refs_6_ = bf16[3072,128]{1,0:T(8,128)(2,1)} collective-permute-done((bf16[3072,128]{1,0:T(8,128)(2,1)}, bf16[3072,128]{1,0:T(8,128)(2,1)}, u32[]{:S(2)}, u32[]{:S(2)}) %collective-permute-start.11) | collective-permute-done | bytes 786464 | tf_op jit(solution)/shard_map/ppermute | solution.py:668
  53.9 14.5 %collective-permute-done.6 = bf16[8,768]{1,0:T(8,128)(2,1)S(1)} collective-permute-done((bf16[8,768]{1,0:T(8,128)(2,1)S(1)}, bf16[8,768]{1,0:T(8,128)(2,1)S(1)}, u32[]{:S(2)}, u32[]{:S(2)}) %collective-permute-start.6) | collective-permute-done | bytes 12320 | tf_op jit(solution)/shard_map/ppermute | solution.py:959
  68.5 2.8 collective-permute-start.7
  77.0 7.2 %collective-permute-done.21 = bf16[200,1024]{1,0:T(8,128)(2,1)S(1)} collective-permute-done((bf16[200,1024]{1,0:T(8,128)(2,1)S(1)}, bf16[200,1024]{1,0:T(8,128)(2,1)S(1)}, u32[]{:S(2)}, u32[]{:S(2)}) %collective-permute-start.21) | collective-permute-done | bytes 409632 | tf_op jit(solution)/shard_map/ppermute | solution.py:933
  84.4 2.1 collective-permute-start.24
  89.3 5.2 %assemble.2.refs_3_ = bf16[6144,1024]{1,0:T(8,128)(2,1)S(1)} custom-call(s32[2,192]{1,0:T(2,128)S(1)} %pad_add_fusion.rows, s32[2,192]{1,0:T(2,128)S(1)} %pad_add_fusion.1.cols, bf16[3072,128]{1,0:T(8,128)(2,1)} %bitcast.83, bf16[3072,128]{1,0:T(8,128)(2,1)} %copy-done.42, bf16[3072,128]{1,0:T(8,128)(2,1)} %collective-permute-done.refs_2_, ...), custom_call_target="tpu_custom_call" | custom-call | bytes 128 | tf_op jit(solution)/shard_map/assemble/pallas_call | solution.py:623
  94.5 2.9 attention_forward.4
  97.5 4.6 %copy-done = bf16[6144,1024]{1,0:T(8,128)(2,1)} copy-done((bf16[6144,1024]{1,0:T(8,128)(2,1)}, bf16[6144,1024]{1,0:T(8,128)(2,1)S(1)}, u32[]{:S(2)}) %copy-start) | copy-done | bytes 12582936
  103.6 2.0 collective-permute-start.31
  107.0 4.6 %copy-done.1 = bf16[6144,1024]{1,0:T(8,128)(2,1)S(1)} copy-done((bf16[6144,1024]{1,0:T(8,128)(2,1)S(1)}, bf16[6144,1024]{1,0:T(8,128)(2,1)}, u32[]{:S(2)}) %copy-start.1) | copy-done | bytes 12582936
  111.5 2.9 attention_forward.5
  114.4 4.9 %mlp_forward.4 = (f32[200,1024]{1,0:T(8,128)S(1)}, bf16[200,1024]{1,0:T(8,128)(2,1)}, bf16[200,2048]{1,0:T(8,128)(2,1)}, bf16[200,2048]{1,0:T(8,128)(2,1)}, bf16...) custom-call(bf16[200,1024]{1,0:T(8,128)(2,1)S(1)} %get-tuple-element.420.refs_0_.hid_ref, ...), custom_call_target="tpu_custom_call", output_to_operand_aliasing={{5}: (4, {})} | custom-call | flops 3355443200 | bytes 12582912 | tf_op jit(solution)/shard_map/mlp_forward/pallas_call | solution.py:211
  119.4 4.6 %copy-done.2 = bf16[6144,1024]{1,0:T(8,128)(2,1)} copy-done((bf16[6144,1024]{1,0:T(8,128)(2,1)}, bf16[6144,1024]{1,0:T(8,128)(2,1)S(1)}, u32[]{:S(2)}) %copy-start.2) | copy-done | bytes 12582936
  129.2 8.9 %collective-permute-done.43.got_ref = bf16[200,1024]{1,0:T(8,128)(2,1)S(1)} collective-permute-done((bf16[200,1024]{1,0:T(8,128)(2,1)S(1)}, bf16[200,1024]{1,0:T(8,128)(2,1)S(1)}, u32[]{:S(2)}, u32[]{:S(2)}) %collective-permute-start.43) | collective-permute-done | bytes 409632 | tf_op jit(solution)/shard_map/ppermute | solution.py:933
  138.1 6.1 %collective-permute-done.35.refs_10_ = bf16[3072,128]{1,0:T(8,128)(2,1)} collective-permute-done((bf16[3072,128]{1,0:T(8,128)(2,1)}, bf16[3072,128]{1,0:T(8,128)(2,1)}, u32[]{:S(2)}, u32[]{:S(2)}) %collective-permute-start.35) | collective-permute-done | bytes 786464 | tf_op jit(solution)/shard_map/ppermute | solution.py:668
  151.1 4.6 %copy-done.3 = bf16[6144,1024]{1,0:T(8,128)(2,1)S(1)} copy-done((bf16[6144,1024]{1,0:T(8,128)(2,1)S(1)}, bf16[6144,1024]{1,0:T(8,128)(2,1)}, u32[]{:S(2)}) %copy-start.3) | copy-done | bytes 12582936
  155.7 4.9 %mlp_forward.5 = (f32[200,1024]{1,0:T(8,128)S(1)}, bf16[200,1024]{1,0:T(8,128)(2,1)}, bf16[200,2048]{1,0:T(8,128)(2,1)}, bf16[200,2048]{1,0:T(8,128)(2,1)}, bf16...) custom-call(bf16[200,1024]{1,0:T(8,128)(2,1)S(1)} %get-tuple-element.203.refs_0_.hid_ref, ...), custom_call_target="tpu_custom_call", output_to_operand_aliasing={{5}: (4, {})} | custom-call | flops 3355443200 | bytes 12582912 | tf_op jit(solution)/shard_map/mlp_forward/pallas_call | solution.py:211
  160.6 4.6 %copy-done.4 = bf16[6144,1024]{1,0:T(8,128)(2,1)} copy-done((bf16[6144,1024]{1,0:T(8,128)(2,1)}, bf16[6144,1024]{1,0:T(8,128)(2,1)S(1)}, u32[]{:S(2)}) %copy-start.4) | copy-done | bytes 12582936
  170.7 5.2 %assemble.3.refs_6_ = bf16[6144,1024]{1,0:T(8,128)(2,1)S(1)} custom-call(s32[2,192]{1,0:T(2,128)S(1)} %pad_add_fusion.2.rows, s32[2,192]{1,0:T(2,128)S(1)} %pad_add_fusion.3.cols, bf16[3072,128]{1,0:T(8,128)(2,1)} %bitcast.22.refs_0_, bf16[3072,128]{1,0:T(8,128)(2,1)} %copy-done.45, bf16[3072,128]{1,0:T(8,128)(2,1)} %collective-permute-done.24.refs_2_, ...), custom_call_target="tpu_custom_call" | custom-call | bytes 128 | tf_op jit(solution)/shard_map/assemble/pallas_call | solution.py:623
  177.5 2.5 attention_forward.6
  180.6 5.7 %collective-permute-done.44.refs_2_ = bf16[200,1024]{1,0:T(8,128)(2,1)S(1)} collective-permute-done((bf16[200,1024]{1,0:T(8,128)(2,1)S(1)}, bf16[200,1024]{1,0:T(8,128)(2,1)S(1)}, u32[]{:S(2)}, u32[]{:S(2)}) %collective-permute-start.44) | collective-permute-done | bytes 409632 | tf_op jit(solution)/shard_map/ppermute | solution.py:933
  186.3 2.5 attention_forward.7
  189.4 5.6 %collective-permute-done.45.got_ref = bf16[200,1024]{1,0:T(8,128)(2,1)S(1)} collective-permute-done((bf16[200,1024]{1,0:T(8,128)(2,1)S(1)}, bf16[200,1024]{1,0:T(8,128)(2,1)S(1)}, u32[]{:S(2)}, u32[]{:S(2)}) %collective-permute-start.45) | collective-permute-done | bytes 409632 | tf_op jit(solution)/shard_map/ppermute | solution.py:933
  195.1 4.2 mlp_forward.6
  200.0 3.4 collective-permute-done.46.got_ref
  203.4 4.2 mlp_forward.7
  207.6 5.1 %mlp_backward.4 = (bf16[200,1024]{1,0:T(8,128)(2,1)S(1)}, bf16[200,2048]{1,0:T(8,128)(2,1)S(1)}, bf16[200,1024]{1,0:T(8,128)(2,1)S(1)}, f32[8,1024]{1,0:T(8,128)S(1)}, bf16[6144,1024]{1,0:T(8,128)(2,1)S(1)}) custom-call(bf16[200,1024]{1,0:T(8,128)(2,1)S(1)} %get-tuple-element.419.refs_0_.grad_ref, ...), custom_call_target="tpu_custom_call", output_to_operand_aliasing={{4}: (4, {})} | custom-call | flops 3355443200 | bytes 12582912 | tf_op jit(solution)/shard_map/mlp_backward/pallas_call | solution.py:310
  213.2 5.2 %mlp_backward.5 = (bf16[200,1024]{1,0:T(8,128)(2,1)S(1)}, bf16[200,2048]{1,0:T(8,128)(2,1)S(1)}, bf16[200,1024]{1,0:T(8,128)(2,1)S(1)}, f32[8,1024]{1,0:T(8,128)S(1)}, bf16[6144,1024]{1,0:T(8,128)(2,1)S(1)}) custom-call(bf16[200,1024]{1,0:T(8,128)(2,1)S(1)} %get-tuple-element.418.refs_0_.grad_ref, ...), custom_call_target="tpu_custom_call", output_to_operand_aliasing={{4}: (4, {})} | custom-call | flops 3355443200 | bytes 12582912 | tf_op jit(solution)/shard_map/mlp_backward/pallas_call | solution.py:310
  220.0 5.0 %collective-permute-done.47.got_ref = bf16[200,1024]{1,0:T(8,128)(2,1)S(1)} collective-permute-done((bf16[200,1024]{1,0:T(8,128)(2,1)S(1)}, bf16[200,1024]{1,0:T(8,128)(2,1)S(1)}, u32[]{:S(2)}, u32[]{:S(2)}) %collective-permute-start.47) | collective-permute-done | bytes 409632 | tf_op jit(solution)/shard_map/ppermute | solution.py:933
  225.1 5.1 %attention_backward.4 = (f32[200,1024]{1,0:T(8,128)S(1)}, bf16[200,1024]{1,0:T(8,128)(2,1)S(1)}, bf16[200,1536]{1,0:T(8,128)(2,1)S(1)}, bf16[200,1024]{1,0:T(8,1...) custom-call(bf16[200,1024]{1,0:T(8,128)(2,1)S(1)} %get-tuple-element.419.refs, ...), custom_call_target="tpu_custom_call", output_to_operand_aliasing={{5}: (9, {})} | custom-call | flops 2516582400 | bytes 8388608 | tf_op jit(solution)/shard_map/attention_backward/pallas_call | solution.py:401
  230.7 10.2 %mlp_grads.2 = (bf16[24576,128]{1,0:T(8,128)(2,1)}, bf16[24576,128]{1,0:T(8,128)(2,1)}) custom-call(s32[192]{0:T(256)S(1)} %get-tuple-element.389.slot_own, s32[192]{0:T(256)S(1)} %get-tuple-element.386.slot_par, bf16[200,2048]{1,0:T(8,128)(2,1)S(1)} %get-tuple-element.255.refs_0_, bf16[200,2048]{1,0:T(8,128)(2,1)S(1)} %get-tuple-element.256.refs_1_, ...), custom_call_target="tpu_custom_call" | custom-call | flops 6710886400 | bytes 16777216 | tf_op jit(solution)/shard_map/mlp_grads/pallas_call | solution.py:475
  240.9 5.1 %attention_backward.5 = (f32[200,1024]{1,0:T(8,128)S(1)}, bf16[200,1024]{1,0:T(8,128)(2,1)S(1)}, bf16[200,1536]{1,0:T(8,128)(2,1)S(1)}, bf16[200,1024]{1,0:T(8,1...) custom-call(bf16[200,1024]{1,0:T(8,128)(2,1)S(1)} %get-tuple-element.418.refs, ...), custom_call_target="tpu_custom_call", output_to_operand_aliasing={{5}: (9, {})} | custom-call | flops 2516582400 | bytes 8388608 | tf_op jit(solution)/shard_map/attention_backward/pallas_call | solution.py:401
  246.0 5.2 %attention_grads.2 = (bf16[24576,128]{1,0:T(8,128)(2,1)}, bf16[24576,128]{1,0:T(8,128)(2,1)}) custom-call(s32[192]{0:T(256)S(1)} %get-tuple-element.389.slot_own, s32[192]{0:T(256)S(1)} %get-tuple-element.386.slot_par, bf16[200,512]{1,0:T(8,128)(2,1)S(1)} %get-tuple-element.243.refs_0_, ...), custom_call_target="tpu_custom_call", output_to_operand_aliasing={{0}: (14, {}), {1}: (15, {})} | custom-call | flops 1677721600 | bytes 8388608 | tf_op jit(solution)/shard_map/attention_grads/pallas_call | solution.py:553
  252.5 2.3 collective-permute-done.50
  260.0 5.6 %mlp_backward.6 = (f32[200,1024]{1,0:T(8,128)S(1)}, bf16[200,1024]{1,0:T(8,128)(2,1)S(1)}, bf16[200,2048]{1,0:T(8,128)(2,1)S(1)}, bf16[200,1024]{1,0:T(8,128)(2,...) custom-call(f32[200,1024]{1,0:T(8,128)S(1)} %get-tuple-element.271.refs_0_, ...), custom_call_target="tpu_custom_call", output_to_operand_aliasing={{5}: (8, {})} | custom-call | flops 3355443200 | bytes 12582912 | tf_op jit(solution)/shard_map/mlp_backward/pallas_call | solution.py:310
  267.1 2.0 collective-permute-done.52
  272.5 5.6 %mlp_backward.7 = (f32[200,1024]{1,0:T(8,128)S(1)}, bf16[200,1024]{1,0:T(8,128)(2,1)S(1)}, bf16[200,2048]{1,0:T(8,128)(2,1)S(1)}, bf16[200,1024]{1,0:T(8,128)(2,...) custom-call(f32[200,1024]{1,0:T(8,128)S(1)} %get-tuple-element.284.refs_0_, ...), custom_call_target="tpu_custom_call", output_to_operand_aliasing={{5}: (8, {})} | custom-call | flops 3355443200 | bytes 12582912 | tf_op jit(solution)/shard_map/mlp_backward/pallas_call | solution.py:310
  278.2 10.2 %mlp_grads.3 = (bf16[24576,128]{1,0:T(8,128)(2,1)}, bf16[24576,128]{1,0:T(8,128)(2,1)}) custom-call(s32[192]{0:T(256)S(1)} %get-tuple-element.394.slot_own, s32[192]{0:T(256)S(1)} %get-tuple-element.392.slot_par, bf16[200,2048]{1,0:T(8,128)(2,1)S(1)} %copy-done.29, bf16[200,2048]{1,0:T(8,128)(2,1)S(1)} %copy-done.30, ...), custom_call_target="tpu_custom_call" | custom-call | flops 6710886400 | bytes 16777216 | tf_op jit(solution)/shard_map/mlp_grads/pallas_call | solution.py:475
  290.3 2.0 collective-permute-start.59
  292.9 5.1 %attention_backward.6 = (f32[200,1024]{1,0:T(8,128)S(1)}, bf16[200,1024]{1,0:T(8,128)(2,1)S(1)}, bf16[200,1536]{1,0:T(8,128)(2,1)S(1)}, bf16[200,1024]{1,0:T(8,1...) custom-call(f32[200,1024]{1,0:T(8,128)S(1)} %get-tuple-element.274.grad_ref, ...), custom_call_target="tpu_custom_call", output_to_operand_aliasing={{5}: (9, {})} | custom-call | flops 2516582400 | bytes 8388608 | tf_op jit(solution)/shard_map/attention_backward/pallas_call | solution.py:401
  301.0 5.1 %attention_backward.7 = (f32[200,1024]{1,0:T(8,128)S(1)}, bf16[200,1024]{1,0:T(8,128)(2,1)S(1)}, bf16[200,1536]{1,0:T(8,128)(2,1)S(1)}, bf16[200,1024]{1,0:T(8,1...) custom-call(f32[200,1024]{1,0:T(8,128)S(1)} %get-tuple-element.301.grad_ref, ...), custom_call_target="tpu_custom_call", output_to_operand_aliasing={{5}: (9, {})} | custom-call | flops 2516582400 | bytes 8388608 | tf_op jit(solution)/shard_map/attention_backward/pallas_call | solution.py:401
  311.7 5.0 %attention_grads.3 = (bf16[24576,128]{1,0:T(8,128)(2,1)}, bf16[24576,128]{1,0:T(8,128)(2,1)}) custom-call(s32[192]{0:T(256)S(1)} %get-tuple-element.394.slot_own, s32[192]{0:T(256)S(1)} %get-tuple-element.392.slot_par, bf16[200,512]{1,0:T(8,128)(2,1)S(1)} %copy-done.21, ...), custom_call_target="tpu_custom_call", output_to_operand_aliasing={{0}: (14, {}), {1}: (15, {})} | custom-call | flops 1677721600 | bytes 8388608 | tf_op jit(solution)/shard_map/attention_grads/pallas_call | solution.py:553
  316.7 2.1 slice.432
  318.8 7.5 %collective-permute-done.61 = bf16[3072,128]{1,0:T(8,128)(2,1)} collective-permute-done((bf16[3072,128]{1,0:T(8,128)(2,1)}, bf16[3072,128]{1,0:T(8,128)(2,1)}, u32[]{:S(2)}, u32[]{:S(2)}) %collective-permute-start.61) | collective-permute-done | bytes 786464 | tf_op jit(solution)/shard_map/ppermute | solution.py:702
  334.1 6.2 %collective-permute-done.64 = bf16[24576,128]{1,0:T(8,128)(2,1)} collective-permute-done((bf16[24576,128]{1,0:T(8,128)(2,1)}, bf16[24576,128]{1,0:T(8,128)(2,1)}, u32[]{:S(2)}, u32[]{:S(2)}) %collective-permute-start.64) | collective-permute-done | bytes 6291488 | tf_op jit(solution)/shard_map/ppermute | solution.py:930
  340.3 2.1 convert_add_fusion.2
  345.1 3.6 collective-permute-done.69
  350.7 2.2 convert_add_fusion.1.grad1
  356.5 10.1 %collective-permute-done.72 = f32[8,768]{1,0:T(8,128)S(1)} collective-permute-done((f32[8,768]{1,0:T(8,128)S(1)}, f32[8,768]{1,0:T(8,128)S(1)}, u32[]{:S(2)}, u32[]{:S(2)}) %collective-permute-start.72) | collective-permute-done | bytes 24608 | tf_op jit(solution)/shard_map/ppermute | solution.py:1154
  368.1 3.6 add_convert_fusion.2
  378.0 13.2 %collective-permute-done.73 = f32[4,768]{1,0:T(4,128)S(1)} collective-permute-done((f32[4,768]{1,0:T(4,128)S(1)}, f32[4,768]{1,0:T(4,128)S(1)}, u32[]{:S(2)}, u32[]{:S(2)}) %collective-permute-start.73) | collective-permute-done | bytes 12320 | tf_op jit(solution)/shard_map/ppermute | solution.py:1154
  391.3 2.9 add_convert_fusion
  397.0 3.0 collective-permute-done.76
  403.1 8.4 %collective-permute-done.79 = bf16[3072,128]{1,0:T(8,128)(2,1)S(1)} collective-permute-done((bf16[3072,128]{1,0:T(8,128)(2,1)S(1)}, bf16[3072,128]{1,0:T(8,128)(2,1)S(1)}, u32[]{:S(2)}, u32[]{:S(2)}) %collective-permute-start.79) | collective-permute-done | bytes 786464 | tf_op jit(solution)/shard_map/ppermute | solution.py:703
  411.8 3.6 multiply_reduce_fusion
  423.5 2.4 collective-permute-done.85
  426.2 2.3 collective-permute-start.86
  428.5 2.2 collective-permute-done.86
  432.6 13.8 %update.1 = (f32[2,24,128,128]{3,2,1,0:T(8,128)}, f32[2,24,128,128]{3,2,1,0:T(8,128)}, f32[2,24,128,128]{3,2,1,0:T(8,128)}, bf16[2,24,128,128]{3,2,1,0:T(8,128)(2,1)}) custom-call(f32[1]{0:T(128)} %bitcast.65.clip_ref, f32[3072,128]{1,0:T(8,128)} %get-tuple-element.382.grad0, f32[3072,128]{1,0:T(8,128)} %copy-done.33, f32[2,24,128,128]{3,2,1,0:T(8,128)} %left.1, ...), custom_call_target="tpu_custom_call" | custom-call | flops 805306368 | bytes 29884416 | tf_op jit(solution)/shard_map/update/pallas_call | solution.py:850
  (503 shorter events, 120.6 us)
Async XLA Ops:
  3.8 34.8 %collective-permute-start.8 = (bf16[3072,128]{1,0:T(8,128)(2,1)S(1)}, bf16[3072,128]{1,0:T(8,128)(2,1)S(1)}, u32[]{:S(2)}, u32[]{:S(2)}) collective-permute-start(bf16[3072,128]{1,0:T(8,128)(2,1)S(1)} %bitcast.80), channel_id=1, source_target_pairs={{0,1},{1,0},{2,3},{3,2},{4,5},{5,4},{6,7},{7,6},{8,9},{9,8},{10,11... | collective-permute-start | bytes 2359304 | tf_op jit(solution)/shard_map/ppermute | solution.py:930
  4.3 20.8 %collective-permute-start = (bf16[3072,128]{1,0:T(8,128)(2,1)S(1)}, bf16[3072,128]{1,0:T(8,128)(2,1)}, u32[]{:S(2)}, u32[]{:S(2)}) collective-permute-start(bf16[3072,128]{1,0:T(8,128)(2,1)S(1)} %bitcast.81), channel_id=1, source_target_pairs={{0,8},{8,16},{16,24},{24,28},{28,20},{20,12},{12,4},{4,0},{1,9},{9... | collective-permute-start | bytes 2359304 | tf_op jit(solution)/shard_map/ppermute | solution.py:668
  6.9 19.8 %collective-permute-start.1 = (bf16[3072,128]{1,0:T(8,128)(2,1)S(1)}, bf16[3072,128]{1,0:T(8,128)(2,1)}, u32[]{:S(2)}, u32[]{:S(2)}) collective-permute-start(bf16[3072,128]{1,0:T(8,128)(2,1)S(1)} %bitcast.82), channel_id=1, source_target_pairs={{8,0},{16,8},{24,16},{28,24},{20,28},{12,20},{4,12},{0,4},{9,1},{1... | collective-permute-start | bytes 2359304 | tf_op jit(solution)/shard_map/ppermute | solution.py:669
  26.6 10.8 %collective-permute-start.4 = (bf16[200,1024]{1,0:T(8,128)(2,1)S(1)}, bf16[200,1024]{1,0:T(8,128)(2,1)}, u32[]{:S(2)}, u32[]{:S(2)}) collective-permute-start(bf16[200,1024]{1,0:T(8,128)(2,1)S(1)} %reshape.576), channel_id=1, source_target_pairs={{0,2},{1,3},{2,0},{3,1},{4,6},{5,7},{6,4},{7,5},{8,10},{9,11},{10,... | collective-permute-start | bytes 1228808 | tf_op jit(solution)/shard_map/ppermute | solution.py:888
  29.3 18.7 %collective-permute-start.11 = (bf16[3072,128]{1,0:T(8,128)(2,1)}, bf16[3072,128]{1,0:T(8,128)(2,1)}, u32[]{:S(2)}, u32[]{:S(2)}) collective-permute-start(bf16[3072,128]{1,0:T(8,128)(2,1)} %collective-permute-done.refs_2_), channel_id=1, source_target_pairs={{0,8},{8,16},{16,24},{24,28},{28,20},{20,12},{12,4},{4,0},{1,9},{9... | collective-permute-start | bytes 2359304 | tf_op jit(solution)/shard_map/ppermute | solution.py:668
  30.9 18.4 %collective-permute-start.13 = (bf16[3072,128]{1,0:T(8,128)(2,1)}, bf16[3072,128]{1,0:T(8,128)(2,1)}, u32[]{:S(2)}, u32[]{:S(2)}) collective-permute-start(bf16[3072,128]{1,0:T(8,128)(2,1)} %collective-permute-done.1.refs_4_), channel_id=1, source_target_pairs={{8,0},{16,8},{24,16},{28,24},{20,28},{12,20},{4,12},{0,4},{9,1},{1... | collective-permute-start | bytes 2359304 | tf_op jit(solution)/shard_map/ppermute | solution.py:669
  32.5 16.8 %collective-permute-start.9 = (bf16[3072,128]{1,0:T(8,128)(2,1)}, bf16[3072,128]{1,0:T(8,128)(2,1)S(1)}, u32[]{:S(2)}, u32[]{:S(2)}) collective-permute-start(bf16[3072,128]{1,0:T(8,128)(2,1)} %collective-permute-done.refs_2_), channel_id=1, source_target_pairs={{0,1},{1,0},{2,3},{3,2},{4,5},{5,4},{6,7},{7,6},{8,9},{9,8},{10,11... | collective-permute-start | bytes 2359304 | tf_op jit(solution)/shard_map/ppermute | solution.py:930
  37.5 11.8 %collective-permute-start.10 = (bf16[3072,128]{1,0:T(8,128)(2,1)}, bf16[3072,128]{1,0:T(8,128)(2,1)S(1)}, u32[]{:S(2)}, u32[]{:S(2)}) collective-permute-start(bf16[3072,128]{1,0:T(8,128)(2,1)} %collective-permute-done.1.refs_4_), channel_id=1, source_target_pairs={{0,1},{1,0},{2,3},{3,2},{4,5},{5,4},{6,7},{7,6},{8,9},{9,8},{10,11... | collective-permute-start | bytes 2359304 | tf_op jit(solution)/shard_map/ppermute | solution.py:930
  49.3 22.0 %collective-permute-start.15 = (bf16[3072,128]{1,0:T(8,128)(2,1)}, bf16[3072,128]{1,0:T(8,128)(2,1)S(1)}, u32[]{:S(2)}, u32[]{:S(2)}) collective-permute-start(bf16[3072,128]{1,0:T(8,128)(2,1)} %collective-permute-done.11.refs_6_), channel_id=1, source_target_pairs={{0,8},{8,16},{16,24},{24,28},{28,20},{20,12},{12,4},{4,0},{1,9},{9... | collective-permute-start | bytes 2359304 | tf_op jit(solution)/shard_map/ppermute | solution.py:668
  51.0 23.6 %collective-permute-start.17 = (bf16[3072,128]{1,0:T(8,128)(2,1)}, bf16[3072,128]{1,0:T(8,128)(2,1)S(1)}, u32[]{:S(2)}, u32[]{:S(2)}) collective-permute-start(bf16[3072,128]{1,0:T(8,128)(2,1)} %collective-permute-done.13.refs_8_), channel_id=1, source_target_pairs={{8,0},{16,8},{24,16},{28,24},{20,28},{12,20},{4,12},{0,4},{9,1},{1... | collective-permute-start | bytes 2359304 | tf_op jit(solution)/shard_map/ppermute | solution.py:669
  51.5 23.2 %collective-permute-start.12 = (bf16[3072,128]{1,0:T(8,128)(2,1)}, bf16[3072,128]{1,0:T(8,128)(2,1)}, u32[]{:S(2)}, u32[]{:S(2)}) collective-permute-start(bf16[3072,128]{1,0:T(8,128)(2,1)} %collective-permute-done.11.refs_6_), channel_id=1, source_target_pairs={{0,1},{1,0},{2,3},{3,2},{4,5},{5,4},{6,7},{7,6},{8,9},{9,8},{10,11... | collective-permute-start | bytes 2359304 | tf_op jit(solution)/shard_map/ppermute | solution.py:930
  51.5 23.2 %collective-permute-start.14 = (bf16[3072,128]{1,0:T(8,128)(2,1)}, bf16[3072,128]{1,0:T(8,128)(2,1)}, u32[]{:S(2)}, u32[]{:S(2)}) collective-permute-start(bf16[3072,128]{1,0:T(8,128)(2,1)} %collective-permute-done.13.refs_8_), channel_id=1, source_target_pairs={{0,1},{1,0},{2,3},{3,2},{4,5},{5,4},{6,7},{7,6},{8,9},{9,8},{10,11... | collective-permute-start | bytes 2359304 | tf_op jit(solution)/shard_map/ppermute | solution.py:930
  52.2 16.2 %collective-permute-start.6 = (bf16[8,768]{1,0:T(8,128)(2,1)S(1)}, bf16[8,768]{1,0:T(8,128)(2,1)S(1)}, u32[]{:S(2)}, u32[]{:S(2)}) collective-permute-start(bf16[8,768]{1,0:T(8,128)(2,1)S(1)} %pad_maximum_fusion.5), channel_id=1, source_target_pairs={{0,8},{4,12},{8,0},{12,4},{16,24},{20,28},{24,16},{28,20},{1,9},{5... | collective-permute-start | bytes 36872 | tf_op jit(solution)/shard_map/ppermute | solution.py:959
  71.3 15.3 %collective-permute-start.16 = (bf16[3072,128]{1,0:T(8,128)(2,1)S(1)}, bf16[3072,128]{1,0:T(8,128)(2,1)}, u32[]{:S(2)}, u32[]{:S(2)}) collective-permute-start(bf16[3072,128]{1,0:T(8,128)(2,1)S(1)} %collective-permute-done.15.refs_10_), channel_id=1, source_target_pairs={{0,1},{1,0},{2,3},{3,2},{4,5},{5,4},{6,7},{7,6},{8,9},{9,8},{10,11... | collective-permute-start | bytes 2359304 | tf_op jit(solution)/shard_map/ppermute | solution.py:930
  74.0 10.2 %collective-permute-start.21 = (bf16[200,1024]{1,0:T(8,128)(2,1)S(1)}, bf16[200,1024]{1,0:T(8,128)(2,1)S(1)}, u32[]{:S(2)}, u32[]{:S(2)}) collective-permute-start(bf16[200,1024]{1,0:T(8,128)(2,1)S(1)} %reshape.578), channel_id=1, source_target_pairs={{0,2},{1,3},{2,0},{3,1},{4,6},{5,7},{6,4},{7,5},{8,10},{9,11},{10,... | collective-permute-start | bytes 1228808 | tf_op jit(solution)/shard_map/ppermute | solution.py:933
  76.9 10.5 %collective-permute-start.18 = (bf16[3072,128]{1,0:T(8,128)(2,1)S(1)}, bf16[3072,128]{1,0:T(8,128)(2,1)}, u32[]{:S(2)}, u32[]{:S(2)}) collective-permute-start(bf16[3072,128]{1,0:T(8,128)(2,1)S(1)} %collective-permute-done.17.refs_12_), channel_id=1, source_target_pairs={{0,1},{1,0},{2,3},{3,2},{4,5},{5,4},{6,7},{7,6},{8,9},{9,8},{10,11... | collective-permute-start | bytes 2359304 | tf_op jit(solution)/shard_map/ppermute | solution.py:930
  84.4 19.1 %collective-permute-start.24 = (bf16[3072,128]{1,0:T(8,128)(2,1)}, bf16[3072,128]{1,0:T(8,128)(2,1)}, u32[]{:S(2)}, u32[]{:S(2)}) collective-permute-start(bf16[3072,128]{1,0:T(8,128)(2,1)} %bitcast.22.refs_0_), channel_id=1, source_target_pairs={{0,8},{8,16},{16,24},{24,28},{28,20},{20,12},{12,4},{4,0},{1,9},{9... | collective-permute-start | bytes 2359304 | tf_op jit(solution)/shard_map/ppermute | solution.py:668
  86.5 17.1 %collective-permute-start.25 = (bf16[3072,128]{1,0:T(8,128)(2,1)}, bf16[3072,128]{1,0:T(8,128)(2,1)}, u32[]{:S(2)}, u32[]{:S(2)}) collective-permute-start(bf16[3072,128]{1,0:T(8,128)(2,1)} %bitcast.22.refs_0_), channel_id=1, source_target_pairs={{8,0},{16,8},{24,16},{28,24},{20,28},{12,20},{4,12},{0,4},{9,1},{1... | collective-permute-start | bytes 2359304 | tf_op jit(solution)/shard_map/ppermute | solution.py:669
  102.1 12.4 %collective-permute-start.26 = (bf16[200,1024]{1,0:T(8,128)(2,1)S(1)}, bf16[200,1024]{1,0:T(8,128)(2,1)S(1)}, u32[]{:S(2)}, u32[]{:S(2)}) collective-permute-start(bf16[200,1024]{1,0:T(8,128)(2,1)S(1)} %get-tuple-element.206.own_ref), channel_id=1, source_target_pairs={{0,2},{1,3},{2,0},{3,1},{4,6},{5,7},{6,4},{7,5},{8,10},{9,11},{10,... | collective-permute-start | bytes 1228808 | tf_op jit(solution)/shard_map/ppermute | solution.py:933
  103.6 20.3 %collective-permute-start.31 = (bf16[3072,128]{1,0:T(8,128)(2,1)}, bf16[3072,128]{1,0:T(8,128)(2,1)}, u32[]{:S(2)}, u32[]{:S(2)}) collective-permute-start(bf16[3072,128]{1,0:T(8,128)(2,1)} %collective-permute-done.24.refs_2_), channel_id=1, source_target_pairs={{0,8},{8,16},{16,24},{24,28},{28,20},{20,12},{12,4},{4,0},{1,9},{9... | collective-permute-start | bytes 2359304 | tf_op jit(solution)/shard_map/ppermute | solution.py:668
  105.5 19.8 %collective-permute-start.33 = (bf16[3072,128]{1,0:T(8,128)(2,1)}, bf16[3072,128]{1,0:T(8,128)(2,1)}, u32[]{:S(2)}, u32[]{:S(2)}) collective-permute-start(bf16[3072,128]{1,0:T(8,128)(2,1)} %collective-permute-done.25.refs_4_), channel_id=1, source_target_pairs={{8,0},{16,8},{24,16},{28,24},{20,28},{12,20},{4,12},{0,4},{9,1},{1... | collective-permute-start | bytes 2359304 | tf_op jit(solution)/shard_map/ppermute | solution.py:669
  107.0 21.6 %collective-permute-start.28 = (bf16[3072,128]{1,0:T(8,128)(2,1)}, bf16[3072,128]{1,0:T(8,128)(2,1)S(1)}, u32[]{:S(2)}, u32[]{:S(2)}) collective-permute-start(bf16[3072,128]{1,0:T(8,128)(2,1)} %bitcast.22.refs_0_), channel_id=1, source_target_pairs={{0,1},{1,0},{2,3},{3,2},{4,5},{5,4},{6,7},{7,6},{8,9},{9,8},{10,11... | collective-permute-start | bytes 2359304 | tf_op jit(solution)/shard_map/ppermute | solution.py:930
  125.3 18.9 %collective-permute-start.35 = (bf16[3072,128]{1,0:T(8,128)(2,1)}, bf16[3072,128]{1,0:T(8,128)(2,1)}, u32[]{:S(2)}, u32[]{:S(2)}) collective-permute-start(bf16[3072,128]{1,0:T(8,128)(2,1)} %collective-permute-done.31.refs_6_), channel_id=1, source_target_pairs={{0,8},{8,16},{16,24},{24,28},{28,20},{20,12},{12,4},{4,0},{1,9},{9... | collective-permute-start | bytes 2359304 | tf_op jit(solution)/shard_map/ppermute | solution.py:668
  126.6 19.3 %collective-permute-start.37 = (bf16[3072,128]{1,0:T(8,128)(2,1)}, bf16[3072,128]{1,0:T(8,128)(2,1)}, u32[]{:S(2)}, u32[]{:S(2)}) collective-permute-start(bf16[3072,128]{1,0:T(8,128)(2,1)} %collective-permute-done.33.refs_8_), channel_id=1, source_target_pairs={{8,0},{16,8},{24,16},{28,24},{20,28},{12,20},{4,12},{0,4},{9,1},{1... | collective-permute-start | bytes 2359304 | tf_op jit(solution)/shard_map/ppermute | solution.py:669
  128.0 10.1 %collective-permute-start.43 = (bf16[200,1024]{1,0:T(8,128)(2,1)S(1)}, bf16[200,1024]{1,0:T(8,128)(2,1)S(1)}, u32[]{:S(2)}, u32[]{:S(2)}) collective-permute-start(bf16[200,1024]{1,0:T(8,128)(2,1)S(1)} %get-tuple-element.218.own_ref), channel_id=1, source_target_pairs={{0,2},{1,3},{2,0},{3,1},{4,6},{5,7},{6,4},{7,5},{8,10},{9,11},{10,... | collective-permute-start | bytes 1228808 | tf_op jit(solution)/shard_map/ppermute | solution.py:933
  128.5 20.4 %collective-permute-start.29 = (bf16[3072,128]{1,0:T(8,128)(2,1)}, bf16[3072,128]{1,0:T(8,128)(2,1)}, u32[]{:S(2)}, u32[]{:S(2)}) collective-permute-start(bf16[3072,128]{1,0:T(8,128)(2,1)} %collective-permute-done.24.refs_2_), channel_id=1, source_target_pairs={{0,1},{1,0},{2,3},{3,2},{4,5},{5,4},{6,7},{7,6},{8,9},{9,8},{10,11... | collective-permute-start | bytes 2359304 | tf_op jit(solution)/shard_map/ppermute | solution.py:930
  128.6 21.6 %collective-permute-start.30 = (bf16[3072,128]{1,0:T(8,128)(2,1)}, bf16[3072,128]{1,0:T(8,128)(2,1)}, u32[]{:S(2)}, u32[]{:S(2)}) collective-permute-start(bf16[3072,128]{1,0:T(8,128)(2,1)} %collective-permute-done.25.refs_4_), channel_id=1, source_target_pairs={{0,1},{1,0},{2,3},{3,2},{4,5},{5,4},{6,7},{7,6},{8,9},{9,8},{10,11... | collective-permute-start | bytes 2359304 | tf_op jit(solution)/shard_map/ppermute | solution.py:930
  138.1 12.9 %collective-permute-start.32 = (bf16[3072,128]{1,0:T(8,128)(2,1)}, bf16[3072,128]{1,0:T(8,128)(2,1)}, u32[]{:S(2)}, u32[]{:S(2)}) collective-permute-start(bf16[3072,128]{1,0:T(8,128)(2,1)} %collective-permute-done.31.refs_6_), channel_id=1, source_target_pairs={{0,1},{1,0},{2,3},{3,2},{4,5},{5,4},{6,7},{7,6},{8,9},{9,8},{10,11... | collective-permute-start | bytes 2359304 | tf_op jit(solution)/shard_map/ppermute | solution.py:930
  144.2 21.0 %collective-permute-start.34 = (bf16[3072,128]{1,0:T(8,128)(2,1)}, bf16[3072,128]{1,0:T(8,128)(2,1)}, u32[]{:S(2)}, u32[]{:S(2)}) collective-permute-start(bf16[3072,128]{1,0:T(8,128)(2,1)} %collective-permute-done.33.refs_8_), channel_id=1, source_target_pairs={{0,1},{1,0},{2,3},{3,2},{4,5},{5,4},{6,7},{7,6},{8,9},{9,8},{10,11... | collective-permute-start | bytes 2359304 | tf_op jit(solution)/shard_map/ppermute | solution.py:930
  145.9 21.3 %collective-permute-start.36 = (bf16[3072,128]{1,0:T(8,128)(2,1)}, bf16[3072,128]{1,0:T(8,128)(2,1)}, u32[]{:S(2)}, u32[]{:S(2)}) collective-permute-start(bf16[3072,128]{1,0:T(8,128)(2,1)} %collective-permute-done.35.refs_10_), channel_id=1, source_target_pairs={{0,1},{1,0},{2,3},{3,2},{4,5},{5,4},{6,7},{7,6},{8,9},{9,8},{10,11... | collective-permute-start | bytes 2359304 | tf_op jit(solution)/shard_map/ppermute | solution.py:930
  148.9 16.8 %collective-permute-start.39 = (bf16[1536,128]{1,0:T(8,128)(2,1)}, bf16[1536,128]{1,0:T(8,128)(2,1)}, u32[]{:S(2)}, u32[]{:S(2)}) collective-permute-start(bf16[1536,128]{1,0:T(8,128)(2,1)} %slice.615), channel_id=1, source_target_pairs={{0,8},{8,16},{16,24},{24,28},{28,20},{20,12},{12,4},{4,0},{1,9},{9... | collective-permute-start | bytes 1179656 | tf_op jit(solution)/shard_map/ppermute | solution.py:668
  150.2 17.0 %collective-permute-start.41 = (bf16[1536,128]{1,0:T(8,128)(2,1)S(1)}, bf16[1536,128]{1,0:T(8,128)(2,1)}, u32[]{:S(2)}, u32[]{:S(2)}) collective-permute-start(bf16[1536,128]{1,0:T(8,128)(2,1)S(1)} %slice.616), channel_id=1, source_target_pairs={{8,0},{16,8},{24,16},{28,24},{20,28},{12,20},{4,12},{0,4},{9,1},{1... | collective-permute-start | bytes 1179656 | tf_op jit(solution)/shard_map/ppermute | solution.py:669
  151.0 16.8 %collective-permute-start.38 = (bf16[3072,128]{1,0:T(8,128)(2,1)}, bf16[3072,128]{1,0:T(8,128)(2,1)}, u32[]{:S(2)}, u32[]{:S(2)}) collective-permute-start(bf16[3072,128]{1,0:T(8,128)(2,1)} %collective-permute-done.37.refs_12_), channel_id=1, source_target_pairs={{0,1},{1,0},{2,3},{3,2},{4,5},{5,4},{6,7},{7,6},{8,9},{9,8},{10,11... | collective-permute-start | bytes 2359304 | tf_op jit(solution)/shard_map/ppermute | solution.py:930
  165.2 12.3 %collective-permute-start.27 = (bf16[200,1024]{1,0:T(8,128)(2,1)S(1)}, bf16[200,1024]{1,0:T(8,128)(2,1)S(1)}, u32[]{:S(2)}, u32[]{:S(2)}) collective-permute-start(bf16[200,1024]{1,0:T(8,128)(2,1)S(1)} %get-tuple-element.209.refs_1_), channel_id=1, source_target_pairs={{0,2},{1,3},{2,0},{3,1},{4,6},{5,7},{6,4},{7,5},{8,10},{9,11},{10,... | collective-permute-start | bytes 1228808 | tf_op jit(solution)/shard_map/ppermute | solution.py:933
  165.7 20.6 %collective-permute-start.44 = (bf16[200,1024]{1,0:T(8,128)(2,1)S(1)}, bf16[200,1024]{1,0:T(8,128)(2,1)S(1)}, u32[]{:S(2)}, u32[]{:S(2)}) collective-permute-start(bf16[200,1024]{1,0:T(8,128)(2,1)S(1)} %get-tuple-element.221.refs_1_), channel_id=1, source_target_pairs={{0,2},{1,3},{2,0},{3,1},{4,6},{5,7},{6,4},{7,5},{8,10},{9,11},{10,... | collective-permute-start | bytes 1228808 | tf_op jit(solution)/shard_map/ppermute | solution.py:933
  180.0 15.1 %collective-permute-start.45 = (bf16[200,1024]{1,0:T(8,128)(2,1)S(1)}, bf16[200,1024]{1,0:T(8,128)(2,1)S(1)}, u32[]{:S(2)}, u32[]{:S(2)}) collective-permute-start(bf16[200,1024]{1,0:T(8,128)(2,1)S(1)} %get-tuple-element.224.own_ref), channel_id=1, source_target_pairs={{0,2},{1,3},{2,0},{3,1},{4,6},{5,7},{6,4},{7,5},{8,10},{9,11},{10,... | collective-permute-start | bytes 1228808 | tf_op jit(solution)/shard_map/ppermute | solution.py:933
  188.8 14.6 %collective-permute-start.46 = (bf16[200,1024]{1,0:T(8,128)(2,1)S(1)}, bf16[200,1024]{1,0:T(8,128)(2,1)S(1)}, u32[]{:S(2)}, u32[]{:S(2)}) collective-permute-start(bf16[200,1024]{1,0:T(8,128)(2,1)S(1)} %get-tuple-element.223.own_ref), channel_id=1, source_target_pairs={{0,2},{1,3},{2,0},{3,1},{4,6},{5,7},{6,4},{7,5},{8,10},{9,11},{10,... | collective-permute-start | bytes 1228808 | tf_op jit(solution)/shard_map/ppermute | solution.py:933
  212.7 12.4 %collective-permute-start.47 = (bf16[200,1024]{1,0:T(8,128)(2,1)S(1)}, bf16[200,1024]{1,0:T(8,128)(2,1)S(1)}, u32[]{:S(2)}, u32[]{:S(2)}) collective-permute-start(bf16[200,1024]{1,0:T(8,128)(2,1)S(1)} %get-tuple-element.236.own_ref), channel_id=1, source_target_pairs={{0,2},{1,3},{2,0},{3,1},{4,6},{5,7},{6,4},{7,5},{8,10},{9,11},{10,... | collective-permute-start | bytes 1228808 | tf_op jit(solution)/shard_map/ppermute | solution.py:933
  218.4 22.5 %collective-permute-start.48 = (bf16[200,1024]{1,0:T(8,128)(2,1)S(1)}, bf16[200,1024]{1,0:T(8,128)(2,1)S(1)}, u32[]{:S(2)}, u32[]{:S(2)}) collective-permute-start(bf16[200,1024]{1,0:T(8,128)(2,1)S(1)} %get-tuple-element.246.own_ref), channel_id=1, source_target_pairs={{0,2},{1,3},{2,0},{3,1},{4,6},{5,7},{6,4},{7,5},{8,10},{9,11},{10,... | collective-permute-start | bytes 1228808 | tf_op jit(solution)/shard_map/ppermute | solution.py:933
  230.1 15.8 %collective-permute-start.49 = (bf16[200,1024]{1,0:T(8,128)(2,1)S(1)}, bf16[200,1024]{1,0:T(8,128)(2,1)S(1)}, u32[]{:S(2)}, u32[]{:S(2)}) collective-permute-start(bf16[200,1024]{1,0:T(8,128)(2,1)S(1)} %get-tuple-element.264.refs_1_), channel_id=1, source_target_pairs={{0,2},{1,3},{2,0},{3,1},{4,6},{5,7},{6,4},{7,5},{8,10},{9,11},{10,... | collective-permute-start | bytes 1228808 | tf_op jit(solution)/shard_map/ppermute | solution.py:933
  256.3 10.4 %collective-permute-start.51 = (bf16[24576,128]{1,0:T(8,128)(2,1)}, bf16[24576,128]{1,0:T(8,128)(2,1)S(1)}, u32[]{:S(2)}, u32[]{:S(2)}) collective-permute-start(bf16[24576,128]{1,0:T(8,128)(2,1)} %get-tuple-element.276), channel_id=1, source_target_pairs={{0,1},{1,0},{2,3},{3,2},{4,5},{5,4},{6,7},{7,6},{8,9},{9,8},{10,11... | collective-permute-start | bytes 18874376 | tf_op jit(solution)/shard_map/ppermute | solution.py:930
  256.5 16.0 %collective-permute-start.56 = (bf16[200,1024]{1,0:T(8,128)(2,1)S(1)}, bf16[200,1024]{1,0:T(8,128)(2,1)S(1)}, u32[]{:S(2)}, u32[]{:S(2)}) collective-permute-start(bf16[200,1024]{1,0:T(8,128)(2,1)S(1)} %get-tuple-element.285.refs_1_), channel_id=1, source_target_pairs={{0,2},{1,3},{2,0},{3,1},{4,6},{5,7},{6,4},{7,5},{8,10},{9,11},{10,... | collective-permute-start | bytes 1228808 | tf_op jit(solution)/shard_map/ppermute | solution.py:933
  258.0 11.1 %collective-permute-start.52 = (bf16[1536,128]{1,0:T(8,128)(2,1)S(1)}, bf16[1536,128]{1,0:T(8,128)(2,1)S(1)}, u32[]{:S(2)}, u32[]{:S(2)}) collective-permute-start(bf16[1536,128]{1,0:T(8,128)(2,1)S(1)} %get-tuple-element.269), channel_id=1, source_target_pairs={{0,8},{8,16},{16,24},{24,28},{28,20},{20,12},{12,4},{4,0},{1,9},{9... | collective-permute-start | bytes 1179656 | tf_op jit(solution)/shard_map/ppermute | solution.py:702
  259.3 10.8 %collective-permute-start.53 = (bf16[1536,128]{1,0:T(8,128)(2,1)S(1)}, bf16[1536,128]{1,0:T(8,128)(2,1)S(1)}, u32[]{:S(2)}, u32[]{:S(2)}) collective-permute-start(bf16[1536,128]{1,0:T(8,128)(2,1)S(1)} %get-tuple-element.270), channel_id=1, source_target_pairs={{8,0},{16,8},{24,16},{28,24},{20,28},{12,20},{4,12},{0,4},{9,1},{1... | collective-permute-start | bytes 1179656 | tf_op jit(solution)/shard_map/ppermute | solution.py:703
  265.7 27.2 %collective-permute-start.57 = (bf16[200,1024]{1,0:T(8,128)(2,1)S(1)}, bf16[200,1024]{1,0:T(8,128)(2,1)S(1)}, u32[]{:S(2)}, u32[]{:S(2)}) collective-permute-start(bf16[200,1024]{1,0:T(8,128)(2,1)S(1)} %get-tuple-element.296.own_ref), channel_id=1, source_target_pairs={{0,2},{1,3},{2,0},{3,1},{4,6},{5,7},{6,4},{7,5},{8,10},{9,11},{10,... | collective-permute-start | bytes 1228808 | tf_op jit(solution)/shard_map/ppermute | solution.py:933
  270.4 18.5 %collective-permute-start.55 = (bf16[3072,128]{1,0:T(8,128)(2,1)S(1)}, bf16[3072,128]{1,0:T(8,128)(2,1)S(1)}, u32[]{:S(2)}, u32[]{:S(2)}) collective-permute-start(bf16[3072,128]{1,0:T(8,128)(2,1)S(1)} %pad_maximum_fusion.1), channel_id=1, source_target_pairs={{8,0},{16,8},{24,16},{28,24},{20,28},{12,20},{4,12},{0,4},{9,1},{1... | collective-permute-start | bytes 2359304 | tf_op jit(solution)/shard_map/ppermute | solution.py:703
  271.1 18.1 %collective-permute-start.54 = (bf16[3072,128]{1,0:T(8,128)(2,1)S(1)}, bf16[3072,128]{1,0:T(8,128)(2,1)S(1)}, u32[]{:S(2)}, u32[]{:S(2)}) collective-permute-start(bf16[3072,128]{1,0:T(8,128)(2,1)S(1)} %pad_maximum_fusion), channel_id=1, source_target_pairs={{0,8},{8,16},{16,24},{24,28},{28,20},{20,12},{12,4},{4,0},{1,9},{9... | collective-permute-start | bytes 2359304 | tf_op jit(solution)/shard_map/ppermute | solution.py:702
  289.9 17.3 %collective-permute-start.60 = (bf16[3072,128]{1,0:T(8,128)(2,1)S(1)}, bf16[3072,128]{1,0:T(8,128)(2,1)S(1)}, u32[]{:S(2)}, u32[]{:S(2)}) collective-permute-start(bf16[3072,128]{1,0:T(8,128)(2,1)S(1)} %get-tuple-element.295), channel_id=1, source_target_pairs={{8,0},{16,8},{24,16},{28,24},{20,28},{12,20},{4,12},{0,4},{9,1},{1... | collective-permute-start | bytes 2359304 | tf_op jit(solution)/shard_map/ppermute | solution.py:703
  290.3 17.6 %collective-permute-start.59 = (bf16[3072,128]{1,0:T(8,128)(2,1)S(1)}, bf16[3072,128]{1,0:T(8,128)(2,1)S(1)}, u32[]{:S(2)}, u32[]{:S(2)}) collective-permute-start(bf16[3072,128]{1,0:T(8,128)(2,1)S(1)} %get-tuple-element.294), channel_id=1, source_target_pairs={{0,8},{8,16},{16,24},{24,28},{28,20},{20,12},{12,4},{4,0},{1,9},{9... | collective-permute-start | bytes 2359304 | tf_op jit(solution)/shard_map/ppermute | solution.py:702
  309.6 16.6 %collective-permute-start.61 = (bf16[3072,128]{1,0:T(8,128)(2,1)}, bf16[3072,128]{1,0:T(8,128)(2,1)}, u32[]{:S(2)}, u32[]{:S(2)}) collective-permute-start(bf16[3072,128]{1,0:T(8,128)(2,1)} %get-tuple-element.313), channel_id=1, source_target_pairs={{0,8},{8,16},{16,24},{24,28},{28,20},{20,12},{12,4},{4,0},{1,9},{9... | collective-permute-start | bytes 2359304 | tf_op jit(solution)/shard_map/ppermute | solution.py:702
  311.1 16.2 %collective-permute-start.62 = (bf16[3072,128]{1,0:T(8,128)(2,1)}, bf16[3072,128]{1,0:T(8,128)(2,1)}, u32[]{:S(2)}, u32[]{:S(2)}) collective-permute-start(bf16[3072,128]{1,0:T(8,128)(2,1)} %get-tuple-element.314), channel_id=1, source_target_pairs={{8,0},{16,8},{24,16},{28,24},{20,28},{12,20},{4,12},{0,4},{9,1},{1... | collective-permute-start | bytes 2359304 | tf_op jit(solution)/shard_map/ppermute | solution.py:703
  329.8 10.5 %collective-permute-start.64 = (bf16[24576,128]{1,0:T(8,128)(2,1)}, bf16[24576,128]{1,0:T(8,128)(2,1)}, u32[]{:S(2)}, u32[]{:S(2)}) collective-permute-start(bf16[24576,128]{1,0:T(8,128)(2,1)} %get-tuple-element.322), channel_id=1, source_target_pairs={{0,1},{1,0},{2,3},{3,2},{4,5},{5,4},{6,7},{7,6},{8,9},{9,8},{10,11... | collective-permute-start | bytes 18874376 | tf_op jit(solution)/shard_map/ppermute | solution.py:930
  331.9 12.3 %collective-permute-start.67 = (bf16[1536,128]{1,0:T(8,128)(2,1)}, bf16[1536,128]{1,0:T(8,128)(2,1)S(1)}, u32[]{:S(2)}, u32[]{:S(2)}) collective-permute-start(bf16[1536,128]{1,0:T(8,128)(2,1)} %get-tuple-element.320), channel_id=1, source_target_pairs={{0,8},{8,16},{16,24},{24,28},{28,20},{20,12},{12,4},{4,0},{1,9},{9... | collective-permute-start | bytes 1179656 | tf_op jit(solution)/shard_map/ppermute | solution.py:702
  333.3 11.7 %collective-permute-start.68 = (bf16[1536,128]{1,0:T(8,128)(2,1)}, bf16[1536,128]{1,0:T(8,128)(2,1)S(1)}, u32[]{:S(2)}, u32[]{:S(2)}) collective-permute-start(bf16[1536,128]{1,0:T(8,128)(2,1)} %get-tuple-element.321), channel_id=1, source_target_pairs={{8,0},{16,8},{24,16},{28,24},{20,28},{12,20},{4,12},{0,4},{9,1},{1... | collective-permute-start | bytes 1179656 | tf_op jit(solution)/shard_map/ppermute | solution.py:703
  348.6 18.1 %collective-permute-start.71 = (bf16[3072,128]{1,0:T(8,128)(2,1)S(1)}, bf16[3072,128]{1,0:T(8,128)(2,1)S(1)}, u32[]{:S(2)}, u32[]{:S(2)}) collective-permute-start(bf16[3072,128]{1,0:T(8,128)(2,1)S(1)} %pad_maximum_fusion.3), channel_id=1, source_target_pairs={{8,0},{16,8},{24,16},{28,24},{20,28},{12,20},{4,12},{0,4},{9,1},{1... | collective-permute-start | bytes 2359304 | tf_op jit(solution)/shard_map/ppermute | solution.py:703
  349.2 18.9 %collective-permute-start.70 = (bf16[3072,128]{1,0:T(8,128)(2,1)S(1)}, bf16[3072,128]{1,0:T(8,128)(2,1)S(1)}, u32[]{:S(2)}, u32[]{:S(2)}) collective-permute-start(bf16[3072,128]{1,0:T(8,128)(2,1)S(1)} %pad_maximum_fusion.2), channel_id=1, source_target_pairs={{0,8},{8,16},{16,24},{24,28},{28,20},{20,12},{12,4},{4,0},{1,9},{9... | collective-permute-start | bytes 2359304 | tf_op jit(solution)/shard_map/ppermute | solution.py:702
  352.9 13.7 %collective-permute-start.66 = (bf16[200,1024]{1,0:T(8,128)(2,1)S(1)}, bf16[200,1024]{1,0:T(8,128)(2,1)S(1)}, u32[]{:S(2)}, u32[]{:S(2)}) collective-permute-start(bf16[200,1024]{1,0:T(8,128)(2,1)S(1)} %broadcast_select_fusion.5), channel_id=1, source_target_pairs={{0,2},{1,3},{2,0},{3,1},{4,6},{5,7},{6,4},{7,5},{8,10},{9,11},{10,... | collective-permute-start | bytes 1228808 | tf_op jit(solution)/shard_map/ppermute | solution.py:933
  354.5 12.1 %collective-permute-start.72 = (f32[8,768]{1,0:T(8,128)S(1)}, f32[8,768]{1,0:T(8,128)S(1)}, u32[]{:S(2)}, u32[]{:S(2)}) collective-permute-start(f32[8,768]{1,0:T(8,128)S(1)} %slice.488), channel_id=1, source_target_pairs={{0,8},{4,12},{8,0},{12,4},{16,24},{20,28},{24,16},{28,20},{1,9},{5... | collective-permute-start | bytes 73736 | tf_op jit(solution)/shard_map/ppermute | solution.py:1154
  354.9 19.3 %collective-permute-start.65 = (bf16[200,1024]{1,0:T(8,128)(2,1)S(1)}, bf16[200,1024]{1,0:T(8,128)(2,1)S(1)}, u32[]{:S(2)}, u32[]{:S(2)}) collective-permute-start(bf16[200,1024]{1,0:T(8,128)(2,1)S(1)} %broadcast_select_fusion.4), channel_id=1, source_target_pairs={{0,2},{1,3},{2,0},{3,1},{4,6},{5,7},{6,4},{7,5},{8,10},{9,11},{10,... | collective-permute-start | bytes 1228808 | tf_op jit(solution)/shard_map/ppermute | solution.py:933
  371.7 19.6 %collective-permute-start.75 = (bf16[3072,128]{1,0:T(8,128)(2,1)}, bf16[3072,128]{1,0:T(8,128)(2,1)}, u32[]{:S(2)}, u32[]{:S(2)}) collective-permute-start(bf16[3072,128]{1,0:T(8,128)(2,1)} %get-tuple-element.343), channel_id=1, source_target_pairs={{8,0},{16,8},{24,16},{28,24},{20,28},{12,20},{4,12},{0,4},{9,1},{1... | collective-permute-start | bytes 2359304 | tf_op jit(solution)/shard_map/ppermute | solution.py:703
  372.8 18.5 %collective-permute-start.74 = (bf16[3072,128]{1,0:T(8,128)(2,1)}, bf16[3072,128]{1,0:T(8,128)(2,1)}, u32[]{:S(2)}, u32[]{:S(2)}) collective-permute-start(bf16[3072,128]{1,0:T(8,128)(2,1)} %get-tuple-element.342), channel_id=1, source_target_pairs={{0,8},{8,16},{16,24},{24,28},{28,20},{20,12},{12,4},{4,0},{1,9},{9... | collective-permute-start | bytes 2359304 | tf_op jit(solution)/shard_map/ppermute | solution.py:702
  377.0 14.3 %collective-permute-start.73 = (f32[4,768]{1,0:T(4,128)S(1)}, f32[4,768]{1,0:T(4,128)S(1)}, u32[]{:S(2)}, u32[]{:S(2)}) collective-permute-start(f32[4,768]{1,0:T(4,128)S(1)} %slice.490), channel_id=1, source_target_pairs={{0,4},{4,0},{8,12},{12,8},{16,20},{20,16},{24,28},{28,24},{1,5},{5... | collective-permute-start | bytes 36872 | tf_op jit(solution)/shard_map/ppermute | solution.py:1154
  394.2 17.3 %collective-permute-start.79 = (bf16[3072,128]{1,0:T(8,128)(2,1)S(1)}, bf16[3072,128]{1,0:T(8,128)(2,1)S(1)}, u32[]{:S(2)}, u32[]{:S(2)}) collective-permute-start(bf16[3072,128]{1,0:T(8,128)(2,1)S(1)} %get-tuple-element.347), channel_id=1, source_target_pairs={{8,0},{16,8},{24,16},{28,24},{20,28},{12,20},{4,12},{0,4},{9,1},{1... | collective-permute-start | bytes 2359304 | tf_op jit(solution)/shard_map/ppermute | solution.py:703
  394.7 17.1 %collective-permute-start.78 = (bf16[3072,128]{1,0:T(8,128)(2,1)S(1)}, bf16[3072,128]{1,0:T(8,128)(2,1)S(1)}, u32[]{:S(2)}, u32[]{:S(2)}) collective-permute-start(bf16[3072,128]{1,0:T(8,128)(2,1)S(1)} %get-tuple-element.346), channel_id=1, source_target_pairs={{0,8},{8,16},{16,24},{24,28},{28,20},{20,12},{12,4},{4,0},{1,9},{9... | collective-permute-start | bytes 2359304 | tf_op jit(solution)/shard_map/ppermute | solution.py:702
  (95 other events, 755.6 us)

commit v5 on v4

--- a/solution.py
+++ b/solution.py
@@ -1125,7 +1125,15 @@
             return own[:unit_len].astype(F32) + got.astype(F32)
 
         pending.unit_of = first_unit
-        pending.step()
+        if layer == 0:
+            backward_bits = mesh_bits()[::-1]
+            small_rows = jnp.take(jnp.concatenate(small_terms, axis=1), by_distance, axis=0)
+            for bit, axis, perm in backward_bits[:per_window]:
+                small_rows = small_rows[:bit] + lax.ppermute(small_rows[bit:], axis, perm)
+            backward_bits = backward_bits[per_window:]
+            pending.step(small_rows)
+        else:
+            pending.step()
         rest = core_swap(after(par, *pending.sent))
         if earlier is not None:
             earlier.up = after(earlier.up, *pending.sent)
@@ -1145,15 +1153,16 @@
     block_output = by_image(final.astype(BF))
     parts = [b[3] for b in back]
     last_part = exchange(after(theirs(parts), rest)).astype(F32)
-    small_rows = jnp.take(jnp.concatenate(small_terms, axis=1), by_distance, axis=0)
     small_rows = after(small_rows, rest)
-    backward_bits = mesh_bits()[::-1]
     local_sum = input_grad = None
     while pending.left > 0:
-        for bit, axis, perm in backward_bits[:per_window]:
-            small_rows = small_rows[:bit] + lax.ppermute(small_rows[bit:], axis, perm)
-        backward_bits = backward_bits[per_window:]
-        pending.step(small_rows)
+        if local_sum is None:
+            pending.step()
+        else:
+            for bit, axis, perm in backward_bits[:per_window]:
+                small_rows = small_rows[:bit] + lax.ppermute(small_rows[bit:], axis, perm)
+            backward_bits = backward_bits[per_window:]
+            pending.step(small_rows)
         early = list(pending.sent)
         if local_sum is None:
             upper = [after(grads, *pending.sent) for grads in reduced[1:]]

time: 455 us -> 488 us (1.073)
  local copies, waits for them, and re-layouts: 46.1 us -> 68.6 us
  other arithmetic: 32.6 us -> 42.5 us
    unnamed x157 -> x225, local copies, waits for them, and re-layouts: 26.5 us -> 48.3 us
    ppermute x16, waiting for transfers between devices: 33.1 us -> 22.9 us  [step(): self.up = lax.ppermute(up, 'wide', self.ahead)]
    ppermute x5, waiting for transfers between devices: 31 us -> 39.3 us  [shards(): small_rows = small_rows[:bit] + lax.ppermute(small_rows[bit:], axis, perm)]
    unnamed x13 -> x12, other arithmetic: 0.1 us -> 5.86 us
  transfers between devices with their start and end apart: 87 -> 87, of which waited for: 52 -> 41; matrix products, arithmetic and copies ran while one was open for 8% -> 10% of each run, Pallas kernels for 22% -> 21%
where the time goes in v5:
time: 488 us; the launch traced here: 480 us
  waiting for transfers between devices  162 us (33%)
  Pallas kernels  127 us (26%)
  starting transfers between devices  71.8 us (15%)
  local copies, waits for them, and re-layouts  68.6 us (14%)
  other arithmetic  42.5 us (9%)
  between operations  7.44 us (2%)
    unnamed x225, local copies, waits for them, and re-layouts  48.3 us
    ppermute x5, waiting for transfers between devices, shards(): small_rows = small_rows[:bit] + lax.ppermute(small_rows[bit:], axis, perm)  39.3 us
    ppermute x15, waiting for transfers between devices, exchange(): return lax.ppermute(part, 'narrow', ACROSS)  37.9 us
    ppermute x16, waiting for transfers between devices, step(): self.up = lax.ppermute(up, 'wide', self.ahead)  22.9 us
    ppermute x16, starting transfers between devices, step(): self.up = lax.ppermute(up, 'wide', self.ahead)  22.8 us
    pallas_call x4, Pallas kernels, call_mlp_backward(): pl.pallas_call(functools.partial(mlp_backward, first), grid=(STEPS,), out...  22.6 us
    pallas_call x4, Pallas kernels, call_attention_backward(): pl.pallas_call(attention_backward, grid=(1,), out_shape=outs + [jax.Shape...  20.5 us
    pallas_call x2, Pallas kernels, call_mlp_grads(): pl.pallas_call(mlp_grads, grid_spec=pltpu.PrefetchScalarGridSpec(num_scal...  20.4 us
  transfers between devices with their start and end apart: 87, of which 41 were waited for; matrix products, arithmetic and copies ran while one was open for 10% of the time, Pallas kernels for 21%

profile of v5, /device:TPU:0, one launch (start us, length us, event | category | flops | bytes accessed | tf_op | source)
XLA Modules:
  0.0 479.7 jit_solution(13188784197409220903)
XLA Ops:
  0.6 2.1 convert.41
  4.3 2.6 collective-permute-start
  19.8 5.3 %collective-permute-done.refs_2_ = bf16[3072,128]{1,0:T(8,128)(2,1)} collective-permute-done((bf16[3072,128]{1,0:T(8,128)(2,1)S(1)}, bf16[3072,128]{1,0:T(8,128)(2,1)}, u32[]{:S(2)}, u32[]{:S(2)}) %collective-permute-start) | collective-permute-done | bytes 786464 | tf_op jit(solution)/shard_map/ppermute | solution.py:668
  32.5 5.0 %collective-permute-done.4 = bf16[200,1024]{1,0:T(8,128)(2,1)} collective-permute-done((bf16[200,1024]{1,0:T(8,128)(2,1)S(1)}, bf16[200,1024]{1,0:T(8,128)(2,1)}, u32[]{:S(2)}, u32[]{:S(2)}) %collective-permute-start.4) | collective-permute-done | bytes 409632 | tf_op jit(solution)/shard_map/ppermute | solution.py:888
  38.7 9.4 %collective-permute-done.11.refs_6_ = bf16[3072,128]{1,0:T(8,128)(2,1)} collective-permute-done((bf16[3072,128]{1,0:T(8,128)(2,1)}, bf16[3072,128]{1,0:T(8,128)(2,1)}, u32[]{:S(2)}, u32[]{:S(2)}) %collective-permute-start.11) | collective-permute-done | bytes 786464 | tf_op jit(solution)/shard_map/ppermute | solution.py:668
  54.4 14.1 %collective-permute-done.6 = bf16[8,768]{1,0:T(8,128)(2,1)S(1)} collective-permute-done((bf16[8,768]{1,0:T(8,128)(2,1)S(1)}, bf16[8,768]{1,0:T(8,128)(2,1)S(1)}, u32[]{:S(2)}, u32[]{:S(2)}) %collective-permute-start.6) | collective-permute-done | bytes 12320 | tf_op jit(solution)/shard_map/ppermute | solution.py:959
  68.5 2.8 collective-permute-start.7
  77.0 7.2 %collective-permute-done.21 = bf16[200,1024]{1,0:T(8,128)(2,1)S(1)} collective-permute-done((bf16[200,1024]{1,0:T(8,128)(2,1)S(1)}, bf16[200,1024]{1,0:T(8,128)(2,1)S(1)}, u32[]{:S(2)}, u32[]{:S(2)}) %collective-permute-start.21) | collective-permute-done | bytes 409632 | tf_op jit(solution)/shard_map/ppermute | solution.py:933
  84.4 2.1 collective-permute-start.24
  89.3 5.2 %assemble.2.refs_3_ = bf16[6144,1024]{1,0:T(8,128)(2,1)S(1)} custom-call(s32[2,192]{1,0:T(2,128)S(1)} %pad_add_fusion.rows, s32[2,192]{1,0:T(2,128)S(1)} %pad_add_fusion.1.cols, bf16[3072,128]{1,0:T(8,128)(2,1)} %bitcast.81, bf16[3072,128]{1,0:T(8,128)(2,1)} %copy-done.64, bf16[3072,128]{1,0:T(8,128)(2,1)} %collective-permute-done.refs_2_, ...), custom_call_target="tpu_custom_call" | custom-call | bytes 128 | tf_op jit(solution)/shard_map/assemble/pallas_call | solution.py:623
  94.6 2.9 attention_forward.4
  97.5 4.6 copy-done
  103.6 2.0 collective-permute-start.31
  107.0 4.6 copy-done.1
  111.6 2.9 attention_forward.5
  117.2 5.0 %mlp_forward.4 = (f32[200,1024]{1,0:T(8,128)S(1)}, bf16[200,1024]{1,0:T(8,128)(2,1)}, bf16[200,2048]{1,0:T(8,128)(2,1)}, bf16[200,2048]{1,0:T(8,128)(2,1)}, bf16...) custom-call(bf16[200,1024]{1,0:T(8,128)(2,1)S(1)} %get-tuple-element.420.refs_0_.hid_ref, ...), custom_call_target="tpu_custom_call", output_to_operand_aliasing={{5}: (4, {})} | custom-call | flops 3355443200 | bytes 12582912 | tf_op jit(solution)/shard_map/mlp_forward/pallas_call | solution.py:211
  122.2 4.6 copy-done.2
  131.7 9.3 %collective-permute-done.43.got_ref = bf16[200,1024]{1,0:T(8,128)(2,1)S(1)} collective-permute-done((bf16[200,1024]{1,0:T(8,128)(2,1)S(1)}, bf16[200,1024]{1,0:T(8,128)(2,1)S(1)}, u32[]{:S(2)}, u32[]{:S(2)}) %collective-permute-start.43) | collective-permute-done | bytes 409632 | tf_op jit(solution)/shard_map/ppermute | solution.py:933
  141.6 5.4 %collective-permute-done.35.refs_10_ = bf16[3072,128]{1,0:T(8,128)(2,1)} collective-permute-done((bf16[3072,128]{1,0:T(8,128)(2,1)}, bf16[3072,128]{1,0:T(8,128)(2,1)}, u32[]{:S(2)}, u32[]{:S(2)}) %collective-permute-start.35) | collective-permute-done | bytes 786464 | tf_op jit(solution)/shard_map/ppermute | solution.py:668
  154.7 4.6 copy-done.3
  160.3 5.0 %mlp_forward.5 = (f32[200,1024]{1,0:T(8,128)S(1)}, bf16[200,1024]{1,0:T(8,128)(2,1)}, bf16[200,2048]{1,0:T(8,128)(2,1)}, bf16[200,2048]{1,0:T(8,128)(2,1)}, bf16...) custom-call(bf16[200,1024]{1,0:T(8,128)(2,1)S(1)} %get-tuple-element.203.refs_0_.hid_ref, ...), custom_call_target="tpu_custom_call", output_to_operand_aliasing={{5}: (4, {})} | custom-call | flops 3355443200 | bytes 12582912 | tf_op jit(solution)/shard_map/mlp_forward/pallas_call | solution.py:211
  165.3 4.6 copy-done.4
  175.4 5.2 %assemble.3.refs_6_ = bf16[6144,1024]{1,0:T(8,128)(2,1)S(1)} custom-call(s32[2,192]{1,0:T(2,128)S(1)} %pad_add_fusion.2.rows, s32[2,192]{1,0:T(2,128)S(1)} %pad_add_fusion.3.cols, bf16[3072,128]{1,0:T(8,128)(2,1)} %bitcast.22.refs_0_, bf16[3072,128]{1,0:T(8,128)(2,1)} %copy-done.67, bf16[3072,128]{1,0:T(8,128)(2,1)} %collective-permute-done.24.refs_2_, ...), custom_call_target="tpu_custom_call" | custom-call | bytes 128 | tf_op jit(solution)/shard_map/assemble/pallas_call | solution.py:623
  182.2 2.5 attention_forward.6
  185.3 5.7 %collective-permute-done.44.refs_2_ = bf16[200,1024]{1,0:T(8,128)(2,1)S(1)} collective-permute-done((bf16[200,1024]{1,0:T(8,128)(2,1)S(1)}, bf16[200,1024]{1,0:T(8,128)(2,1)S(1)}, u32[]{:S(2)}, u32[]{:S(2)}) %collective-permute-start.44) | collective-permute-done | bytes 409632 | tf_op jit(solution)/shard_map/ppermute | solution.py:933
  191.0 2.5 attention_forward.7
  194.1 5.7 %collective-permute-done.45.got_ref = bf16[200,1024]{1,0:T(8,128)(2,1)S(1)} collective-permute-done((bf16[200,1024]{1,0:T(8,128)(2,1)S(1)}, bf16[200,1024]{1,0:T(8,128)(2,1)S(1)}, u32[]{:S(2)}, u32[]{:S(2)}) %collective-permute-start.45) | collective-permute-done | bytes 409632 | tf_op jit(solution)/shard_map/ppermute | solution.py:933
  199.8 4.1 mlp_forward.6
  204.7 3.4 collective-permute-done.46.got_ref
  208.1 4.1 mlp_forward.7
  212.2 5.1 %mlp_backward.4 = (bf16[200,1024]{1,0:T(8,128)(2,1)S(1)}, bf16[200,2048]{1,0:T(8,128)(2,1)S(1)}, bf16[200,1024]{1,0:T(8,128)(2,1)S(1)}, f32[8,1024]{1,0:T(8,128)S(1)}, bf16[6144,1024]{1,0:T(8,128)(2,1)S(1)}) custom-call(bf16[200,1024]{1,0:T(8,128)(2,1)S(1)} %get-tuple-element.419.refs_0_.grad_ref, ...), custom_call_target="tpu_custom_call", output_to_operand_aliasing={{4}: (4, {})} | custom-call | flops 3355443200 | bytes 12582912 | tf_op jit(solution)/shard_map/mlp_backward/pallas_call | solution.py:310
  217.9 5.2 %mlp_backward.5 = (bf16[200,1024]{1,0:T(8,128)(2,1)S(1)}, bf16[200,2048]{1,0:T(8,128)(2,1)S(1)}, bf16[200,1024]{1,0:T(8,128)(2,1)S(1)}, f32[8,1024]{1,0:T(8,128)S(1)}, bf16[6144,1024]{1,0:T(8,128)(2,1)S(1)}) custom-call(bf16[200,1024]{1,0:T(8,128)(2,1)S(1)} %get-tuple-element.418.refs_0_.grad_ref, ...), custom_call_target="tpu_custom_call", output_to_operand_aliasing={{4}: (4, {})} | custom-call | flops 3355443200 | bytes 12582912 | tf_op jit(solution)/shard_map/mlp_backward/pallas_call | solution.py:310
  224.7 5.0 %collective-permute-done.47.got_ref = bf16[200,1024]{1,0:T(8,128)(2,1)S(1)} collective-permute-done((bf16[200,1024]{1,0:T(8,128)(2,1)S(1)}, bf16[200,1024]{1,0:T(8,128)(2,1)S(1)}, u32[]{:S(2)}, u32[]{:S(2)}) %collective-permute-start.47) | collective-permute-done | bytes 409632 | tf_op jit(solution)/shard_map/ppermute | solution.py:933
  229.7 5.1 %attention_backward.4 = (f32[200,1024]{1,0:T(8,128)S(1)}, bf16[200,1024]{1,0:T(8,128)(2,1)S(1)}, bf16[200,1536]{1,0:T(8,128)(2,1)S(1)}, bf16[200,1024]{1,0:T(8,1...) custom-call(bf16[200,1024]{1,0:T(8,128)(2,1)S(1)} %get-tuple-element.419.refs, ...), custom_call_target="tpu_custom_call", output_to_operand_aliasing={{5}: (9, {})} | custom-call | flops 2516582400 | bytes 8388608 | tf_op jit(solution)/shard_map/attention_backward/pallas_call | solution.py:401
  235.4 10.2 %mlp_grads.2 = (bf16[24576,128]{1,0:T(8,128)(2,1)}, bf16[24576,128]{1,0:T(8,128)(2,1)}) custom-call(s32[192]{0:T(256)S(1)} %get-tuple-element.389.slot_own, s32[192]{0:T(256)S(1)} %get-tuple-element.386.slot_par, bf16[200,2048]{1,0:T(8,128)(2,1)S(1)} %get-tuple-element.255.refs_0_, bf16[200,2048]{1,0:T(8,128)(2,1)S(1)} %get-tuple-element.256.refs_1_, ...), custom_call_target="tpu_custom_call" | custom-call | flops 6710886400 | bytes 16777216 | tf_op jit(solution)/shard_map/mlp_grads/pallas_call | solution.py:475
  245.7 5.1 %attention_backward.5 = (f32[200,1024]{1,0:T(8,128)S(1)}, bf16[200,1024]{1,0:T(8,128)(2,1)S(1)}, bf16[200,1536]{1,0:T(8,128)(2,1)S(1)}, bf16[200,1024]{1,0:T(8,1...) custom-call(bf16[200,1024]{1,0:T(8,128)(2,1)S(1)} %get-tuple-element.418.refs, ...), custom_call_target="tpu_custom_call", output_to_operand_aliasing={{5}: (9, {})} | custom-call | flops 2516582400 | bytes 8388608 | tf_op jit(solution)/shard_map/attention_backward/pallas_call | solution.py:401
  250.8 5.2 %attention_grads.2 = (bf16[24576,128]{1,0:T(8,128)(2,1)}, bf16[24576,128]{1,0:T(8,128)(2,1)}) custom-call(s32[192]{0:T(256)S(1)} %copy-done.51, s32[192]{0:T(256)S(1)} %copy-done.49, bf16[200,512]{1,0:T(8,128)(2,1)S(1)} %get-tuple-element.243.refs_0_, ...), custom_call_target="tpu_custom_call", output_to_operand_aliasing={{0}: (14, {}), {1}: (15, {})} | custom-call | flops 1677721600 | bytes 8388608 | tf_op jit(solution)/shard_map/attention_grads/pallas_call | solution.py:553
  257.3 2.3 collective-permute-done.50
  276.6 4.6 copy-done.5
  286.6 5.6 %mlp_backward.6 = (f32[200,1024]{1,0:T(8,128)S(1)}, bf16[200,1024]{1,0:T(8,128)(2,1)S(1)}, bf16[200,2048]{1,0:T(8,128)(2,1)S(1)}, bf16[200,1024]{1,0:T(8,128)(2,...) custom-call(f32[200,1024]{1,0:T(8,128)S(1)} %copy-done.27, ...), custom_call_target="tpu_custom_call", output_to_operand_aliasing={{5}: (8, {})} | custom-call | flops 3355443200 | bytes 12582912 | tf_op jit(solution)/shard_map/mlp_backward/pallas_call | solution.py:310
  292.2 4.6 copy-done.6
  297.3 2.3 convert_add_fusion.4
  303.3 6.8 %mlp_backward.7 = (f32[200,1024]{1,0:T(8,128)S(1)}, bf16[200,1024]{1,0:T(8,128)(2,1)S(1)}, bf16[200,2048]{1,0:T(8,128)(2,1)S(1)}, bf16[200,1024]{1,0:T(8,128)(2,...) custom-call(f32[200,1024]{1,0:T(8,128)S(1)} %copy-done.25, ...), custom_call_target="tpu_custom_call", output_to_operand_aliasing={{5}: (8, {})} | custom-call | flops 3355443200 | bytes 12582912 | tf_op jit(solution)/shard_map/mlp_backward/pallas_call | solution.py:310
  311.8 10.2 %mlp_grads.3 = (bf16[24576,128]{1,0:T(8,128)(2,1)}, bf16[24576,128]{1,0:T(8,128)(2,1)}) custom-call(s32[192]{0:T(256)S(1)} %get-tuple-element.394.slot_own, s32[192]{0:T(256)S(1)} %get-tuple-element.392.slot_par, bf16[200,2048]{1,0:T(8,128)(2,1)S(1)} %copy-done.52, bf16[200,2048]{1,0:T(8,128)(2,1)S(1)} %copy-done.53, ...), custom_call_target="tpu_custom_call" | custom-call | flops 6710886400 | bytes 16777216 | tf_op jit(solution)/shard_map/mlp_grads/pallas_call | solution.py:475
  322.1 2.0 add_convert_fusion.7
  326.6 5.1 %attention_backward.6 = (f32[200,1024]{1,0:T(8,128)S(1)}, bf16[200,1024]{1,0:T(8,128)(2,1)S(1)}, bf16[200,1536]{1,0:T(8,128)(2,1)S(1)}, bf16[200,1024]{1,0:T(8,1...) custom-call(f32[200,1024]{1,0:T(8,128)S(1)} %get-tuple-element.274.grad_ref, ...), custom_call_target="tpu_custom_call", output_to_operand_aliasing={{5}: (9, {})} | custom-call | flops 2516582400 | bytes 8388608 | tf_op jit(solution)/shard_map/attention_backward/pallas_call | solution.py:401
  331.8 5.2 %attention_backward.7 = (f32[200,1024]{1,0:T(8,128)S(1)}, bf16[200,1024]{1,0:T(8,128)(2,1)S(1)}, bf16[200,1536]{1,0:T(8,128)(2,1)S(1)}, bf16[200,1024]{1,0:T(8,1...) custom-call(f32[200,1024]{1,0:T(8,128)S(1)} %get-tuple-element.301.grad_ref, ...), custom_call_target="tpu_custom_call", output_to_operand_aliasing={{5}: (9, {})} | custom-call | flops 2516582400 | bytes 8388608 | tf_op jit(solution)/shard_map/attention_backward/pallas_call | solution.py:401
  337.2 5.4 %collective-permute-done.60 = bf16[3072,128]{1,0:T(8,128)(2,1)S(1)} collective-permute-done((bf16[3072,128]{1,0:T(8,128)(2,1)S(1)}, bf16[3072,128]{1,0:T(8,128)(2,1)S(1)}, u32[]{:S(2)}, u32[]{:S(2)}) %collective-permute-start.60) | collective-permute-done | bytes 786464 | tf_op jit(solution)/shard_map/ppermute | solution.py:703
  343.2 3.1 add_convert_fusion.5
  348.4 5.0 %attention_grads.3 = (bf16[24576,128]{1,0:T(8,128)(2,1)}, bf16[24576,128]{1,0:T(8,128)(2,1)}) custom-call(s32[192]{0:T(256)S(1)} %get-tuple-element.394.slot_own, s32[192]{0:T(256)S(1)} %get-tuple-element.392.slot_par, bf16[200,512]{1,0:T(8,128)(2,1)S(1)} %copy-done.44, ...), custom_call_target="tpu_custom_call", output_to_operand_aliasing={{0}: (14, {}), {1}: (15, {})} | custom-call | flops 1677721600 | bytes 8388608 | tf_op jit(solution)/shard_map/attention_grads/pallas_call | solution.py:553
  355.6 2.4 collective-permute-start.64
  358.0 10.0 %collective-permute-done.64 = f32[16,768]{1,0:T(8,128)S(1)} collective-permute-done((f32[16,768]{1,0:T(8,128)S(1)}, f32[16,768]{1,0:T(8,128)S(1)}, u32[]{:S(2)}, u32[]{:S(2)}) %collective-permute-start.64) | collective-permute-done | bytes 49184 | tf_op jit(solution)/shard_map/ppermute | solution.py:1132
  370.6 2.1 collective-permute-start.69
  372.7 7.6 %collective-permute-done.65 = bf16[24576,128]{1,0:T(8,128)(2,1)S(1)} collective-permute-done((bf16[24576,128]{1,0:T(8,128)(2,1)}, bf16[24576,128]{1,0:T(8,128)(2,1)S(1)}, u32[]{:S(2)}, u32[]{:S(2)}) %collective-permute-start.65) | collective-permute-done | bytes 6291488 | tf_op jit(solution)/shard_map/ppermute | solution.py:930
  384.5 2.2 convert_add_fusion.1.grad1
  390.3 11.8 %collective-permute-done.72 = f32[8,768]{1,0:T(8,128)S(1)} collective-permute-done((f32[8,768]{1,0:T(8,128)S(1)}, f32[8,768]{1,0:T(8,128)S(1)}, u32[]{:S(2)}, u32[]{:S(2)}) %collective-permute-start.72) | collective-permute-done | bytes 24608 | tf_op jit(solution)/shard_map/ppermute | solution.py:1163
  411.0 12.9 %collective-permute-done.73 = f32[4,768]{1,0:T(4,128)S(1)} collective-permute-done((f32[4,768]{1,0:T(4,128)S(1)}, f32[4,768]{1,0:T(4,128)S(1)}, u32[]{:S(2)}, u32[]{:S(2)}) %collective-permute-start.73) | collective-permute-done | bytes 12320 | tf_op jit(solution)/shard_map/ppermute | solution.py:1163
  423.9 2.9 add_convert_fusion
  429.2 3.4 collective-permute-done.76
  435.7 8.1 %collective-permute-done.79 = bf16[3072,128]{1,0:T(8,128)(2,1)S(1)} collective-permute-done((bf16[3072,128]{1,0:T(8,128)(2,1)S(1)}, bf16[3072,128]{1,0:T(8,128)(2,1)S(1)}, u32[]{:S(2)}, u32[]{:S(2)}) %collective-permute-start.79) | collective-permute-done | bytes 786464 | tf_op jit(solution)/shard_map/ppermute | solution.py:703
  444.1 3.6 multiply_reduce_fusion
  455.7 2.4 collective-permute-done.85
  459.4 3.3 collective-permute-done.86
  464.6 13.8 %update.1 = (f32[2,24,128,128]{3,2,1,0:T(8,128)}, f32[2,24,128,128]{3,2,1,0:T(8,128)}, f32[2,24,128,128]{3,2,1,0:T(8,128)}, bf16[2,24,128,128]{3,2,1,0:T(8,128)(2,1)}) custom-call(f32[1]{0:T(128)} %bitcast.65.clip_ref, f32[3072,128]{1,0:T(8,128)} %get-tuple-element.382.grad0, f32[3072,128]{1,0:T(8,128)} %copy-done.57, f32[2,24,128,128]{3,2,1,0:T(8,128)} %left.1, ...), custom_call_target="tpu_custom_call" | custom-call | flops 805306368 | bytes 29884416 | tf_op jit(solution)/shard_map/update/pallas_call | solution.py:850
  (570 shorter events, 138.5 us)
Async XLA Ops:
  3.8 34.8 %collective-permute-start.8 = (bf16[3072,128]{1,0:T(8,128)(2,1)S(1)}, bf16[3072,128]{1,0:T(8,128)(2,1)S(1)}, u32[]{:S(2)}, u32[]{:S(2)}) collective-permute-start(bf16[3072,128]{1,0:T(8,128)(2,1)S(1)} %bitcast.78), channel_id=1, source_target_pairs={{0,1},{1,0},{2,3},{3,2},{4,5},{5,4},{6,7},{7,6},{8,9},{9,8},{10,11... | collective-permute-start | bytes 2359304 | tf_op jit(solution)/shard_map/ppermute | solution.py:930
  4.3 20.8 %collective-permute-start = (bf16[3072,128]{1,0:T(8,128)(2,1)S(1)}, bf16[3072,128]{1,0:T(8,128)(2,1)}, u32[]{:S(2)}, u32[]{:S(2)}) collective-permute-start(bf16[3072,128]{1,0:T(8,128)(2,1)S(1)} %bitcast.79), channel_id=1, source_target_pairs={{0,8},{8,16},{16,24},{24,28},{28,20},{20,12},{12,4},{4,0},{1,9},{9... | collective-permute-start | bytes 2359304 | tf_op jit(solution)/shard_map/ppermute | solution.py:668
  6.9 19.8 %collective-permute-start.1 = (bf16[3072,128]{1,0:T(8,128)(2,1)S(1)}, bf16[3072,128]{1,0:T(8,128)(2,1)}, u32[]{:S(2)}, u32[]{:S(2)}) collective-permute-start(bf16[3072,128]{1,0:T(8,128)(2,1)S(1)} %bitcast.80), channel_id=1, source_target_pairs={{8,0},{16,8},{24,16},{28,24},{20,28},{12,20},{4,12},{0,4},{9,1},{1... | collective-permute-start | bytes 2359304 | tf_op jit(solution)/shard_map/ppermute | solution.py:669
  26.6 10.8 %collective-permute-start.4 = (bf16[200,1024]{1,0:T(8,128)(2,1)S(1)}, bf16[200,1024]{1,0:T(8,128)(2,1)}, u32[]{:S(2)}, u32[]{:S(2)}) collective-permute-start(bf16[200,1024]{1,0:T(8,128)(2,1)S(1)} %reshape.576), channel_id=1, source_target_pairs={{0,2},{1,3},{2,0},{3,1},{4,6},{5,7},{6,4},{7,5},{8,10},{9,11},{10,... | collective-permute-start | bytes 1228808 | tf_op jit(solution)/shard_map/ppermute | solution.py:888
  29.3 18.7 %collective-permute-start.11 = (bf16[3072,128]{1,0:T(8,128)(2,1)}, bf16[3072,128]{1,0:T(8,128)(2,1)}, u32[]{:S(2)}, u32[]{:S(2)}) collective-permute-start(bf16[3072,128]{1,0:T(8,128)(2,1)} %collective-permute-done.refs_2_), channel_id=1, source_target_pairs={{0,8},{8,16},{16,24},{24,28},{28,20},{20,12},{12,4},{4,0},{1,9},{9... | collective-permute-start | bytes 2359304 | tf_op jit(solution)/shard_map/ppermute | solution.py:668
  30.9 18.4 %collective-permute-start.13 = (bf16[3072,128]{1,0:T(8,128)(2,1)}, bf16[3072,128]{1,0:T(8,128)(2,1)}, u32[]{:S(2)}, u32[]{:S(2)}) collective-permute-start(bf16[3072,128]{1,0:T(8,128)(2,1)} %collective-permute-done.1.refs_4_), channel_id=1, source_target_pairs={{8,0},{16,8},{24,16},{28,24},{20,28},{12,20},{4,12},{0,4},{9,1},{1... | collective-permute-start | bytes 2359304 | tf_op jit(solution)/shard_map/ppermute | solution.py:669
  32.5 16.8 %collective-permute-start.9 = (bf16[3072,128]{1,0:T(8,128)(2,1)}, bf16[3072,128]{1,0:T(8,128)(2,1)S(1)}, u32[]{:S(2)}, u32[]{:S(2)}) collective-permute-start(bf16[3072,128]{1,0:T(8,128)(2,1)} %collective-permute-done.refs_2_), channel_id=1, source_target_pairs={{0,1},{1,0},{2,3},{3,2},{4,5},{5,4},{6,7},{7,6},{8,9},{9,8},{10,11... | collective-permute-start | bytes 2359304 | tf_op jit(solution)/shard_map/ppermute | solution.py:930
  37.5 11.8 %collective-permute-start.10 = (bf16[3072,128]{1,0:T(8,128)(2,1)}, bf16[3072,128]{1,0:T(8,128)(2,1)S(1)}, u32[]{:S(2)}, u32[]{:S(2)}) collective-permute-start(bf16[3072,128]{1,0:T(8,128)(2,1)} %collective-permute-done.1.refs_4_), channel_id=1, source_target_pairs={{0,1},{1,0},{2,3},{3,2},{4,5},{5,4},{6,7},{7,6},{8,9},{9,8},{10,11... | collective-permute-start | bytes 2359304 | tf_op jit(solution)/shard_map/ppermute | solution.py:930
  49.3 22.0 %collective-permute-start.15 = (bf16[3072,128]{1,0:T(8,128)(2,1)}, bf16[3072,128]{1,0:T(8,128)(2,1)S(1)}, u32[]{:S(2)}, u32[]{:S(2)}) collective-permute-start(bf16[3072,128]{1,0:T(8,128)(2,1)} %collective-permute-done.11.refs_6_), channel_id=1, source_target_pairs={{0,8},{8,16},{16,24},{24,28},{28,20},{20,12},{12,4},{4,0},{1,9},{9... | collective-permute-start | bytes 2359304 | tf_op jit(solution)/shard_map/ppermute | solution.py:668
  51.0 23.6 %collective-permute-start.17 = (bf16[3072,128]{1,0:T(8,128)(2,1)}, bf16[3072,128]{1,0:T(8,128)(2,1)S(1)}, u32[]{:S(2)}, u32[]{:S(2)}) collective-permute-start(bf16[3072,128]{1,0:T(8,128)(2,1)} %collective-permute-done.13.refs_8_), channel_id=1, source_target_pairs={{8,0},{16,8},{24,16},{28,24},{20,28},{12,20},{4,12},{0,4},{9,1},{1... | collective-permute-start | bytes 2359304 | tf_op jit(solution)/shard_map/ppermute | solution.py:669
  51.5 23.2 %collective-permute-start.12 = (bf16[3072,128]{1,0:T(8,128)(2,1)}, bf16[3072,128]{1,0:T(8,128)(2,1)}, u32[]{:S(2)}, u32[]{:S(2)}) collective-permute-start(bf16[3072,128]{1,0:T(8,128)(2,1)} %collective-permute-done.11.refs_6_), channel_id=1, source_target_pairs={{0,1},{1,0},{2,3},{3,2},{4,5},{5,4},{6,7},{7,6},{8,9},{9,8},{10,11... | collective-permute-start | bytes 2359304 | tf_op jit(solution)/shard_map/ppermute | solution.py:930
  51.5 23.2 %collective-permute-start.14 = (bf16[3072,128]{1,0:T(8,128)(2,1)}, bf16[3072,128]{1,0:T(8,128)(2,1)}, u32[]{:S(2)}, u32[]{:S(2)}) collective-permute-start(bf16[3072,128]{1,0:T(8,128)(2,1)} %collective-permute-done.13.refs_8_), channel_id=1, source_target_pairs={{0,1},{1,0},{2,3},{3,2},{4,5},{5,4},{6,7},{7,6},{8,9},{9,8},{10,11... | collective-permute-start | bytes 2359304 | tf_op jit(solution)/shard_map/ppermute | solution.py:930
  52.8 15.7 %collective-permute-start.6 = (bf16[8,768]{1,0:T(8,128)(2,1)S(1)}, bf16[8,768]{1,0:T(8,128)(2,1)S(1)}, u32[]{:S(2)}, u32[]{:S(2)}) collective-permute-start(bf16[8,768]{1,0:T(8,128)(2,1)S(1)} %pad_maximum_fusion.5), channel_id=1, source_target_pairs={{0,8},{4,12},{8,0},{12,4},{16,24},{20,28},{24,16},{28,20},{1,9},{5... | collective-permute-start | bytes 36872 | tf_op jit(solution)/shard_map/ppermute | solution.py:959
  71.3 15.3 %collective-permute-start.16 = (bf16[3072,128]{1,0:T(8,128)(2,1)S(1)}, bf16[3072,128]{1,0:T(8,128)(2,1)}, u32[]{:S(2)}, u32[]{:S(2)}) collective-permute-start(bf16[3072,128]{1,0:T(8,128)(2,1)S(1)} %collective-permute-done.15.refs_10_), channel_id=1, source_target_pairs={{0,1},{1,0},{2,3},{3,2},{4,5},{5,4},{6,7},{7,6},{8,9},{9,8},{10,11... | collective-permute-start | bytes 2359304 | tf_op jit(solution)/shard_map/ppermute | solution.py:930
  84.4 19.1 %collective-permute-start.24 = (bf16[3072,128]{1,0:T(8,128)(2,1)}, bf16[3072,128]{1,0:T(8,128)(2,1)}, u32[]{:S(2)}, u32[]{:S(2)}) collective-permute-start(bf16[3072,128]{1,0:T(8,128)(2,1)} %bitcast.22.refs_0_), channel_id=1, source_target_pairs={{0,8},{8,16},{16,24},{24,28},{28,20},{20,12},{12,4},{4,0},{1,9},{9... | collective-permute-start | bytes 2359304 | tf_op jit(solution)/shard_map/ppermute | solution.py:668
  86.5 17.1 %collective-permute-start.25 = (bf16[3072,128]{1,0:T(8,128)(2,1)}, bf16[3072,128]{1,0:T(8,128)(2,1)}, u32[]{:S(2)}, u32[]{:S(2)}) collective-permute-start(bf16[3072,128]{1,0:T(8,128)(2,1)} %bitcast.22.refs_0_), channel_id=1, source_target_pairs={{8,0},{16,8},{24,16},{28,24},{20,28},{12,20},{4,12},{0,4},{9,1},{1... | collective-permute-start | bytes 2359304 | tf_op jit(solution)/shard_map/ppermute | solution.py:669
  102.0 12.4 %collective-permute-start.26 = (bf16[200,1024]{1,0:T(8,128)(2,1)S(1)}, bf16[200,1024]{1,0:T(8,128)(2,1)S(1)}, u32[]{:S(2)}, u32[]{:S(2)}) collective-permute-start(bf16[200,1024]{1,0:T(8,128)(2,1)S(1)} %get-tuple-element.206.own_ref), channel_id=1, source_target_pairs={{0,2},{1,3},{2,0},{3,1},{4,6},{5,7},{6,4},{7,5},{8,10},{9,11},{10,... | collective-permute-start | bytes 1228808 | tf_op jit(solution)/shard_map/ppermute | solution.py:933
  103.6 23.2 %collective-permute-start.31 = (bf16[3072,128]{1,0:T(8,128)(2,1)}, bf16[3072,128]{1,0:T(8,128)(2,1)}, u32[]{:S(2)}, u32[]{:S(2)}) collective-permute-start(bf16[3072,128]{1,0:T(8,128)(2,1)} %collective-permute-done.24.refs_2_), channel_id=1, source_target_pairs={{0,8},{8,16},{16,24},{24,28},{28,20},{20,12},{12,4},{4,0},{1,9},{9... | collective-permute-start | bytes 2359304 | tf_op jit(solution)/shard_map/ppermute | solution.py:668
  105.6 21.2 %collective-permute-start.33 = (bf16[3072,128]{1,0:T(8,128)(2,1)}, bf16[3072,128]{1,0:T(8,128)(2,1)}, u32[]{:S(2)}, u32[]{:S(2)}) collective-permute-start(bf16[3072,128]{1,0:T(8,128)(2,1)} %collective-permute-done.25.refs_4_), channel_id=1, source_target_pairs={{8,0},{16,8},{24,16},{28,24},{20,28},{12,20},{4,12},{0,4},{9,1},{1... | collective-permute-start | bytes 2359304 | tf_op jit(solution)/shard_map/ppermute | solution.py:669
  107.0 24.2 %collective-permute-start.28 = (bf16[3072,128]{1,0:T(8,128)(2,1)}, bf16[3072,128]{1,0:T(8,128)(2,1)S(1)}, u32[]{:S(2)}, u32[]{:S(2)}) collective-permute-start(bf16[3072,128]{1,0:T(8,128)(2,1)} %bitcast.22.refs_0_), channel_id=1, source_target_pairs={{0,1},{1,0},{2,3},{3,2},{4,5},{5,4},{6,7},{7,6},{8,9},{9,8},{10,11... | collective-permute-start | bytes 2359304 | tf_op jit(solution)/shard_map/ppermute | solution.py:930
  126.8 20.3 %collective-permute-start.35 = (bf16[3072,128]{1,0:T(8,128)(2,1)}, bf16[3072,128]{1,0:T(8,128)(2,1)}, u32[]{:S(2)}, u32[]{:S(2)}) collective-permute-start(bf16[3072,128]{1,0:T(8,128)(2,1)} %collective-permute-done.31.refs_6_), channel_id=1, source_target_pairs={{0,8},{8,16},{16,24},{24,28},{28,20},{20,12},{12,4},{4,0},{1,9},{9... | collective-permute-start | bytes 2359304 | tf_op jit(solution)/shard_map/ppermute | solution.py:668
  128.8 20.0 %collective-permute-start.37 = (bf16[3072,128]{1,0:T(8,128)(2,1)}, bf16[3072,128]{1,0:T(8,128)(2,1)}, u32[]{:S(2)}, u32[]{:S(2)}) collective-permute-start(bf16[3072,128]{1,0:T(8,128)(2,1)} %collective-permute-done.33.refs_8_), channel_id=1, source_target_pairs={{8,0},{16,8},{24,16},{28,24},{20,28},{12,20},{4,12},{0,4},{9,1},{1... | collective-permute-start | bytes 2359304 | tf_op jit(solution)/shard_map/ppermute | solution.py:669
  129.4 11.6 %collective-permute-start.43 = (bf16[200,1024]{1,0:T(8,128)(2,1)S(1)}, bf16[200,1024]{1,0:T(8,128)(2,1)S(1)}, u32[]{:S(2)}, u32[]{:S(2)}) collective-permute-start(bf16[200,1024]{1,0:T(8,128)(2,1)S(1)} %get-tuple-element.218.own_ref), channel_id=1, source_target_pairs={{0,2},{1,3},{2,0},{3,1},{4,6},{5,7},{6,4},{7,5},{8,10},{9,11},{10,... | collective-permute-start | bytes 1228808 | tf_op jit(solution)/shard_map/ppermute | solution.py:933
  130.6 21.9 %collective-permute-start.29 = (bf16[3072,128]{1,0:T(8,128)(2,1)}, bf16[3072,128]{1,0:T(8,128)(2,1)}, u32[]{:S(2)}, u32[]{:S(2)}) collective-permute-start(bf16[3072,128]{1,0:T(8,128)(2,1)} %collective-permute-done.24.refs_2_), channel_id=1, source_target_pairs={{0,1},{1,0},{2,3},{3,2},{4,5},{5,4},{6,7},{7,6},{8,9},{9,8},{10,11... | collective-permute-start | bytes 2359304 | tf_op jit(solution)/shard_map/ppermute | solution.py:930
  131.2 22.6 %collective-permute-start.30 = (bf16[3072,128]{1,0:T(8,128)(2,1)}, bf16[3072,128]{1,0:T(8,128)(2,1)}, u32[]{:S(2)}, u32[]{:S(2)}) collective-permute-start(bf16[3072,128]{1,0:T(8,128)(2,1)} %collective-permute-done.25.refs_4_), channel_id=1, source_target_pairs={{0,1},{1,0},{2,3},{3,2},{4,5},{5,4},{6,7},{7,6},{8,9},{9,8},{10,11... | collective-permute-start | bytes 2359304 | tf_op jit(solution)/shard_map/ppermute | solution.py:930
  141.0 13.6 %collective-permute-start.32 = (bf16[3072,128]{1,0:T(8,128)(2,1)}, bf16[3072,128]{1,0:T(8,128)(2,1)}, u32[]{:S(2)}, u32[]{:S(2)}) collective-permute-start(bf16[3072,128]{1,0:T(8,128)(2,1)} %collective-permute-done.31.refs_6_), channel_id=1, source_target_pairs={{0,1},{1,0},{2,3},{3,2},{4,5},{5,4},{6,7},{7,6},{8,9},{9,8},{10,11... | collective-permute-start | bytes 2359304 | tf_op jit(solution)/shard_map/ppermute | solution.py:930
  147.0 22.8 %collective-permute-start.34 = (bf16[3072,128]{1,0:T(8,128)(2,1)}, bf16[3072,128]{1,0:T(8,128)(2,1)}, u32[]{:S(2)}, u32[]{:S(2)}) collective-permute-start(bf16[3072,128]{1,0:T(8,128)(2,1)} %collective-permute-done.33.refs_8_), channel_id=1, source_target_pairs={{0,1},{1,0},{2,3},{3,2},{4,5},{5,4},{6,7},{7,6},{8,9},{9,8},{10,11... | collective-permute-start | bytes 2359304 | tf_op jit(solution)/shard_map/ppermute | solution.py:930
  148.8 23.2 %collective-permute-start.36 = (bf16[3072,128]{1,0:T(8,128)(2,1)}, bf16[3072,128]{1,0:T(8,128)(2,1)}, u32[]{:S(2)}, u32[]{:S(2)}) collective-permute-start(bf16[3072,128]{1,0:T(8,128)(2,1)} %collective-permute-done.35.refs_10_), channel_id=1, source_target_pairs={{0,1},{1,0},{2,3},{3,2},{4,5},{5,4},{6,7},{7,6},{8,9},{9,8},{10,11... | collective-permute-start | bytes 2359304 | tf_op jit(solution)/shard_map/ppermute | solution.py:930
  152.6 17.8 %collective-permute-start.39 = (bf16[1536,128]{1,0:T(8,128)(2,1)}, bf16[1536,128]{1,0:T(8,128)(2,1)}, u32[]{:S(2)}, u32[]{:S(2)}) collective-permute-start(bf16[1536,128]{1,0:T(8,128)(2,1)} %slice.615), channel_id=1, source_target_pairs={{0,8},{8,16},{16,24},{24,28},{28,20},{20,12},{12,4},{4,0},{1,9},{9... | collective-permute-start | bytes 1179656 | tf_op jit(solution)/shard_map/ppermute | solution.py:668
  153.8 18.1 %collective-permute-start.41 = (bf16[1536,128]{1,0:T(8,128)(2,1)}, bf16[1536,128]{1,0:T(8,128)(2,1)}, u32[]{:S(2)}, u32[]{:S(2)}) collective-permute-start(bf16[1536,128]{1,0:T(8,128)(2,1)} %slice.616), channel_id=1, source_target_pairs={{8,0},{16,8},{24,16},{28,24},{20,28},{12,20},{4,12},{0,4},{9,1},{1... | collective-permute-start | bytes 1179656 | tf_op jit(solution)/shard_map/ppermute | solution.py:669
  154.6 17.9 %collective-permute-start.38 = (bf16[3072,128]{1,0:T(8,128)(2,1)}, bf16[3072,128]{1,0:T(8,128)(2,1)}, u32[]{:S(2)}, u32[]{:S(2)}) collective-permute-start(bf16[3072,128]{1,0:T(8,128)(2,1)} %collective-permute-done.37.refs_12_), channel_id=1, source_target_pairs={{0,1},{1,0},{2,3},{3,2},{4,5},{5,4},{6,7},{7,6},{8,9},{9,8},{10,11... | collective-permute-start | bytes 2359304 | tf_op jit(solution)/shard_map/ppermute | solution.py:930
  169.9 12.3 %collective-permute-start.27 = (bf16[200,1024]{1,0:T(8,128)(2,1)S(1)}, bf16[200,1024]{1,0:T(8,128)(2,1)S(1)}, u32[]{:S(2)}, u32[]{:S(2)}) collective-permute-start(bf16[200,1024]{1,0:T(8,128)(2,1)S(1)} %get-tuple-element.209.refs_1_), channel_id=1, source_target_pairs={{0,2},{1,3},{2,0},{3,1},{4,6},{5,7},{6,4},{7,5},{8,10},{9,11},{10,... | collective-permute-start | bytes 1228808 | tf_op jit(solution)/shard_map/ppermute | solution.py:933
  170.4 20.6 %collective-permute-start.44 = (bf16[200,1024]{1,0:T(8,128)(2,1)S(1)}, bf16[200,1024]{1,0:T(8,128)(2,1)S(1)}, u32[]{:S(2)}, u32[]{:S(2)}) collective-permute-start(bf16[200,1024]{1,0:T(8,128)(2,1)S(1)} %get-tuple-element.221.refs_1_), channel_id=1, source_target_pairs={{0,2},{1,3},{2,0},{3,1},{4,6},{5,7},{6,4},{7,5},{8,10},{9,11},{10,... | collective-permute-start | bytes 1228808 | tf_op jit(solution)/shard_map/ppermute | solution.py:933
  184.7 15.1 %collective-permute-start.45 = (bf16[200,1024]{1,0:T(8,128)(2,1)S(1)}, bf16[200,1024]{1,0:T(8,128)(2,1)S(1)}, u32[]{:S(2)}, u32[]{:S(2)}) collective-permute-start(bf16[200,1024]{1,0:T(8,128)(2,1)S(1)} %get-tuple-element.224.own_ref), channel_id=1, source_target_pairs={{0,2},{1,3},{2,0},{3,1},{4,6},{5,7},{6,4},{7,5},{8,10},{9,11},{10,... | collective-permute-start | bytes 1228808 | tf_op jit(solution)/shard_map/ppermute | solution.py:933
  193.4 14.6 %collective-permute-start.46 = (bf16[200,1024]{1,0:T(8,128)(2,1)S(1)}, bf16[200,1024]{1,0:T(8,128)(2,1)S(1)}, u32[]{:S(2)}, u32[]{:S(2)}) collective-permute-start(bf16[200,1024]{1,0:T(8,128)(2,1)S(1)} %get-tuple-element.223.own_ref), channel_id=1, source_target_pairs={{0,2},{1,3},{2,0},{3,1},{4,6},{5,7},{6,4},{7,5},{8,10},{9,11},{10,... | collective-permute-start | bytes 1228808 | tf_op jit(solution)/shard_map/ppermute | solution.py:933
  217.3 12.4 %collective-permute-start.47 = (bf16[200,1024]{1,0:T(8,128)(2,1)S(1)}, bf16[200,1024]{1,0:T(8,128)(2,1)S(1)}, u32[]{:S(2)}, u32[]{:S(2)}) collective-permute-start(bf16[200,1024]{1,0:T(8,128)(2,1)S(1)} %get-tuple-element.236.own_ref), channel_id=1, source_target_pairs={{0,2},{1,3},{2,0},{3,1},{4,6},{5,7},{6,4},{7,5},{8,10},{9,11},{10,... | collective-permute-start | bytes 1228808 | tf_op jit(solution)/shard_map/ppermute | solution.py:933
  223.1 22.6 %collective-permute-start.48 = (bf16[200,1024]{1,0:T(8,128)(2,1)S(1)}, bf16[200,1024]{1,0:T(8,128)(2,1)S(1)}, u32[]{:S(2)}, u32[]{:S(2)}) collective-permute-start(bf16[200,1024]{1,0:T(8,128)(2,1)S(1)} %get-tuple-element.246.own_ref), channel_id=1, source_target_pairs={{0,2},{1,3},{2,0},{3,1},{4,6},{5,7},{6,4},{7,5},{8,10},{9,11},{10,... | collective-permute-start | bytes 1228808 | tf_op jit(solution)/shard_map/ppermute | solution.py:933
  234.8 16.0 %collective-permute-start.49 = (bf16[200,1024]{1,0:T(8,128)(2,1)S(1)}, bf16[200,1024]{1,0:T(8,128)(2,1)S(1)}, u32[]{:S(2)}, u32[]{:S(2)}) collective-permute-start(bf16[200,1024]{1,0:T(8,128)(2,1)S(1)} %get-tuple-element.264.refs_1_), channel_id=1, source_target_pairs={{0,2},{1,3},{2,0},{3,1},{4,6},{5,7},{6,4},{7,5},{8,10},{9,11},{10,... | collective-permute-start | bytes 1228808 | tf_op jit(solution)/shard_map/ppermute | solution.py:933
  261.9 35.3 %collective-permute-start.51 = (bf16[24576,128]{1,0:T(8,128)(2,1)}, bf16[24576,128]{1,0:T(8,128)(2,1)}, u32[]{:S(2)}, u32[]{:S(2)}) collective-permute-start(bf16[24576,128]{1,0:T(8,128)(2,1)} %get-tuple-element.276), channel_id=1, source_target_pairs={{0,1},{1,0},{2,3},{3,2},{4,5},{5,4},{6,7},{7,6},{8,9},{9,8},{10,11... | collective-permute-start | bytes 18874376 | tf_op jit(solution)/shard_map/ppermute | solution.py:930
  262.1 40.0 %collective-permute-start.56 = (bf16[200,1024]{1,0:T(8,128)(2,1)}, bf16[200,1024]{1,0:T(8,128)(2,1)}, u32[]{:S(2)}, u32[]{:S(2)}) collective-permute-start(bf16[200,1024]{1,0:T(8,128)(2,1)} %copy-done.32), channel_id=1, source_target_pairs={{0,2},{1,3},{2,0},{3,1},{4,6},{5,7},{6,4},{7,5},{8,10},{9,11},{10,... | collective-permute-start | bytes 1228808 | tf_op jit(solution)/shard_map/ppermute | solution.py:933
  274.5 25.1 %collective-permute-start.52 = (bf16[1536,128]{1,0:T(8,128)(2,1)}, bf16[1536,128]{1,0:T(8,128)(2,1)S(1)}, u32[]{:S(2)}, u32[]{:S(2)}) collective-permute-start(bf16[1536,128]{1,0:T(8,128)(2,1)} %get-tuple-element.269), channel_id=1, source_target_pairs={{0,8},{8,16},{16,24},{24,28},{28,20},{20,12},{12,4},{4,0},{1,9},{9... | collective-permute-start | bytes 1179656 | tf_op jit(solution)/shard_map/ppermute | solution.py:702
  275.8 23.9 %collective-permute-start.53 = (bf16[1536,128]{1,0:T(8,128)(2,1)}, bf16[1536,128]{1,0:T(8,128)(2,1)S(1)}, u32[]{:S(2)}, u32[]{:S(2)}) collective-permute-start(bf16[1536,128]{1,0:T(8,128)(2,1)} %get-tuple-element.270), channel_id=1, source_target_pairs={{8,0},{16,8},{24,16},{28,24},{20,28},{12,20},{4,12},{0,4},{9,1},{1... | collective-permute-start | bytes 1179656 | tf_op jit(solution)/shard_map/ppermute | solution.py:703
  296.8 29.8 %collective-permute-start.57 = (bf16[200,1024]{1,0:T(8,128)(2,1)S(1)}, bf16[200,1024]{1,0:T(8,128)(2,1)S(1)}, u32[]{:S(2)}, u32[]{:S(2)}) collective-permute-start(bf16[200,1024]{1,0:T(8,128)(2,1)S(1)} %get-tuple-element.296.own_ref), channel_id=1, source_target_pairs={{0,2},{1,3},{2,0},{3,1},{4,6},{5,7},{6,4},{7,5},{8,10},{9,11},{10,... | collective-permute-start | bytes 1228808 | tf_op jit(solution)/shard_map/ppermute | solution.py:933
  300.0 22.0 %collective-permute-start.55 = (bf16[3072,128]{1,0:T(8,128)(2,1)S(1)}, bf16[3072,128]{1,0:T(8,128)(2,1)S(1)}, u32[]{:S(2)}, u32[]{:S(2)}) collective-permute-start(bf16[3072,128]{1,0:T(8,128)(2,1)S(1)} %pad_maximum_fusion.1), channel_id=1, source_target_pairs={{8,0},{16,8},{24,16},{28,24},{20,28},{12,20},{4,12},{0,4},{9,1},{1... | collective-permute-start | bytes 2359304 | tf_op jit(solution)/shard_map/ppermute | solution.py:703
  300.5 21.5 %collective-permute-start.54 = (bf16[3072,128]{1,0:T(8,128)(2,1)S(1)}, bf16[3072,128]{1,0:T(8,128)(2,1)S(1)}, u32[]{:S(2)}, u32[]{:S(2)}) collective-permute-start(bf16[3072,128]{1,0:T(8,128)(2,1)S(1)} %pad_maximum_fusion), channel_id=1, source_target_pairs={{0,8},{8,16},{16,24},{24,28},{28,20},{20,12},{12,4},{4,0},{1,9},{9... | collective-permute-start | bytes 2359304 | tf_op jit(solution)/shard_map/ppermute | solution.py:702
  310.1 21.6 %collective-permute-start.58 = (bf16[200,1024]{1,0:T(8,128)(2,1)S(1)}, bf16[200,1024]{1,0:T(8,128)(2,1)S(1)}, u32[]{:S(2)}, u32[]{:S(2)}) collective-permute-start(bf16[200,1024]{1,0:T(8,128)(2,1)S(1)} %get-tuple-element.303.own_ref), channel_id=1, source_target_pairs={{0,2},{1,3},{2,0},{3,1},{4,6},{5,7},{6,4},{7,5},{8,10},{9,11},{10,... | collective-permute-start | bytes 1228808 | tf_op jit(solution)/shard_map/ppermute | solution.py:933
  324.1 18.5 %collective-permute-start.60 = (bf16[3072,128]{1,0:T(8,128)(2,1)S(1)}, bf16[3072,128]{1,0:T(8,128)(2,1)S(1)}, u32[]{:S(2)}, u32[]{:S(2)}) collective-permute-start(bf16[3072,128]{1,0:T(8,128)(2,1)S(1)} %get-tuple-element.295), channel_id=1, source_target_pairs={{8,0},{16,8},{24,16},{28,24},{20,28},{12,20},{4,12},{0,4},{9,1},{1... | collective-permute-start | bytes 2359304 | tf_op jit(solution)/shard_map/ppermute | solution.py:703
  324.6 18.6 %collective-permute-start.59 = (bf16[3072,128]{1,0:T(8,128)(2,1)S(1)}, bf16[3072,128]{1,0:T(8,128)(2,1)S(1)}, u32[]{:S(2)}, u32[]{:S(2)}) collective-permute-start(bf16[3072,128]{1,0:T(8,128)(2,1)S(1)} %get-tuple-element.294), channel_id=1, source_target_pairs={{0,8},{8,16},{16,24},{24,28},{28,20},{20,12},{12,4},{4,0},{1,9},{9... | collective-permute-start | bytes 2359304 | tf_op jit(solution)/shard_map/ppermute | solution.py:702
  346.3 21.7 %collective-permute-start.61 = (bf16[3072,128]{1,0:T(8,128)(2,1)}, bf16[3072,128]{1,0:T(8,128)(2,1)}, u32[]{:S(2)}, u32[]{:S(2)}) collective-permute-start(bf16[3072,128]{1,0:T(8,128)(2,1)} %get-tuple-element.313), channel_id=1, source_target_pairs={{0,8},{8,16},{16,24},{24,28},{28,20},{20,12},{12,4},{4,0},{1,9},{9... | collective-permute-start | bytes 2359304 | tf_op jit(solution)/shard_map/ppermute | solution.py:702
  347.9 20.1 %collective-permute-start.62 = (bf16[3072,128]{1,0:T(8,128)(2,1)}, bf16[3072,128]{1,0:T(8,128)(2,1)}, u32[]{:S(2)}, u32[]{:S(2)}) collective-permute-start(bf16[3072,128]{1,0:T(8,128)(2,1)} %get-tuple-element.314), channel_id=1, source_target_pairs={{8,0},{16,8},{24,16},{28,24},{20,28},{12,20},{4,12},{0,4},{9,1},{1... | collective-permute-start | bytes 2359304 | tf_op jit(solution)/shard_map/ppermute | solution.py:703
  354.6 13.5 %collective-permute-start.63 = (bf16[3072,128]{1,0:T(8,128)(2,1)S(1)}, bf16[3072,128]{1,0:T(8,128)(2,1)}, u32[]{:S(2)}, u32[]{:S(2)}) collective-permute-start(bf16[3072,128]{1,0:T(8,128)(2,1)S(1)} %slice.432), channel_id=1, source_target_pairs={{0,1},{1,0},{2,3},{3,2},{4,5},{5,4},{6,7},{7,6},{8,9},{9,8},{10,11... | collective-permute-start | bytes 2359304 | tf_op jit(solution)/shard_map/ppermute | solution.py:930
  355.6 12.5 %collective-permute-start.64 = (f32[16,768]{1,0:T(8,128)S(1)}, f32[16,768]{1,0:T(8,128)S(1)}, u32[]{:S(2)}, u32[]{:S(2)}) collective-permute-start(f32[16,768]{1,0:T(8,128)S(1)} %slice.652), channel_id=1, source_target_pairs={{0,16},{4,20},{8,24},{12,28},{16,0},{20,4},{24,8},{28,12},{1,17},{... | collective-permute-start | bytes 147464 | tf_op jit(solution)/shard_map/ppermute | solution.py:1132
  370.5 11.6 %collective-permute-start.68 = (bf16[1536,128]{1,0:T(8,128)(2,1)S(1)}, bf16[1536,128]{1,0:T(8,128)(2,1)S(1)}, u32[]{:S(2)}, u32[]{:S(2)}) collective-permute-start(bf16[1536,128]{1,0:T(8,128)(2,1)S(1)} %get-tuple-element.328), channel_id=1, source_target_pairs={{0,8},{8,16},{16,24},{24,28},{28,20},{20,12},{12,4},{4,0},{1,9},{9... | collective-permute-start | bytes 1179656 | tf_op jit(solution)/shard_map/ppermute | solution.py:702
  370.6 11.7 %collective-permute-start.69 = (bf16[1536,128]{1,0:T(8,128)(2,1)S(1)}, bf16[1536,128]{1,0:T(8,128)(2,1)S(1)}, u32[]{:S(2)}, u32[]{:S(2)}) collective-permute-start(bf16[1536,128]{1,0:T(8,128)(2,1)S(1)} %get-tuple-element.329), channel_id=1, source_target_pairs={{8,0},{16,8},{24,16},{28,24},{20,28},{12,20},{4,12},{0,4},{9,1},{1... | collective-permute-start | bytes 1179656 | tf_op jit(solution)/shard_map/ppermute | solution.py:703
  382.5 19.8 %collective-permute-start.71 = (bf16[3072,128]{1,0:T(8,128)(2,1)S(1)}, bf16[3072,128]{1,0:T(8,128)(2,1)S(1)}, u32[]{:S(2)}, u32[]{:S(2)}) collective-permute-start(bf16[3072,128]{1,0:T(8,128)(2,1)S(1)} %pad_maximum_fusion.3), channel_id=1, source_target_pairs={{8,0},{16,8},{24,16},{28,24},{20,28},{12,20},{4,12},{0,4},{9,1},{1... | collective-permute-start | bytes 2359304 | tf_op jit(solution)/shard_map/ppermute | solution.py:703
  384.2 18.5 %collective-permute-start.70 = (bf16[3072,128]{1,0:T(8,128)(2,1)S(1)}, bf16[3072,128]{1,0:T(8,128)(2,1)S(1)}, u32[]{:S(2)}, u32[]{:S(2)}) collective-permute-start(bf16[3072,128]{1,0:T(8,128)(2,1)S(1)} %pad_maximum_fusion.2), channel_id=1, source_target_pairs={{0,8},{8,16},{16,24},{24,28},{28,20},{20,12},{12,4},{4,0},{1,9},{9... | collective-permute-start | bytes 2359304 | tf_op jit(solution)/shard_map/ppermute | solution.py:702
  386.8 15.4 %collective-permute-start.67 = (bf16[200,1024]{1,0:T(8,128)(2,1)S(1)}, bf16[200,1024]{1,0:T(8,128)(2,1)S(1)}, u32[]{:S(2)}, u32[]{:S(2)}) collective-permute-start(bf16[200,1024]{1,0:T(8,128)(2,1)S(1)} %broadcast_select_fusion.5), channel_id=1, source_target_pairs={{0,2},{1,3},{2,0},{3,1},{4,6},{5,7},{6,4},{7,5},{8,10},{9,11},{10,... | collective-permute-start | bytes 1228808 | tf_op jit(solution)/shard_map/ppermute | solution.py:933
  388.1 14.1 %collective-permute-start.72 = (f32[8,768]{1,0:T(8,128)S(1)}, f32[8,768]{1,0:T(8,128)S(1)}, u32[]{:S(2)}, u32[]{:S(2)}) collective-permute-start(f32[8,768]{1,0:T(8,128)S(1)} %slice.488), channel_id=1, source_target_pairs={{0,8},{4,12},{8,0},{12,4},{16,24},{20,28},{24,16},{28,20},{1,9},{5... | collective-permute-start | bytes 73736 | tf_op jit(solution)/shard_map/ppermute | solution.py:1163
  388.5 18.5 %collective-permute-start.66 = (bf16[200,1024]{1,0:T(8,128)(2,1)S(1)}, bf16[200,1024]{1,0:T(8,128)(2,1)S(1)}, u32[]{:S(2)}, u32[]{:S(2)}) collective-permute-start(bf16[200,1024]{1,0:T(8,128)(2,1)S(1)} %broadcast_select_fusion.4), channel_id=1, source_target_pairs={{0,2},{1,3},{2,0},{3,1},{4,6},{5,7},{6,4},{7,5},{8,10},{9,11},{10,... | collective-permute-start | bytes 1228808 | tf_op jit(solution)/shard_map/ppermute | solution.py:933
  404.4 19.4 %collective-permute-start.75 = (bf16[3072,128]{1,0:T(8,128)(2,1)}, bf16[3072,128]{1,0:T(8,128)(2,1)}, u32[]{:S(2)}, u32[]{:S(2)}) collective-permute-start(bf16[3072,128]{1,0:T(8,128)(2,1)} %get-tuple-element.343), channel_id=1, source_target_pairs={{8,0},{16,8},{24,16},{28,24},{20,28},{12,20},{4,12},{0,4},{9,1},{1... | collective-permute-start | bytes 2359304 | tf_op jit(solution)/shard_map/ppermute | solution.py:703
  405.7 18.2 %collective-permute-start.74 = (bf16[3072,128]{1,0:T(8,128)(2,1)}, bf16[3072,128]{1,0:T(8,128)(2,1)}, u32[]{:S(2)}, u32[]{:S(2)}) collective-permute-start(bf16[3072,128]{1,0:T(8,128)(2,1)} %get-tuple-element.342), channel_id=1, source_target_pairs={{0,8},{8,16},{16,24},{24,28},{28,20},{20,12},{12,4},{4,0},{1,9},{9... | collective-permute-start | bytes 2359304 | tf_op jit(solution)/shard_map/ppermute | solution.py:702
  409.8 14.1 %collective-permute-start.73 = (f32[4,768]{1,0:T(4,128)S(1)}, f32[4,768]{1,0:T(4,128)S(1)}, u32[]{:S(2)}, u32[]{:S(2)}) collective-permute-start(f32[4,768]{1,0:T(4,128)S(1)} %slice.490), channel_id=1, source_target_pairs={{0,4},{4,0},{8,12},{12,8},{16,20},{20,16},{24,28},{28,24},{1,5},{5... | collective-permute-start | bytes 36872 | tf_op jit(solution)/shard_map/ppermute | solution.py:1163
  426.8 17.0 %collective-permute-start.79 = (bf16[3072,128]{1,0:T(8,128)(2,1)S(1)}, bf16[3072,128]{1,0:T(8,128)(2,1)S(1)}, u32[]{:S(2)}, u32[]{:S(2)}) collective-permute-start(bf16[3072,128]{1,0:T(8,128)(2,1)S(1)} %get-tuple-element.347), channel_id=1, source_target_pairs={{8,0},{16,8},{24,16},{28,24},{20,28},{12,20},{4,12},{0,4},{9,1},{1... | collective-permute-start | bytes 2359304 | tf_op jit(solution)/shard_map/ppermute | solution.py:703
  427.3 16.8 %collective-permute-start.78 = (bf16[3072,128]{1,0:T(8,128)(2,1)S(1)}, bf16[3072,128]{1,0:T(8,128)(2,1)S(1)}, u32[]{:S(2)}, u32[]{:S(2)}) collective-permute-start(bf16[3072,128]{1,0:T(8,128)(2,1)S(1)} %get-tuple-element.346), channel_id=1, source_target_pairs={{0,8},{8,16},{16,24},{24,28},{28,20},{20,12},{12,4},{4,0},{1,9},{9... | collective-permute-start | bytes 2359304 | tf_op jit(solution)/shard_map/ppermute | solution.py:702
  (129 other events, 1713.4 us)
